TPU v7x, 32 devices: a whole 2x2x4 slice. The times are simulated.
32 devices in a mesh: rows: 8 (over z, x), heads: 4 (over y, core).
Axes of the slice: x: 2, y: 2, z: 4, core: 2. Of those that a mesh axis runs over, the one named last changes fastest.
Arguments:
- patches: float32 [16384, 48], P(('rows', 'heads')), may hold values from -6 to 6
- segments: int32 [16384], P('rows'), may hold values from 0 to 3, as said below
- labels: int32 [64, 4], P(('rows', 'heads')), may hold values from 0 to 999
- w_in: bfloat16 [48, 768], replicated, may hold values from -0.875 to 0.875
- b_in: float32 [768], replicated, may hold values from -3 to 3
- pos_table: bfloat16 [256, 768], replicated, may hold values from -3 to 3
- cls_table: bfloat16 [1000, 768], replicated, may hold values from -3 to 3
- ln1_gain: float32 [1, 768], replicated, may hold values from 0.1 to 1.9
- ln1_bias: float32 [1, 768], replicated, may hold values from -2 to 2
- w_query: bfloat16 [1, 768, 768], P(None, None, 'heads'), may hold values from -0.21875 to 0.21875
- w_key: bfloat16 [1, 768, 768], P(None, None, 'heads'), may hold values from -0.21875 to 0.21875
- w_value: bfloat16 [1, 768, 768], P(None, None, 'heads'), may hold values from -0.21875 to 0.21875
- w_attn_out: bfloat16 [1, 768, 768], P(None, 'heads'), may hold values from -1.25 to 1.25
- ln2_gain: float32 [1, 768], replicated, may hold values from 0.1 to 1.9
- ln2_bias: float32 [1, 768], replicated, may hold values from -2 to 2
- w_up: bfloat16 [1, 768, 3072], P(None, None, 'heads'), may hold values from -0.21875 to 0.21875
- b_up: bfloat16 [1, 3072], P(None, 'heads'), may hold values from -3 to 3
- w_down: bfloat16 [1, 3072, 768], P(None, 'heads'), may hold values from -0.109375 to 0.109375
- b_down: float32 [1, 768], replicated, may hold values from -3 to 3
- w_out: bfloat16 [768, 96], replicated, may hold values from -0.02734375 to 0.02734375
- b_out: float32 [96], replicated, may hold values from -2 to 2
- latent_grad: float32 [16384, 48], P(('rows', 'heads')), may hold values from -6 to 6
- logdet_grad: float32 [16384], P(('rows', 'heads')), may hold values from -6 to 6
Outputs:
- latents: float32 [16384, 48], P(('rows', 'heads'))
- logdet: float32 [16384], P(('rows', 'heads'))
- patches_grad: float32 [16384, 48], P(('rows', 'heads'))
- scale_mean: float32 [64], P(('rows', 'heads'))
- scale_max: float32 [64], P(('rows', 'heads'))
- w_in_grad: float32 [48, 768], replicated
- b_in_grad: float32 [768], replicated
- pos_table_grad: float32 [256, 768], replicated
- cls_table_grad: float32 [1000, 768], replicated
- ln1_gain_grad: float32 [1, 768], replicated
- ln1_bias_grad: float32 [1, 768], replicated
- w_query_grad: float32 [1, 768, 768], P(None, None, 'heads')
- w_key_grad: float32 [1, 768, 768], P(None, None, 'heads')
- w_value_grad: float32 [1, 768, 768], P(None, None, 'heads')
- w_attn_out_grad: float32 [1, 768, 768], P(None, 'heads')
- ln2_gain_grad: float32 [1, 768], replicated
- ln2_bias_grad: float32 [1, 768], replicated
- w_up_grad: float32 [1, 768, 3072], P(None, None, 'heads')
- b_up_grad: float32 [1, 3072], P(None, 'heads')
- w_down_grad: float32 [1, 3072, 768], P(None, 'heads')
- b_down_grad: float32 [1, 768], replicated
- w_out_grad: float32 [768, 96], replicated
- b_out_grad: float32 [96], replicated
Inputs may be any that keep to these rules, and one draw needn't show every extreme that they name: Each row of 256 patches is either one segment numbered 0, or 4 segments of 64 patches numbered 0 to 3 in order; the first row is of the second kind.
All inputs are finite; a program needn't handle non-finite values.
Results may differ from a plain program's by a relative error of at most 0.034.
Values may be sent and summed in bfloat16 or wider, within the bound.
No kernel may reach another device: no remote copies, remote signals or barrier semaphores. Data moves between devices by JAX's collectives and lax.ppermute only.
A program may use at most 128 MiB of HBM per device.

v0:
```python
import jax
import jax.numpy as jnp
from jax import lax
from jax.sharding import PartitionSpec as P

HEAD_DIM = 64


EPSILON = 1e-05
PRECISE = lax.Precision.HIGHEST


def norm_rows(values, gains, offset):
    average = jnp.mean(values, -1, keepdims=True)
    centered = values - average
    spread = jnp.mean(centered * centered, -1, keepdims=True)
    return centered * lax.rsqrt(spread + EPSILON) * gains + offset


def gelu_exact(values):
    return jax.nn.gelu(values, approximate=False)


def matmul(matrix, other):
    return jnp.dot(matrix, other, preferred_element_type=jnp.float32)


def matmul_tn(matrix, other):
    return lax.dot_general(
        matrix, other, (((0,), (0,)), ((), ())), preferred_element_type=jnp.float32
    )


def matmul_nt(matrix, other):
    return lax.dot_general(
        matrix, other, (((1,), (1,)), ((), ())), preferred_element_type=jnp.float32
    )


def masked_scores(queries, key_rows, seg_block):
    length = seg_block.shape[-1]
    causal = lax.broadcasted_iota(jnp.int32, (length, length), 0) >= lax.broadcasted_iota(
        jnp.int32, (length, length), 1
    )
    allowed = (seg_block[:, :, None] == seg_block[:, None, :]) & causal[None]
    scores = jnp.einsum("bqhe,bkhe->bhqk", queries, key_rows, preferred_element_type=jnp.float32)
    return jnp.where(allowed[:, None], scores * HEAD_DIM ** (-0.5), -1e30)


def attend_forward(pieces):
    queries, key_rows, values, seg_block = pieces
    scores = masked_scores(queries, key_rows, seg_block)
    row_top = jnp.max(scores, -1, keepdims=True)
    denominator = jnp.sum(jnp.exp(scores - row_top), -1, keepdims=True)
    log_total = row_top + jnp.log(denominator)
    probs = jnp.exp(scores - log_total).astype(jnp.bfloat16)
    result = jnp.einsum("bhqk,bkhe->bqhe", probs, values, preferred_element_type=jnp.float32)
    return (result.astype(jnp.bfloat16), log_total)


def attend_backward(pieces):
    queries, key_rows, values, seg_block, log_total, grad_result = pieces
    scores = masked_scores(queries, key_rows, seg_block)
    probs = jnp.exp(scores - log_total)
    grad_probs = jnp.einsum(
        "bqhe,bkhe->bhqk", grad_result, values, preferred_element_type=jnp.float32
    )
    inner_sum = jnp.sum(probs * grad_probs, -1, keepdims=True)
    grad_scores = (probs * (grad_probs - inner_sum) * HEAD_DIM ** (-0.5)).astype(jnp.bfloat16)
    grad_query = jnp.einsum(
        "bhqk,bkhe->bqhe", grad_scores, key_rows, preferred_element_type=jnp.float32
    )
    grad_key = jnp.einsum(
        "bhqk,bqhe->bkhe", grad_scores, queries, preferred_element_type=jnp.float32
    )
    grad_value = jnp.einsum(
        "bhqk,bqhe->bkhe",
        probs.astype(jnp.bfloat16),
        grad_result,
        preferred_element_type=jnp.float32,
    )
    return (
        grad_query.astype(jnp.bfloat16),
        grad_key.astype(jnp.bfloat16),
        grad_value.astype(jnp.bfloat16),
    )


def per_device(
    patches,
    segments,
    labels,
    w_in,
    b_in,
    pos_table,
    cls_table,
    ln1_gain,
    ln1_bias,
    w_query,
    w_key,
    w_value,
    w_attn_out,
    ln2_gain,
    ln2_bias,
    w_up,
    b_up,
    w_down,
    b_down,
    w_out,
    b_out,
    latent_grad,
    logdet_grad,
):
    tokens_here = patches.shape[0]
    length = pos_table.shape[0]
    slot_count = labels.shape[1]
    channels = patches.shape[1]
    classes = cls_table.shape[0]
    width = pos_table.shape[1]
    heads_here = w_query.shape[2] // HEAD_DIM
    layers = w_query.shape[0]
    own_start = lax.axis_index("heads") * tokens_here
    own_segs = lax.dynamic_slice_in_dim(segments, own_start, tokens_here)
    seg_rows = own_segs.reshape(-1, length)
    row_count = seg_rows.shape[0]
    causal = lax.broadcasted_iota(jnp.int32, (length, length), 0) >= lax.broadcasted_iota(
        jnp.int32, (length, length), 1
    )
    matching = (seg_rows[:, :, None] == seg_rows[:, None, :]) & causal[None]
    position = (jnp.sum(matching.astype(jnp.int32), -1) - 1).reshape(-1)
    slot_ids = lax.broadcasted_iota(jnp.int32, (1, 1, slot_count), 2)
    token_label = jnp.sum(
        jnp.where(seg_rows[:, :, None] == slot_ids, labels[:, None, :], 0), -1
    ).reshape(-1)
    pos_onehot = (position[:, None] == lax.broadcasted_iota(jnp.int32, (1, length), 1)).astype(
        jnp.bfloat16
    )
    cls_onehot = (token_label[:, None] == lax.broadcasted_iota(jnp.int32, (1, classes), 1)).astype(
        jnp.bfloat16
    )
    patch_low = patches.astype(jnp.bfloat16)
    hidden = (
        matmul(patch_low, w_in)
        + b_in
        + matmul(pos_onehot, pos_table)
        + matmul(cls_onehot, cls_table)
    )
    group_rows = segments.shape[0] // length
    blocks = group_rows // 2
    seg_blocks = segments.reshape(blocks, 2, length)

    def to_blocks(matrix):
        return matrix.reshape(blocks, 2, length, heads_here, HEAD_DIM)

    def from_blocks(tensor):
        return tensor.reshape(group_rows * length, heads_here * HEAD_DIM)

    depth = 0
    normed1 = norm_rows(hidden, ln1_gain[depth], ln1_bias[depth]).astype(jnp.bfloat16)
    rows_norm = lax.all_gather(normed1, "heads", axis=0, tiled=True)
    queries = matmul(rows_norm, w_query[depth]).astype(jnp.bfloat16)
    key_rows = matmul(rows_norm, w_key[depth]).astype(jnp.bfloat16)
    values = matmul(rows_norm, w_value[depth]).astype(jnp.bfloat16)
    attended, log_total = lax.map(
        attend_forward, (to_blocks(queries), to_blocks(key_rows), to_blocks(values), seg_blocks)
    )
    attended = from_blocks(attended)
    weight_out = w_attn_out[depth]
    attn_mix = lax.psum_scatter(
        matmul(attended, weight_out).astype(jnp.bfloat16), "heads", scatter_dimension=0, tiled=True
    ).astype(jnp.float32)
    hidden1 = hidden + attn_mix
    normed2 = norm_rows(hidden1, ln2_gain[depth], ln2_bias[depth]).astype(jnp.bfloat16)
    mlp_input = lax.all_gather(normed2, "heads", axis=0, tiled=True)
    full_up = w_up[depth]
    full_bias = b_up[depth]
    full_down = w_down[depth]
    pre_act = matmul(mlp_input, full_up) + full_bias.astype(jnp.float32)
    activated = gelu_exact(pre_act).astype(jnp.bfloat16)
    branch = lax.psum_scatter(
        matmul(activated, full_down).astype(jnp.bfloat16), "heads", scatter_dimension=0, tiled=True
    ).astype(jnp.float32)
    hidden2 = hidden1 + branch + b_down[depth]
    stored = [
        (
            hidden,
            rows_norm,
            queries,
            key_rows,
            values,
            attended,
            log_total,
            hidden1,
            mlp_input,
            pre_act,
            activated,
            full_up,
            full_down,
        )
    ]
    top_low = hidden2.astype(jnp.bfloat16)
    head_out = matmul(top_low, w_out) + b_out
    carried = jnp.concatenate(
        [jnp.zeros((row_count, 1), dtype=bool), seg_rows[:, 1:] == seg_rows[:, :-1]], 1
    ).reshape(-1)

    def flow_head(head_vals, patch_vals):
        previous = jnp.concatenate([jnp.zeros_like(head_vals[:1]), head_vals[:-1]], 0)
        previous = jnp.where(carried[:, None], previous, 0.0)
        shifts = previous[:, :channels]
        logscale = previous[:, channels:]
        latent_vals = (patch_vals - shifts) * jnp.exp(-logscale)
        return ((latent_vals, -jnp.sum(logscale, -1)), logscale)

    (latents, logdet), head_pull, logscale = jax.vjp(flow_head, head_out, patches, has_aux=True)
    grad_head, grad_direct = head_pull((latent_grad, logdet_grad))
    scale_rows = logscale.reshape(row_count, -1)
    scale_mean = jnp.mean(scale_rows, -1)
    scale_max = jnp.max(scale_rows, -1)
    grad_low = grad_head.astype(jnp.bfloat16)
    grad_w_out = matmul_tn(top_low, grad_low)
    grad_b_out = jnp.sum(grad_low.astype(jnp.float32), 0)
    grad_hidden = matmul_nt(grad_low, w_out)
    per_layer = [None] * layers
    for depth in reversed(range(layers)):
        (
            hidden0,
            rows_norm,
            queries,
            key_rows,
            values,
            attended,
            log_total,
            hidden1,
            mlp_input,
            pre_act,
            activated,
            full_up,
            full_down,
        ) = stored[depth]
        grad_b_down = jnp.sum(grad_hidden, 0)
        grad_branch = grad_hidden.astype(jnp.bfloat16)
        grad_branch_rows = lax.all_gather(grad_branch, "heads", axis=0, tiled=True)
        grad_activated = matmul_nt(grad_branch_rows, full_down)
        gelu_values, gelu_pull = jax.vjp(gelu_exact, pre_act)
        grad_pre = gelu_pull(grad_activated)[0].astype(jnp.bfloat16)
        grad_w_down = matmul_tn(activated, grad_branch_rows)
        grad_w_up = matmul_tn(mlp_input, grad_pre)
        grad_b_up = jnp.sum(grad_pre.astype(jnp.float32), 0)
        grad_normed2 = lax.psum_scatter(
            matmul_nt(grad_pre, full_up).astype(jnp.bfloat16),
            "heads",
            scatter_dimension=0,
            tiled=True,
        ).astype(jnp.float32)
        norm_values, norm_pull = jax.vjp(norm_rows, hidden1, ln2_gain[depth], ln2_bias[depth])
        back_hidden1, grad_gain2, grad_bias2 = norm_pull(grad_normed2)
        grad_hidden1 = grad_hidden + back_hidden1
        grad_mix = grad_hidden1.astype(jnp.bfloat16)
        grad_mix_rows = lax.all_gather(grad_mix, "heads", axis=0, tiled=True)
        weight_out = w_attn_out[depth]
        grad_attended = matmul_nt(grad_mix_rows, weight_out).astype(jnp.bfloat16)
        grad_w_attn = matmul_tn(attended, grad_mix_rows)
        grad_query, grad_key, grad_value = lax.map(
            attend_backward,
            (
                to_blocks(queries),
                to_blocks(key_rows),
                to_blocks(values),
                seg_blocks,
                log_total,
                to_blocks(grad_attended),
            ),
        )
        grad_query = from_blocks(grad_query)
        grad_key = from_blocks(grad_key)
        grad_value = from_blocks(grad_value)
        grad_w_query = matmul_tn(rows_norm, grad_query)
        grad_w_key = matmul_tn(rows_norm, grad_key)
        grad_w_value = matmul_tn(rows_norm, grad_value)
        weight_query, weight_key, weight_value = (w_query[depth], w_key[depth], w_value[depth])
        total = matmul_nt(grad_query, weight_query)
        total = total + matmul_nt(grad_key, weight_key)
        grad_normed1 = lax.psum_scatter(
            (total + matmul_nt(grad_value, weight_value)).astype(jnp.bfloat16),
            "heads",
            scatter_dimension=0,
            tiled=True,
        ).astype(jnp.float32)
        norm_values1, norm_pull1 = jax.vjp(norm_rows, hidden0, ln1_gain[depth], ln1_bias[depth])
        back_hidden0, grad_gain1, grad_bias1 = norm_pull1(grad_normed1)
        grad_hidden = grad_hidden1 + back_hidden0
        per_layer[depth] = (
            grad_w_query,
            grad_w_key,
            grad_w_value,
            grad_w_attn,
            grad_w_up,
            grad_b_up,
            grad_w_down,
            grad_gain1,
            grad_bias1,
            grad_gain2,
            grad_bias2,
            grad_b_down,
        )

    def stacked(index):
        return jnp.stack([entry[index] for entry in per_layer], 0)

    grad_embed = grad_hidden.astype(jnp.bfloat16)
    grad_w_in = matmul_tn(patch_low, grad_embed)
    grad_b_in = jnp.sum(grad_embed.astype(jnp.float32), 0)
    patches_grad = grad_direct + matmul_nt(grad_embed, w_in)
    quarter = length // slot_count
    packed_row = seg_rows[:, -1] > 0
    grad_slots = grad_hidden.reshape(row_count, slot_count, quarter, width)
    single_part = jnp.sum(
        jnp.where(packed_row[:, None, None], 0.0, grad_hidden.reshape(row_count, length, width)), 0
    )
    packed_part = jnp.sum(jnp.where(packed_row[:, None, None, None], grad_slots, 0.0), (0, 1))
    grad_pos = single_part + jnp.concatenate(
        [packed_part, jnp.zeros((length - quarter, width), jnp.float32)], 0
    )
    slot_sums = jnp.sum(grad_slots, 2)
    row_total = jnp.sum(slot_sums, 1)
    first_slot = lax.broadcasted_iota(jnp.int32, (1, slot_count, 1), 1) == 0
    slot_vectors = jnp.where(
        packed_row[:, None, None], slot_sums, jnp.where(first_slot, row_total[:, None, :], 0.0)
    )
    label_onehot = (
        labels.reshape(-1)[:, None] == lax.broadcasted_iota(jnp.int32, (1, classes), 1)
    ).astype(jnp.float32)
    grad_cls = lax.dot_general(
        label_onehot, slot_vectors.reshape(-1, width), (((0,), (0,)), ((), ())), precision=PRECISE
    )
    sum_query, sum_key, sum_value, sum_attn, sum_up, sum_b_up, sum_down = lax.psum(
        (stacked(0), stacked(1), stacked(2), stacked(3), stacked(4), stacked(5), stacked(6)), "rows"
    )
    (
        sum_w_in,
        sum_b_in,
        sum_pos,
        sum_cls,
        sum_gain1,
        sum_bias1,
        sum_gain2,
        sum_bias2,
        sum_b_down,
        sum_w_out,
        sum_b_out,
    ) = lax.psum(
        (
            grad_w_in,
            grad_b_in,
            grad_pos,
            grad_cls,
            stacked(7),
            stacked(8),
            stacked(9),
            stacked(10),
            stacked(11),
            grad_w_out,
            grad_b_out,
        ),
        ("rows", "heads"),
    )
    return (
        latents,
        logdet,
        patches_grad,
        scale_mean,
        scale_max,
        sum_w_in,
        sum_b_in,
        sum_pos,
        sum_cls,
        sum_gain1,
        sum_bias1,
        sum_query,
        sum_key,
        sum_value,
        sum_attn,
        sum_gain2,
        sum_bias2,
        sum_up,
        sum_b_up,
        sum_down,
        sum_b_down,
        sum_w_out,
        sum_b_out,
    )


def solution(mesh):
    in_specs = (
        P(("rows", "heads"), None),
        P("rows"),
        P(("rows", "heads"), None),
        P(),
        P(),
        P(),
        P(),
        P(),
        P(),
        P(None, None, "heads"),
        P(None, None, "heads"),
        P(None, None, "heads"),
        P(None, "heads", None),
        P(),
        P(),
        P(None, None, "heads"),
        P(None, "heads"),
        P(None, "heads", None),
        P(),
        P(),
        P(),
        P(("rows", "heads"), None),
        P(("rows", "heads")),
    )
    out_specs = (
        P(("rows", "heads"), None),
        P(("rows", "heads")),
        P(("rows", "heads"), None),
        P(("rows", "heads")),
        P(("rows", "heads")),
        P(),
        P(),
        P(),
        P(),
        P(),
        P(),
        P(None, None, "heads"),
        P(None, None, "heads"),
        P(None, None, "heads"),
        P(None, "heads", None),
        P(),
        P(),
        P(None, None, "heads"),
        P(None, "heads"),
        P(None, "heads", None),
        P(),
        P(),
        P(),
    )
    return jax.shard_map(
        per_device, mesh=mesh, in_specs=in_specs, out_specs=out_specs, check_vma=False
    )
```

profile of v0, /device:TPU:0, one launch (start us, length us, event | category | flops | bytes accessed | tf_op | source)
XLA Modules:
  0.0 904.0 jit_solution(2534567188782438305)
XLA Ops:
  14.9 30.8 %all-gather.5.cloned.1.call-done = bf16[2048,768]{1,0:T(8,128)(2,1)} async-done(((bf16[512,768]{1,0:T(8,128)(2,1)}), bf16[2048,768]{1,0:T(8,128)(2,1)}) %all-gather.5.cloned.1.call-update) | async-done | bytes 3145744 | tf_op jit(solution)/shard_map/all_gather | solution.py:160
  45.7 3.1 convolution_convert_fusion.8
  51.6 3.9 convolution_convert_fusion.7
  55.5 3.3 reshape.257
  58.8 2.2 copy.80
  61.0 3.9 convolution_convert_fusion.6
  64.9 3.2 reshape.258
  68.2 2.2 copy.81
  71.7 12.9 %while.26 = (s32[]{:T(128)}, bf16[4,2,256,3,64]{2,1,0,4,3:T(2,128)(2,1)}, f32[4,2,3,256,1]{3,2,1,4,0:T(4,128)S(1)}, bf16[4,2,256,3,64]{2,4,3,1,0:T(8,128)(2,1)S(...) while((s32[]{:T(128)}, ...), condition=%wide.region_7.8_spmd, body=%wide.region_4.7_spmd.sunk | while | flops 103840256 | bytes 6358625 | solution.py:164
  85.5 2.5 reshape.259
  88.0 2.7 convolution_convert_fusion.4
  91.4 37.4 %reduce-scatter.5.cloned.1.call-done = bf16[512,768]{1,0:T(8,128)(2,1)} async-done(((bf16[2048,768]{1,0:T(8,128)(2,1)}), bf16[512,768]{1,0:T(8,128)(2,1)}) %reduce-scatter.5.cloned.1.call-update) | async-done | bytes 786448 | tf_op jit(solution)/shard_map/reduce_scatter | solution.py:169
  132.8 28.4 %all-gather.7.cloned.1.call-done = bf16[2048,768]{1,0:T(8,128)(2,1)} async-done(((bf16[512,768]{1,0:T(8,128)(2,1)}), bf16[2048,768]{1,0:T(8,128)(2,1)}) %all-gather.7.cloned.1.call-update) | async-done | bytes 3145744 | tf_op jit(solution)/shard_map/all_gather | solution.py:174
  161.3 18.8 %multiply_convert_fusion.1 = (bf16[2048,768]{1,0:T(8,128)(2,1)S(1)}, f32[2048,768]{1,0:T(8,128)}, f32[2048,768]{1,0:T(8,128)}) fusion(f32[768]{0:T(1024)S(1)} %convert_reduce_fusion.6, bf16[2048,768]{1,0:T(8,128)(2,1)} %all-gather.7.cloned.1.call-done, bf16[1,768,768]{2,1,0:T(8,128)(2,1)} %param.42), kind=kOutput, calls=%fused_computation.70 | convolution fusion | flops 2519728128 | bytes 20057088 | tf_op jit(solution)/shard_map/dot_general | solution.py:25
  181.8 3.9 convolution_convert_fusion.3
  186.7 37.1 %reduce-scatter.7.cloned.1.call-done = bf16[512,768]{1,0:T(8,128)(2,1)} async-done(((bf16[2048,768]{1,0:T(8,128)(2,1)}), bf16[512,768]{1,0:T(8,128)(2,1)}) %reduce-scatter.7.cloned.1.call-update) | async-done | bytes 786448 | tf_op jit(solution)/shard_map/reduce_scatter | solution.py:180
  223.8 1.8 add_convert_fusion.2
  228.0 1.8 fusion.125
  229.8 28.6 %all-gather.9.cloned.1.call-done = bf16[2048,768]{1,0:T(8,128)(2,1)} async-done(((bf16[512,768]{1,0:T(8,128)(2,1)}), bf16[2048,768]{1,0:T(8,128)(2,1)}) %all-gather.9.cloned.1.call-update) | async-done | bytes 3145744 | tf_op jit(solution)/shard_map/all_gather | solution.py:243
  258.5 11.2 %convert_reduce_fusion = (f32[768]{0:T(1024)}, bf16[2048,768]{1,0:T(8,128)(2,1)S(1)}) fusion(f32[2048,768]{1,0:T(8,128)} %get-tuple-element.240, bf16[2048,768]{1,0:T(8,128)(2,1)} %all-gather.9.cloned.1.call-done, bf16[1,768,768]{2,1,0:T(8,128)(2,1)} %param.44, f32[2048,768]{1,0:T(8,128)} %get-tuple-element.255, f32[768]{0:T(1024)S(1)} %convert_reduce_fusion.6), kind=kOutput, calls=%fused_computation.67 | convolution fusion | flops 2442657024 | bytes 20060160 | tf_op jit(solution)/shard_map/dot_general | solution.py:35
  271.3 4.0 convolution_convert_fusion.2
  275.6 37.9 %reduce-scatter.9.cloned.1.call-done = bf16[512,768]{1,0:T(8,128)(2,1)} async-done(((bf16[2048,768]{1,0:T(8,128)(2,1)}), bf16[512,768]{1,0:T(8,128)(2,1)}) %reduce-scatter.9.cloned.1.call-update) | async-done | bytes 786448 | tf_op jit(solution)/shard_map/reduce_scatter | solution.py:250
  313.5 3.0 fusion.69
  316.5 2.2 fusion.120
  321.0 28.6 %all-gather.11.cloned.1.call-done = bf16[2048,768]{1,0:T(8,128)(2,1)} async-done(((bf16[512,768]{1,0:T(8,128)(2,1)}), bf16[2048,768]{1,0:T(8,128)(2,1)}) %all-gather.11.cloned.1.call-update) | async-done | bytes 3145744 | tf_op jit(solution)/shard_map/all_gather | solution.py:260
  349.7 3.9 convolution_convert_fusion.5
  353.6 3.3 reshape.260
  360.8 69.2 %while.27 = (s32[]{:T(128)}, bf16[4,2,256,3,64]{2,1,0,4,3:T(2,128)(2,1)}, bf16[4,2,256,3,64]{2,1,0,4,3:T(2,128)(2,1)}, bf16[4,2,256,3,64]{2,1,0,4,3:T(2,128)(2,1...) while((s32[]{:T(128)}, ...), condition=%wide.region_18.19_spmd, body=%wide.region_16.18_spmd.sunk | while | flops 257789440 | bytes 21261944 | solution.py:264
  361.0 2.7 subtract_exponential_fusion.2
  364.8 2.5 fusion.187
  367.3 3.5 fusion.190
  373.8 3.5 fusion.188
  378.3 2.7 subtract_exponential_fusion.2
  382.1 2.5 fusion.187
  384.6 3.5 fusion.190
  388.1 1.8 fusion.189
  391.0 3.5 fusion.188
  395.6 2.7 subtract_exponential_fusion.2
  399.4 2.5 fusion.187
  401.9 3.5 fusion.190
  405.4 1.8 fusion.189
  408.4 3.4 fusion.188
  412.9 2.7 subtract_exponential_fusion.2
  416.7 2.5 fusion.187
  419.2 3.5 fusion.190
  422.7 1.8 fusion.189
  425.7 3.4 fusion.188
  430.0 3.1 reshape.263
  433.1 3.2 reshape.262
  436.3 3.5 reshape.261
  439.9 2.3 fusion.83
  443.4 2.8 add_convert_fusion
  446.3 7.1 convolution_bitcast_fusion
  453.4 4.1 convolution_bitcast_fusion.1
  466.9 17.5 %reduce-scatter.11.cloned.1.call-done = bf16[512,768]{1,0:T(8,128)(2,1)} async-done(((bf16[2048,768]{1,0:T(8,128)(2,1)}), bf16[512,768]{1,0:T(8,128)(2,1)}) %reduce-scatter.11.cloned.1.call-update) | async-done | bytes 786448 | tf_op jit(solution)/shard_map/reduce_scatter | solution.py:284
  484.3 1.8 convert_reduce_fusion.1
  489.7 1.8 select_reduce_fusion.1
  493.6 3.3 fusion.101
  499.0 22.7 %psum.139 = f32[1,768]{1,0:T(1,128)} all-reduce(f32[1,768]{1,0:T(1,128)S(1)} %stack.33), channel_id=1, replica_groups=mesh['rows'=8,'heads'=4] {'rows'}, use_global_device_ids=true, to_apply=%region_48.49 | all-reduce | flops 768 | bytes 6144 | tf_op jit(solution)/shard_map/psum | solution.py:337
  521.8 41.5 %all-reduce.6 = (f32[768]{0:T(1024)}, f32[1,768]{1,0:T(1,128)}, f32[1,768]{1,0:T(1,128)}, f32[1,768]{1,0:T(1,128)}, f32[1,768]{1,0:T(1,128)}, /*index=5*/f32[1,768]{1,0:T(1,128)}, f32[96]{0:T(128)}) all-reduce(f32[768]{0:T(1024)S(1)} %get-tuple-element.235, ...), channel_id=1, replica_groups=mesh['rows'=8,'heads'=4] {'rows','heads'}, use_global_device_ids=true, to_apply=%region_27.28 | all-reduce | flops 4704 | bytes 37632 | tf_op jit(solution)/shard_map/psum | solution.py:352
  564.2 165.1 %all-reduce.14.cloned.1.call-done = (f32[1,768,192]{1,2,0:T(8,128)}, f32[1,768,192]{1,2,0:T(8,128)}, f32[1,768,192]{1,2,0:T(8,128)}, f32[1,192,768]{2,1,0:T(8,12...) async-done(((f32[1,768,192]{1,2,0:T(8,128)}, f32[1,768,192]{1,2,0:T(8,128)}, f32[1,768,192]{1,2,0:T(8,128)}, f32[1,192,768]{2,1,0:T(8,128)}, f32[1,768,768]{2,1,0:T(8,128)}, ...) | async-done | bytes 7077904 | tf_op jit(solution)/shard_map/psum | solution.py:337
  729.3 152.3 %all-reduce.12.cloned.1.call-done = (f32[48,768]{1,0:T(8,128)}, f32[256,768]{1,0:T(8,128)}, f32[1000,768]{1,0:T(8,128)}, f32[768,96]{0,1:T(8,128)}) async-done(((f32[48,768]{1,0:T(8,128)}, f32[256,768]{1,0:T(8,128)}, f32[1000,768]{1,0:T(8,128)}, f32[768,96]{0,1:T(8,128)}), (f32[48,768]{1,0:T(8,128)}, f32[256,768]{1,0:T(8,128)}, f32[1000,768]{1,0:T(8,128)}, ...) | async-done | bytes 4300816 | tf_op jit(solution)/shard_map/psum | solution.py:352
  883.1 2.1 copy.162
  885.2 3.8 copy.163
  (300 shorter events, 87.1 us)
Async XLA Ops:
  7.2 3.9 copy-start
  7.2 3.5 copy-start.23
  7.2 3.5 copy-start.36
  7.2 38.5 %all-gather.5.cloned.1.call-start = ((), (), s32[]{:S(2)}) async-start(), calls=%async_computation.4 | async-start | bytes 3932160 | tf_op jit(solution)/shard_map/all_gather | solution.py:160
  9.2 1.8 copy-start.59
  13.1 1.8 copy-start.44
  13.1 32.6 %copy-start.40 = (bf16[1,768,192]{1,2,0:T(8,128)(2,1)S(1)}, bf16[1,768,192]{1,2,0:T(8,128)(2,1)}, u32[]{:S(2)}) copy-start(bf16[1,768,192]{1,2,0:T(8,128)(2,1)} %param.38) | copy-start | bytes 884740
  14.3 114.5 %reduce-scatter.5.cloned.1.call-start = ((), (), s32[]{:S(2)}) async-start(), calls=%async_computation.5 | async-start | bytes 3932160 | tf_op jit(solution)/shard_map/reduce_scatter | solution.py:169
  48.8 2.8 copy-start.33
  55.5 5.5 copy-start.31
  85.4 2.5 copy-start.38
  90.7 70.6 %all-gather.7.cloned.1.call-start = ((), (), s32[]{:S(2)}) async-start(), calls=%async_computation.6 | async-start | bytes 3932160 | tf_op jit(solution)/shard_map/all_gather | solution.py:174
  130.2 1.1 copy-start.2
  131.3 1.4 copy-start.47
  132.6 91.2 %reduce-scatter.7.cloned.1.call-start = ((), (), s32[]{:S(2)}) async-start(), calls=%async_computation.7 | async-start | bytes 3932160 | tf_op jit(solution)/shard_map/reduce_scatter | solution.py:180
  161.2 20.5 %copy-start.57 = (bf16[1,768,768]{2,1,0:T(8,128)(2,1)S(1)}, bf16[1,768,768]{2,1,0:T(8,128)(2,1)}, u32[]{:S(2)}) copy-start(bf16[1,768,768]{2,1,0:T(8,128)(2,1)} %param.44) | copy-start | bytes 3538948
  180.1 1.7 copy-start.60
  185.7 72.8 %all-gather.9.cloned.1.call-start = ((), (), s32[]{:S(2)}) async-start(), calls=%async_computation.8 | async-start | bytes 3932160 | tf_op jit(solution)/shard_map/all_gather | solution.py:243
  186.7 38.9 %copy-start.24 = (bf16[768,96]{0,1:T(8,128)(2,1)S(1)}, bf16[768,96]{0,1:T(8,128)(2,1)}, u32[]{:S(2)}) copy-start(bf16[768,96]{0,1:T(8,128)(2,1)} %param.46) | copy-start | bytes 442372
  186.7 39.3 %copy-start.55 = (f32[96]{0:T(128)S(1)}, f32[96]{0:T(128)}, u32[]{:S(2)}) copy-start(f32[96]{0:T(128)} %param.47) | copy-start | bytes 1156
  225.6 4.2 copy-start.16
  225.6 1.0 copy-start.29
  229.8 83.7 %reduce-scatter.9.cloned.1.call-start = ((), (), s32[]{:S(2)}) async-start(), calls=%async_computation.9 | async-start | bytes 3932160 | tf_op jit(solution)/shard_map/reduce_scatter | solution.py:250
  258.5 12.8 %copy-start.58 = (bf16[1,768,768]{2,1,0:T(8,128)(2,1)S(1)}, bf16[1,768,768]{2,1,0:T(8,128)(2,1)}, u32[]{:S(2)}) copy-start(bf16[1,768,768]{2,1,0:T(8,128)(2,1)} %param.42) | copy-start | bytes 3538948
  269.6 1.7 copy-start.61
  275.4 74.3 %all-gather.11.cloned.1.call-start = ((), (), s32[]{:S(2)}) async-start(), calls=%async_computation.10 | async-start | bytes 3932160 | tf_op jit(solution)/shard_map/all_gather | solution.py:260
  313.5 3.0 copy-start.20
  316.5 3.4 copy-start.6
  318.6 1.2 copy-start.8
  319.9 29.8 %copy-start.39 = (bf16[1,192,768]{2,1,0:T(8,128)(2,1)S(1)}, bf16[1,192,768]{2,1,0:T(8,128)(2,1)}, u32[]{:S(2)}) copy-start(bf16[1,192,768]{2,1,0:T(8,128)(2,1)} %param.39) | copy-start | bytes 884740
  321.0 163.3 %reduce-scatter.11.cloned.1.call-start = ((), (), s32[]{:S(2)}) async-start(), calls=%async_computation.11 | async-start | bytes 3932160 | tf_op jit(solution)/shard_map/reduce_scatter | solution.py:284
  433.1 6.7 copy-start.32
  439.9 2.3 copy-start.12
  439.9 2.3 copy-start.34
  442.2 1.1 copy-start.14
  442.2 1.2 copy-start.41
  446.2 283.1 %all-reduce.14.cloned.1.call-start = ((), (), s32[]{:S(2)}) async-start(), calls=%async_computation.13 | async-start | bytes 14155776 | tf_op jit(solution)/shard_map/psum | solution.py:337
  446.3 7.1 copy-start.56
  446.3 7.1 copy-start.62
  453.4 4.1 copy-start.19
  457.5 2.1 copy-start.5
  457.5 2.3 copy-start.15
  459.8 1.6 copy-start.11
  461.4 1.6 copy-start.13
  464.7 1.2 copy-start.17
  464.7 416.9 %all-reduce.12.cloned.1.call-start = ((), (), s32[]{:S(2)}) async-start(), calls=%async_computation.12 | async-start | bytes 8601600 | tf_op jit(solution)/shard_map/psum | solution.py:352
  484.3 1.9 copy-start.18
  484.3 2.8 copy-start.9
  486.2 1.4 copy-start.7
  488.4 1.1 copy-start.3
  489.7 1.9 copy-start.4
  496.9 2.1 copy-start.46
  496.9 24.8 %copy-start.43 = (f32[768]{0:T(1024)S(1)}, f32[768]{0:T(1024)}, u32[]{:S(2)}) copy-start(f32[768]{0:T(1024)} %get-tuple-element.173) | copy-start | bytes 9220
  496.9 24.8 %copy-start.42 = (f32[768]{0:T(1024)S(1)}, f32[768]{0:T(1024)}, u32[]{:S(2)}) copy-start(f32[768]{0:T(1024)} %get-tuple-element.177) | copy-start | bytes 9220
  496.9 66.3 %copy-start.30 = (f32[512,48]{0,1:T(8,128)S(1)}, f32[512,48]{0,1:T(8,128)}, u32[]{:S(2)}) copy-start(f32[512,48]{0,1:T(8,128)} %param.48) | copy-start | bytes 294916
  496.9 66.3 %copy-start.37 = (bf16[48,768]{1,0:T(8,128)(2,1)S(1)}, bf16[48,768]{1,0:T(8,128)(2,1)}, u32[]{:S(2)}) copy-start(bf16[48,768]{1,0:T(8,128)(2,1)} %param.30) | copy-start | bytes 221188
  885.2 3.8 copy-start.28
  885.2 4.6 copy-start.27
  889.0 1.6 copy-start.26
  889.0 2.5 copy-start.25
  889.8 2.5 copy-start.22
  892.3 2.5 copy-start.21
  892.3 4.6 copy-start.1
  894.8 1.4 copy-start.35
  (9 other events, 6.6 us)
Sparse Core Ops, SparseCore 0:
  14.4 31.2 all-gather.4
  90.8 37.9 reduce-scatter.4
  132.7 28.5 all-gather.6
  185.8 37.9 reduce-scatter.6
  229.9 28.5 all-gather.8
  275.5 37.9 reduce-scatter.8
  321.1 28.5 all-gather.10
  446.3 37.9 reduce-scatter.10
  490.6 238.7 all-reduce.13
  738.1 143.3 all-reduce.11
where the time goes:
time: 908 us; the launch traced here: 904 us
  waiting for transfers between devices  564 us (62%)
  matrix products  154 us (17%)
  local copies, waits for them, and re-layouts  78.8 us (9%)
  blocking collectives  64.2 us (7%)
  other arithmetic  26.4 us (3%)
  between operations  15 us (2%)
    psum x1, waiting for transfers between devices, per_device(): lax.psum((stacked(0), stacked(1), stacked(2), stacked(3), stacked(4), sta...  165 us
    psum x1, waiting for transfers between devices, per_device(): lax.psum((grad_w_in, grad_b_in, grad_pos, grad_cls, stacked(7), stacked(8...  152 us
    psum x1, blocking collectives, per_device(): lax.psum((grad_w_in, grad_b_in, grad_pos, grad_cls, stacked(7), stacked(8...  41.5 us
    dot_general x10, matrix products, matmul(): return jnp.dot(matrix, other, preferred_element_type=jnp.float32)  39.8 us
    reduce_scatter x1, waiting for transfers between devices, per_device(): lax.psum_scatter(matmul_nt(grad_pre, full_up).astype(jnp.bfloat16), 'head...  37.9 us
    reduce_scatter x1, waiting for transfers between devices, per_device(): lax.psum_scatter(matmul(attended, weight_out).astype(jnp.bfloat16), 'head...  37.4 us
    reduce_scatter x1, waiting for transfers between devices, per_device(): lax.psum_scatter(matmul(activated, full_down).astype(jnp.bfloat16), 'head...  37.1 us
    all_gather x1, waiting for transfers between devices, per_device(): rows_norm = lax.all_gather(normed1, 'heads', axis=0, tiled=True)  30.8 us
  transfers between devices with their start and end apart: 10, of which 10 were waited for; matrix products, arithmetic and copies ran while one was open for 4% of the time, Pallas kernels for 0%

commit v1 on v0

v1 whole, which is shorter than its diff:
```python
import jax
import jax.numpy as jnp
from jax import lax
from jax.sharding import PartitionSpec as P

HEAD_DIM = 64
EPSILON = 1e-05
BF = jnp.bfloat16
F32 = jnp.float32


def norm_parts(values):
    average = jnp.mean(values, -1, keepdims=True)
    centered = values - average
    spread = jnp.mean(centered * centered, -1, keepdims=True)
    rstd = lax.rsqrt(spread + EPSILON)
    return centered * rstd, rstd


def gelu_exact(values):
    return jax.nn.gelu(values, approximate=False)


def nn(matrix, other):
    return jnp.dot(matrix, other, preferred_element_type=F32)


def tn(matrix, other):
    return lax.dot_general(matrix, other, (((0,), (0,)), ((), ())), preferred_element_type=F32)


def nt(matrix, other):
    return lax.dot_general(matrix, other, (((1,), (1,)), ((), ())), preferred_element_type=F32)


def make_program(rows_size, heads_size):
    levels = rows_size.bit_length() - 1

    def swap_heads(array, bit):
        pairs = [(i, i ^ bit) for i in range(heads_size)]
        return lax.ppermute(array, "heads", pairs)

    def swap_rows(array, bit):
        pairs = [(i, i ^ bit) for i in range(rows_size)]
        return lax.ppermute(array, "rows", pairs)

    def gather_slots(own, row_bit):
        half = own.shape[0] // 2
        near = swap_heads(own, 1)
        mine = lax.dynamic_slice_in_dim(own, row_bit * half, half, 0)
        mine = swap_heads(mine, 2)
        other = swap_rows(mine, 1)
        low = jnp.where(row_bit == 0, mine, other)
        high = jnp.where(row_bit == 0, other, mine)
        far = jnp.concatenate([low, high], 0)
        return [own, near, far, swap_heads(far, 1)]

    def gather_all(array):
        for bit in (1, 2):
            array = jnp.concatenate([array, swap_heads(array, bit)], 0)
        for level in range(levels):
            array = jnp.concatenate([array, swap_rows(array, 1 << level)], 0)
        return array

    def relative(array, row_index):
        pieces = array.reshape((2,) * levels + (array.shape[0] // rows_size,) + array.shape[1:])
        for level in range(levels):
            bit = (row_index >> level) & 1
            pieces = jnp.where(bit == 1, jnp.flip(pieces, level), pieces)
        return pieces

    def add_low(first, second):
        return (first.astype(F32) + second.astype(F32)).astype(BF)

    def reduce_slots(slots, row_index):
        shape = slots[0].shape
        zero = add_low(slots[0], swap_heads(slots[1], 1))
        two = add_low(slots[2], swap_heads(slots[3], 1))
        total = add_low(zero, swap_heads(two, 2))
        total = relative(total, row_index)
        for level in range(levels):
            total = add_low(total[0], swap_rows(total[1], 1 << level))
        for level in reversed(range(levels)):
            total = jnp.stack([total, swap_rows(total, 1 << level)], 0)
        return relative(total.reshape(shape), row_index).reshape(shape).astype(F32)

    def program(
        patches,
        segments,
        labels,
        w_in,
        b_in,
        pos_table,
        cls_table,
        ln1_gain,
        ln1_bias,
        w_query,
        w_key,
        w_value,
        w_attn_out,
        ln2_gain,
        ln2_bias,
        w_up,
        b_up,
        w_down,
        b_down,
        w_out,
        b_out,
        latent_grad,
        logdet_grad,
    ):
        tokens = patches.shape[0]
        length, width = pos_table.shape
        slot_count = labels.shape[1]
        channels = patches.shape[1]
        classes = cls_table.shape[0]
        part = w_query.shape[2]
        heads_here = part // HEAD_DIM
        head_index = lax.axis_index("heads")
        row_index = lax.axis_index("rows")
        row_bit = row_index & 1

        pack_t = jnp.concatenate(
            [w_query[0], w_key[0], w_value[0], w_attn_out[0].T], 1
        )
        slots_t = gather_slots(pack_t, row_bit)
        slots_u = gather_slots(w_up[0], row_bit)
        slots_d = gather_slots(w_down[0], row_bit)
        bias_up = [b_up, swap_heads(b_up, 1), swap_heads(b_up, 2), swap_heads(b_up, 3)]
        bias_up = [bias.astype(F32) for bias in bias_up]
        all_labels = gather_all(labels)

        own_segs = lax.dynamic_slice_in_dim(segments, head_index * tokens, tokens)
        seg_rows = own_segs.reshape(-1, length)
        row_count = seg_rows.shape[0]
        causal = lax.broadcasted_iota(jnp.int32, (length, length), 0) >= lax.broadcasted_iota(
            jnp.int32, (length, length), 1
        )
        allowed = (seg_rows[:, :, None] == seg_rows[:, None, :]) & causal[None]
        position = (jnp.sum(allowed.astype(jnp.int32), -1) - 1).reshape(-1)
        slot_ids = lax.broadcasted_iota(jnp.int32, (1, 1, slot_count), 2)
        token_label = jnp.sum(
            jnp.where(seg_rows[:, :, None] == slot_ids, labels[:, None, :], 0), -1
        ).reshape(-1)
        pos_onehot = (position[:, None] == lax.broadcasted_iota(jnp.int32, (1, length), 1)).astype(BF)
        cls_onehot = (
            token_label[:, None] == lax.broadcasted_iota(jnp.int32, (1, classes), 1)
        ).astype(BF)
        patch_low = patches.astype(BF)
        hidden0 = (
            nn(patch_low, w_in) + b_in + nn(pos_onehot, pos_table) + nn(cls_onehot, cls_table)
        )

        xhat1, rstd1 = norm_parts(hidden0)
        normed1 = (xhat1 * ln1_gain[0] + ln1_bias[0]).astype(BF)

        def per_row(matrix):
            return matrix.reshape(row_count, length, -1, HEAD_DIM)

        weight_t = jnp.concatenate(slots_t, 1).reshape(width, heads_size, 4, part)
        weight_qkv = [weight_t[:, :, i].reshape(width, heads_size * part) for i in range(4)]
        queries = per_row(nn(normed1, weight_qkv[0]).astype(BF))
        keys = per_row(nn(normed1, weight_qkv[1]).astype(BF))
        values = per_row(nn(normed1, weight_qkv[2]).astype(BF))
        scores = jnp.einsum("bqhe,bkhe->bhqk", queries, keys, preferred_element_type=F32)
        scores = jnp.where(allowed[:, None], scores * HEAD_DIM ** (-0.5), -1e30)
        probs = jax.nn.softmax(scores, -1)
        probs_low = probs.astype(BF)
        attended = jnp.einsum("bhqk,bkhe->bqhe", probs_low, values, preferred_element_type=F32)
        attended = attended.astype(BF).reshape(tokens, width)
        hidden1 = hidden0 + nt(attended, weight_qkv[3])
        xhat2, rstd2 = norm_parts(hidden1)
        normed2 = (xhat2 * ln2_gain[0] + ln2_bias[0]).astype(BF)

        slot_order = [head_index ^ j for j in range(heads_size)]
        pre_act = [nn(normed2, slots_u[j]) + bias_up[j] for j in range(heads_size)]
        activated = [gelu_exact(p).astype(BF) for p in pre_act]
        branch = sum(nn(activated[j], slots_d[j]) for j in range(heads_size))
        hidden2 = hidden1 + branch + b_down[0]
        top_low = hidden2.astype(BF)
        head_out = nn(top_low, w_out) + b_out
        carried = jnp.concatenate(
            [jnp.zeros((row_count, 1), dtype=bool), seg_rows[:, 1:] == seg_rows[:, :-1]], 1
        ).reshape(-1, 1)
        previous = jnp.concatenate([jnp.zeros_like(head_out[:1]), head_out[:-1]], 0)
        previous = jnp.where(carried, previous, 0.0)
        shifts = previous[:, :channels]
        logscale = previous[:, channels:]
        shrink = jnp.exp(-logscale)
        latents = (patches - shifts) * shrink
        logdet = -jnp.sum(logscale, -1)
        scale_rows = logscale.reshape(row_count, -1)
        scale_mean = jnp.mean(scale_rows, -1)
        scale_max = jnp.max(scale_rows, -1)

        grad_direct = latent_grad * shrink
        grad_prev = jnp.concatenate(
            [-grad_direct, -latent_grad * latents - logdet_grad[:, None]], 1
        )
        grad_prev = jnp.where(carried, grad_prev, 0.0)
        grad_head = jnp.concatenate([grad_prev[1:], jnp.zeros_like(grad_prev[:1])], 0).astype(BF)
        grad_w_out = tn(grad_head, top_low)
        grad_b_out = jnp.sum(grad_head.astype(F32), 0)
        grad_hidden2 = nt(grad_head, w_out)
        grad_b_down = jnp.sum(grad_hidden2, 0)
        grad_branch = grad_hidden2.astype(BF)

        grads_d = [tn(activated[j], grad_branch).astype(BF) for j in range(heads_size)]
        sum_down = reduce_slots(grads_d, row_index)
        grad_pre = []
        for j in range(heads_size):
            grad_act = nt(grad_branch, slots_d[j])
            _, pull = jax.vjp(gelu_exact, pre_act[j])
            grad_pre.append(pull(grad_act)[0].astype(BF))
        grads_u = [tn(normed2, grad_pre[j]).astype(BF) for j in range(heads_size)]
        sum_up = reduce_slots(grads_u, row_index)
        grad_b_up = [jnp.sum(g.astype(F32), 0) for g in grad_pre]
        grad_normed2 = sum(nt(grad_pre[j], slots_u[j]) for j in range(heads_size))

        def norm_back(grad, gain, xhat, rstd):
            d = grad * gain
            back = rstd * (
                d - jnp.mean(d, -1, keepdims=True) - xhat * jnp.mean(d * xhat, -1, keepdims=True)
            )
            return back, jnp.sum(grad * xhat, 0), jnp.sum(grad, 0)

        back1, grad_gain2, grad_bias2 = norm_back(grad_normed2, ln2_gain[0], xhat2, rstd2)
        grad_hidden1 = grad_hidden2 + back1
        grad_mix = grad_hidden1.astype(BF)
        grad_attended = per_row(nn(grad_mix, weight_qkv[3]).astype(BF))
        grad_probs = jnp.einsum("bqhe,bkhe->bhqk", grad_attended, values, preferred_element_type=F32)
        inner = jnp.sum(probs * grad_probs, -1, keepdims=True)
        grad_scores = (probs * (grad_probs - inner) * HEAD_DIM ** (-0.5)).astype(BF)
        grad_query = jnp.einsum("bhqk,bkhe->bqhe", grad_scores, keys, preferred_element_type=F32)
        grad_key = jnp.einsum("bhqk,bqhe->bkhe", grad_scores, queries, preferred_element_type=F32)
        grad_value = jnp.einsum(
            "bhqk,bqhe->bkhe", probs_low, grad_attended, preferred_element_type=F32
        )
        grad_query, grad_key, grad_value = (
            g.astype(BF).reshape(tokens, width) for g in (grad_query, grad_key, grad_value)
        )
        grad_normed1 = (
            nt(grad_query, weight_qkv[0])
            + nt(grad_key, weight_qkv[1])
            + nt(grad_value, weight_qkv[2])
        )
        back0, grad_gain1, grad_bias1 = norm_back(grad_normed1, ln1_gain[0], xhat1, rstd1)
        grad_hidden0 = grad_hidden1 + back0
        grad_embed = grad_hidden0.astype(BF)
        grad_w_in = tn(patch_low, grad_embed)
        grad_b_in = jnp.sum(grad_embed.astype(F32), 0)
        patches_grad = grad_direct + nt(grad_embed, w_in)

        quarter = length // slot_count
        packed_row = seg_rows[:, -1] > 0
        grad_slots = grad_hidden0.reshape(row_count, slot_count, quarter, width)
        single_part = jnp.sum(
            jnp.where(
                packed_row[:, None, None], 0.0, grad_hidden0.reshape(row_count, length, width)
            ),
            0,
        )
        packed_part = jnp.sum(jnp.where(packed_row[:, None, None, None], grad_slots, 0.0), (0, 1))
        grad_pos = single_part + jnp.concatenate(
            [packed_part, jnp.zeros((length - quarter, width), F32)], 0
        )
        slot_sums = jnp.sum(grad_slots, 2)
        row_total = jnp.sum(slot_sums, 1)
        first_slot = lax.broadcasted_iota(jnp.int32, (1, slot_count, 1), 1) == 0
        slot_vectors = jnp.where(
            packed_row[:, None, None], slot_sums, jnp.where(first_slot, row_total[:, None, :], 0.0)
        )
        all_slots = gather_all(slot_vectors.reshape(-1, width).astype(BF))
        label_onehot = (
            lax.broadcasted_iota(jnp.int32, (classes, 1), 0) == all_labels.reshape(1, -1)
        ).astype(BF)
        sum_cls = nn(label_onehot, all_slots)

        small = jnp.concatenate(
            [
                grad_w_in,
                grad_w_out,
                grad_pos,
                jnp.stack(
                    [
                        grad_b_in,
                        grad_gain1,
                        grad_bias1,
                        grad_gain2,
                        grad_bias2,
                        grad_b_down,
                        jnp.pad(grad_b_out, (0, width - 2 * channels)),
                    ]
                ),
            ],
            0,
        ).astype(BF)
        block = -(-small.shape[0] // (16 * heads_size)) * 16
        small = jnp.pad(small, ((0, block * heads_size - small.shape[0]), (0, 0)))
        small = small.reshape(heads_size, block, width)
        grads_t = []
        for j in range(heads_size):
            columns = slice(j * part, (j + 1) * part)
            grads_t.append(
                jnp.concatenate(
                    [
                        jnp.concatenate(
                            [
                                tn(normed1, grad_query[:, columns]),
                                tn(normed1, grad_key[:, columns]),
                                tn(normed1, grad_value[:, columns]),
                                tn(grad_mix, attended[:, columns]),
                            ],
                            1,
                        ).astype(BF),
                        lax.dynamic_index_in_dim(small, slot_order[j], 0, keepdims=False),
                        jnp.pad(grad_b_up[j][None].astype(BF), ((0, 15), (0, 0))),
                    ],
                    0,
                )
            )
        sum_t = reduce_slots(grads_t, row_index)
        own_small = sum_t[width : width + block].astype(BF)
        pair = jnp.stack([own_small, swap_heads(own_small, 1)], 0)
        quad = jnp.concatenate([pair, swap_heads(pair, 2)], 0)
        ordered = jnp.stack(
            [lax.dynamic_index_in_dim(quad, slot_order[j], 0, keepdims=False) for j in range(heads_size)]
        )
        flat = ordered.reshape(-1, width).astype(F32)
        sizes = [channels, 2 * channels, length]
        sum_w_in = flat[: sizes[0]]
        sum_w_out = flat[sizes[0] : sizes[0] + sizes[1]].T
        start = sizes[0] + sizes[1]
        sum_pos = flat[start : start + length]
        start += length
        sum_b_in, sum_gain1, sum_bias1, sum_gain2, sum_bias2, sum_b_down = (
            flat[start + i] for i in range(6)
        )
        sum_b_out = flat[start + 6, : 2 * channels]
        sum_b_up = sum_t[width + block]
        return (
            latents,
            logdet,
            patches_grad,
            scale_mean,
            scale_max,
            sum_w_in,
            sum_b_in,
            sum_pos,
            sum_cls,
            sum_gain1[None],
            sum_bias1[None],
            sum_t[None, :width, :part],
            sum_t[None, :width, part : 2 * part],
            sum_t[None, :width, 2 * part : 3 * part],
            sum_t[:width, 3 * part :].T[None],
            sum_gain2[None],
            sum_bias2[None],
            sum_up[None],
            sum_b_up[None],
            sum_down[None],
            sum_b_down[None],
            sum_w_out,
            sum_b_out,
        )

    return program


def solution(mesh):
    tokens = P(("rows", "heads"))
    tokens2 = P(("rows", "heads"), None)
    last = P(None, None, "heads")
    middle = P(None, "heads", None)
    in_specs = (
        (tokens2, P("rows"), tokens2)
        + (P(),) * 6
        + (last, last, last, middle)
        + (P(), P(), last, P(None, "heads"), middle, P(), P(), P())
        + (tokens2, tokens)
    )
    out_specs = (
        (tokens2, tokens, tokens2, tokens, tokens)
        + (P(),) * 6
        + (last, last, last, middle)
        + (P(), P(), last, P(None, "heads"), middle, P(), P(), P())
    )
    program = make_program(mesh.shape["rows"], mesh.shape["heads"])
    return jax.shard_map(
        program, mesh=mesh, in_specs=in_specs, out_specs=out_specs, check_vma=False
    )
```

time: 908 us -> 490 us (0.54)
  waiting for transfers between devices: 564 us -> 169 us
  blocking collectives: 64.2 us -> 0 us
  starting transfers between devices: 1.49 us -> 56.7 us
  other arithmetic: 26.4 us -> 43.2 us
  matrix products: 154 us -> 140 us
  between operations: 15 us -> 2.71 us
    psum x2 -> x0, waiting for transfers between devices: 317 us -> none  [the longest x1 165 us: per_device(): lax.psum((stacked(0), stacked(1), stacked(2), stacked(3), stacked(4), sta...]
    ppermute x0 -> x54, waiting for transfers between devices: none -> 169 us  [the longest x27 91.6 us: swap_rows(): return lax.ppermute(array, 'rows', pairs)]
    reduce_scatter x4 -> x0, waiting for transfers between devices: 130 us -> none  [the longest x1 37.9 us: per_device(): lax.psum_scatter(matmul_nt(grad_pre, full_up).astype(jnp.bfloat16), 'head...]
    all_gather x4 -> x0, waiting for transfers between devices: 117 us -> none  [the longest x1 30.8 us: per_device(): rows_norm = lax.all_gather(normed1, 'heads', axis=0, tiled=True)]
    psum x2 -> x0, blocking collectives: 64.2 us -> none  [the longest x1 41.5 us: per_device(): lax.psum((grad_w_in, grad_b_in, grad_pos, grad_cls, stacked(7), stacked(8...]
    ppermute x0 -> x54, starting transfers between devices: none -> 56.7 us  [the longest x27 38.3 us: swap_rows(): return lax.ppermute(array, 'rows', pairs)]
    convert_element_type x0 -> x14, local copies, waits for them, and re-layouts: none -> 15.7 us  [the longest x3 2.44 us: program(): g.astype(BF).reshape(tokens, width)]
    dot_general x55 -> x63, matrix products: 154 us -> 140 us  [the longest x17 49 us: nn(): return jnp.dot(matrix, other, preferred_element_type=F32)]
  transfers between devices with their start and end apart: 10 -> 54, of which waited for: 10 -> 27; matrix products, arithmetic and copies ran while one was open for 4% -> 29% of each run, Pallas kernels for 0% -> 0%
where the time goes in v1:
time: 490 us; the launch traced here: 483 us
  waiting for transfers between devices  169 us (34%)
  matrix products  140 us (29%)
  local copies, waits for them, and re-layouts  71.8 us (15%)
  starting transfers between devices  56.7 us (12%)
  other arithmetic  43.2 us (9%)
    ppermute x27, waiting for transfers between devices, swap_rows(): return lax.ppermute(array, 'rows', pairs)  91.6 us
    ppermute x27, waiting for transfers between devices, swap_heads(): return lax.ppermute(array, 'heads', pairs)  77 us
    dot_general x17, matrix products, nn(): return jnp.dot(matrix, other, preferred_element_type=F32)  49 us
    ppermute x27, starting transfers between devices, swap_rows(): return lax.ppermute(array, 'rows', pairs)  38.3 us
    dot_general x26, matrix products, tn(): lax.dot_general(matrix, other, (((0,), (0,)), ((), ())), preferred_elemen...  33.8 us
    dot_general x14, matrix products, nt(): lax.dot_general(matrix, other, (((1,), (1,)), ((), ())), preferred_elemen...  22.2 us
    ppermute x27, starting transfers between devices, swap_heads(): return lax.ppermute(array, 'heads', pairs)  18.4 us
    unnamed x179, local copies, waits for them, and re-layouts  18.1 us
  transfers between devices with their start and end apart: 54, of which 27 were waited for; matrix products, arithmetic and copies ran while one was open for 29% of the time, Pallas kernels for 0%

profile of v1, /device:TPU:0, one launch (start us, length us, event | category | flops | bytes accessed | tf_op | source)
XLA Modules:
  0.0 482.8 jit_solution(1810104268861136665)
XLA Ops:
  0.7 2.4 pad_maximum_fusion.1
  5.6 2.5 collective-permute-start.1
  28.0 7.1 %collective-permute-done.27 = s32[4,4]{0,1:T(4,128)S(1)} collective-permute-done((s32[4,4]{0,1:T(4,128)S(1)}, s32[4,4]{0,1:T(4,128)S(1)}, u32[]{:S(2)}, u32[]{:S(2)}) %collective-permute-start.27) | collective-permute-done | bytes 96 | tf_op jit(solution)/shard_map/ppermute | solution.py:41
  42.5 2.8 collective-permute-start.30
  53.1 2.4 constant_dynamic-update-slice_fusion.2
  57.3 4.2 collective-permute-done.10
  63.1 4.6 collective-permute-done.8
  70.1 9.8 %collective-permute-done.11 = bf16[384,768]{0,1:T(8,128)(2,1)S(1)} collective-permute-done((bf16[384,768]{0,1:T(8,128)(2,1)S(1)}, bf16[384,768]{0,1:T(8,128)(2,1)S(1)}, u32[]{:S(2)}, u32[]{:S(2)}) %collective-permute-start.11) | collective-permute-done | bytes 589856 | tf_op jit(solution)/shard_map/ppermute | solution.py:45
  87.8 2.3 copy.177
  90.1 3.4 reshape.281
  93.5 3.0 convolution_convert_fusion.9
  96.5 2.3 copy.178
  98.8 2.9 reshape.282
  101.7 3.0 convolution_convert_fusion.11
  104.7 2.3 copy.176
  106.9 2.9 reshape.280
  109.9 2.4 fusion.90
  114.8 2.0 copy-done.78
  119.7 5.8 %multiply_convert_fusion.4 = (bf16[512,768]{1,0:T(8,128)(2,1)S(1)}, f32[512,768]{1,0:T(8,128)S(1)}, f32[512,768]{1,0:T(8,128)S(1)}) fusion(f32[768]{0:T(1024)S(1)} %convert_reduce_fusion.4, bf16[512,768]{1,0:T(8,128)(2,1)S(1)} %add_convert_fusion.14, bf16[1,768,768]{2,1,0:T(8,128)(2,1)} %param.38), kind=kOutput, calls=%fused_computation.114 | convolution fusion | flops 629932032 | bytes 5901312 | tf_op jit(solution)/shard_map/dot_general | solution.py:25
  125.5 5.8 %multiply_convert_fusion.1 = (bf16[512,768]{1,0:T(8,128)(2,1)S(1)}, f32[512,768]{1,0:T(8,128)S(1)}, f32[512,768]{1,0:T(8,128)S(1)}) fusion(f32[768]{0:T(1024)S(1)} %convert_reduce_fusion.1, bf16[512,768]{1,0:T(8,128)(2,1)S(1)} %add_convert_fusion.14, bf16[768,768]{0,1:T(8,128)(2,1)} %collective-permute-done.12), kind=kOutput, calls=%fused_computation.75 | convolution fusion | flops 629932032 | bytes 5901312 | tf_op jit(solution)/shard_map/dot_general | solution.py:25
  131.3 2.1 fusion.134
  133.4 10.3 %multiply_convert_fusion.2 = (bf16[512,768]{1,0:T(8,128)(2,1)S(1)}, f32[512,768]{1,0:T(8,128)S(1)}, f32[512,768]{1,0:T(8,128)S(1)}) fusion(f32[768]{0:T(1024)S(1)} %convert_reduce_fusion.2, bf16[512,768]{1,0:T(8,128)(2,1)S(1)} %add_convert_fusion.14, bf16[384,768]{0,1:T(8,128)(2,1)S(1)} %copy-done.12, bf16[384,768]{0,1:T(8,128)(2,1)S(1)} %get-tuple-element.165), kind=kOutput, calls=%fused_computation.88 | convolution fusion | flops 632291328 | bytes 5901312 | tf_op jit(solution)/shard_map/dot_general | solution.py:25
  143.8 2.4 fusion.173
  146.2 5.7 %multiply_convert_fusion.3 = (bf16[512,768]{1,0:T(8,128)(2,1)S(1)}, f32[512,768]{1,0:T(8,128)S(1)}, f32[512,768]{1,0:T(8,128)S(1)}) fusion(f32[768]{0:T(1024)S(1)} %convert_reduce_fusion.3, bf16[512,768]{1,0:T(8,128)(2,1)S(1)} %add_convert_fusion.14, bf16[768,768]{1,0:T(8,128)(2,1)} %collective-permute-done.4), kind=kOutput, calls=%fused_computation.101 | convolution fusion | flops 629932032 | bytes 5901312 | tf_op jit(solution)/shard_map/dot_general | solution.py:25
  151.9 2.1 fusion.172
  160.9 2.5 fusion.156
  165.2 2.5 fusion.157
  169.5 2.5 fusion.171
  172.0 2.4 fusion.138
  175.6 2.4 fusion.175
  177.9 2.1 fusion.176
  181.3 2.2 fusion.158
  186.0 2.3 copy.186
  188.3 2.9 reshape.284
  191.2 5.0 %fusion.85 = f32[2,12,256,256]{2,3,1,0:T(8,128)} fusion(bf16[2,256,12,64]{1,0,3,2:T(2,128)(2,1)} %reshape.284, bf16[2,256,12,64]{1,0,3,2:T(2,128)(2,1)} %reshape.280), kind=kOutput, calls=%fused_computation.211 | convolution fusion | flops 201326592 | bytes 7864320 | tf_op jit(solution)/shard_map/bqhe,bkhe->bhqk/dot_general | solution.py:231
  196.3 11.3 %fusion.73 = bf16[2,256,12,64]{1,3,2,0:T(8,128)(2,1)} fusion(f32[2,12,256,256]{2,3,1,0:T(8,128)} %fusion.85, bf16[2,256,12,64]{1,0,3,2:T(2,128)(2,1)} %reshape.281, f32[2,12,256,256]{2,3,1,0:T(8,128)} %copy-done.78, f32[2,12,256]{2,1,0:T(8,128)S(1)} %copy-done.80), kind=kOutput, calls=%fused_computation.174 | convolution fusion | flops 212736256 | bytes 14180352 | tf_op jit(solution)/shard_map/bhqk,bqhe->bkhe/dot_general | solution.py:235
  207.6 11.3 %fusion.76 = bf16[2,256,12,64]{1,3,2,0:T(8,128)(2,1)} fusion(f32[2,12,256,256]{2,3,1,0:T(8,128)} %fusion.85, bf16[2,256,12,64]{1,0,3,2:T(2,128)(2,1)} %reshape.282, f32[2,12,256,256]{2,3,1,0:T(8,128)} %copy-done.78, f32[2,12,256]{2,1,0:T(8,128)S(1)} %copy-done.80), kind=kOutput, calls=%fused_computation.175 | convolution fusion | flops 212736256 | bytes 14180352 | tf_op jit(solution)/shard_map/bhqk,bkhe->bqhe/dot_general | solution.py:234
  218.9 4.2 fusion.67
  233.6 2.1 bitcast_reduce_fusion
  254.0 2.0 concatenate.116
  259.8 2.3 fusion.63
  278.6 2.2 collective-permute-done.34
  282.0 2.3 add_convert_fusion.7
  286.2 2.1 add_convert_fusion.8
  288.3 2.7 collective-permute-start.35
  291.0 2.1 add_convert_fusion.4
  293.7 2.1 add_convert_fusion.5
  297.9 15.4 %collective-permute-done.38 = bf16[768,768]{1,0:T(8,128)(2,1)S(1)} collective-permute-done((bf16[768,768]{1,0:T(8,128)(2,1)S(1)}, bf16[768,768]{1,0:T(8,128)(2,1)S(1)}, u32[]{:S(2)}, u32[]{:S(2)}) %collective-permute-start.38) | collective-permute-done | bytes 1179680 | tf_op jit(solution)/shard_map/ppermute | solution.py:41
  316.9 21.7 %collective-permute-done.47 = bf16[768,768]{1,0:T(8,128)(2,1)S(1)} collective-permute-done((bf16[768,768]{1,0:T(8,128)(2,1)S(1)}, bf16[768,768]{1,0:T(8,128)(2,1)S(1)}, u32[]{:S(2)}, u32[]{:S(2)}) %collective-permute-start.47) | collective-permute-done | bytes 1179680 | tf_op jit(solution)/shard_map/ppermute | solution.py:41
  342.1 25.1 %collective-permute-done.17 = bf16[896,768]{0,1:T(8,128)(2,1)S(1)} collective-permute-done((bf16[896,768]{0,1:T(8,128)(2,1)S(1)}, bf16[896,768]{0,1:T(8,128)(2,1)S(1)}, u32[]{:S(2)}, u32[]{:S(2)}) %collective-permute-start.17) | collective-permute-done | bytes 1376288 | tf_op jit(solution)/shard_map/ppermute | solution.py:41
  376.6 8.2 %collective-permute-done.40 = bf16[2,96,768]{2,1,0:T(8,128)(2,1)S(1)} collective-permute-done((bf16[2,96,768]{2,1,0:T(8,128)(2,1)S(1)}, bf16[2,96,768]{2,1,0:T(8,128)(2,1)S(1)}, u32[]{:S(2)}, u32[]{:S(2)}) %collective-permute-start.40) | collective-permute-done | bytes 294944 | tf_op jit(solution)/shard_map/ppermute | solution.py:45
  385.9 3.1 collective-permute-done.49
  389.2 2.7 collective-permute-start.50
  391.8 6.8 %collective-permute-done.41 = bf16[96,768]{1,0:T(8,128)(2,1)S(1)} collective-permute-done((bf16[96,768]{1,0:T(8,128)(2,1)S(1)}, bf16[96,768]{1,0:T(8,128)(2,1)S(1)}, u32[]{:S(2)}, u32[]{:S(2)}) %collective-permute-start.41) | collective-permute-done | bytes 147488 | tf_op jit(solution)/shard_map/ppermute | solution.py:45
  399.0 3.9 collective-permute-start.19
  403.0 6.5 %collective-permute-done.42 = bf16[96,768]{1,0:T(8,128)(2,1)S(1)} collective-permute-done((bf16[96,768]{1,0:T(8,128)(2,1)S(1)}, bf16[96,768]{1,0:T(8,128)(2,1)S(1)}, u32[]{:S(2)}, u32[]{:S(2)}) %collective-permute-start.42) | collective-permute-done | bytes 147488 | tf_op jit(solution)/shard_map/ppermute | solution.py:45
  409.6 6.5 %collective-permute-done.19 = bf16[2,112,768]{2,1,0:T(8,128)(2,1)S(1)} collective-permute-done((bf16[2,112,768]{2,1,0:T(8,128)(2,1)S(1)}, bf16[2,112,768]{2,1,0:T(8,128)(2,1)S(1)}, u32[]{:S(2)}, u32[]{:S(2)}) %collective-permute-start.19) | collective-permute-done | bytes 344096 | tf_op jit(solution)/shard_map/ppermute | solution.py:45
  417.4 2.5 collective-permute-start.52
  419.9 4.3 collective-permute-done.43
  426.1 6.3 %collective-permute-done.52 = bf16[2,96,768]{2,1,0:T(8,128)(2,1)S(1)} collective-permute-done((bf16[2,96,768]{2,1,0:T(8,128)(2,1)S(1)}, bf16[2,96,768]{2,1,0:T(8,128)(2,1)S(1)}, u32[]{:S(2)}, u32[]{:S(2)}) %collective-permute-start.52) | collective-permute-done | bytes 294944 | tf_op jit(solution)/shard_map/ppermute | solution.py:45
  433.6 2.2 fusion.83
  437.6 10.0 %collective-permute-done.53 = bf16[2,2,96,768]{3,2,1,0:T(8,128)(2,1)S(1)} collective-permute-done((bf16[2,2,96,768]{3,2,1,0:T(8,128)(2,1)S(1)}, bf16[2,2,96,768]{3,2,1,0:T(8,128)(2,1)S(1)}, u32[]{:S(2)}, u32[]{:S(2)}) %collective-permute-start.53) | collective-permute-done | bytes 589856 | tf_op jit(solution)/shard_map/ppermute | solution.py:45
  449.0 13.7 %collective-permute-done.23 = bf16[2,2,112,768]{3,2,1,0:T(8,128)(2,1)S(1)} collective-permute-done((bf16[2,2,112,768]{3,2,1,0:T(8,128)(2,1)S(1)}, bf16[2,2,112,768]{3,2,1,0:T(8,128)(2,1)S(1)}, u32[]{:S(2)}, u32[]{:S(2)}) %collective-permute-start.23) | collective-permute-done | bytes 688160 | tf_op jit(solution)/shard_map/ppermute | solution.py:45
  474.1 3.0 slice_bitcast_fusion.6
  (471 shorter events, 168.5 us)
Async XLA Ops:
  0.7 15.4 %copy-start = (bf16[1000,768]{1,0:T(8,128)(2,1)S(1)}, bf16[1000,768]{1,0:T(8,128)(2,1)}, u32[]{:S(2)}) copy-start(bf16[1000,768]{1,0:T(8,128)(2,1)} %param.29) | copy-start | bytes 4608004
  3.1 48.2 %collective-permute-start = (bf16[768,768]{0,1:T(8,128)(2,1)}, bf16[768,768]{0,1:T(8,128)(2,1)}, u32[]{:S(2)}, u32[]{:S(2)}) collective-permute-start(bf16[768,768]{0,1:T(8,128)(2,1)} %pad_maximum_fusion.1), channel_id=1, source_target_pairs={{0,1},{1,0},{2,3},{3,2},{4,5},{5,4},{6,7},{7,6},{8,9},{9,8},{10,11... | collective-permute-start | bytes 3538952 | tf_op jit(solution)/shard_map/ppermute | solution.py:41
  5.6 17.0 %collective-permute-start.1 = (bf16[384,768]{0,1:T(8,128)(2,1)}, bf16[384,768]{0,1:T(8,128)(2,1)}, u32[]{:S(2)}, u32[]{:S(2)}) collective-permute-start(bf16[384,768]{0,1:T(8,128)(2,1)} %constant_dynamic-slice_fusion.8), channel_id=1, source_target_pairs={{0,2},{1,3},{2,0},{3,1},{4,6},{5,7},{6,4},{7,5},{8,10},{9,11},{10,... | collective-permute-start | bytes 1769480 | tf_op jit(solution)/shard_map/ppermute | solution.py:41
  10.3 41.0 %collective-permute-start.7 = (bf16[384,768]{0,1:T(8,128)(2,1)}, bf16[384,768]{0,1:T(8,128)(2,1)}, u32[]{:S(2)}, u32[]{:S(2)}) collective-permute-start(bf16[384,768]{0,1:T(8,128)(2,1)} %copy.184), channel_id=1, source_target_pairs={{0,2},{1,3},{2,0},{3,1},{4,6},{5,7},{6,4},{7,5},{8,10},{9,11},{10,... | collective-permute-start | bytes 1769480 | tf_op jit(solution)/shard_map/ppermute | solution.py:41
  10.3 46.4 %collective-permute-start.13 = (bf16[1,768]{1,0:T(2,128)(2,1)S(1)}, bf16[1,768]{1,0:T(2,128)(2,1)S(1)}, u32[]{:S(2)}, u32[]{:S(2)}) collective-permute-start(bf16[1,768]{1,0:T(2,128)(2,1)S(1)} %copy-done.65), channel_id=1, source_target_pairs={{0,3},{1,2},{2,1},{3,0},{4,7},{5,6},{6,5},{7,4},{8,11},{9,10},{10,... | collective-permute-start | bytes 4616 | tf_op jit(solution)/shard_map/ppermute | solution.py:41
  11.9 14.4 %collective-permute-start.26 = (s32[2,4]{0,1:T(4,128)S(1)}, s32[2,4]{0,1:T(4,128)S(1)}, u32[]{:S(2)}, u32[]{:S(2)}) collective-permute-start(s32[2,4]{0,1:T(4,128)S(1)} %copy.212), channel_id=1, source_target_pairs={{0,1},{1,0},{2,3},{3,2},{4,5},{5,4},{6,7},{7,6},{8,9},{9,8},{10,11... | collective-permute-start | bytes 104 | tf_op jit(solution)/shard_map/ppermute | solution.py:41
  17.3 214.4 %copy-start.2 = (f32[512,768]{1,0:T(8,128)}, f32[512,768]{1,0:T(8,128)S(1)}, u32[]{:S(2)}) copy-start(f32[512,768]{1,0:T(8,128)S(1)} %get-tuple-element.201) | copy-start | bytes 4718596
  22.6 27.0 %collective-permute-start.2 = (bf16[384,768]{0,1:T(8,128)(2,1)}, bf16[384,768]{0,1:T(8,128)(2,1)}, u32[]{:S(2)}, u32[]{:S(2)}) collective-permute-start(bf16[384,768]{0,1:T(8,128)(2,1)} %collective-permute-done.1), channel_id=1, source_target_pairs={{0,4},{4,0},{8,12},{12,8},{16,20},{20,16},{24,28},{28,24},{1,5},{5... | collective-permute-start | bytes 1769480 | tf_op jit(solution)/shard_map/ppermute | solution.py:45
  26.4 8.6 %collective-permute-start.27 = (s32[4,4]{0,1:T(4,128)S(1)}, s32[4,4]{0,1:T(4,128)S(1)}, u32[]{:S(2)}, u32[]{:S(2)}) collective-permute-start(s32[4,4]{0,1:T(4,128)S(1)} %pad_add_fusion), channel_id=1, source_target_pairs={{0,2},{1,3},{2,0},{3,1},{4,6},{5,7},{6,4},{7,5},{8,10},{9,11},{10,... | collective-permute-start | bytes 200 | tf_op jit(solution)/shard_map/ppermute | solution.py:41
  35.2 3.6 collective-permute-start.28
  38.8 3.6 collective-permute-start.29
  42.5 4.5 collective-permute-start.30
  47.0 9.9 %collective-permute-start.9 = (bf16[1,768]{1,0:T(2,128)(2,1)S(1)}, bf16[1,768]{1,0:T(2,128)(2,1)S(1)}, u32[]{:S(2)}, u32[]{:S(2)}) collective-permute-start(bf16[1,768]{1,0:T(2,128)(2,1)S(1)} %copy-done.65), channel_id=1, source_target_pairs={{0,2},{1,3},{2,0},{3,1},{4,6},{5,7},{6,4},{7,5},{8,10},{9,11},{10,... | collective-permute-start | bytes 4616 | tf_op jit(solution)/shard_map/ppermute | solution.py:41
  49.6 11.9 %collective-permute-start.10 = (bf16[384,768]{0,1:T(8,128)(2,1)}, bf16[384,768]{0,1:T(8,128)(2,1)S(1)}, u32[]{:S(2)}, u32[]{:S(2)}) collective-permute-start(bf16[384,768]{0,1:T(8,128)(2,1)} %copy.185), channel_id=1, source_target_pairs={{0,2},{1,3},{2,0},{3,1},{4,6},{5,7},{6,4},{7,5},{8,10},{9,11},{10,... | collective-permute-start | bytes 1769480 | tf_op jit(solution)/shard_map/ppermute | solution.py:41
  51.3 11.8 %collective-permute-start.5 = (bf16[1,768]{1,0:T(2,128)(2,1)S(1)}, bf16[1,768]{1,0:T(2,128)(2,1)S(1)}, u32[]{:S(2)}, u32[]{:S(2)}) collective-permute-start(bf16[1,768]{1,0:T(2,128)(2,1)S(1)} %copy-done.65), channel_id=1, source_target_pairs={{0,1},{1,0},{2,3},{3,2},{4,5},{5,4},{6,7},{7,6},{8,9},{9,8},{10,11... | collective-permute-start | bytes 4616 | tf_op jit(solution)/shard_map/ppermute | solution.py:41
  51.3 16.4 %collective-permute-start.8 = (bf16[384,768]{0,1:T(8,128)(2,1)}, bf16[384,768]{0,1:T(8,128)(2,1)S(1)}, u32[]{:S(2)}, u32[]{:S(2)}) collective-permute-start(bf16[384,768]{0,1:T(8,128)(2,1)} %collective-permute-done.7), channel_id=1, source_target_pairs={{0,4},{4,0},{8,12},{12,8},{16,20},{20,16},{24,28},{28,24},{1,5},{5... | collective-permute-start | bytes 1769480 | tf_op jit(solution)/shard_map/ppermute | solution.py:45
  56.7 24.5 %collective-permute-start.3 = (bf16[768,768]{0,1:T(8,128)(2,1)S(1)}, bf16[768,768]{0,1:T(8,128)(2,1)S(1)}, u32[]{:S(2)}, u32[]{:S(2)}) collective-permute-start(bf16[768,768]{0,1:T(8,128)(2,1)S(1)} %get-tuple-element.167), channel_id=1, source_target_pairs={{0,1},{1,0},{2,3},{3,2},{4,5},{5,4},{6,7},{7,6},{8,9},{9,8},{10,11... | collective-permute-start | bytes 3538952 | tf_op jit(solution)/shard_map/ppermute | solution.py:41
  56.9 89.3 %collective-permute-start.4 = (bf16[768,768]{1,0:T(8,128)(2,1)}, bf16[768,768]{1,0:T(8,128)(2,1)}, u32[]{:S(2)}, u32[]{:S(2)}) collective-permute-start(bf16[768,768]{1,0:T(8,128)(2,1)} %bitcast.12), channel_id=1, source_target_pairs={{0,1},{1,0},{2,3},{3,2},{4,5},{5,4},{6,7},{7,6},{8,9},{9,8},{10,11... | collective-permute-start | bytes 3538952 | tf_op jit(solution)/shard_map/ppermute | solution.py:41
  61.5 18.4 %collective-permute-start.11 = (bf16[384,768]{0,1:T(8,128)(2,1)S(1)}, bf16[384,768]{0,1:T(8,128)(2,1)S(1)}, u32[]{:S(2)}, u32[]{:S(2)}) collective-permute-start(bf16[384,768]{0,1:T(8,128)(2,1)S(1)} %collective-permute-done.10), channel_id=1, source_target_pairs={{0,4},{4,0},{8,12},{12,8},{16,20},{20,16},{24,28},{28,24},{1,5},{5... | collective-permute-start | bytes 1769480 | tf_op jit(solution)/shard_map/ppermute | solution.py:45
  63.0 88.9 %collective-permute-start.6 = (bf16[768,768]{1,0:T(8,128)(2,1)}, bf16[768,768]{1,0:T(8,128)(2,1)}, u32[]{:S(2)}, u32[]{:S(2)}) collective-permute-start(bf16[768,768]{1,0:T(8,128)(2,1)} %bitcast.13), channel_id=1, source_target_pairs={{0,1},{1,0},{2,3},{3,2},{4,5},{5,4},{6,7},{7,6},{8,9},{9,8},{10,11... | collective-permute-start | bytes 3538952 | tf_op jit(solution)/shard_map/ppermute | solution.py:41
  70.1 55.4 %collective-permute-start.12 = (bf16[768,768]{0,1:T(8,128)(2,1)}, bf16[768,768]{0,1:T(8,128)(2,1)}, u32[]{:S(2)}, u32[]{:S(2)}) collective-permute-start(bf16[768,768]{0,1:T(8,128)(2,1)} %pad_maximum_fusion.3), channel_id=1, source_target_pairs={{0,1},{1,0},{2,3},{3,2},{4,5},{5,4},{6,7},{7,6},{8,9},{9,8},{10,11... | collective-permute-start | bytes 3538952 | tf_op jit(solution)/shard_map/ppermute | solution.py:41
  81.2 62.6 %collective-permute-start.14 = (bf16[768,768]{0,1:T(8,128)(2,1)}, bf16[768,768]{0,1:T(8,128)(2,1)}, u32[]{:S(2)}, u32[]{:S(2)}) collective-permute-start(bf16[768,768]{0,1:T(8,128)(2,1)} %pad_maximum_fusion.4), channel_id=1, source_target_pairs={{0,1},{1,0},{2,3},{3,2},{4,5},{5,4},{6,7},{7,6},{8,9},{9,8},{10,11... | collective-permute-start | bytes 3538952 | tf_op jit(solution)/shard_map/ppermute | solution.py:41
  119.7 47.9 %copy-start.47 = (bf16[512,768]{1,0:T(8,128)(2,1)}, bf16[512,768]{1,0:T(8,128)(2,1)S(1)}, u32[]{:S(2)}) copy-start(bf16[512,768]{1,0:T(8,128)(2,1)S(1)} %add_convert_fusion.14) | copy-start | bytes 2359300
  157.2 17.1 %copy-start.49 = (bf16[512,768]{1,0:T(8,128)(2,1)}, bf16[512,768]{1,0:T(8,128)(2,1)S(1)}, u32[]{:S(2)}) copy-start(bf16[512,768]{1,0:T(8,128)(2,1)S(1)} %get-tuple-element.210) | copy-start | bytes 2359300
  250.9 33.5 %collective-permute-start.36 = (bf16[768,768]{1,0:T(8,128)(2,1)}, bf16[768,768]{1,0:T(8,128)(2,1)}, u32[]{:S(2)}, u32[]{:S(2)}) collective-permute-start(bf16[768,768]{1,0:T(8,128)(2,1)} %convolution_convert_fusion.6), channel_id=1, source_target_pairs={{0,1},{1,0},{2,3},{3,2},{4,5},{5,4},{6,7},{7,6},{8,9},{9,8},{10,11... | collective-permute-start | bytes 3538952 | tf_op jit(solution)/shard_map/ppermute | solution.py:41
  251.0 30.5 %collective-permute-start.37 = (bf16[768,768]{1,0:T(8,128)(2,1)}, bf16[768,768]{1,0:T(8,128)(2,1)}, u32[]{:S(2)}, u32[]{:S(2)}) collective-permute-start(bf16[768,768]{1,0:T(8,128)(2,1)} %convolution_convert_fusion.4), channel_id=1, source_target_pairs={{0,1},{1,0},{2,3},{3,2},{4,5},{5,4},{6,7},{7,6},{8,9},{9,8},{10,11... | collective-permute-start | bytes 3538952 | tf_op jit(solution)/shard_map/ppermute | solution.py:41
  251.5 41.6 %collective-permute-start.45 = (bf16[768,768]{1,0:T(8,128)(2,1)}, bf16[768,768]{1,0:T(8,128)(2,1)}, u32[]{:S(2)}, u32[]{:S(2)}) collective-permute-start(bf16[768,768]{1,0:T(8,128)(2,1)} %convolution_convert_fusion.2), channel_id=1, source_target_pairs={{0,1},{1,0},{2,3},{3,2},{4,5},{5,4},{6,7},{7,6},{8,9},{9,8},{10,11... | collective-permute-start | bytes 3538952 | tf_op jit(solution)/shard_map/ppermute | solution.py:41
  252.3 15.9 %collective-permute-start.31 = (bf16[8,768]{1,0:T(8,128)(2,1)S(1)}, bf16[8,768]{1,0:T(8,128)(2,1)S(1)}, u32[]{:S(2)}, u32[]{:S(2)}) collective-permute-start(bf16[8,768]{1,0:T(8,128)(2,1)S(1)} %get-tuple-element.128), channel_id=1, source_target_pairs={{0,1},{1,0},{2,3},{3,2},{4,5},{5,4},{6,7},{7,6},{8,9},{9,8},{10,11... | collective-permute-start | bytes 36872 | tf_op jit(solution)/shard_map/ppermute | solution.py:41
  264.6 17.4 %copy-start.43 = (bf16[512,768]{1,0:T(8,128)(2,1)S(1)}, bf16[512,768]{1,0:T(8,128)(2,1)}, u32[]{:S(2)}) copy-start(bf16[512,768]{1,0:T(8,128)(2,1)} %copy-done.42) | copy-start | bytes 2359300
  265.8 22.5 %collective-permute-start.46 = (bf16[768,768]{1,0:T(8,128)(2,1)}, bf16[768,768]{1,0:T(8,128)(2,1)}, u32[]{:S(2)}, u32[]{:S(2)}) collective-permute-start(bf16[768,768]{1,0:T(8,128)(2,1)} %convolution_convert_fusion), channel_id=1, source_target_pairs={{0,1},{1,0},{2,3},{3,2},{4,5},{5,4},{6,7},{7,6},{8,9},{9,8},{10,11... | collective-permute-start | bytes 3538952 | tf_op jit(solution)/shard_map/ppermute | solution.py:41
  268.1 3.8 collective-permute-start.32
  272.0 4.1 collective-permute-start.33
  276.1 4.7 collective-permute-start.34
  280.8 15.0 %collective-permute-start.16 = (bf16[896,768]{0,1:T(8,128)(2,1)S(1)}, bf16[896,768]{0,1:T(8,128)(2,1)S(1)}, u32[]{:S(2)}, u32[]{:S(2)}) collective-permute-start(bf16[896,768]{0,1:T(8,128)(2,1)S(1)} %fusion.65), channel_id=1, source_target_pairs={{0,1},{1,0},{2,3},{3,2},{4,5},{5,4},{6,7},{7,6},{8,9},{9,8},{10,11... | collective-permute-start | bytes 4128776 | tf_op jit(solution)/shard_map/ppermute | solution.py:41
  281.5 60.7 %collective-permute-start.15 = (bf16[896,768]{0,1:T(8,128)(2,1)}, bf16[896,768]{0,1:T(8,128)(2,1)S(1)}, u32[]{:S(2)}, u32[]{:S(2)}) collective-permute-start(bf16[896,768]{0,1:T(8,128)(2,1)} %fusion.63), channel_id=1, source_target_pairs={{0,1},{1,0},{2,3},{3,2},{4,5},{5,4},{6,7},{7,6},{8,9},{9,8},{10,11... | collective-permute-start | bytes 4128776 | tf_op jit(solution)/shard_map/ppermute | solution.py:41
  284.4 28.9 %collective-permute-start.38 = (bf16[768,768]{1,0:T(8,128)(2,1)S(1)}, bf16[768,768]{1,0:T(8,128)(2,1)S(1)}, u32[]{:S(2)}, u32[]{:S(2)}) collective-permute-start(bf16[768,768]{1,0:T(8,128)(2,1)S(1)} %add_convert_fusion.7), channel_id=1, source_target_pairs={{0,2},{1,3},{2,0},{3,1},{4,6},{5,7},{6,4},{7,5},{8,10},{9,11},{10,... | collective-permute-start | bytes 3538952 | tf_op jit(solution)/shard_map/ppermute | solution.py:41
  288.3 144.3 %collective-permute-start.35 = (bf16[128,768]{1,0:T(8,128)(2,1)}, bf16[128,768]{1,0:T(8,128)(2,1)S(1)}, u32[]{:S(2)}, u32[]{:S(2)}) collective-permute-start(bf16[128,768]{1,0:T(8,128)(2,1)} %get-tuple-element.192), channel_id=1, source_target_pairs={{0,16},{4,20},{8,24},{12,28},{16,0},{20,4},{24,8},{28,12},{1,17},{... | collective-permute-start | bytes 589832 | tf_op jit(solution)/shard_map/ppermute | solution.py:45
  293.1 45.4 %collective-permute-start.47 = (bf16[768,768]{1,0:T(8,128)(2,1)S(1)}, bf16[768,768]{1,0:T(8,128)(2,1)S(1)}, u32[]{:S(2)}, u32[]{:S(2)}) collective-permute-start(bf16[768,768]{1,0:T(8,128)(2,1)S(1)} %add_convert_fusion.4), channel_id=1, source_target_pairs={{0,2},{1,3},{2,0},{3,1},{4,6},{5,7},{6,4},{7,5},{8,10},{9,11},{10,... | collective-permute-start | bytes 3538952 | tf_op jit(solution)/shard_map/ppermute | solution.py:41
  296.3 70.9 %collective-permute-start.17 = (bf16[896,768]{0,1:T(8,128)(2,1)S(1)}, bf16[896,768]{0,1:T(8,128)(2,1)S(1)}, u32[]{:S(2)}, u32[]{:S(2)}) collective-permute-start(bf16[896,768]{0,1:T(8,128)(2,1)S(1)} %add_convert_fusion.1), channel_id=1, source_target_pairs={{0,2},{1,3},{2,0},{3,1},{4,6},{5,7},{6,4},{7,5},{8,10},{9,11},{10,... | collective-permute-start | bytes 4128776 | tf_op jit(solution)/shard_map/ppermute | solution.py:41
  315.2 56.8 %collective-permute-start.39 = (bf16[2,2,96,768]{3,2,1,0:T(8,128)(2,1)}, bf16[2,2,96,768]{3,2,1,0:T(8,128)(2,1)}, u32[]{:S(2)}, u32[]{:S(2)}) collective-permute-start(bf16[2,2,96,768]{3,2,1,0:T(8,128)(2,1)} %slice_bitcast_fusion.4), channel_id=1, source_target_pairs={{0,4},{4,0},{8,12},{12,8},{16,20},{20,16},{24,28},{28,24},{1,5},{5... | collective-permute-start | bytes 1769480 | tf_op jit(solution)/shard_map/ppermute | solution.py:45
  339.3 27.9 %copy-start.27 = (bf16[768,192]{0,1:T(8,128)(2,1)S(1)}, bf16[768,192]{0,1:T(8,128)(2,1)}, u32[]{:S(2)}) copy-start(bf16[768,192]{0,1:T(8,128)(2,1)} %convolution_convert_fusion.24) | copy-start | bytes 884740
  339.3 27.9 %copy-start.28 = (bf16[768,192]{0,1:T(8,128)(2,1)S(1)}, bf16[768,192]{0,1:T(8,128)(2,1)}, u32[]{:S(2)}) copy-start(bf16[768,192]{0,1:T(8,128)(2,1)} %convolution_convert_fusion.26) | copy-start | bytes 884740
  339.3 27.9 %copy-start.29 = (bf16[768,192]{0,1:T(8,128)(2,1)S(1)}, bf16[768,192]{0,1:T(8,128)(2,1)}, u32[]{:S(2)}) copy-start(bf16[768,192]{0,1:T(8,128)(2,1)} %convolution_convert_fusion.27) | copy-start | bytes 884740
  339.3 27.9 %copy-start.30 = (bf16[768,192]{0,1:T(8,128)(2,1)S(1)}, bf16[768,192]{0,1:T(8,128)(2,1)}, u32[]{:S(2)}) copy-start(bf16[768,192]{0,1:T(8,128)(2,1)} %convolution_convert_fusion.25) | copy-start | bytes 884740
  339.6 27.7 %copy-start.21 = (bf16[2,2,2,96,768]{4,3,2,1,0:T(8,128)(2,1)}, bf16[2,2,2,96,768]{4,3,2,1,0:T(8,128)(2,1)S(1)}, u32[]{:S(2)}) copy-start(bf16[2,2,2,96,768]{4,3,2,1,0:T(8,128)(2,1)S(1)} %reverse_select_fusion.9) | copy-start | bytes 3538948
  340.4 34.4 %collective-permute-start.48 = (bf16[2,2,96,768]{3,2,1,0:T(8,128)(2,1)}, bf16[2,2,96,768]{3,2,1,0:T(8,128)(2,1)}, u32[]{:S(2)}, u32[]{:S(2)}) collective-permute-start(bf16[2,2,96,768]{3,2,1,0:T(8,128)(2,1)} %slice_bitcast_fusion.2), channel_id=1, source_target_pairs={{0,4},{4,0},{8,12},{12,8},{16,20},{20,16},{24,28},{28,24},{1,5},{5... | collective-permute-start | bytes 1769480 | tf_op jit(solution)/shard_map/ppermute | solution.py:45
  370.1 28.6 %collective-permute-start.18 = (bf16[2,2,112,768]{3,2,1,0:T(8,128)(2,1)S(1)}, bf16[2,2,112,768]{3,2,1,0:T(8,128)(2,1)S(1)}, u32[]{:S(2)}, u32[]{:S(2)}) collective-permute-start(bf16[2,2,112,768]{3,2,1,0:T(8,128)(2,1)S(1)} %slice_bitcast_fusion), channel_id=1, source_target_pairs={{0,4},{4,0},{8,12},{12,8},{16,20},{20,16},{24,28},{28,24},{1,5},{5... | collective-permute-start | bytes 2064392 | tf_op jit(solution)/shard_map/ppermute | solution.py:45
  373.2 11.6 %collective-permute-start.40 = (bf16[2,96,768]{2,1,0:T(8,128)(2,1)S(1)}, bf16[2,96,768]{2,1,0:T(8,128)(2,1)S(1)}, u32[]{:S(2)}, u32[]{:S(2)}) collective-permute-start(bf16[2,96,768]{2,1,0:T(8,128)(2,1)S(1)} %slice_bitcast_fusion.15), channel_id=1, source_target_pairs={{0,8},{4,12},{8,0},{12,4},{16,24},{20,28},{24,16},{28,20},{1,9},{5... | collective-permute-start | bytes 884744 | tf_op jit(solution)/shard_map/ppermute | solution.py:45
  376.1 13.0 %collective-permute-start.49 = (bf16[2,96,768]{2,1,0:T(8,128)(2,1)S(1)}, bf16[2,96,768]{2,1,0:T(8,128)(2,1)S(1)}, u32[]{:S(2)}, u32[]{:S(2)}) collective-permute-start(bf16[2,96,768]{2,1,0:T(8,128)(2,1)S(1)} %slice_bitcast_fusion.13), channel_id=1, source_target_pairs={{0,8},{4,12},{8,0},{12,4},{16,24},{20,28},{24,16},{28,20},{1,9},{5... | collective-permute-start | bytes 884744 | tf_op jit(solution)/shard_map/ppermute | solution.py:45
  384.9 13.8 %collective-permute-start.41 = (bf16[96,768]{1,0:T(8,128)(2,1)S(1)}, bf16[96,768]{1,0:T(8,128)(2,1)S(1)}, u32[]{:S(2)}, u32[]{:S(2)}) collective-permute-start(bf16[96,768]{1,0:T(8,128)(2,1)S(1)} %slice_bitcast_fusion.21), channel_id=1, source_target_pairs={{0,16},{4,20},{8,24},{12,28},{16,0},{20,4},{24,8},{28,12},{1,17},{... | collective-permute-start | bytes 442376 | tf_op jit(solution)/shard_map/ppermute | solution.py:45
  389.2 13.7 %collective-permute-start.50 = (bf16[96,768]{1,0:T(8,128)(2,1)S(1)}, bf16[96,768]{1,0:T(8,128)(2,1)S(1)}, u32[]{:S(2)}, u32[]{:S(2)}) collective-permute-start(bf16[96,768]{1,0:T(8,128)(2,1)S(1)} %slice_bitcast_fusion.19), channel_id=1, source_target_pairs={{0,16},{4,20},{8,24},{12,28},{16,0},{20,4},{24,8},{28,12},{1,17},{... | collective-permute-start | bytes 442376 | tf_op jit(solution)/shard_map/ppermute | solution.py:45
  398.7 10.8 %collective-permute-start.42 = (bf16[96,768]{1,0:T(8,128)(2,1)S(1)}, bf16[96,768]{1,0:T(8,128)(2,1)S(1)}, u32[]{:S(2)}, u32[]{:S(2)}) collective-permute-start(bf16[96,768]{1,0:T(8,128)(2,1)S(1)} %fusion.101), channel_id=1, source_target_pairs={{0,16},{4,20},{8,24},{12,28},{16,0},{20,4},{24,8},{28,12},{1,17},{... | collective-permute-start | bytes 442376 | tf_op jit(solution)/shard_map/ppermute | solution.py:45
  399.0 17.1 %collective-permute-start.19 = (bf16[2,112,768]{2,1,0:T(8,128)(2,1)S(1)}, bf16[2,112,768]{2,1,0:T(8,128)(2,1)S(1)}, u32[]{:S(2)}, u32[]{:S(2)}) collective-permute-start(bf16[2,112,768]{2,1,0:T(8,128)(2,1)S(1)} %slice_bitcast_fusion.10), channel_id=1, source_target_pairs={{0,8},{4,12},{8,0},{12,4},{16,24},{20,28},{24,16},{28,20},{1,9},{5... | collective-permute-start | bytes 1032200 | tf_op jit(solution)/shard_map/ppermute | solution.py:45
  402.9 14.4 %collective-permute-start.51 = (bf16[96,768]{1,0:T(8,128)(2,1)S(1)}, bf16[96,768]{1,0:T(8,128)(2,1)S(1)}, u32[]{:S(2)}, u32[]{:S(2)}) collective-permute-start(bf16[96,768]{1,0:T(8,128)(2,1)S(1)} %fusion.100), channel_id=1, source_target_pairs={{0,16},{4,20},{8,24},{12,28},{16,0},{20,4},{24,8},{28,12},{1,17},{... | collective-permute-start | bytes 442376 | tf_op jit(solution)/shard_map/ppermute | solution.py:45
  409.5 14.7 %collective-permute-start.43 = (bf16[2,96,768]{2,1,0:T(8,128)(2,1)S(1)}, bf16[2,96,768]{2,1,0:T(8,128)(2,1)S(1)}, u32[]{:S(2)}, u32[]{:S(2)}) collective-permute-start(bf16[2,96,768]{2,1,0:T(8,128)(2,1)S(1)} %get-tuple-element.190), channel_id=1, source_target_pairs={{0,8},{4,12},{8,0},{12,4},{16,24},{20,28},{24,16},{28,20},{1,9},{5... | collective-permute-start | bytes 884744 | tf_op jit(solution)/shard_map/ppermute | solution.py:45
  416.2 8.7 %collective-permute-start.20 = (bf16[112,768]{1,0:T(8,128)(2,1)S(1)}, bf16[112,768]{1,0:T(8,128)(2,1)S(1)}, u32[]{:S(2)}, u32[]{:S(2)}) collective-permute-start(bf16[112,768]{1,0:T(8,128)(2,1)S(1)} %slice_bitcast_fusion.17), channel_id=1, source_target_pairs={{0,16},{4,20},{8,24},{12,28},{16,0},{20,4},{24,8},{28,12},{1,17},{... | collective-permute-start | bytes 516104 | tf_op jit(solution)/shard_map/ppermute | solution.py:45
  417.4 15.0 %collective-permute-start.52 = (bf16[2,96,768]{2,1,0:T(8,128)(2,1)S(1)}, bf16[2,96,768]{2,1,0:T(8,128)(2,1)S(1)}, u32[]{:S(2)}, u32[]{:S(2)}) collective-permute-start(bf16[2,96,768]{2,1,0:T(8,128)(2,1)S(1)} %get-tuple-element.188), channel_id=1, source_target_pairs={{0,8},{4,12},{8,0},{12,4},{16,24},{20,28},{24,16},{28,20},{1,9},{5... | collective-permute-start | bytes 884744 | tf_op jit(solution)/shard_map/ppermute | solution.py:45
  424.3 13.1 %collective-permute-start.44 = (bf16[2,2,96,768]{3,2,1,0:T(8,128)(2,1)S(1)}, bf16[2,2,96,768]{3,2,1,0:T(8,128)(2,1)S(1)}, u32[]{:S(2)}, u32[]{:S(2)}) collective-permute-start(bf16[2,2,96,768]{3,2,1,0:T(8,128)(2,1)S(1)} %get-tuple-element.184), channel_id=1, source_target_pairs={{0,4},{4,0},{8,12},{12,8},{16,20},{20,16},{24,28},{28,24},{1,5},{5... | collective-permute-start | bytes 1769480 | tf_op jit(solution)/shard_map/ppermute | solution.py:45
  425.0 8.4 %collective-permute-start.21 = (bf16[112,768]{1,0:T(8,128)(2,1)S(1)}, bf16[112,768]{1,0:T(8,128)(2,1)S(1)}, u32[]{:S(2)}, u32[]{:S(2)}) collective-permute-start(bf16[112,768]{1,0:T(8,128)(2,1)S(1)} %fusion.99), channel_id=1, source_target_pairs={{0,16},{4,20},{8,24},{12,28},{16,0},{20,4},{24,8},{28,12},{1,17},{... | collective-permute-start | bytes 516104 | tf_op jit(solution)/shard_map/ppermute | solution.py:45
  432.5 15.0 %collective-permute-start.53 = (bf16[2,2,96,768]{3,2,1,0:T(8,128)(2,1)S(1)}, bf16[2,2,96,768]{3,2,1,0:T(8,128)(2,1)S(1)}, u32[]{:S(2)}, u32[]{:S(2)}) collective-permute-start(bf16[2,2,96,768]{3,2,1,0:T(8,128)(2,1)S(1)} %get-tuple-element.182), channel_id=1, source_target_pairs={{0,4},{4,0},{8,12},{12,8},{16,20},{20,16},{24,28},{28,24},{1,5},{5... | collective-permute-start | bytes 1769480 | tf_op jit(solution)/shard_map/ppermute | solution.py:45
  433.5 14.2 %collective-permute-start.22 = (bf16[2,112,768]{2,1,0:T(8,128)(2,1)S(1)}, bf16[2,112,768]{2,1,0:T(8,128)(2,1)S(1)}, u32[]{:S(2)}, u32[]{:S(2)}) collective-permute-start(bf16[2,112,768]{2,1,0:T(8,128)(2,1)S(1)} %get-tuple-element.186), channel_id=1, source_target_pairs={{0,8},{4,12},{8,0},{12,4},{16,24},{20,28},{24,16},{28,20},{1,9},{5... | collective-permute-start | bytes 1032200 | tf_op jit(solution)/shard_map/ppermute | solution.py:45
  447.7 14.9 %collective-permute-start.23 = (bf16[2,2,112,768]{3,2,1,0:T(8,128)(2,1)S(1)}, bf16[2,2,112,768]{3,2,1,0:T(8,128)(2,1)S(1)}, u32[]{:S(2)}, u32[]{:S(2)}) collective-permute-start(bf16[2,2,112,768]{3,2,1,0:T(8,128)(2,1)S(1)} %get-tuple-element.176), channel_id=1, source_target_pairs={{0,4},{4,0},{8,12},{12,8},{16,20},{20,16},{24,28},{28,24},{1,5},{5... | collective-permute-start | bytes 2064392 | tf_op jit(solution)/shard_map/ppermute | solution.py:45
  463.6 1.5 collective-permute-start.24
  465.8 11.4 %collective-permute-start.25 = (bf16[2,112,768]{2,1,0:T(8,128)(2,1)}, bf16[2,112,768]{2,1,0:T(8,128)(2,1)}, u32[]{:S(2)}, u32[]{:S(2)}) collective-permute-start(bf16[2,112,768]{2,1,0:T(8,128)(2,1)} %pad_maximum_fusion.13), channel_id=1, source_target_pairs={{0,2},{1,3},{2,0},{3,1},{4,6},{5,7},{6,4},{7,5},{8,10},{9,11},{10,... | collective-permute-start | bytes 1032200 | tf_op jit(solution)/shard_map/ppermute | solution.py:41
  (71 other events, 245.4 us)

commit v2 on v1

v2 whole, which is shorter than its diff:
```python
import functools

import jax
import jax.numpy as jnp
from jax import lax
from jax.experimental import pallas as pl
from jax.experimental.pallas import tpu as pltpu
from jax.sharding import PartitionSpec as P

HEAD_DIM = 64
EPSILON = 1e-05
SCALE = HEAD_DIM**-0.5
BF = jnp.bfloat16
F32 = jnp.float32
PIECES = 4
EXTRA = 16
GROUP = 32
CHAIN_ORDERS = ("yxz", "zxy", "yzx", "xyz")
BEFORE_FAR = (0, 1)
BEFORE_NEAR = ()
BEFORE_EMBED = (0, 1, 2)
TAIL = (0, 3, 0, 2, 1, 3, 1, 0, 2, 3, 2, 1, 0, 3, 1, 2, 3, 2, 3)
CHUNK = 64

VMEM = pl.BlockSpec(memory_space=pltpu.VMEM)
SMEM = pl.BlockSpec(memory_space=pltpu.SMEM)
HBM = pl.BlockSpec(memory_space=pl.ANY)


def nn(matrix, other):
    return lax.dot_general(matrix, other, (((1,), (0,)), ((), ())), preferred_element_type=F32)


def tn(matrix, other):
    return lax.dot_general(matrix, other, (((0,), (0,)), ((), ())), preferred_element_type=F32)


def nt(matrix, other):
    return lax.dot_general(matrix, other, (((1,), (1,)), ((), ())), preferred_element_type=F32)


def norm_parts(values):
    average = jnp.mean(values, -1, keepdims=True)
    centered = values - average
    spread = jnp.mean(centered * centered, -1, keepdims=True)
    rstd = lax.rsqrt(spread + EPSILON)
    return centered * rstd, rstd


def norm_back(grad, gain, xhat, rstd):
    scaled = grad * gain
    back = scaled - jnp.mean(scaled, -1, keepdims=True)
    back = back - xhat * jnp.mean(scaled * xhat, -1, keepdims=True)
    return rstd * back


def column_sum(values):
    return jnp.sum(values, 0, keepdims=True)


def over_rows(tokens, body):
    def step(index, carry):
        body(pl.ds(pl.multiple_of(index * CHUNK, CHUNK), CHUNK))
        return carry

    lax.fori_loop(0, tokens // CHUNK, step, 0)


def gelu_pair(values):
    scaled = jnp.abs(values) * 0.7071067811865476
    t = 1.0 / (1.0 + 0.3275911 * scaled)
    bell = jnp.exp(-0.5 * values * values)
    poly = 1.061405429 * t - 1.453152027
    poly = poly * t + 1.421413741
    poly = poly * t - 0.284496736
    poly = poly * t + 0.254829592
    tail = 0.5 * poly * t * bell
    below = jnp.where(values >= 0.0, 1.0 - tail, tail)
    return values * below, below + values * bell * 0.3989422804014327


def packed_flag(where_ref, seg_ref, row, length):
    start = where_ref[0] + row * length
    return seg_ref[start + length - 1] > 0


def embed_kernel(
    where_ref, seg_ref, patch_ref, w_ref, b_ref, pos_ref, cls_ref, gain_ref, bias_ref, hid_ref, norm_ref
):
    tokens, width = hid_ref.shape
    length = pos_ref.shape[0]
    slots = cls_ref.shape[0] // (tokens // length)
    quarter = length // slots
    hid_ref[...] = tn(patch_ref[...].astype(BF), w_ref[...]) + b_ref[...]
    for row in range(tokens // length):
        packed = packed_flag(where_ref, seg_ref, row, length)
        for slot in range(slots):
            at = slice(row * length + slot * quarter, row * length + (slot + 1) * quarter)
            here = pos_ref[slot * quarter : (slot + 1) * quarter].astype(F32)
            first = pos_ref[:quarter].astype(F32)
            one = cls_ref[row * slots + slot : row * slots + slot + 1]
            start = cls_ref[row * slots : row * slots + 1]
            value = hid_ref[at] + jnp.where(packed, first, here) + jnp.where(packed, one, start)
            hid_ref[at] = value
            xhat, _ = norm_parts(value)
            norm_ref[at] = (xhat * gain_ref[...] + bias_ref[...]).astype(BF)


def fetch_near(parts, weight_ref, sems):
    unit = weight_ref.shape[1] // 2
    copies = []
    for slot, ref in enumerate(parts):
        for half in range(2):
            for u in range(2):
                source = ref.at[half, pl.ds(unit * u, unit)]
                copies.append((source, weight_ref.at[2 * half + u, pl.ds(unit * slot, unit)]))
    return start_copies(copies, sems)


def fetch_far(where_ref, parts, weight_ref, sems):
    far, far_other, cross, cross_other = parts
    unit = weight_ref.shape[1] // 2
    x = where_ref[1]
    copies = []
    for slot, ref, half in ((0, far, x), (0, far_other, 1 - x), (1, cross, x), (1, cross_other, 1 - x)):
        for u in range(2):
            source = ref.at[pl.ds(unit * u, unit)]
            copies.append((source, weight_ref.at[2 * half + u, pl.ds(unit * slot, unit)]))
    return start_copies(copies, sems)


def fetch_half(where_ref, parts, weight_ref, sems):
    if len(parts) == 2:
        return fetch_near(parts, weight_ref, sems)
    return fetch_far(where_ref, parts, weight_ref, sems)


def start_copies(copies, sems):
    made = [pltpu.make_async_copy(src, dst, sems.at[i]) for i, (src, dst) in enumerate(copies)]
    for copy in made:
        copy.start()
    return made


def fetch_full(where_ref, parts, weight_ref, sems):
    own, near, far, far_other, cross, cross_other = parts
    half = weight_ref.shape[1] // 2
    mine = pl.ds(pl.multiple_of(where_ref[1] * half, half), half)
    other = pl.ds(pl.multiple_of((1 - where_ref[1]) * half, half), half)
    copies = [
        (own, weight_ref.at[0]),
        (near, weight_ref.at[1]),
        (far, weight_ref.at[2, mine]),
        (far_other, weight_ref.at[2, other]),
        (cross, weight_ref.at[3, mine]),
        (cross_other, weight_ref.at[3, other]),
    ]
    return start_copies(copies, sems)


def allowed_mask(packed, quarter, first, rows, keys):
    q = lax.broadcasted_iota(jnp.int32, (rows, keys), 0) + first
    k = lax.broadcasted_iota(jnp.int32, (rows, keys), 1)
    shift = quarter.bit_length() - 1
    same = (q >> shift) == (k >> shift)
    return (k <= q) & (same | jnp.logical_not(packed))


def attend_kernel(where_ref, seg_ref, hid_ref, norm_ref, *rest, length, quarter, count):
    parts = rest[:count]
    q_ref, k_ref, v_ref, prob_ref, att_ref, out_ref, weight_ref, sems = rest[count:]
    tokens = hid_ref.shape[0]
    for copy in fetch_half(where_ref, parts, weight_ref, sems):
        copy.wait()
    q_ref[...] = nt(norm_ref[...], weight_ref[0]).astype(BF)
    k_ref[...] = nt(norm_ref[...], weight_ref[1]).astype(BF)
    v_ref[...] = nt(norm_ref[...], weight_ref[2]).astype(BF)
    pairs = q_ref.shape[1] // 128
    lane = lax.broadcasted_iota(jnp.int32, (1, 128), 1)
    lefts = [(lane < HEAD_DIM).astype(BF), (lane >= HEAD_DIM).astype(BF)]
    block = length // 2

    def step(index, carry):
        row = index // pairs
        pair = index % pairs
        packed = packed_flag(where_ref, seg_ref, row, length)
        lanes = pl.ds(pl.multiple_of(pair * 128, 128), 128)
        for part in range(2):
            keys = (part + 1) * block
            here = pl.ds(pl.multiple_of(row * length + part * block, block), block)
            upto = pl.ds(pl.multiple_of(row * length, length), keys)
            mask = allowed_mask(packed, quarter, part * block, block, keys)
            queries = q_ref[here, lanes]
            key_rows = k_ref[upto, lanes]
            values = v_ref[upto, lanes]
            result = None
            for head in range(2):
                scores = nt(queries * lefts[head], key_rows) * SCALE
                scores = jnp.where(mask, scores, -1e30)
                top = jnp.max(scores, -1, keepdims=True)
                grown = jnp.exp(scores - top)
                probs = (grown / jnp.sum(grown, -1, keepdims=True)).astype(BF)
                prob_ref[2 * index + head, part * block : (part + 1) * block, :keys] = probs
                term = nn(probs, values * lefts[head])
                result = term if result is None else result + term
            att_ref[here, lanes] = result.astype(BF)
        return carry

    lax.fori_loop(0, tokens // length * pairs, step, 0)
    out_ref[...] = hid_ref[...] + nn(att_ref[...], weight_ref[3])


def up_kernel(
    where_ref, hid_ref, gain_ref, bias_ref, own, near, far, far_other, cross, cross_other,
    own_t, near_t, far_t, cross_t,
    norm_ref, act_ref, slope_ref, weight_ref, bup_ref, sems, bias_sems,
):
    tokens, width = hid_ref.shape
    copies = fetch_full(where_ref, (own, near, far, far_other, cross, cross_other), weight_ref, sems)
    last = pl.ds(far_t.shape[0] - EXTRA, EXTRA)
    packs = (own_t.at[0, last], near_t.at[0, last], far_t.at[last], cross_t.at[last])
    copies += start_copies([(pack, bup_ref.at[slot]) for slot, pack in enumerate(packs)], bias_sems)

    def normalize(at):
        xhat, _ = norm_parts(hid_ref[at])
        norm_ref[at] = (xhat * gain_ref[...] + bias_ref[...]).astype(BF)

    over_rows(tokens, normalize)
    for copy in copies:
        copy.wait()
    block = 128

    def step(slot, carry):
        bias = bup_ref[slot, :1].astype(F32)
        for first in range(0, tokens, block):
            at = slice(first, first + block)
            pre = nn(norm_ref[at], weight_ref[slot]) + bias
            value, slope = gelu_pair(pre)
            act_ref[slot, at] = value.astype(BF)
            slope_ref[slot, at] = slope.astype(BF)
        return carry

    lax.fori_loop(0, act_ref.shape[0], step, 0)


def send_pieces(where_ref, stage_ref, slot, keep, send, sems, rows):
    even = slot % 2 == 0
    place = slot // 2

    for piece in range(PIECES):
        target = piece ^ where_ref[2]
        source = stage_ref.at[piece * rows : (piece + 1) * rows]

        @pl.when(even)
        def _():
            pltpu.make_async_copy(source, keep.at[place, target, :rows], sems.at[piece]).start()

        @pl.when(jnp.logical_not(even))
        def _():
            pltpu.make_async_copy(source, send.at[place, target, :rows], sems.at[piece]).start()


def wait_pieces(stage_ref, keep, sems, rows):
    for piece in range(PIECES):
        source = stage_ref.at[piece * rows : (piece + 1) * rows]
        pltpu.make_async_copy(source, keep.at[0, 0, :rows], sems.at[piece]).wait()


def down_kernel(
    where_ref, seg_ref, hid_ref, act_ref, bdown_ref, wout_ref, bout_ref, patch_ref, lgrad_ref, dgrad_ref,
    own, near, far, far_other, cross, cross_other,
    latent_ref, logdet_ref, stat_ref, direct_ref, grad_ref, gwout_ref, gvec_ref, keep_ref, send_ref,
    weight_ref, branch_ref, stage_ref, sems, out_sems,
    *, length, quarter,
):
    tokens, width = hid_ref.shape
    channels = patch_ref.shape[0]
    for copy in fetch_full(where_ref, (own, near, far, far_other, cross, cross_other), weight_ref, sems):
        copy.wait()
    total = nn(act_ref[0], weight_ref[0])
    for slot in range(1, 4):
        total = total + nn(act_ref[slot], weight_ref[slot])
    top_low = (hid_ref[...] + total + bdown_ref[...]).astype(BF)
    head_out = nt(wout_ref[...], top_low) + bout_ref[...]
    token = lax.broadcasted_iota(jnp.int32, (1, tokens), 1)
    row_count = tokens // length
    starts = jnp.zeros((1, tokens), jnp.bool_)
    for row in range(row_count):
        packed = packed_flag(where_ref, seg_ref, row, length)
        inside = (token >= row * length) & (token < (row + 1) * length)
        fresh = (token & jnp.where(packed, quarter - 1, length - 1)) == 0
        starts = starts | (inside & fresh)
    previous = jnp.where(starts, 0.0, pltpu.roll(head_out, 1, 1))
    shifts = previous[:channels]
    logscale = previous[channels:]
    shrink = jnp.exp(-logscale)
    latents = (patch_ref[...] - shifts) * shrink
    latent_ref[...] = latents
    logdet_ref[...] = -column_sum(logscale)
    stats = jnp.zeros(stat_ref.shape, F32)
    lane = lax.broadcasted_iota(jnp.int32, stat_ref.shape, 1)
    kind = lax.broadcasted_iota(jnp.int32, stat_ref.shape, 0)
    for row in range(row_count):
        part = logscale[:, row * length : (row + 1) * length]
        mean = jnp.sum(part) * (1.0 / (length * channels))
        stats = jnp.where((lane == row) & (kind == 0), mean, stats)
        stats = jnp.where((lane == row) & (kind == 1), jnp.max(part), stats)
    stat_ref[...] = stats
    lgrad = lgrad_ref[...]
    direct = lgrad * shrink
    direct_ref[...] = direct
    grad_prev = jnp.concatenate([-direct, -lgrad * latents - dgrad_ref[...]], 0)
    grad_prev = jnp.where(starts, 0.0, grad_prev)
    grad_head = pltpu.roll(grad_prev, tokens - 1, 1).astype(BF)
    gwout_ref[...] = nn(grad_head, top_low)
    grad_hidden = tn(grad_head, wout_ref[...])
    grad_ref[...] = grad_hidden
    branch_ref[...] = grad_hidden.astype(BF)
    gvec_ref[...] = jnp.zeros(gvec_ref.shape, F32)
    gvec_ref[0:1, :] = column_sum(grad_hidden)
    row_of = nt(jnp.ones((8, tokens), BF), grad_head)
    gvec_ref[1:2, : 2 * channels] = row_of[:1]
    rows = width // PIECES

    def step(slot, carry):
        @pl.when(slot >= 2)
        def _():
            wait_pieces(stage_ref.at[slot % 2], keep_ref, out_sems.at[slot % 2], rows)

        stage_ref[slot % 2] = tn(act_ref[slot], branch_ref[...]).astype(BF)
        send_pieces(where_ref, stage_ref.at[slot % 2], slot, keep_ref, send_ref, out_sems.at[slot % 2], rows)
        return carry

    lax.fori_loop(0, 4, step, 0)
    for slot in range(2):
        wait_pieces(stage_ref.at[slot], keep_ref, out_sems.at[slot], rows)


def up_back_kernel(
    where_ref, grad_ref, slope_ref, norm_ref, hid_ref, gain_ref,
    own_d, near_d, far_d, far_other_d, cross_d, cross_other_d,
    own_u, near_u, far_u, far_other_u, cross_u, cross_other_u,
    gout_ref, mix_ref, gvec_ref, keep_ref, send_ref,
    down_ref, up_ref, branch_ref, total_ref, pre_ref, stage_ref, sems, out_sems,
):
    tokens, width = grad_ref.shape
    copies = fetch_full(
        where_ref, (own_d, near_d, far_d, far_other_d, cross_d, cross_other_d), down_ref, sems.at[0]
    )
    copies += fetch_full(
        where_ref, (own_u, near_u, far_u, far_other_u, cross_u, cross_other_u), up_ref, sems.at[1]
    )
    branch_ref[...] = grad_ref[...].astype(BF)
    total_ref[...] = jnp.zeros(total_ref.shape, F32)
    gvec_ref[...] = jnp.zeros(gvec_ref.shape, F32)
    for copy in copies:
        copy.wait()
    rows = width // PIECES

    def step(slot, carry):
        @pl.when(slot >= 2)
        def _():
            wait_pieces(stage_ref.at[slot % 2], keep_ref, out_sems.at[slot % 2], rows)

        grad_pre = (nt(branch_ref[...], down_ref[slot]) * slope_ref[slot].astype(F32)).astype(BF)
        pre_ref[...] = grad_pre
        gvec_ref[pl.ds(slot, 1), :] = column_sum(grad_pre.astype(F32))
        stage_ref[slot % 2] = tn(norm_ref[...], pre_ref[...]).astype(BF)
        send_pieces(where_ref, stage_ref.at[slot % 2], slot, keep_ref, send_ref, out_sems.at[slot % 2], rows)
        total_ref[...] += nt(pre_ref[...], up_ref[slot])
        return carry

    lax.fori_loop(0, 4, step, 0)

    def finish(at):
        xhat, rstd = norm_parts(hid_ref[at])
        grad = total_ref[at]
        value = grad_ref[at] + norm_back(grad, gain_ref[...], xhat, rstd)
        gout_ref[at] = value
        mix_ref[at] = value.astype(BF)
        gvec_ref[4:5, :] += column_sum(grad * xhat)
        gvec_ref[5:6, :] += column_sum(grad)

    over_rows(tokens, finish)
    for slot in range(2):
        wait_pieces(stage_ref.at[slot], keep_ref, out_sems.at[slot], rows)


def attend_back_kernel(
    where_ref, mix_ref, q_ref, k_ref, v_ref, prob_ref, att_ref, norm_ref, *rest, length, quarter, count, chained
):
    before_ref = rest[0] if chained else None
    rest = rest[1:] if chained else rest
    parts = rest[:count]
    (
        total_ref, gq_ref, keep_ref, send_ref,
        weight_ref, gatt_ref, dq_ref, dk_ref, dv_ref, stage_ref, sems, out_sems,
    ) = rest[count:]
    tokens = mix_ref.shape[0]
    for copy in fetch_half(where_ref, parts, weight_ref, sems):
        copy.wait()
    gatt_ref[...] = nt(mix_ref[...], weight_ref[3]).astype(BF)
    pairs = q_ref.shape[1] // 128
    lane = lax.broadcasted_iota(jnp.int32, (1, 128), 1)
    lefts = [(lane < HEAD_DIM).astype(BF), (lane >= HEAD_DIM).astype(BF)]
    block = length // 2
    unit = weight_ref.shape[1] // 2
    rows = unit // PIECES

    def publish(kind, left, right):
        stage_ref[kind] = tn(left, right).astype(BF)
        for slot, into in enumerate((keep_ref, send_ref)):
            for piece in range(PIECES):
                at = slot * unit + piece * rows
                pltpu.make_async_copy(
                    stage_ref.at[kind, at : at + rows],
                    into.at[piece ^ where_ref[2], kind * rows : (kind + 1) * rows],
                    out_sems.at[kind, slot * PIECES + piece],
                ).start()

    publish(2, att_ref[...], mix_ref[...])

    def step(index, carry):
        row = index // pairs
        pair = index % pairs
        lanes = pl.ds(pl.multiple_of(pair * 128, 128), 128)
        grads_k = [None, None]
        grads_v = [None, None]
        for part in range(2):
            keys = (part + 1) * block
            here = pl.ds(pl.multiple_of(row * length + part * block, block), block)
            upto = pl.ds(pl.multiple_of(row * length, length), keys)
            queries = q_ref[here, lanes]
            key_rows = k_ref[upto, lanes]
            values = v_ref[upto, lanes]
            grad_out = gatt_ref[here, lanes]
            result = None
            for head in range(2):
                probs = prob_ref[2 * index + head, part * block : (part + 1) * block, :keys]
                wide = probs.astype(F32)
                grad_mine = grad_out * lefts[head]
                grad_probs = nt(grad_mine, values)
                inner = jnp.sum(wide * grad_probs, -1, keepdims=True)
                grad_scores = (wide * (grad_probs - inner) * SCALE).astype(BF)
                term = nn(grad_scores, key_rows * lefts[head])
                result = term if result is None else result + term
                term_k = tn(grad_scores, queries * lefts[head])
                term_v = tn(probs, grad_mine)
                grads_k[part] = term_k if grads_k[part] is None else grads_k[part] + term_k
                grads_v[part] = term_v if grads_v[part] is None else grads_v[part] + term_v
            dq_ref[here, lanes] = result.astype(BF)
        low = pl.ds(pl.multiple_of(row * length, length), block)
        high = pl.ds(pl.multiple_of(row * length + block, block), block)
        dk_ref[low, lanes] = (grads_k[0] + grads_k[1][:block]).astype(BF)
        dk_ref[high, lanes] = grads_k[1][block:].astype(BF)
        dv_ref[low, lanes] = (grads_v[0] + grads_v[1][:block]).astype(BF)
        dv_ref[high, lanes] = grads_v[1][block:].astype(BF)
        return carry

    lax.fori_loop(0, tokens // length * pairs, step, 0)
    publish(0, dk_ref[...], norm_ref[...])
    publish(1, dv_ref[...], norm_ref[...])
    gq_ref[...] = tn(dq_ref[...], norm_ref[...]).astype(BF)
    total = nn(dq_ref[...], weight_ref[0]) + nn(dk_ref[...], weight_ref[1]) + nn(dv_ref[...], weight_ref[2])
    if chained:
        total = total + before_ref[...]
    total_ref[...] = total
    for kind in range(3):
        for piece in range(2 * PIECES):
            pltpu.make_async_copy(
                stage_ref.at[kind, :rows], keep_ref.at[0, :rows], out_sems.at[kind, piece]
            ).wait()


def embed_back_kernel(
    where_ref, seg_ref, label_ref, grad_ref, total_ref, hid_ref, gain_ref, patch_ref, direct_ref, win_ref,
    gwout_ref, gdown_ref, gup_ref, gq_near, gq_far,
    pgrad_ref, slot_ref, keep_ref, send_ref,
    value_ref, embed_ref, acc_ref, small_ref, sems,
    *, length, quarter,
):
    tokens, width = hid_ref.shape
    channels = patch_ref.shape[0]
    unit = width // 4
    rows = unit // PIECES
    sources = []
    for slot in range(4):
        source = (gq_near, gq_far)[slot // 2]
        into = (keep_ref, send_ref)[slot % 2]
        for piece in range(PIECES):
            at = (slot % 2) * unit + piece * rows
            sources.append((source.at[at : at + rows], into.at[slot // 2, piece ^ where_ref[2], :rows]))
    copies = start_copies(sources, sems.at[0])
    acc_ref[...] = jnp.zeros(acc_ref.shape, F32)

    def finish(at):
        xhat, rstd = norm_parts(hid_ref[at])
        grad = total_ref[at]
        acc_ref[1:2, :] += column_sum(grad * xhat)
        acc_ref[2:3, :] += column_sum(grad)
        value = grad_ref[at] + norm_back(grad, gain_ref[...], xhat, rstd)
        value_ref[at] = value
        embed = value.astype(BF)
        embed_ref[at] = embed
        acc_ref[0:1, :] += column_sum(embed.astype(F32))

    over_rows(tokens, finish)
    acc_ref[3:5, :] = gup_ref[4:6, :]
    acc_ref[5:7, :] = gdown_ref[0:2, :]
    for slot in range(4):
        acc_ref[pl.ds(7 + (slot ^ where_ref[3]), 1), :] = gup_ref[slot : slot + 1, :]
    small_ref[:channels] = nn(patch_ref[...].astype(BF), embed_ref[...]).astype(BF)
    small_ref[channels : 3 * channels] = gwout_ref[...].astype(BF)
    first = 3 * channels
    rows_here = tokens // length
    slots = length // quarter
    packed = [packed_flag(where_ref, seg_ref, row, length) for row in range(rows_here)]
    zero = jnp.zeros((quarter, width), F32)
    for slot in range(slots):
        value = zero
        for row in range(rows_here):
            at = row * length + slot * quarter
            here = value_ref[at : at + quarter]
            value = value + jnp.where(packed[row], 0.0, here)
            if slot == 0:
                every = here
                for later in range(1, slots):
                    every = every + value_ref[at + later * quarter : at + (later + 1) * quarter]
                value = value + jnp.where(packed[row], every, 0.0)
        small_ref[first + slot * quarter : first + (slot + 1) * quarter] = value.astype(BF)
    start = first + length
    small_ref[start : start + EXTRA] = acc_ref[...].astype(BF)
    start += EXTRA
    small_ref[start:] = jnp.zeros((small_ref.shape[0] - start, width), BF)
    moved = []
    for block in range(4):
        slot = block ^ where_ref[3]
        for piece in range(PIECES):
            at = (block * PIECES + piece) * GROUP
            moved.append((slot, piece ^ where_ref[2], small_ref.at[at : at + GROUP]))
    for index, (slot, piece, source) in enumerate(moved):

        @pl.when(slot % 2 == 0)
        def _():
            into = keep_ref.at[slot // 2, piece, rows:]
            pltpu.make_async_copy(source, into, sems.at[1, index]).start()

        @pl.when(slot % 2 == 1)
        def _():
            into = send_ref.at[slot // 2, piece, rows:]
            pltpu.make_async_copy(source, into, sems.at[1, index]).start()

    lane = lax.broadcasted_iota(jnp.int32, (1, slot_ref.shape[1] - width), 1)
    for row in range(rows_here):
        sums = []
        for slot in range(slots):
            at = row * length + slot * quarter
            sums.append(column_sum(value_ref[at : at + quarter]))
        every = sums[0]
        for slot in range(1, slots):
            every = every + sums[slot]
        for slot in range(slots):
            other = every if slot == 0 else jnp.zeros_like(every)
            index = row * slots + slot
            slot_ref[index : index + 1, :width] = jnp.where(packed[row], sums[slot], other)
            label = label_ref[row, slot]
            digits = jnp.where(lane == 0, label >> 5, jnp.where(lane == 1, label & 31, 0))
            slot_ref[index : index + 1, width:] = digits.astype(F32)
    pgrad_ref[...] = direct_ref[...] + nt(win_ref[...], embed_ref[...])
    for copy in copies:
        copy.wait()
    for index in range(4 * PIECES):
        pltpu.make_async_copy(
            small_ref.at[:GROUP], keep_ref.at[0, 0, rows:], sems.at[1, index]
        ).wait()


def piece_list(low, high):
    found = []
    for bit, ref in ((0, low), (1, high)):
        for i in range(ref.shape[0]):
            for j in range(ref.shape[1]):
                found.append((ref, i, j, i + (bit if low.shape[0] == 1 else 0), j + (bit if low.shape[1] == 1 else 0)))
    return [(ref, i, j, 2 * x + z) for ref, i, j, x, z in found]


def place_kernel(where_ref, low_ref, high_ref, out_ref):
    rows = low_ref.shape[2]
    for ref, i, j, piece in piece_list(low_ref, high_ref):
        at = pl.multiple_of((piece ^ where_ref[2]) * rows, rows)
        out_ref[pl.ds(at, rows)] = ref[i, j].astype(F32)


def place_last_kernel(
    where_ref, mix_low, mix_high, low_ref, high_ref, all_ref,
    gk_ref, gv_ref, go_ref, gq_ref, gin_ref, gout_ref, gpos_ref, *rest,
):
    *vectors, bup_ref, bout_ref, flat_ref = rest
    rows = gq_ref.shape[0] // PIECES
    for ref, i, j, piece in piece_list(mix_low, mix_high):
        at = pl.ds(pl.multiple_of((piece ^ where_ref[2]) * rows, rows), rows)
        gk_ref[at] = ref[i, j, :rows].astype(F32)
        gv_ref[at] = ref[i, j, rows : 2 * rows].astype(F32)
        go_ref[at] = ref[i, j, 2 * rows :].astype(F32)
    for ref, i, j, piece in piece_list(low_ref, high_ref):
        at = pl.ds(pl.multiple_of((piece ^ where_ref[2]) * rows, rows), rows)
        gq_ref[at] = ref[i, j, :rows].astype(F32)
    channels = gin_ref.shape[0]
    for slot in range(4):
        rel = (0, 2, 1, 3)[slot]
        for piece in range(PIECES):
            group = (rel ^ where_ref[3]) * PIECES + (piece ^ where_ref[2])
            flat_ref[pl.ds(pl.multiple_of(group * GROUP, GROUP), GROUP)] = all_ref[slot, piece].astype(F32)
    start = 3 * channels
    gin_ref[...] = flat_ref[:channels]
    gout_ref[...] = flat_ref[channels:start]
    length = gpos_ref.shape[0]
    gpos_ref[...] = flat_ref[start : start + length]
    start += length
    for index, ref in enumerate(vectors):
        ref[...] = flat_ref[start + index : start + index + 1]
    bout_ref[...] = flat_ref[start + 6 : start + 7, : bout_ref.shape[1]]
    bup_ref[...] = flat_ref[pl.ds(start + 7 + where_ref[3], 1)]


def make_program(rows_size, heads_size):
    levels = rows_size.bit_length() - 1

    def swap_heads(array, bit):
        return lax.ppermute(array, "heads", [(i, i ^ bit) for i in range(heads_size)])

    def swap_rows(array, bit):
        return lax.ppermute(array, "rows", [(i, i ^ bit) for i in range(rows_size)])

    def add_low(arrays):
        total = arrays[0].astype(F32)
        for other in arrays[1:]:
            total = total + other.astype(F32)
        return total.astype(BF)

    def ordered(value, token):
        value, token = lax.optimization_barrier((value, token))
        return value

    class Chain:
        axes = {"x": (1, 1), "z": (2, 2)}

        def __init__(self, order):
            self.order = order
            self.near, self.far, self.both = [], [], []
            self.left = list(order) + ["w"] + [a for a in reversed(order) if a != "y"]

        def add(self, group, *arrays):
            for array in arrays:
                group.append(array.reshape((-1, 2, 2) + array.shape[-2:]))

        def core(self, group, send, token):
            send = ordered(send, token)
            self.add(group, swap_heads(send, 1))
            return send

        def side(self, arrays, axis, index):
            return [lax.slice_in_dim(t, index, index + 1, axis=axis) for t in arrays]

        def step(self, token):
            kind = self.left.pop(0)
            reducing = "w" in self.left
            if kind == "y":
                send = ordered(add_low(self.side(self.both, 0, 1) + self.far), token)
                self.both = self.side(self.both, 0, 0) + self.near + [swap_heads(send, 2)]
            elif kind == "w":
                total = add_low(self.both)
                for level in range(2, levels):
                    send = ordered(total, token)
                    total = add_low([send, swap_rows(send, 1 << level)])
                self.total = total
            elif reducing:
                axis, bit = self.axes[kind]
                send = ordered(add_low(self.side(self.both, axis, 1)), token)
                self.both = self.side(self.both, axis, 0) + [swap_rows(send, bit)]
            else:
                axis, bit = self.axes[kind]
                send = ordered(self.total, token)
                got = swap_rows(send, bit)
                if self.left:
                    self.total = jnp.concatenate([send, got], axis)
                else:
                    self.low, self.high = send[0], got[0]
            return send

    def program(
        patches, segments, labels, w_in, b_in, pos_table, cls_table, ln1_gain, ln1_bias,
        w_query, w_key, w_value, w_attn_out, ln2_gain, ln2_bias, w_up, b_up, w_down, b_down,
        w_out, b_out, latent_grad, logdet_grad,
    ):
        tokens, channels = patches.shape
        length, width = pos_table.shape
        slot_count = labels.shape[1]
        quarter = length // slot_count
        classes = cls_table.shape[0]
        part = w_query.shape[2]
        row_count = tokens // length
        head_index = lax.axis_index("heads")
        row_index = lax.axis_index("rows")
        row_bit = row_index & 1
        mask = ((row_index & 1) << 1) | ((row_index >> 1) & 1)
        where = jnp.stack([head_index * tokens, row_bit, mask, head_index]).astype(jnp.int32)
        rows = width // PIECES
        unit = part // PIECES
        heads = width // HEAD_DIM
        square = 2 * tokens * width * width

        def shape(*dims, dtype=F32):
            return jax.ShapeDtypeStruct(dims, dtype)

        def call(kernel, operands, specs, outs, out_specs, scratch=(), work=1.0, **options):
            return pl.pallas_call(
                functools.partial(kernel, **options) if options else kernel,
                in_specs=specs,
                out_specs=out_specs,
                out_shape=outs,
                scratch_shapes=list(scratch),
                compiler_params=pltpu.CompilerParams(vmem_limit_bytes=60 << 20),
                cost_estimate=pl.CostEstimate(
                    flops=int(work * square), transcendentals=0, bytes_accessed=8 << 20
                ),
            )(*operands)

        dma = pltpu.SemaphoreType.DMA
        low = shape(tokens, width, dtype=BF)
        full = shape(tokens, width)
        half_low = shape(tokens, width // 2, dtype=BF)

        bias_rows = jnp.pad(b_up, ((0, EXTRA - 1), (0, 0)))
        pack_t = jnp.stack(
            [
                jnp.concatenate([w_query[0].T, w_key[0].T, bias_rows], 0),
                jnp.concatenate([w_value[0].T, w_attn_out[0], bias_rows], 0),
            ]
        )
        own_u, own_d = w_up[0], w_down[0]
        half_rows = width // 2
        half_t = lax.dynamic_index_in_dim(pack_t, row_bit, 0, keepdims=False)
        far_t = swap_heads(half_t, 2)
        near_t = swap_heads(ordered(pack_t, half_t), 1)
        half_u = lax.dynamic_slice_in_dim(own_u, row_bit * half_rows, half_rows, 0)
        half_d = lax.dynamic_slice_in_dim(own_d, row_bit * half_rows, half_rows, 0)
        near_u = swap_heads(ordered(own_u, half_t), 1)
        near_d = swap_heads(ordered(own_d, half_t), 1)
        cls_rows = cls_table[labels.reshape(-1)].astype(F32)
        patches_t = patches.T
        hidden0, normed1 = call(
            embed_kernel,
            (
                where, segments, ordered(patches_t, half_t), w_in, b_in[None], pos_table, cls_rows,
                ln1_gain, ln1_bias,
            ),
            [SMEM, SMEM] + [VMEM] * 7,
            (full, low),
            (VMEM, VMEM),
            work=0.3,
        )
        far_t = ordered(far_t, normed1)
        far_other_t = swap_rows(far_t, 1)
        half_u = ordered(half_u, far_t)
        far_u = swap_heads(half_u, 2)
        cross_t = swap_heads(far_t, 1)

        def attend(hidden, normed, parts):
            return call(
                attend_kernel,
                (where, segments, hidden, normed) + parts,
                [SMEM, SMEM, VMEM, VMEM] + [HBM] * len(parts),
                (
                    half_low, half_low, half_low,
                    shape(row_count * heads // 2, length, length, dtype=BF), half_low, full,
                ),
                (VMEM,) * 6,
                [pltpu.VMEM((4, width // 2, width), BF), dma((8,))],
                work=5.0,
                length=length,
                quarter=quarter,
                count=len(parts),
            )

        parts_near = (pack_t, near_t)
        *saved_near, mixed = attend(hidden0, ordered(normed1, half_u), parts_near)
        far_other_t = ordered(far_other_t, mixed)
        cross_other_t = swap_heads(far_other_t, 1)
        far_u = ordered(far_u, far_other_t)
        far_other_u = swap_rows(far_u, 1)
        half_d = ordered(half_d, far_u)
        far_d = swap_heads(half_d, 2)
        cross_u = swap_heads(far_u, 1)
        parts_far = (far_t, far_other_t, cross_t, cross_other_t)
        *saved_far, hidden1 = attend(mixed, ordered(normed1, half_d), parts_far)
        far_other_u = ordered(far_other_u, hidden1)
        cross_other_u = swap_heads(far_other_u, 1)
        far_d = ordered(far_d, hidden1)
        far_other_d = swap_rows(far_d, 1)
        cross_d = swap_heads(far_d, 1)
        parts_u = (own_u, near_u, far_u, far_other_u, cross_u, cross_other_u)
        four = shape(heads_size, tokens, width, dtype=BF)
        normed2, activated, slope = call(
            up_kernel,
            (where, ordered(hidden1, far_d), ln2_gain, ln2_bias)
            + parts_u
            + (pack_t, near_t, far_t, cross_t),
            [SMEM] + [VMEM] * 3 + [HBM] * 10,
            (low, four, four),
            (VMEM,) * 3,
            [
                pltpu.VMEM((heads_size, width, width), BF),
                pltpu.VMEM((heads_size, EXTRA, width), BF),
                dma((6,)),
                dma((4,)),
            ],
            work=6.0,
        )
        far_other_d = ordered(far_other_d, normed2)
        cross_other_d = swap_heads(far_other_d, 1)
        parts_d = (own_d, near_d, far_d, far_other_d, cross_d, cross_other_d)
        pieces = shape(2, PIECES, rows, width, dtype=BF)
        stage = pltpu.VMEM((2, width, width), BF)
        out_sems = dma((2, PIECES))
        latents, logdet, stats, direct, grad_hidden2, grad_w_out, gdown, keep_d, send_d = call(
            down_kernel,
            (
                where, segments, hidden1, activated, b_down, w_out.T, b_out[:, None], patches_t, latent_grad.T,
                logdet_grad[None],
            )
            + parts_d,
            [SMEM, SMEM] + [VMEM] * 8 + [HBM] * 6,
            (
                shape(channels, tokens), shape(1, tokens), shape(8, 128), shape(channels, tokens),
                full, shape(2 * channels, width), shape(8, width), pieces, pieces,
            ),
            (VMEM,) * 7 + (HBM, HBM),
            [pltpu.VMEM((heads_size, width, width), BF), pltpu.VMEM((tokens, width), BF), stage, dma((6,)), out_sems],
            work=8.0,
            length=length,
            quarter=quarter,
        )
        chains = [Chain(order) for order in CHAIN_ORDERS]
        down, up, mix, last = chains
        down.add(down.both, keep_d)
        token = down.core(down.both, send_d, grad_hidden2)
        grad_hidden1, grad_mix, gup, keep_u, send_u = call(
            up_back_kernel,
            (where, ordered(grad_hidden2, token), slope, normed2, hidden1, ln2_gain) + parts_d + parts_u,
            [SMEM] + [VMEM] * 5 + [HBM] * 12,
            (full, low, shape(8, width), pieces, pieces),
            (VMEM, VMEM, VMEM, HBM, HBM),
            [
                pltpu.VMEM((heads_size, width, width), BF),
                pltpu.VMEM((heads_size, width, width), BF),
                pltpu.VMEM((tokens, width), BF),
                pltpu.VMEM((tokens, width), F32),
                pltpu.VMEM((tokens, width), BF),
                stage,
                dma((2, 6)),
                out_sems,
            ],
            work=12.0,
        )
        up.add(up.both, keep_u)
        token = up.core(up.both, send_u, grad_mix)

        def advance(order, token):
            for index in order:
                token = chains[index].step(token)
            return token

        def attend_back(saved, parts, before, token):
            chained = () if before is None else (before,)
            mixed_pieces = shape(PIECES, 3 * unit, width, dtype=BF)
            return call(
                attend_back_kernel,
                (where, ordered(grad_mix, token)) + tuple(saved) + (normed1,) + chained + parts,
                [SMEM] + [VMEM] * (7 + len(chained)) + [HBM] * len(parts),
                (full, shape(width // 2, width, dtype=BF), mixed_pieces, mixed_pieces),
                (VMEM, VMEM, HBM, HBM),
                [pltpu.VMEM((4, width // 2, width), BF)]
                + [pltpu.VMEM((tokens, width // 2), BF)] * 4
                + [pltpu.VMEM((3, width // 2, width), BF), dma((8,)), dma((3, 2 * PIECES))],
                work=8.0,
                length=length,
                quarter=quarter,
                count=len(parts),
                chained=before is not None,
            )

        token = advance(BEFORE_FAR, token)
        total_far, gq_far, keep_far, send_far = attend_back(saved_far, parts_far, None, token)
        mix.add(mix.far, keep_far)
        token = mix.core(mix.far, send_far, total_far)
        token = advance(BEFORE_NEAR, token)
        total_near, gq_near, keep_near, send_near = attend_back(saved_near, parts_near, total_far, token)
        mix.add(mix.near, keep_near)
        token = mix.core(mix.near, send_near, total_near)
        token = advance(BEFORE_EMBED, token)
        groups = 4 * PIECES
        last_pieces = shape(2, PIECES, unit + GROUP, width, dtype=BF)
        patches_grad, slot_rows, keep_q, send_q = call(
            embed_back_kernel,
            (
                where, segments, labels, ordered(grad_hidden1, token), total_near, hidden0, ln1_gain, patches_t,
                direct, w_in, grad_w_out, gdown, gup, gq_near, gq_far,
            ),
            [SMEM, SMEM, SMEM] + [VMEM] * 12,
            (shape(channels, tokens), shape(row_count * slot_count, width + 128), last_pieces, last_pieces),
            (VMEM, VMEM, HBM, HBM),
            [
                pltpu.VMEM((tokens, width), F32),
                pltpu.VMEM((tokens, width), BF),
                pltpu.VMEM((EXTRA, width), F32),
                pltpu.VMEM((groups * GROUP, width), BF),
                dma((2, groups)),
            ],
            work=3.0,
            length=length,
            quarter=quarter,
        )
        last.add(last.both, keep_q)
        token = last.core(last.both, send_q, patches_grad)
        gathered = slot_rows.astype(BF)
        steps = list(TAIL)
        gathers = [("r", 1 << level) for level in reversed(range(levels))] + [("h", 2), ("h", 1)]
        while steps or gathers:
            if steps:
                token = advance(steps[:1], token)
                steps = steps[1:]
            if gathers:
                kind, bit = gathers.pop(0)
                gathered = ordered(gathered, token)
                token = gathered
                swap = swap_rows if kind == "r" else swap_heads
                gathered = jnp.concatenate([gathered, swap(gathered, bit)], 0)
        digits = gathered[:, width : width + 2].astype(jnp.int32)
        slot_label = digits[:, 0] * 32 + digits[:, 1]
        label_onehot = (
            lax.broadcasted_iota(jnp.int32, (classes, 1), 0) == slot_label[None, :]
        ).astype(BF)
        sum_cls = nn(label_onehot, gathered[:, :width])

        def place(chain):
            return call(
                place_kernel, (where, chain.low, chain.high), [SMEM, VMEM, VMEM], shape(width, width), VMEM
            )

        sum_down, sum_up = place(down), place(up)
        axis = Chain.axes[[a for a in last.order if a != "y"][0]][0] - 1
        small = jnp.concatenate([last.low[:, :, unit:], last.high[:, :, unit:]], axis)
        small = small.reshape(1, PIECES, GROUP, width)
        small = jnp.concatenate([small, swap_heads(small, 2)], 0)
        small = jnp.concatenate([small, swap_heads(small, 1)], 0)
        units = shape(part, width)
        line = shape(1, width)
        sum_k, sum_v, sum_o, sum_q, sum_w_in, sum_w_out, sum_pos, *lines = call(
            place_last_kernel,
            (where, mix.low, mix.high, last.low, last.high, small),
            [SMEM] + [VMEM] * 5,
            (units,) * 4
            + (shape(channels, width), shape(2 * channels, width), shape(length, width))
            + (line,) * 7
            + (shape(1, 2 * channels),),
            (VMEM,) * 15,
            [pltpu.VMEM((groups * GROUP, width), F32)],
        )
        sum_b_in, sum_gain1, sum_bias1, sum_gain2, sum_bias2, sum_b_down, sum_b_up, sum_b_out = lines
        return (
            latents.T,
            logdet.reshape(tokens),
            patches_grad.T,
            stats[0, :row_count],
            stats[1, :row_count],
            sum_w_in,
            sum_b_in.reshape(width),
            sum_pos,
            sum_cls,
            sum_gain1,
            sum_bias1,
            sum_q.T[None],
            sum_k.T[None],
            sum_v.T[None],
            sum_o[None],
            sum_gain2,
            sum_bias2,
            sum_up[None],
            sum_b_up,
            sum_down[None],
            sum_b_down,
            sum_w_out.T,
            sum_b_out.reshape(2 * channels),
        )

    return program


def solution(mesh):
    tokens = P(("rows", "heads"))
    tokens2 = P(("rows", "heads"), None)
    last = P(None, None, "heads")
    middle = P(None, "heads", None)
    in_specs = (
        (tokens2, P("rows"), tokens2)
        + (P(),) * 6
        + (last, last, last, middle)
        + (P(), P(), last, P(None, "heads"), middle, P(), P(), P())
        + (tokens2, tokens)
    )
    out_specs = (
        (tokens2, tokens, tokens2, tokens, tokens)
        + (P(),) * 6
        + (last, last, last, middle)
        + (P(), P(), last, P(None, "heads"), middle, P(), P(), P())
    )
    program = make_program(mesh.shape["rows"], mesh.shape["heads"])
    return jax.shard_map(
        program, mesh=mesh, in_specs=in_specs, out_specs=out_specs, check_vma=False
    )
```

time: 490 us -> 298 us (0.61); the launches traced: 483 us -> 297 us
  matrix products: 140 us -> 2.22 us
  Pallas kernels: 0 us -> 121 us
  waiting for transfers between devices: 169 us -> 93.2 us
  local copies, waits for them, and re-layouts: 71.8 us -> 9.06 us
  other arithmetic: 43.2 us -> 24.6 us
  starting transfers between devices: 56.7 us -> 45.4 us
    dot_general x63 -> x1, matrix products: 140 us -> 2.22 us  [nn(): lax.dot_general(matrix, other, (((1,), (0,)), ((), ())), preferred_elemen...]
    pallas_call x0 -> x12, Pallas kernels: none -> 121 us  [call(): pl.pallas_call(functools.partial(kernel, **options) if options else kerne...]
    ppermute x54 -> x51, waiting for transfers between devices: 169 us -> 93.2 us  [the longest x26 74 us: swap_rows(): return lax.ppermute(array, 'rows', [(i, i ^ bit) for i in range(rows_size)])]
    convert_element_type x14 -> x0, local copies, waits for them, and re-layouts: 15.7 us -> none  [the longest x3 2.44 us: program(): g.astype(BF).reshape(tokens, width)]
    unnamed x179 -> x57, local copies, waits for them, and re-layouts: 18.1 us -> 2.86 us
    reshape x5 -> x1, local copies, waits for them, and re-layouts: 12.1 us -> 0.08 us  [program(): cls_rows = cls_table[labels.reshape(-1)].astype(F32)]
    ppermute x54 -> x51, starting transfers between devices: 56.7 us -> 45.4 us  [the longest x26 30.6 us: swap_rows(): return lax.ppermute(array, 'rows', [(i, i ^ bit) for i in range(rows_size)])]
    dynamic_slice x12 -> x1, local copies, waits for them, and re-layouts: 10.4 us -> 1.32 us  [program(): half_d = lax.dynamic_slice_in_dim(own_d, row_bit * half_rows, half_rows, 0)]
  transfers between devices with their start and end apart: 54 -> 51, of which waited for: 27 -> 23; matrix products, arithmetic and copies ran while one was open for 29% -> 9% of each run, Pallas kernels for 0% -> 32%
where the time goes in v2:
time: 298 us; the launch traced here: 297 us
  Pallas kernels  121 us (41%)
  waiting for transfers between devices  93.2 us (31%)
  starting transfers between devices  45.4 us (15%)
  other arithmetic  24.6 us (8%)
  local copies, waits for them, and re-layouts  9.06 us (3%)
    pallas_call x12, Pallas kernels, call(): pl.pallas_call(functools.partial(kernel, **options) if options else kerne...  121 us
    ppermute x26, waiting for transfers between devices, swap_rows(): return lax.ppermute(array, 'rows', [(i, i ^ bit) for i in range(rows_size)])  74 us
    ppermute x26, starting transfers between devices, swap_rows(): return lax.ppermute(array, 'rows', [(i, i ^ bit) for i in range(rows_size)])  30.6 us
    ppermute x25, waiting for transfers between devices, swap_heads(): lax.ppermute(array, 'heads', [(i, i ^ bit) for i in range(heads_size)])  19.3 us
    convert_element_type x20, other arithmetic, add_low(): return total.astype(BF)  16.9 us
    ppermute x25, starting transfers between devices, swap_heads(): lax.ppermute(array, 'heads', [(i, i ^ bit) for i in range(heads_size)])  14.8 us
  transfers between devices with their start and end apart: 51, of which 23 were waited for; matrix products, arithmetic and copies ran while one was open for 9% of the time, Pallas kernels for 32%

profile of v2, /device:TPU:0, one launch (start us, length us, event | category | flops | bytes accessed | tf_op | source)
XLA Modules:
  0.0 297.1 jit_solution(10605456012074861950)
XLA Ops:
  0.7 1.4 fusion.6
  3.0 2.6 collective-permute-start
  8.2 3.0 %shard_map.398 = (f32[512,768]{1,0:T(8,128)}, bf16[512,768]{1,0:T(8,128)(2,1)}) custom-call(s32[4]{0:T(128)} %pad_add_fusion.where_ref, s32[2048]{0:T(1024)} %seg_ref.9, f32[48,512]{1,0:T(8,128)} %bitcast.189, bf16[48,768]{1,0:T(8,128)(2,1)} %win_ref.1, f32[1,768]{1,0:T(1,128)} %broadcast_in_dim.29.b_ref, bf16[256,768]{1,0:T(8,128)(2,1)} %pos_ref.1, ...), custom_call_target="tpu_custom_call" | custom-call | flops 181193936 | bytes 8388608 | tf_op jit(solution)/shard_map/pallas_call | solution.py:717
  11.2 9.0 %collective-permute-done.rest_0_.far_t = bf16[400,768]{1,0:T(8,128)(2,1)} collective-permute-done((bf16[400,768]{1,0:T(8,128)(2,1)S(1)}, bf16[400,768]{1,0:T(8,128)(2,1)}, u32[]{:S(2)}, u32[]{:S(2)}) %collective-permute-start) | collective-permute-done | bytes 614432 | tf_op jit(solution)/shard_map/ppermute | solution.py:630
  20.2 1.7 collective-permute-start.3
  21.9 1.3 dynamic-slice_bitcast_fusion
  23.2 1.6 collective-permute-start.2
  24.8 11.6 %shard_map.399 = (bf16[512,384]{1,0:T(8,128)(2,1)}, bf16[512,384]{1,0:T(8,128)(2,1)}, bf16[512,384]{1,0:T(8,128)(2,1)}, bf16[12,256,256]{2,1,0:T(8,128)(2,1)}, b...) custom-call(s32[4]{0:T(128)} %pad_add_fusion.where_ref, s32[2048]{0:T(1024)} %seg_ref.9, ...), custom_call_target="tpu_custom_call" | custom-call | flops 3019898880 | bytes 8388608 | tf_op jit(solution)/shard_map/pallas_call | solution.py:717
  38.5 1.6 collective-permute-start.6
  40.3 11.4 %shard_map.400 = (bf16[512,384]{1,0:T(8,128)(2,1)}, bf16[512,384]{1,0:T(8,128)(2,1)}, bf16[512,384]{1,0:T(8,128)(2,1)}, bf16[12,256,256]{2,1,0:T(8,128)(2,1)}, b...) custom-call(s32[4]{0:T(128)} %pad_add_fusion.where_ref, s32[2048]{0:T(1024)} %seg_ref.9, ...), custom_call_target="tpu_custom_call" | custom-call | flops 3019898880 | bytes 8388608 | tf_op jit(solution)/shard_map/pallas_call | solution.py:717
  52.6 1.8 collective-permute-done.6.far.far_d
  54.4 1.5 collective-permute-start.12
  56.4 13.9 %shard_map.401 = (bf16[512,768]{1,0:T(8,128)(2,1)}, bf16[4,512,768]{2,1,0:T(8,128)(2,1)}, bf16[4,512,768]{2,1,0:T(8,128)(2,1)}) custom-call(s32[4]{0:T(128)} %pad_add_fusion.where_ref, f32[512,768]{1,0:T(8,128)} %get-tuple-element.148.hid_ref, f32[1,768]{1,0:T(1,128)} %gain_ref.6, f32[1,768]{1,0:T(1,128)} %bias_ref.3, bf16[768,768]{1,0:T(8,128)(2,1)} %bitcast.178, ...), custom_call_target="tpu_custom_call" | custom-call | flops 3623878656 | bytes 8388608 | tf_op jit(solution)/shard_map/pallas_call | solution.py:717
  71.2 1.2 collective-permute-done.14.cross_other.cross_other_d
  73.2 15.0 %shard_map.402 = (f32[48,512]{1,0:T(8,128)}, f32[1,512]{1,0:T(1,128)}, f32[8,128]{1,0:T(8,128)}, f32[48,512]{1,0:T(8,128)}, f32[512,768]{1,0:T(8,128)}, /*index=...) custom-call(s32[4]{0:T(128)} %pad_add_fusion.where_ref, ...), custom_call_target="tpu_custom_call" | custom-call | flops 4831838208 | bytes 8388608 | tf_op jit(solution)/shard_map/pallas_call | solution.py:717
  88.5 19.5 %shard_map.403 = (f32[512,768]{1,0:T(8,128)}, bf16[512,768]{1,0:T(8,128)(2,1)}, f32[8,768]{1,0:T(8,128)}, bf16[2,4,192,768]{3,2,1,0:T(8,128)(2,1)}, bf16[2,4,192,768]{3,2,1,0:T(8,128)(2,1)}) custom-call(s32[4]{0:T(128)} %pad_add_fusion.where_ref, f32[512,768]{1,0:T(8,128)} %get-tuple-element.160.grad_ref, bf16[4,512,768]{2,1,0:T(8,128)(2,1)} %get-tuple-element.161.slope_ref, ...), custom_call_target="tpu_custom_call" | custom-call | flops 7247757312 | bytes 8388608 | tf_op jit(solution)/shard_map/pallas_call | solution.py:717
  108.4 3.5 %add_convert_fusion = bf16[1,4,192,768]{3,2,1,0:T(8,128)(2,1)} fusion(bf16[2,4,192,768]{3,2,1,0:T(8,128)(2,1)S(1)} %collective-permute-done.16, bf16[2,4,192,768]{3,2,1,0:T(8,128)(2,1)} %get-tuple-element.167), kind=kLoop, calls=%fused_computation.1 | loop fusion | flops 2359296 | bytes 3538944 | tf_op jit(solution)/shard_map/convert_element_type | solution.py:639
  111.9 1.5 collective-permute-start.19
  113.5 1.6 add_convert_fusion.1
  115.2 14.6 %shard_map.404 = (f32[512,768]{1,0:T(8,128)}, bf16[384,768]{1,0:T(8,128)(2,1)}, bf16[4,144,768]{2,1,0:T(8,128)(2,1)}, bf16[4,144,768]{2,1,0:T(8,128)(2,1)}) custom-call(s32[4]{0:T(128)} %pad_add_fusion.where_ref, bf16[512,768]{1,0:T(8,128)(2,1)} %get-tuple-element.180.mix_ref, bf16[512,384]{1,0:T(8,128)(2,1)} %get-tuple-element.171.q_ref, ...), custom_call_target="tpu_custom_call" | custom-call | flops 4831838208 | bytes 8388608 | tf_op jit(solution)/shard_map/pallas_call | solution.py:717
  129.9 1.6 collective-permute-start.18
  131.7 15.0 %shard_map.405 = (f32[512,768]{1,0:T(8,128)}, bf16[384,768]{1,0:T(8,128)(2,1)}, bf16[4,144,768]{2,1,0:T(8,128)(2,1)}, bf16[4,144,768]{2,1,0:T(8,128)(2,1)}) custom-call(s32[4]{0:T(128)} %pad_add_fusion.where_ref, bf16[512,768]{1,0:T(8,128)(2,1)} %get-tuple-element.180.mix_ref, bf16[512,384]{1,0:T(8,128)(2,1)} %get-tuple-element.181.q_ref, ...), custom_call_target="tpu_custom_call" | custom-call | flops 4831838208 | bytes 8388608 | tf_op jit(solution)/shard_map/pallas_call | solution.py:717
  146.7 1.4 slice.307
  148.2 1.4 add_convert_fusion.2
  149.6 2.1 add_convert_fusion.3
  151.7 7.0 %collective-permute-done.18 = bf16[2,2,1,192,768]{4,3,1,2,0:T(8,128)(2,1)} collective-permute-done((bf16[2,2,1,192,768]{4,3,1,2,0:T(8,128)(2,1)}, bf16[2,2,1,192,768]{4,3,1,2,0:T(8,128)(2,1)}, u32[]{:S(2)}, u32[]{:S(2)}) %collective-permute-start.18) | collective-permute-done | bytes 1179680 | tf_op jit(solution)/shard_map/ppermute | solution.py:633
  158.6 2.4 add_convert_fusion.4
  161.1 8.3 %shard_map.406 = (f32[48,512]{1,0:T(8,128)}, f32[8,896]{1,0:T(8,128)}, bf16[2,4,80,768]{3,2,1,0:T(8,128)(2,1)}, bf16[2,4,80,768]{3,2,1,0:T(8,128)(2,1)}) custom-call(s32[4]{0:T(128)} %pad_add_fusion.where_ref, s32[2048]{0:T(1024)} %seg_ref.9, s32[2,4]{1,0:T(2,128)} %label_ref.1, f32[512,768]{1,0:T(8,128)} %get-tuple-element.192.grad_ref, ...), custom_call_target="tpu_custom_call" | custom-call | flops 1811939328 | bytes 8388608 | tf_op jit(solution)/shard_map/pallas_call | solution.py:717
  171.3 14.1 %collective-permute-done.22 = bf16[1,1,2,192,768]{4,3,2,1,0:T(8,128)(2,1)S(1)} collective-permute-done((bf16[1,1,2,192,768]{4,3,2,1,0:T(8,128)(2,1)}, bf16[1,1,2,192,768]{4,3,2,1,0:T(8,128)(2,1)S(1)}, u32[]{:S(2)}, u32[]{:S(2)}) %collective-permute-start.22) | collective-permute-done | bytes 589856 | tf_op jit(solution)/shard_map/ppermute | solution.py:633
  186.5 2.7 collective-permute-start.23
  189.8 1.4 collective-permute-done.23
  191.2 1.6 collective-permute-start.26
  193.4 5.5 %collective-permute-done.26 = bf16[1,1,1,192,768]{4,3,2,1,0:T(8,128)(2,1)S(1)} collective-permute-done((bf16[1,1,1,192,768]{4,3,2,1,0:T(8,128)(2,1)S(1)}, bf16[1,1,1,192,768]{4,3,2,1,0:T(8,128)(2,1)S(1)}, u32[]{:S(2)}, u32[]{:S(2)}) %collective-permute-start.26) | collective-permute-done | bytes 294944 | tf_op jit(solution)/shard_map/ppermute | solution.py:633
  198.9 1.2 add_convert_fusion.11
  201.0 2.6 collective-permute-start.28
  203.6 1.4 collective-permute-done.30
  206.0 1.3 add_convert_fusion.9
  207.9 1.6 collective-permute-start.27
  209.5 1.2 collective-permute-start.31
  210.7 3.6 %collective-permute-done.28 = bf16[1,1,1,192,768]{4,3,2,1,0:T(8,128)(2,1)S(1)} collective-permute-done((bf16[1,1,1,192,768]{4,3,2,1,0:T(8,128)(2,1)S(1)}, bf16[1,1,1,192,768]{4,3,2,1,0:T(8,128)(2,1)S(1)}, u32[]{:S(2)}, u32[]{:S(2)}) %collective-permute-start.28) | collective-permute-done | bytes 294944 | tf_op jit(solution)/shard_map/ppermute | solution.py:633
  214.4 1.9 collective-permute-done.31
  216.2 1.3 add_convert_fusion.8
  217.6 4.7 %collective-permute-done.27 = bf16[1,2,1,144,768]{4,3,1,2,0:T(8,128)(2,1)S(1)} collective-permute-done((bf16[1,2,1,144,768]{4,3,1,2,0:T(8,128)(2,1)S(1)}, bf16[1,2,1,144,768]{4,3,1,2,0:T(8,128)(2,1)S(1)}, u32[]{:S(2)}, u32[]{:S(2)}) %collective-permute-start.27) | collective-permute-done | bytes 442400 | tf_op jit(solution)/shard_map/ppermute | solution.py:633
  222.5 1.5 collective-permute-start.34
  224.0 1.2 collective-permute-start.35
  225.2 3.2 %collective-permute-start.37 = (bf16[1,1,1,192,768]{4,3,1,2,0:T(8,128)(2,1)S(1)}, bf16[1,1,1,192,768]{4,3,1,2,0:T(8,128)(2,1)S(1)}, u32[]{:S(2)}, u32[]{:S(2)}) collective-permute-start(bf16[1,1,1,192,768]{4,3,1,2,0:T(8,128)(2,1)S(1)} %add_convert_fusion.8), channel_id=1, source_target_pairs={{0,16},{4,20},{8,24},{12,28},{16,0},{20,4},{24,8},{28,12},{1,17},{... | collective-permute-start | bytes 884744 | tf_op jit(solution)/shard_map/ppermute | solution.py:633
  228.7 1.5 collective-permute-done.35
  230.3 3.2 %collective-permute-start.36 = (bf16[1,1,1,144,768]{4,3,1,2,0:T(8,128)(2,1)S(1)}, bf16[1,1,1,144,768]{4,3,1,2,0:T(8,128)(2,1)S(1)}, u32[]{:S(2)}, u32[]{:S(2)}) collective-permute-start(bf16[1,1,1,144,768]{4,3,1,2,0:T(8,128)(2,1)S(1)} %add_convert_fusion.15), channel_id=1, source_target_pairs={{0,16},{4,20},{8,24},{12,28},{16,0},{20,4},{24,8},{28,12},{1,17},{... | collective-permute-start | bytes 663560 | tf_op jit(solution)/shard_map/ppermute | solution.py:633
  233.5 14.8 %collective-permute-done.37 = bf16[1,1,1,192,768]{4,3,1,2,0:T(8,128)(2,1)S(1)} collective-permute-done((bf16[1,1,1,192,768]{4,3,1,2,0:T(8,128)(2,1)S(1)}, bf16[1,1,1,192,768]{4,3,1,2,0:T(8,128)(2,1)S(1)}, u32[]{:S(2)}, u32[]{:S(2)}) %collective-permute-start.37) | collective-permute-done | bytes 294944 | tf_op jit(solution)/shard_map/ppermute | solution.py:633
  249.3 2.5 collective-permute-done.36
  251.9 4.1 %collective-permute-done.42 = bf16[1,1,1,80,768]{4,3,2,1,0:T(8,128)(2,1)S(1)} collective-permute-done((bf16[1,1,1,80,768]{4,3,2,1,0:T(8,128)(2,1)S(1)}, bf16[1,1,1,80,768]{4,3,2,1,0:T(8,128)(2,1)S(1)}, u32[]{:S(2)}, u32[]{:S(2)}) %collective-permute-start.42) | collective-permute-done | bytes 122912 | tf_op jit(solution)/shard_map/ppermute | solution.py:633
  257.7 4.2 %collective-permute-done.44 = bf16[1,1,1,80,768]{4,3,2,1,0:T(8,128)(2,1)S(1)} collective-permute-done((bf16[1,1,1,80,768]{4,3,2,1,0:T(8,128)(2,1)S(1)}, bf16[1,1,1,80,768]{4,3,2,1,0:T(8,128)(2,1)S(1)}, u32[]{:S(2)}, u32[]{:S(2)}) %collective-permute-start.44) | collective-permute-done | bytes 122912 | tf_op jit(solution)/shard_map/ppermute | solution.py:633
  262.0 3.2 %collective-permute-done.41 = bf16[1,1,1,144,768]{4,3,1,2,0:T(8,128)(2,1)S(1)} collective-permute-done((bf16[1,1,1,144,768]{4,3,1,2,0:T(8,128)(2,1)S(1)}, bf16[1,1,1,144,768]{4,3,1,2,0:T(8,128)(2,1)S(1)}, u32[]{:S(2)}, u32[]{:S(2)}) %collective-permute-start.41) | collective-permute-done | bytes 221216 | tf_op jit(solution)/shard_map/ppermute | solution.py:633
  265.3 1.3 slice_bitcast_fusion.14
  266.6 2.1 collective-permute-start.50
  268.7 5.4 %collective-permute-done.45 = bf16[1,1,2,80,768]{4,3,2,1,0:T(8,128)(2,1)S(1)} collective-permute-done((bf16[1,1,2,80,768]{4,3,2,1,0:T(8,128)(2,1)S(1)}, bf16[1,1,2,80,768]{4,3,2,1,0:T(8,128)(2,1)S(1)}, u32[]{:S(2)}, u32[]{:S(2)}) %collective-permute-start.45) | collective-permute-done | bytes 245792 | tf_op jit(solution)/shard_map/ppermute | solution.py:633
  274.7 2.0 collective-permute-start.49
  277.0 2.9 collective-permute-done.46
  280.7 2.2 fusion.1
  283.8 2.8 shard_map.409
  287.4 2.8 shard_map.408
  290.2 2.1 pad_maximum_fusion.1.all_ref
  292.3 3.5 %shard_map.407 = (f32[192,768]{1,0:T(8,128)}, f32[192,768]{1,0:T(8,128)}, f32[192,768]{1,0:T(8,128)}, f32[192,768]{1,0:T(8,128)}, f32[48,768]{1,0:T(8,128)}, /*i...) custom-call(s32[4]{0:T(128)} %pad_add_fusion.where_ref, ...), custom_call_target="tpu_custom_call" | custom-call | flops 603979776 | bytes 8388608 | tf_op jit(solution)/shard_map/pallas_call | solution.py:717
  295.8 1.3 reduce
  (162 shorter events, 23.4 us)
Async XLA Ops:
  2.2 8.9 %copy-start.8 = (bf16[2,400,768]{2,1,0:T(8,128)(2,1)}, bf16[2,400,768]{2,1,0:T(8,128)(2,1)S(1)}, u32[]{:S(2)}) copy-start(bf16[2,400,768]{2,1,0:T(8,128)(2,1)S(1)} %pad_maximum_fusion.rest_0_.own_t.rest_1_) | copy-start | bytes 3686404
  2.5 22.3 %collective-permute-start.1 = (bf16[2,400,768]{2,1,0:T(8,128)(2,1)S(1)}, bf16[2,400,768]{2,1,0:T(8,128)(2,1)}, u32[]{:S(2)}, u32[]{:S(2)}) collective-permute-start(bf16[2,400,768]{2,1,0:T(8,128)(2,1)S(1)} %pad_maximum_fusion.rest_0_.own_t.rest_1_), channel_id=1, source_target_pairs={{0,1},{1,0},{2,3},{3,2},{4,5},{5,4},{6,7},{7,6},{8,9},{9,8},{10,11... | collective-permute-start | bytes 3686408 | tf_op jit(solution)/shard_map/ppermute | solution.py:630
  3.0 17.1 %collective-permute-start = (bf16[400,768]{1,0:T(8,128)(2,1)S(1)}, bf16[400,768]{1,0:T(8,128)(2,1)}, u32[]{:S(2)}, u32[]{:S(2)}) collective-permute-start(bf16[400,768]{1,0:T(8,128)(2,1)S(1)} %fusion.3), channel_id=1, source_target_pairs={{0,2},{1,3},{2,0},{3,1},{4,6},{5,7},{6,4},{7,5},{8,10},{9,11},{10,... | collective-permute-start | bytes 1843208 | tf_op jit(solution)/shard_map/ppermute | solution.py:630
  20.2 16.3 %collective-permute-start.3 = (bf16[400,768]{1,0:T(8,128)(2,1)}, bf16[400,768]{1,0:T(8,128)(2,1)}, u32[]{:S(2)}, u32[]{:S(2)}) collective-permute-start(bf16[400,768]{1,0:T(8,128)(2,1)} %collective-permute-done.rest_0_.far_t), channel_id=1, source_target_pairs={{0,4},{4,0},{8,12},{12,8},{16,20},{20,16},{24,28},{28,24},{1,5},{5... | collective-permute-start | bytes 1843208 | tf_op jit(solution)/shard_map/ppermute | solution.py:633
  23.2 14.8 %collective-permute-start.2 = (bf16[384,768]{1,0:T(8,128)(2,1)S(1)}, bf16[384,768]{1,0:T(8,128)(2,1)}, u32[]{:S(2)}, u32[]{:S(2)}) collective-permute-start(bf16[384,768]{1,0:T(8,128)(2,1)S(1)} %get-tuple-element.138), channel_id=1, source_target_pairs={{0,2},{1,3},{2,0},{3,1},{4,6},{5,7},{6,4},{7,5},{8,10},{9,11},{10,... | collective-permute-start | bytes 1769480 | tf_op jit(solution)/shard_map/ppermute | solution.py:630
  24.8 15.3 %collective-permute-start.4 = (bf16[400,768]{1,0:T(8,128)(2,1)}, bf16[400,768]{1,0:T(8,128)(2,1)}, u32[]{:S(2)}, u32[]{:S(2)}) collective-permute-start(bf16[400,768]{1,0:T(8,128)(2,1)} %collective-permute-done.rest_0_.far_t), channel_id=1, source_target_pairs={{0,1},{1,0},{2,3},{3,2},{4,5},{5,4},{6,7},{7,6},{8,9},{9,8},{10,11... | collective-permute-start | bytes 1843208 | tf_op jit(solution)/shard_map/ppermute | solution.py:630
  24.8 13.7 %copy-start.17 = (bf16[1,768,768]{2,1,0:T(8,128)(2,1)S(1)}, bf16[1,768,768]{2,1,0:T(8,128)(2,1)}, u32[]{:S(2)}) copy-start(bf16[1,768,768]{2,1,0:T(8,128)(2,1)} %param.38) | copy-start | bytes 3538948
  36.5 3.8 %collective-permute-start.5 = (bf16[400,768]{1,0:T(8,128)(2,1)}, bf16[400,768]{1,0:T(8,128)(2,1)}, u32[]{:S(2)}, u32[]{:S(2)}) collective-permute-start(bf16[400,768]{1,0:T(8,128)(2,1)} %collective-permute-done.3.rest_1_), channel_id=1, source_target_pairs={{0,1},{1,0},{2,3},{3,2},{4,5},{5,4},{6,7},{7,6},{8,9},{9,8},{10,11... | collective-permute-start | bytes 1843208 | tf_op jit(solution)/shard_map/ppermute | solution.py:630
  38.0 14.6 %collective-permute-start.8 = (bf16[384,768]{1,0:T(8,128)(2,1)}, bf16[384,768]{1,0:T(8,128)(2,1)S(1)}, u32[]{:S(2)}, u32[]{:S(2)}) collective-permute-start(bf16[384,768]{1,0:T(8,128)(2,1)} %collective-permute-done.2.far.far_u), channel_id=1, source_target_pairs={{0,4},{4,0},{8,12},{12,8},{16,20},{20,16},{24,28},{28,24},{1,5},{5... | collective-permute-start | bytes 1769480 | tf_op jit(solution)/shard_map/ppermute | solution.py:633
  38.5 17.4 %collective-permute-start.7 = (bf16[768,768]{1,0:T(8,128)(2,1)S(1)}, bf16[768,768]{1,0:T(8,128)(2,1)}, u32[]{:S(2)}, u32[]{:S(2)}) collective-permute-start(bf16[768,768]{1,0:T(8,128)(2,1)S(1)} %bitcast.180), channel_id=1, source_target_pairs={{0,1},{1,0},{2,3},{3,2},{4,5},{5,4},{6,7},{7,6},{8,9},{9,8},{10,11... | collective-permute-start | bytes 3538952 | tf_op jit(solution)/shard_map/ppermute | solution.py:630
  38.5 17.4 %copy-start.18 = (bf16[1,768,768]{2,1,0:T(8,128)(2,1)S(1)}, bf16[1,768,768]{2,1,0:T(8,128)(2,1)}, u32[]{:S(2)}) copy-start(bf16[1,768,768]{2,1,0:T(8,128)(2,1)} %param.40) | copy-start | bytes 3538948
  38.5 15.8 %collective-permute-start.6 = (bf16[384,768]{1,0:T(8,128)(2,1)S(1)}, bf16[384,768]{1,0:T(8,128)(2,1)}, u32[]{:S(2)}, u32[]{:S(2)}) collective-permute-start(bf16[384,768]{1,0:T(8,128)(2,1)S(1)} %get-tuple-element.144), channel_id=1, source_target_pairs={{0,2},{1,3},{2,0},{3,1},{4,6},{5,7},{6,4},{7,5},{8,10},{9,11},{10,... | collective-permute-start | bytes 1769480 | tf_op jit(solution)/shard_map/ppermute | solution.py:630
  40.2 16.3 %collective-permute-start.9 = (bf16[384,768]{1,0:T(8,128)(2,1)}, bf16[384,768]{1,0:T(8,128)(2,1)}, u32[]{:S(2)}, u32[]{:S(2)}) collective-permute-start(bf16[384,768]{1,0:T(8,128)(2,1)} %collective-permute-done.2.far.far_u), channel_id=1, source_target_pairs={{0,1},{1,0},{2,3},{3,2},{4,5},{5,4},{6,7},{7,6},{8,9},{9,8},{10,11... | collective-permute-start | bytes 1769480 | tf_op jit(solution)/shard_map/ppermute | solution.py:630
  52.6 3.8 %collective-permute-start.10 = (bf16[384,768]{1,0:T(8,128)(2,1)S(1)}, bf16[384,768]{1,0:T(8,128)(2,1)}, u32[]{:S(2)}, u32[]{:S(2)}) collective-permute-start(bf16[384,768]{1,0:T(8,128)(2,1)S(1)} %collective-permute-done.8.far_other.far_other_u), channel_id=1, source_target_pairs={{0,1},{1,0},{2,3},{3,2},{4,5},{5,4},{6,7},{7,6},{8,9},{9,8},{10,11... | collective-permute-start | bytes 1769480 | tf_op jit(solution)/shard_map/ppermute | solution.py:630
  52.6 17.9 %copy-start.22 = (f32[96]{0:T(128)S(1)}, f32[96]{0:T(128)}, u32[]{:S(2)}) copy-start(f32[96]{0:T(128)} %param.43) | copy-start | bytes 1156
  54.4 16.0 %collective-permute-start.12 = (bf16[384,768]{1,0:T(8,128)(2,1)}, bf16[384,768]{1,0:T(8,128)(2,1)S(1)}, u32[]{:S(2)}, u32[]{:S(2)}) collective-permute-start(bf16[384,768]{1,0:T(8,128)(2,1)} %collective-permute-done.6.far.far_d), channel_id=1, source_target_pairs={{0,4},{4,0},{8,12},{12,8},{16,20},{20,16},{24,28},{28,24},{1,5},{5... | collective-permute-start | bytes 1769480 | tf_op jit(solution)/shard_map/ppermute | solution.py:633
  55.9 15.3 %collective-permute-start.11 = (bf16[768,768]{1,0:T(8,128)(2,1)S(1)}, bf16[768,768]{1,0:T(8,128)(2,1)}, u32[]{:S(2)}, u32[]{:S(2)}) collective-permute-start(bf16[768,768]{1,0:T(8,128)(2,1)S(1)} %bitcast.183), channel_id=1, source_target_pairs={{0,1},{1,0},{2,3},{3,2},{4,5},{5,4},{6,7},{7,6},{8,9},{9,8},{10,11... | collective-permute-start | bytes 3538952 | tf_op jit(solution)/shard_map/ppermute | solution.py:630
  55.9 15.3 %collective-permute-start.13 = (bf16[384,768]{1,0:T(8,128)(2,1)}, bf16[384,768]{1,0:T(8,128)(2,1)S(1)}, u32[]{:S(2)}, u32[]{:S(2)}) collective-permute-start(bf16[384,768]{1,0:T(8,128)(2,1)} %collective-permute-done.6.far.far_d), channel_id=1, source_target_pairs={{0,1},{1,0},{2,3},{3,2},{4,5},{5,4},{6,7},{7,6},{8,9},{9,8},{10,11... | collective-permute-start | bytes 1769480 | tf_op jit(solution)/shard_map/ppermute | solution.py:630
  70.4 2.1 collective-permute-start.14
  88.2 20.2 %collective-permute-start.16 = (bf16[2,4,192,768]{3,2,1,0:T(8,128)(2,1)}, bf16[2,4,192,768]{3,2,1,0:T(8,128)(2,1)S(1)}, u32[]{:S(2)}, u32[]{:S(2)}) collective-permute-start(bf16[2,4,192,768]{3,2,1,0:T(8,128)(2,1)} %get-tuple-element.159), channel_id=1, source_target_pairs={{0,1},{1,0},{2,3},{3,2},{4,5},{5,4},{6,7},{7,6},{8,9},{9,8},{10,11... | collective-permute-start | bytes 7077896 | tf_op jit(solution)/shard_map/ppermute | solution.py:630
  108.0 5.5 %collective-permute-start.15 = (bf16[2,4,192,768]{3,2,1,0:T(8,128)(2,1)}, bf16[2,4,192,768]{3,2,1,0:T(8,128)(2,1)S(1)}, u32[]{:S(2)}, u32[]{:S(2)}) collective-permute-start(bf16[2,4,192,768]{3,2,1,0:T(8,128)(2,1)} %get-tuple-element.166), channel_id=1, source_target_pairs={{0,1},{1,0},{2,3},{3,2},{4,5},{5,4},{6,7},{7,6},{8,9},{9,8},{10,11... | collective-permute-start | bytes 7077896 | tf_op jit(solution)/shard_map/ppermute | solution.py:630
  111.9 37.6 %collective-permute-start.19 = (bf16[1,2,2,192,768]{4,3,2,1,0:T(8,128)(2,1)}, bf16[1,2,2,192,768]{4,3,2,1,0:T(8,128)(2,1)}, u32[]{:S(2)}, u32[]{:S(2)}) collective-permute-start(bf16[1,2,2,192,768]{4,3,2,1,0:T(8,128)(2,1)} %bitcast.28), channel_id=1, source_target_pairs={{0,2},{1,3},{2,0},{3,1},{4,6},{5,7},{6,4},{7,5},{8,10},{9,11},{10,... | collective-permute-start | bytes 3538952 | tf_op jit(solution)/shard_map/ppermute | solution.py:630
  115.2 16.3 %copy-start.3 = (bf16[2,4,192,768]{3,2,1,0:T(8,128)(2,1)S(1)}, bf16[2,4,192,768]{3,2,1,0:T(8,128)(2,1)}, u32[]{:S(2)}) copy-start(bf16[2,4,192,768]{3,2,1,0:T(8,128)(2,1)} %get-tuple-element.167) | copy-start | bytes 7077892
  129.9 18.2 %collective-permute-start.17 = (bf16[4,144,768]{2,1,0:T(8,128)(2,1)}, bf16[4,144,768]{2,1,0:T(8,128)(2,1)}, u32[]{:S(2)}, u32[]{:S(2)}) collective-permute-start(bf16[4,144,768]{2,1,0:T(8,128)(2,1)} %get-tuple-element.179), channel_id=1, source_target_pairs={{0,1},{1,0},{2,3},{3,2},{4,5},{5,4},{6,7},{7,6},{8,9},{9,8},{10,11... | collective-permute-start | bytes 2654216 | tf_op jit(solution)/shard_map/ppermute | solution.py:630
  129.9 28.7 %collective-permute-start.18 = (bf16[2,2,1,192,768]{4,3,1,2,0:T(8,128)(2,1)}, bf16[2,2,1,192,768]{4,3,1,2,0:T(8,128)(2,1)}, u32[]{:S(2)}, u32[]{:S(2)}) collective-permute-start(bf16[2,2,1,192,768]{4,3,1,2,0:T(8,128)(2,1)} %add_convert_fusion.1), channel_id=1, source_target_pairs={{0,8},{4,12},{8,0},{12,4},{16,24},{20,28},{24,16},{28,20},{1,9},{5... | collective-permute-start | bytes 3538952 | tf_op jit(solution)/shard_map/ppermute | solution.py:633
  169.4 19.8 %copy-start.12 = (bf16[2,1,1,192,768]{4,3,1,2,0:T(8,128)(2,1)S(1)}, bf16[2,1,1,192,768]{4,3,1,2,0:T(8,128)(2,1)}, u32[]{:S(2)}) copy-start(bf16[2,1,1,192,768]{4,3,1,2,0:T(8,128)(2,1)} %add_convert_fusion.4) | copy-start | bytes 1769476
  169.4 23.4 %collective-permute-start.24 = (bf16[2,4,80,768]{3,2,1,0:T(8,128)(2,1)}, bf16[2,4,80,768]{3,2,1,0:T(8,128)(2,1)S(1)}, u32[]{:S(2)}, u32[]{:S(2)}) collective-permute-start(bf16[2,4,80,768]{3,2,1,0:T(8,128)(2,1)} %get-tuple-element.204), channel_id=1, source_target_pairs={{0,1},{1,0},{2,3},{3,2},{4,5},{5,4},{6,7},{7,6},{8,9},{9,8},{10,11... | collective-permute-start | bytes 2949128 | tf_op jit(solution)/shard_map/ppermute | solution.py:630
  169.4 16.0 %collective-permute-start.22 = (bf16[1,1,2,192,768]{4,3,2,1,0:T(8,128)(2,1)}, bf16[1,1,2,192,768]{4,3,2,1,0:T(8,128)(2,1)S(1)}, u32[]{:S(2)}, u32[]{:S(2)}) collective-permute-start(bf16[1,1,2,192,768]{4,3,2,1,0:T(8,128)(2,1)} %add_convert_fusion.3), channel_id=1, source_target_pairs={{0,4},{4,0},{8,12},{12,8},{16,20},{20,16},{24,28},{28,24},{1,5},{5... | collective-permute-start | bytes 1769480 | tf_op jit(solution)/shard_map/ppermute | solution.py:633
  170.1 30.7 %collective-permute-start.20 = (bf16[4,144,768]{2,1,0:T(8,128)(2,1)}, bf16[4,144,768]{2,1,0:T(8,128)(2,1)S(1)}, u32[]{:S(2)}, u32[]{:S(2)}) collective-permute-start(bf16[4,144,768]{2,1,0:T(8,128)(2,1)} %get-tuple-element.188), channel_id=1, source_target_pairs={{0,1},{1,0},{2,3},{3,2},{4,5},{5,4},{6,7},{7,6},{8,9},{9,8},{10,11... | collective-permute-start | bytes 2654216 | tf_op jit(solution)/shard_map/ppermute | solution.py:630
  170.3 22.5 %copy-start.9 = (bf16[2,4,80,768]{3,2,1,0:T(8,128)(2,1)S(1)}, bf16[2,4,80,768]{3,2,1,0:T(8,128)(2,1)}, u32[]{:S(2)}) copy-start(bf16[2,4,80,768]{3,2,1,0:T(8,128)(2,1)} %get-tuple-element.207) | copy-start | bytes 2949124
  170.4 30.4 %collective-permute-start.21 = (bf16[1,2,2,144,768]{4,3,1,2,0:T(8,128)(2,1)S(1)}, bf16[1,2,2,144,768]{4,3,1,2,0:T(8,128)(2,1)S(1)}, u32[]{:S(2)}, u32[]{:S(2)}) collective-permute-start(bf16[1,2,2,144,768]{4,3,1,2,0:T(8,128)(2,1)S(1)} %copy.56), channel_id=1, source_target_pairs={{0,2},{1,3},{2,0},{3,1},{4,6},{5,7},{6,4},{7,5},{8,10},{9,11},{10,... | collective-permute-start | bytes 2654216 | tf_op jit(solution)/shard_map/ppermute | solution.py:630
  186.5 4.7 %collective-permute-start.23 = (bf16[8,896]{1,0:T(8,128)(2,1)S(1)}, bf16[8,896]{1,0:T(8,128)(2,1)S(1)}, u32[]{:S(2)}, u32[]{:S(2)}) collective-permute-start(bf16[8,896]{1,0:T(8,128)(2,1)S(1)} %convert_element_type.349), channel_id=1, source_target_pairs={{0,16},{4,20},{8,24},{12,28},{16,0},{20,4},{24,8},{28,12},{1,17},{... | collective-permute-start | bytes 43016 | tf_op jit(solution)/shard_map/ppermute | solution.py:633
  189.2 16.8 %collective-permute-start.29 = (bf16[2,1,1,192,768]{4,3,1,2,0:T(8,128)(2,1)S(1)}, bf16[2,1,1,192,768]{4,3,1,2,0:T(8,128)(2,1)S(1)}, u32[]{:S(2)}, u32[]{:S(2)}) collective-permute-start(bf16[2,1,1,192,768]{4,3,1,2,0:T(8,128)(2,1)S(1)} %copy-done.12), channel_id=1, source_target_pairs={{0,4},{4,0},{8,12},{12,8},{16,20},{20,16},{24,28},{28,24},{1,5},{5... | collective-permute-start | bytes 1769480 | tf_op jit(solution)/shard_map/ppermute | solution.py:633
  191.2 7.7 %collective-permute-start.26 = (bf16[1,1,1,192,768]{4,3,2,1,0:T(8,128)(2,1)S(1)}, bf16[1,1,1,192,768]{4,3,2,1,0:T(8,128)(2,1)S(1)}, u32[]{:S(2)}, u32[]{:S(2)}) collective-permute-start(bf16[1,1,1,192,768]{4,3,2,1,0:T(8,128)(2,1)S(1)} %add_convert_fusion.12), channel_id=1, source_target_pairs={{0,8},{4,12},{8,0},{12,4},{16,24},{20,28},{24,16},{28,20},{1,9},{5... | collective-permute-start | bytes 884744 | tf_op jit(solution)/shard_map/ppermute | solution.py:633
  192.9 7.9 %copy-start.10 = (bf16[4,144,768]{2,1,0:T(8,128)(2,1)S(1)}, bf16[4,144,768]{2,1,0:T(8,128)(2,1)}, u32[]{:S(2)}) copy-start(bf16[4,144,768]{2,1,0:T(8,128)(2,1)} %get-tuple-element.201) | copy-start | bytes 2654212
  192.9 7.2 %collective-permute-start.25 = (bf16[16,896]{1,0:T(8,128)(2,1)S(1)}, bf16[16,896]{1,0:T(8,128)(2,1)S(1)}, u32[]{:S(2)}, u32[]{:S(2)}) collective-permute-start(bf16[16,896]{1,0:T(8,128)(2,1)S(1)} %pad_maximum_fusion.11), channel_id=1, source_target_pairs={{0,8},{4,12},{8,0},{12,4},{16,24},{20,28},{24,16},{28,20},{1,9},{5... | collective-permute-start | bytes 86024 | tf_op jit(solution)/shard_map/ppermute | solution.py:633
  200.1 4.9 %collective-permute-start.30 = (bf16[32,896]{1,0:T(8,128)(2,1)S(1)}, bf16[32,896]{1,0:T(8,128)(2,1)S(1)}, u32[]{:S(2)}, u32[]{:S(2)}) collective-permute-start(bf16[32,896]{1,0:T(8,128)(2,1)S(1)} %pad_maximum_fusion.10), channel_id=1, source_target_pairs={{0,4},{4,0},{8,12},{12,8},{16,20},{20,16},{24,28},{28,24},{1,5},{5... | collective-permute-start | bytes 172040 | tf_op jit(solution)/shard_map/ppermute | solution.py:633
  201.0 13.3 %collective-permute-start.28 = (bf16[1,1,1,192,768]{4,3,2,1,0:T(8,128)(2,1)S(1)}, bf16[1,1,1,192,768]{4,3,2,1,0:T(8,128)(2,1)S(1)}, u32[]{:S(2)}, u32[]{:S(2)}) collective-permute-start(bf16[1,1,1,192,768]{4,3,2,1,0:T(8,128)(2,1)S(1)} %add_convert_fusion.11), channel_id=1, source_target_pairs={{0,16},{4,20},{8,24},{12,28},{16,0},{20,4},{24,8},{28,12},{1,17},{... | collective-permute-start | bytes 884744 | tf_op jit(solution)/shard_map/ppermute | solution.py:633
  205.0 5.6 %collective-permute-start.33 = (bf16[64,896]{1,0:T(8,128)(2,1)S(1)}, bf16[64,896]{1,0:T(8,128)(2,1)S(1)}, u32[]{:S(2)}, u32[]{:S(2)}) collective-permute-start(bf16[64,896]{1,0:T(8,128)(2,1)S(1)} %pad_maximum_fusion.9), channel_id=1, source_target_pairs={{0,2},{1,3},{2,0},{3,1},{4,6},{5,7},{6,4},{7,5},{8,10},{9,11},{10,... | collective-permute-start | bytes 344072 | tf_op jit(solution)/shard_map/ppermute | solution.py:630
  207.2 15.2 %collective-permute-start.32 = (bf16[2,1,2,80,768]{4,3,2,1,0:T(8,128)(2,1)S(1)}, bf16[2,1,2,80,768]{4,3,2,1,0:T(8,128)(2,1)S(1)}, u32[]{:S(2)}, u32[]{:S(2)}) collective-permute-start(bf16[2,1,2,80,768]{4,3,2,1,0:T(8,128)(2,1)S(1)} %add_convert_fusion.5), channel_id=1, source_target_pairs={{0,4},{4,0},{8,12},{12,8},{16,20},{20,16},{24,28},{28,24},{1,5},{5... | collective-permute-start | bytes 1474568 | tf_op jit(solution)/shard_map/ppermute | solution.py:633
  207.9 14.4 %collective-permute-start.27 = (bf16[1,2,1,144,768]{4,3,1,2,0:T(8,128)(2,1)S(1)}, bf16[1,2,1,144,768]{4,3,1,2,0:T(8,128)(2,1)S(1)}, u32[]{:S(2)}, u32[]{:S(2)}) collective-permute-start(bf16[1,2,1,144,768]{4,3,1,2,0:T(8,128)(2,1)S(1)} %add_convert_fusion.6), channel_id=1, source_target_pairs={{0,8},{4,12},{8,0},{12,4},{16,24},{20,28},{24,16},{28,20},{1,9},{5... | collective-permute-start | bytes 1327112 | tf_op jit(solution)/shard_map/ppermute | solution.py:633
  209.5 6.7 %collective-permute-start.31 = (bf16[1,1,1,192,768]{4,3,1,2,0:T(8,128)(2,1)S(1)}, bf16[1,1,1,192,768]{4,3,1,2,0:T(8,128)(2,1)S(1)}, u32[]{:S(2)}, u32[]{:S(2)}) collective-permute-start(bf16[1,1,1,192,768]{4,3,1,2,0:T(8,128)(2,1)S(1)} %add_convert_fusion.9), channel_id=1, source_target_pairs={{0,2},{1,3},{2,0},{3,1},{4,6},{5,7},{6,4},{7,5},{8,10},{9,11},{10,... | collective-permute-start | bytes 884744 | tf_op jit(solution)/shard_map/ppermute | solution.py:630
  222.5 6.0 %collective-permute-start.34 = (bf16[1,1,1,144,768]{4,3,1,2,0:T(8,128)(2,1)S(1)}, bf16[1,1,1,144,768]{4,3,1,2,0:T(8,128)(2,1)S(1)}, u32[]{:S(2)}, u32[]{:S(2)}) collective-permute-start(bf16[1,1,1,144,768]{4,3,1,2,0:T(8,128)(2,1)S(1)} %add_convert_fusion.16), channel_id=1, source_target_pairs={{0,4},{4,0},{8,12},{12,8},{16,20},{20,16},{24,28},{28,24},{1,5},{5... | collective-permute-start | bytes 663560 | tf_op jit(solution)/shard_map/ppermute | solution.py:633
  224.0 6.2 %collective-permute-start.35 = (bf16[1,1,2,80,768]{4,3,2,1,0:T(8,128)(2,1)S(1)}, bf16[1,1,2,80,768]{4,3,2,1,0:T(8,128)(2,1)S(1)}, u32[]{:S(2)}, u32[]{:S(2)}) collective-permute-start(bf16[1,1,2,80,768]{4,3,2,1,0:T(8,128)(2,1)S(1)} %add_convert_fusion.13), channel_id=1, source_target_pairs={{0,2},{1,3},{2,0},{3,1},{4,6},{5,7},{6,4},{7,5},{8,10},{9,11},{10,... | collective-permute-start | bytes 737288 | tf_op jit(solution)/shard_map/ppermute | solution.py:630
  225.2 23.9 %collective-permute-start.40 = (bf16[1,1,1,192,768]{4,3,2,1,0:T(8,128)(2,1)S(1)}, bf16[1,1,1,192,768]{4,3,2,1,0:T(8,128)(2,1)S(1)}, u32[]{:S(2)}, u32[]{:S(2)}) collective-permute-start(bf16[1,1,1,192,768]{4,3,2,1,0:T(8,128)(2,1)S(1)} %add_convert_fusion.10), channel_id=1, source_target_pairs={{0,8},{4,12},{8,0},{12,4},{16,24},{20,28},{24,16},{28,20},{1,9},{5... | collective-permute-start | bytes 884744 | tf_op jit(solution)/shard_map/ppermute | solution.py:633
  225.2 23.2 %collective-permute-start.37 = (bf16[1,1,1,192,768]{4,3,1,2,0:T(8,128)(2,1)S(1)}, bf16[1,1,1,192,768]{4,3,1,2,0:T(8,128)(2,1)S(1)}, u32[]{:S(2)}, u32[]{:S(2)}) collective-permute-start(bf16[1,1,1,192,768]{4,3,1,2,0:T(8,128)(2,1)S(1)} %add_convert_fusion.8), channel_id=1, source_target_pairs={{0,16},{4,20},{8,24},{12,28},{16,0},{20,4},{24,8},{28,12},{1,17},{... | collective-permute-start | bytes 884744 | tf_op jit(solution)/shard_map/ppermute | solution.py:633
  230.3 18.9 %collective-permute-start.39 = (bf16[1,1,1,80,768]{4,3,2,1,0:T(8,128)(2,1)S(1)}, bf16[1,1,1,80,768]{4,3,2,1,0:T(8,128)(2,1)S(1)}, u32[]{:S(2)}, u32[]{:S(2)}) collective-permute-start(bf16[1,1,1,80,768]{4,3,2,1,0:T(8,128)(2,1)S(1)} %add_convert_fusion.19), channel_id=1, source_target_pairs={{0,8},{4,12},{8,0},{12,4},{16,24},{20,28},{24,16},{28,20},{1,9},{5... | collective-permute-start | bytes 368648 | tf_op jit(solution)/shard_map/ppermute | solution.py:633
  230.3 21.5 %collective-permute-start.36 = (bf16[1,1,1,144,768]{4,3,1,2,0:T(8,128)(2,1)S(1)}, bf16[1,1,1,144,768]{4,3,1,2,0:T(8,128)(2,1)S(1)}, u32[]{:S(2)}, u32[]{:S(2)}) collective-permute-start(bf16[1,1,1,144,768]{4,3,1,2,0:T(8,128)(2,1)S(1)} %add_convert_fusion.15), channel_id=1, source_target_pairs={{0,16},{4,20},{8,24},{12,28},{16,0},{20,4},{24,8},{28,12},{1,17},{... | collective-permute-start | bytes 663560 | tf_op jit(solution)/shard_map/ppermute | solution.py:633
  248.4 8.5 %collective-permute-start.38 = (bf16[1,1,1,192,768]{4,3,1,2,0:T(8,128)(2,1)S(1)}, bf16[1,1,1,192,768]{4,3,1,2,0:T(8,128)(2,1)S(1)}, u32[]{:S(2)}, u32[]{:S(2)}) collective-permute-start(bf16[1,1,1,192,768]{4,3,1,2,0:T(8,128)(2,1)S(1)} %add_convert_fusion.7), channel_id=1, source_target_pairs={{0,4},{4,0},{8,12},{12,8},{16,20},{20,16},{24,28},{28,24},{1,5},{5... | collective-permute-start | bytes 884744 | tf_op jit(solution)/shard_map/ppermute | solution.py:633
  249.1 17.5 %copy-start.6 = (bf16[1,1,2,192,768]{4,3,2,1,0:T(8,128)(2,1)}, bf16[1,1,2,192,768]{4,3,2,1,0:T(8,128)(2,1)S(1)}, u32[]{:S(2)}) copy-start(bf16[1,1,2,192,768]{4,3,2,1,0:T(8,128)(2,1)S(1)} %pad_maximum_fusion.3) | copy-start | bytes 1769476
  249.2 6.8 %collective-permute-start.42 = (bf16[1,1,1,80,768]{4,3,2,1,0:T(8,128)(2,1)S(1)}, bf16[1,1,1,80,768]{4,3,2,1,0:T(8,128)(2,1)S(1)}, u32[]{:S(2)}, u32[]{:S(2)}) collective-permute-start(bf16[1,1,1,80,768]{4,3,2,1,0:T(8,128)(2,1)S(1)} %add_convert_fusion.18), channel_id=1, source_target_pairs={{0,16},{4,20},{8,24},{12,28},{16,0},{20,4},{24,8},{28,12},{1,17},{... | collective-permute-start | bytes 368648 | tf_op jit(solution)/shard_map/ppermute | solution.py:633
  257.0 17.7 %copy-start.7 = (bf16[1,2,1,192,768]{4,3,1,2,0:T(8,128)(2,1)}, bf16[1,2,1,192,768]{4,3,1,2,0:T(8,128)(2,1)S(1)}, u32[]{:S(2)}) copy-start(bf16[1,2,1,192,768]{4,3,1,2,0:T(8,128)(2,1)S(1)} %pad_maximum_fusion.2) | copy-start | bytes 1769476
  257.0 4.9 %collective-permute-start.44 = (bf16[1,1,1,80,768]{4,3,2,1,0:T(8,128)(2,1)S(1)}, bf16[1,1,1,80,768]{4,3,2,1,0:T(8,128)(2,1)S(1)}, u32[]{:S(2)}, u32[]{:S(2)}) collective-permute-start(bf16[1,1,1,80,768]{4,3,2,1,0:T(8,128)(2,1)S(1)} %add_convert_fusion.17), channel_id=1, source_target_pairs={{0,8},{4,12},{8,0},{12,4},{16,24},{20,28},{24,16},{28,20},{1,9},{5... | collective-permute-start | bytes 368648 | tf_op jit(solution)/shard_map/ppermute | solution.py:633
  257.0 8.1 %collective-permute-start.41 = (bf16[1,1,1,144,768]{4,3,1,2,0:T(8,128)(2,1)S(1)}, bf16[1,1,1,144,768]{4,3,1,2,0:T(8,128)(2,1)S(1)}, u32[]{:S(2)}, u32[]{:S(2)}) collective-permute-start(bf16[1,1,1,144,768]{4,3,1,2,0:T(8,128)(2,1)S(1)} %add_convert_fusion.14), channel_id=1, source_target_pairs={{0,4},{4,0},{8,12},{12,8},{16,20},{20,16},{24,28},{28,24},{1,5},{5... | collective-permute-start | bytes 663560 | tf_op jit(solution)/shard_map/ppermute | solution.py:633
  257.7 8.9 %collective-permute-start.48 = (bf16[128,896]{1,0:T(8,128)(2,1)S(1)}, bf16[128,896]{1,0:T(8,128)(2,1)S(1)}, u32[]{:S(2)}, u32[]{:S(2)}) collective-permute-start(bf16[128,896]{1,0:T(8,128)(2,1)S(1)} %pad_maximum_fusion.7), channel_id=1, source_target_pairs={{0,1},{1,0},{2,3},{3,2},{4,5},{5,4},{6,7},{7,6},{8,9},{9,8},{10,11... | collective-permute-start | bytes 688136 | tf_op jit(solution)/shard_map/ppermute | solution.py:630
  261.9 12.2 %copy-start.15 = (bf16[1,1,2,80,768]{4,3,2,1,0:T(8,128)(2,1)}, bf16[1,1,2,80,768]{4,3,2,1,0:T(8,128)(2,1)S(1)}, u32[]{:S(2)}) copy-start(bf16[1,1,2,80,768]{4,3,2,1,0:T(8,128)(2,1)S(1)} %pad_maximum_fusion.6) | copy-start | bytes 737284
  265.2 15.5 %copy-start.16 = (bf16[1,2,1,144,768]{4,3,1,2,0:T(8,128)(2,1)}, bf16[1,2,1,144,768]{4,3,1,2,0:T(8,128)(2,1)S(1)}, u32[]{:S(2)}) copy-start(bf16[1,2,1,144,768]{4,3,1,2,0:T(8,128)(2,1)S(1)} %pad_maximum_fusion.4) | copy-start | bytes 1327108
  265.2 9.0 %collective-permute-start.45 = (bf16[1,1,2,80,768]{4,3,2,1,0:T(8,128)(2,1)S(1)}, bf16[1,1,2,80,768]{4,3,2,1,0:T(8,128)(2,1)S(1)}, u32[]{:S(2)}, u32[]{:S(2)}) collective-permute-start(bf16[1,1,2,80,768]{4,3,2,1,0:T(8,128)(2,1)S(1)} %pad_maximum_fusion.6), channel_id=1, source_target_pairs={{0,4},{4,0},{8,12},{12,8},{16,20},{20,16},{24,28},{28,24},{1,5},{5... | collective-permute-start | bytes 737288 | tf_op jit(solution)/shard_map/ppermute | solution.py:633
  266.6 16.3 %collective-permute-start.50 = (bf16[1,1,2,192,768]{4,3,2,1,0:T(8,128)(2,1)S(1)}, bf16[1,1,2,192,768]{4,3,2,1,0:T(8,128)(2,1)S(1)}, u32[]{:S(2)}, u32[]{:S(2)}) collective-permute-start(bf16[1,1,2,192,768]{4,3,2,1,0:T(8,128)(2,1)S(1)} %pad_maximum_fusion.3), channel_id=1, source_target_pairs={{0,4},{4,0},{8,12},{12,8},{16,20},{20,16},{24,28},{28,24},{1,5},{5... | collective-permute-start | bytes 1769480 | tf_op jit(solution)/shard_map/ppermute | solution.py:633
  274.1 8.8 %copy-start.19 = (bf16[1,1,2,80,768]{4,3,2,1,0:T(8,128)(2,1)}, bf16[1,1,2,80,768]{4,3,2,1,0:T(8,128)(2,1)S(1)}, u32[]{:S(2)}) copy-start(bf16[1,1,2,80,768]{4,3,2,1,0:T(8,128)(2,1)S(1)} %collective-permute-done.45) | copy-start | bytes 737284
  274.2 5.7 %collective-permute-start.46 = (bf16[1,4,32,768]{3,2,1,0:T(8,128)(2,1)S(1)}, bf16[1,4,32,768]{3,2,1,0:T(8,128)(2,1)S(1)}, u32[]{:S(2)}, u32[]{:S(2)}) collective-permute-start(bf16[1,4,32,768]{3,2,1,0:T(8,128)(2,1)S(1)} %bitcast.152), channel_id=1, source_target_pairs={{0,2},{1,3},{2,0},{3,1},{4,6},{5,7},{6,4},{7,5},{8,10},{9,11},{10,... | collective-permute-start | bytes 589832 | tf_op jit(solution)/shard_map/ppermute | solution.py:630
  274.7 11.9 %collective-permute-start.49 = (bf16[1,2,1,192,768]{4,3,1,2,0:T(8,128)(2,1)S(1)}, bf16[1,2,1,192,768]{4,3,1,2,0:T(8,128)(2,1)S(1)}, u32[]{:S(2)}, u32[]{:S(2)}) collective-permute-start(bf16[1,2,1,192,768]{4,3,1,2,0:T(8,128)(2,1)S(1)} %pad_maximum_fusion.2), channel_id=1, source_target_pairs={{0,8},{4,12},{8,0},{12,4},{16,24},{20,28},{24,16},{28,20},{1,9},{5... | collective-permute-start | bytes 1769480 | tf_op jit(solution)/shard_map/ppermute | solution.py:633
  276.9 15.4 %collective-permute-start.43 = (bf16[1,2,1,144,768]{4,3,1,2,0:T(8,128)(2,1)S(1)}, bf16[1,2,1,144,768]{4,3,1,2,0:T(8,128)(2,1)}, u32[]{:S(2)}, u32[]{:S(2)}) collective-permute-start(bf16[1,2,1,144,768]{4,3,1,2,0:T(8,128)(2,1)S(1)} %pad_maximum_fusion.4), channel_id=1, source_target_pairs={{0,8},{4,12},{8,0},{12,4},{16,24},{20,28},{24,16},{28,20},{1,9},{5... | collective-permute-start | bytes 1327112 | tf_op jit(solution)/shard_map/ppermute | solution.py:633
  280.7 9.5 %collective-permute-start.47 = (bf16[2,4,32,768]{3,2,1,0:T(8,128)(2,1)}, bf16[2,4,32,768]{3,2,1,0:T(8,128)(2,1)}, u32[]{:S(2)}, u32[]{:S(2)}) collective-permute-start(bf16[2,4,32,768]{3,2,1,0:T(8,128)(2,1)} %pad_maximum_fusion.5), channel_id=1, source_target_pairs={{0,1},{1,0},{2,3},{3,2},{4,5},{5,4},{6,7},{7,6},{8,9},{9,8},{10,11... | collective-permute-start | bytes 1179656 | tf_op jit(solution)/shard_map/ppermute | solution.py:630
  (15 other events, 41.8 us)

commit v3 on v2

--- a/solution.py
+++ b/solution.py
@@ -15,12 +15,10 @@
 PIECES = 4
 EXTRA = 16
 GROUP = 32
-CHAIN_ORDERS = ("yxz", "zxy", "yzx", "xyz")
-BEFORE_FAR = (0, 1)
-BEFORE_NEAR = ()
-BEFORE_EMBED = (0, 1, 2)
-TAIL = (0, 3, 0, 2, 1, 3, 1, 0, 2, 3, 2, 1, 0, 3, 1, 2, 3, 2, 3)
 CHUNK = 64
+GATHER_ROWS = 32
+CHAIN_ORDERS = ("yxz", "zxy", "yxz", "zyx")
+TAIL = (1, 3, 4, 0, 1, 3, 2, 4, 1, 3, 2, 3, 0, 2, 4, 3, 1, 4, 3, 0, 4, 2, 5, 1, 2, 5)
 
 VMEM = pl.BlockSpec(memory_space=pltpu.VMEM)
 SMEM = pl.BlockSpec(memory_space=pltpu.SMEM)
@@ -68,7 +66,9 @@
 
 def gelu_pair(values):
     scaled = jnp.abs(values) * 0.7071067811865476
-    t = 1.0 / (1.0 + 0.3275911 * scaled)
+    base = 1.0 + 0.3275911 * scaled
+    t = pl.reciprocal(base, approx=True)
+    t = t * (2.0 - base * t)
     bell = jnp.exp(-0.5 * values * values)
     poly = 1.061405429 * t - 1.453152027
     poly = poly * t + 1.421413741
@@ -148,60 +148,71 @@
     mine = pl.ds(pl.multiple_of(where_ref[1] * half, half), half)
     other = pl.ds(pl.multiple_of((1 - where_ref[1]) * half, half), half)
     copies = [
-        (own, weight_ref.at[0]),
-        (near, weight_ref.at[1]),
-        (far, weight_ref.at[2, mine]),
-        (far_other, weight_ref.at[2, other]),
-        (cross, weight_ref.at[3, mine]),
-        (cross_other, weight_ref.at[3, other]),
+        (own, weight_ref.at[0], 0),
+        (near, weight_ref.at[1], 1),
+        (far, weight_ref.at[2, mine], 2),
+        (far_other, weight_ref.at[2, other], 2),
+        (cross, weight_ref.at[3, mine], 3),
+        (cross_other, weight_ref.at[3, other], 3),
     ]
-    return start_copies(copies, sems)
-
-
-def allowed_mask(packed, quarter, first, rows, keys):
-    q = lax.broadcasted_iota(jnp.int32, (rows, keys), 0) + first
-    k = lax.broadcasted_iota(jnp.int32, (rows, keys), 1)
+    for source, target, slot in copies:
+        pltpu.make_async_copy(source, target, sems.at[slot]).start()
+
+
+def wait_slot(source, into_ref, sems, slot):
+    pltpu.make_async_copy(source, into_ref.at[slot], sems.at[slot]).wait()
+
+
+def mask_bias(packed, quarter, length):
+    q = lax.broadcasted_iota(jnp.int32, (length, length), 1)
+    k = lax.broadcasted_iota(jnp.int32, (length, length), 0)
     shift = quarter.bit_length() - 1
     same = (q >> shift) == (k >> shift)
-    return (k <= q) & (same | jnp.logical_not(packed))
+    return jnp.where((k <= q) & (same | jnp.logical_not(packed)), 0.0, -1e30)
+
+
+def head_lanes(value):
+    lane = lax.broadcasted_iota(jnp.int32, (1, 128), 1)
+    return [jnp.where(side, value, 0.0).astype(BF) for side in (lane < HEAD_DIM, lane >= HEAD_DIM)]
 
 
 def attend_kernel(where_ref, seg_ref, hid_ref, norm_ref, *rest, length, quarter, count):
     parts = rest[:count]
-    q_ref, k_ref, v_ref, prob_ref, att_ref, out_ref, weight_ref, sems = rest[count:]
+    q_ref, k_ref, v_ref, prob_ref, att_ref, out_ref, weight_ref, bias_ref, sems = rest[count:]
     tokens = hid_ref.shape[0]
-    for copy in fetch_half(where_ref, parts, weight_ref, sems):
+    copies = fetch_half(where_ref, parts, weight_ref, sems)
+    for row in range(tokens // length):
+        bias_ref[row] = mask_bias(packed_flag(where_ref, seg_ref, row, length), quarter, length)
+    for copy in copies:
         copy.wait()
     q_ref[...] = nt(norm_ref[...], weight_ref[0]).astype(BF)
     k_ref[...] = nt(norm_ref[...], weight_ref[1]).astype(BF)
     v_ref[...] = nt(norm_ref[...], weight_ref[2]).astype(BF)
     pairs = q_ref.shape[1] // 128
-    lane = lax.broadcasted_iota(jnp.int32, (1, 128), 1)
-    lefts = [(lane < HEAD_DIM).astype(BF), (lane >= HEAD_DIM).astype(BF)]
+    lefts = head_lanes(1.0)
+    scaled = head_lanes(SCALE)
     block = length // 2
 
     def step(index, carry):
         row = index // pairs
         pair = index % pairs
-        packed = packed_flag(where_ref, seg_ref, row, length)
         lanes = pl.ds(pl.multiple_of(pair * 128, 128), 128)
         for part in range(2):
             keys = (part + 1) * block
             here = pl.ds(pl.multiple_of(row * length + part * block, block), block)
             upto = pl.ds(pl.multiple_of(row * length, length), keys)
-            mask = allowed_mask(packed, quarter, part * block, block, keys)
+            bias = bias_ref[row, :keys, part * block : (part + 1) * block]
             queries = q_ref[here, lanes]
             key_rows = k_ref[upto, lanes]
             values = v_ref[upto, lanes]
             result = None
             for head in range(2):
-                scores = nt(queries * lefts[head], key_rows) * SCALE
-                scores = jnp.where(mask, scores, -1e30)
-                top = jnp.max(scores, -1, keepdims=True)
+                scores = nt(key_rows, queries * scaled[head]) + bias
+                top = jnp.max(scores, 0, keepdims=True)
                 grown = jnp.exp(scores - top)
-                probs = (grown / jnp.sum(grown, -1, keepdims=True)).astype(BF)
-                prob_ref[2 * index + head, part * block : (part + 1) * block, :keys] = probs
-                term = nn(probs, values * lefts[head])
+                probs = (grown * (1.0 / jnp.sum(grown, 0, keepdims=True))).astype(BF)
+                prob_ref[2 * index + head, :keys, part * block : (part + 1) * block] = probs
+                term = tn(probs, values * lefts[head])
                 result = term if result is None else result + term
             att_ref[here, lanes] = result.astype(BF)
         return carry
@@ -213,24 +224,25 @@
 def up_kernel(
     where_ref, hid_ref, gain_ref, bias_ref, own, near, far, far_other, cross, cross_other,
     own_t, near_t, far_t, cross_t,
-    norm_ref, act_ref, slope_ref, weight_ref, bup_ref, sems, bias_sems,
+    norm_ref, act_out, slope_out, weight_ref, bup_ref, act_ref, slope_ref, sems, bias_sems, out_sems,
 ):
     tokens, width = hid_ref.shape
-    copies = fetch_full(where_ref, (own, near, far, far_other, cross, cross_other), weight_ref, sems)
+    fetch_full(where_ref, (own, near, far, far_other, cross, cross_other), weight_ref, sems)
     last = pl.ds(far_t.shape[0] - EXTRA, EXTRA)
     packs = (own_t.at[0, last], near_t.at[0, last], far_t.at[last], cross_t.at[last])
-    copies += start_copies([(pack, bup_ref.at[slot]) for slot, pack in enumerate(packs)], bias_sems)
+    biases = start_copies([(pack, bup_ref.at[slot]) for slot, pack in enumerate(packs)], bias_sems)
 
     def normalize(at):
         xhat, _ = norm_parts(hid_ref[at])
         norm_ref[at] = (xhat * gain_ref[...] + bias_ref[...]).astype(BF)
 
     over_rows(tokens, normalize)
-    for copy in copies:
-        copy.wait()
+    for bias in biases:
+        bias.wait()
     block = 128
 
     def step(slot, carry):
+        wait_slot(own, weight_ref, sems, slot)
         bias = bup_ref[slot, :1].astype(F32)
         for first in range(0, tokens, block):
             at = slice(first, first + block)
@@ -238,26 +250,30 @@
             value, slope = gelu_pair(pre)
             act_ref[slot, at] = value.astype(BF)
             slope_ref[slot, at] = slope.astype(BF)
+        pltpu.make_async_copy(act_ref.at[slot], act_out.at[slot], out_sems.at[0, slot]).start()
+        pltpu.make_async_copy(slope_ref.at[slot], slope_out.at[slot], out_sems.at[1, slot]).start()
         return carry
 
-    lax.fori_loop(0, act_ref.shape[0], step, 0)
-
-
-def send_pieces(where_ref, stage_ref, slot, keep, send, sems, rows):
-    even = slot % 2 == 0
-    place = slot // 2
-
+    lax.fori_loop(0, 4, step, 0)
+    for slot in range(4):
+        pltpu.make_async_copy(act_ref.at[slot], act_out.at[slot], out_sems.at[0, slot]).wait()
+        pltpu.make_async_copy(slope_ref.at[slot], slope_out.at[slot], out_sems.at[1, slot]).wait()
+
+
+def send_pieces(where_ref, stage_ref, slot, keep, sends, sems, rows):
     for piece in range(PIECES):
+        source = stage_ref.at[piece * rows : (piece + 1) * rows]
         target = piece ^ where_ref[2]
-        source = stage_ref.at[piece * rows : (piece + 1) * rows]
-
-        @pl.when(even)
+
+        @pl.when(slot % 2 == 0)
         def _():
-            pltpu.make_async_copy(source, keep.at[place, target, :rows], sems.at[piece]).start()
-
-        @pl.when(jnp.logical_not(even))
-        def _():
-            pltpu.make_async_copy(source, send.at[place, target, :rows], sems.at[piece]).start()
+            pltpu.make_async_copy(source, keep.at[slot // 2, target], sems.at[piece]).start()
+
+        for index, send in enumerate(sends):
+
+            @pl.when(slot == 2 * index + 1)
+            def _():
+                pltpu.make_async_copy(source, send.at[target], sems.at[piece]).start()
 
 
 def wait_pieces(stage_ref, keep, sems, rows):
@@ -267,20 +283,27 @@
 
 
 def down_kernel(
-    where_ref, seg_ref, hid_ref, act_ref, bdown_ref, wout_ref, bout_ref, patch_ref, lgrad_ref, dgrad_ref,
+    where_ref, seg_ref, hid_ref, act_in, bdown_ref, wout_ref, bout_ref, patch_ref, lgrad_ref, dgrad_ref,
     own, near, far, far_other, cross, cross_other,
-    latent_ref, logdet_ref, stat_ref, direct_ref, grad_ref, gwout_ref, gvec_ref, keep_ref, send_ref,
-    weight_ref, branch_ref, stage_ref, sems, out_sems,
+    latent_ref, logdet_ref, stat_ref, direct_ref, grad_ref, gwout_ref, gvec_ref, keep_ref, send_near, send_far,
+    weight_ref, act_ref, total_ref, branch_ref, stage_ref, sems, act_sems, out_sems,
     *, length, quarter,
 ):
     tokens, width = hid_ref.shape
     channels = patch_ref.shape[0]
-    for copy in fetch_full(where_ref, (own, near, far, far_other, cross, cross_other), weight_ref, sems):
-        copy.wait()
-    total = nn(act_ref[0], weight_ref[0])
-    for slot in range(1, 4):
-        total = total + nn(act_ref[slot], weight_ref[slot])
-    top_low = (hid_ref[...] + total + bdown_ref[...]).astype(BF)
+    send_refs = (send_near, send_far)
+    start_copies([(act_in.at[slot], act_ref.at[slot]) for slot in range(4)], act_sems)
+    fetch_full(where_ref, (own, near, far, far_other, cross, cross_other), weight_ref, sems)
+    total_ref[...] = hid_ref[...] + bdown_ref[...]
+
+    def gather(slot, carry):
+        wait_slot(act_in.at[slot], act_ref, act_sems, slot)
+        wait_slot(own, weight_ref, sems, slot)
+        total_ref[...] += nn(act_ref[slot], weight_ref[slot])
+        return carry
+
+    lax.fori_loop(0, 4, gather, 0)
+    top_low = total_ref[...].astype(BF)
     head_out = nt(wout_ref[...], top_low) + bout_ref[...]
     token = lax.broadcasted_iota(jnp.int32, (1, tokens), 1)
     row_count = tokens // length
@@ -322,13 +345,14 @@
     gvec_ref[1:2, : 2 * channels] = row_of[:1]
     rows = width // PIECES
 
+
     def step(slot, carry):
         @pl.when(slot >= 2)
         def _():
             wait_pieces(stage_ref.at[slot % 2], keep_ref, out_sems.at[slot % 2], rows)
 
         stage_ref[slot % 2] = tn(act_ref[slot], branch_ref[...]).astype(BF)
-        send_pieces(where_ref, stage_ref.at[slot % 2], slot, keep_ref, send_ref, out_sems.at[slot % 2], rows)
+        send_pieces(where_ref, stage_ref.at[slot % 2], slot, keep_ref, send_refs, out_sems.at[slot % 2], rows)
         return carry
 
     lax.fori_loop(0, 4, step, 0)
@@ -336,25 +360,39 @@
         wait_pieces(stage_ref.at[slot], keep_ref, out_sems.at[slot], rows)
 
 
+def grad_pre_kernel(
+    where_ref, grad_ref, slope_in, own, near, far, far_other, cross, cross_other,
+    pre_out, sum_ref, weight_ref, slope_ref, branch_ref, pre_ref, sems, slope_sems, out_sems,
+):
+    start_copies([(slope_in.at[slot], slope_ref.at[slot]) for slot in range(4)], slope_sems)
+    fetch_full(where_ref, (own, near, far, far_other, cross, cross_other), weight_ref, sems)
+    branch_ref[...] = grad_ref[...].astype(BF)
+
+    def step(slot, carry):
+        wait_slot(slope_in.at[slot], slope_ref, slope_sems, slot)
+        wait_slot(own, weight_ref, sems, slot)
+        grad_pre = (nt(branch_ref[...], weight_ref[slot]) * slope_ref[slot].astype(F32)).astype(BF)
+        pre_ref[slot] = grad_pre
+        pltpu.make_async_copy(pre_ref.at[slot], pre_out.at[slot], out_sems.at[slot]).start()
+        sum_ref[pl.ds(slot, 1), :] = column_sum(grad_pre.astype(F32))
+        return carry
+
+    lax.fori_loop(0, 4, step, 0)
+    for slot in range(4):
+        pltpu.make_async_copy(pre_ref.at[slot], pre_out.at[slot], out_sems.at[slot]).wait()
+
+
 def up_back_kernel(
-    where_ref, grad_ref, slope_ref, norm_ref, hid_ref, gain_ref,
-    own_d, near_d, far_d, far_other_d, cross_d, cross_other_d,
-    own_u, near_u, far_u, far_other_u, cross_u, cross_other_u,
-    gout_ref, mix_ref, gvec_ref, keep_ref, send_ref,
-    down_ref, up_ref, branch_ref, total_ref, pre_ref, stage_ref, sems, out_sems,
+    where_ref, grad_ref, pre_in, norm_ref, hid_ref, gain_ref, own, near, far, far_other, cross, cross_other,
+    gout_ref, mix_ref, gvec_ref, keep_ref, send_near, send_far,
+    weight_ref, pre_ref, total_ref, stage_ref, sems, pre_sems, out_sems,
 ):
     tokens, width = grad_ref.shape
-    copies = fetch_full(
-        where_ref, (own_d, near_d, far_d, far_other_d, cross_d, cross_other_d), down_ref, sems.at[0]
-    )
-    copies += fetch_full(
-        where_ref, (own_u, near_u, far_u, far_other_u, cross_u, cross_other_u), up_ref, sems.at[1]
-    )
-    branch_ref[...] = grad_ref[...].astype(BF)
+    send_refs = (send_near, send_far)
+    start_copies([(pre_in.at[slot], pre_ref.at[slot]) for slot in range(4)], pre_sems)
     total_ref[...] = jnp.zeros(total_ref.shape, F32)
+    fetch_full(where_ref, (own, near, far, far_other, cross, cross_other), weight_ref, sems)
     gvec_ref[...] = jnp.zeros(gvec_ref.shape, F32)
-    for copy in copies:
-        copy.wait()
     rows = width // PIECES
 
     def step(slot, carry):
@@ -362,12 +400,11 @@
         def _():
             wait_pieces(stage_ref.at[slot % 2], keep_ref, out_sems.at[slot % 2], rows)
 
-        grad_pre = (nt(branch_ref[...], down_ref[slot]) * slope_ref[slot].astype(F32)).astype(BF)
-        pre_ref[...] = grad_pre
-        gvec_ref[pl.ds(slot, 1), :] = column_sum(grad_pre.astype(F32))
-        stage_ref[slot % 2] = tn(norm_ref[...], pre_ref[...]).astype(BF)
-        send_pieces(where_ref, stage_ref.at[slot % 2], slot, keep_ref, send_ref, out_sems.at[slot % 2], rows)
-        total_ref[...] += nt(pre_ref[...], up_ref[slot])
+        wait_slot(pre_in.at[slot], pre_ref, pre_sems, slot)
+        wait_slot(own, weight_ref, sems, slot)
+        stage_ref[slot % 2] = tn(norm_ref[...], pre_ref[slot]).astype(BF)
+        send_pieces(where_ref, stage_ref.at[slot % 2], slot, keep_ref, send_refs, out_sems.at[slot % 2], rows)
+        total_ref[...] += nt(pre_ref[slot], weight_ref[slot])
         return carry
 
     lax.fori_loop(0, 4, step, 0)
@@ -378,8 +415,8 @@
         value = grad_ref[at] + norm_back(grad, gain_ref[...], xhat, rstd)
         gout_ref[at] = value
         mix_ref[at] = value.astype(BF)
-        gvec_ref[4:5, :] += column_sum(grad * xhat)
-        gvec_ref[5:6, :] += column_sum(grad)
+        gvec_ref[0:1, :] += column_sum(grad * xhat)
+        gvec_ref[1:2, :] += column_sum(grad)
 
     over_rows(tokens, finish)
     for slot in range(2):
@@ -401,8 +438,8 @@
         copy.wait()
     gatt_ref[...] = nt(mix_ref[...], weight_ref[3]).astype(BF)
     pairs = q_ref.shape[1] // 128
-    lane = lax.broadcasted_iota(jnp.int32, (1, 128), 1)
-    lefts = [(lane < HEAD_DIM).astype(BF), (lane >= HEAD_DIM).astype(BF)]
+    lefts = head_lanes(1.0)
+    scaled = head_lanes(SCALE)
     block = length // 2
     unit = weight_ref.shape[1] // 2
     rows = unit // PIECES
@@ -436,16 +473,16 @@
             grad_out = gatt_ref[here, lanes]
             result = None
             for head in range(2):
-                probs = prob_ref[2 * index + head, part * block : (part + 1) * block, :keys]
+                probs = prob_ref[2 * index + head, :keys, part * block : (part + 1) * block]
                 wide = probs.astype(F32)
                 grad_mine = grad_out * lefts[head]
-                grad_probs = nt(grad_mine, values)
-                inner = jnp.sum(wide * grad_probs, -1, keepdims=True)
-                grad_scores = (wide * (grad_probs - inner) * SCALE).astype(BF)
-                term = nn(grad_scores, key_rows * lefts[head])
+                grad_probs = nt(values, grad_mine)
+                inner = jnp.sum(wide * grad_probs, 0, keepdims=True)
+                grad_scores = (wide * (grad_probs - inner)).astype(BF)
+                term = tn(grad_scores, key_rows * scaled[head])
                 result = term if result is None else result + term
-                term_k = tn(grad_scores, queries * lefts[head])
-                term_v = tn(probs, grad_mine)
+                term_k = nn(grad_scores, queries * scaled[head])
+                term_v = nn(probs, grad_mine)
                 grads_k[part] = term_k if grads_k[part] is None else grads_k[part] + term_k
                 grads_v[part] = term_v if grads_v[part] is None else grads_v[part] + term_v
             dq_ref[here, lanes] = result.astype(BF)
@@ -474,7 +511,7 @@
 
 def embed_back_kernel(
     where_ref, seg_ref, label_ref, grad_ref, total_ref, hid_ref, gain_ref, patch_ref, direct_ref, win_ref,
-    gwout_ref, gdown_ref, gup_ref, gq_near, gq_far,
+    gwout_ref, gdown_ref, gup_ref, gpre_ref, gq_near, gq_far,
     pgrad_ref, slot_ref, keep_ref, send_ref,
     value_ref, embed_ref, acc_ref, small_ref, sems,
     *, length, quarter,
@@ -505,10 +542,10 @@
         acc_ref[0:1, :] += column_sum(embed.astype(F32))
 
     over_rows(tokens, finish)
-    acc_ref[3:5, :] = gup_ref[4:6, :]
+    acc_ref[3:5, :] = gup_ref[0:2, :]
     acc_ref[5:7, :] = gdown_ref[0:2, :]
     for slot in range(4):
-        acc_ref[pl.ds(7 + (slot ^ where_ref[3]), 1), :] = gup_ref[slot : slot + 1, :]
+        acc_ref[pl.ds(7 + (slot ^ where_ref[3]), 1), :] = gpre_ref[slot : slot + 1, :]
     small_ref[:channels] = nn(patch_ref[...].astype(BF), embed_ref[...]).astype(BF)
     small_ref[channels : 3 * channels] = gwout_ref[...].astype(BF)
     first = 3 * channels
@@ -575,6 +612,14 @@
         ).wait()
 
 
+def add_kernel(*refs):
+    *sources, out_ref = refs
+    total = sources[0][...].astype(F32)
+    for ref in sources[1:]:
+        total = total + ref[...].astype(F32)
+    out_ref[...] = total.astype(BF)
+
+
 def piece_list(low, high):
     found = []
     for bit, ref in ((0, low), (1, high)):
@@ -638,55 +683,77 @@
             total = total + other.astype(F32)
         return total.astype(BF)
 
+    def tie(*values):
+        return lax.optimization_barrier(values)
+
     def ordered(value, token):
-        value, token = lax.optimization_barrier((value, token))
-        return value
+        return tie(value, token)[0]
+
+    class View:
+        def __init__(self, array, start=(0, 0, 0), size=None):
+            self.array, self.start = array, tuple(start)
+            self.size = tuple(size or array.shape[:3])
+
+        def narrow(self, axis, index):
+            start, size = list(self.start), list(self.size)
+            if size[axis] > 1:
+                start[axis] += index
+            size[axis] = 1
+            return View(self.array, start, size)
+
+        def value(self):
+            stop = [a + b for a, b in zip(self.start, self.size)] + list(self.array.shape[3:])
+            return lax.slice(self.array, self.start + (0, 0), stop)
+
+    def add_views(views):
+        return add_low([view.value() for view in views])
 
     class Chain:
-        axes = {"x": (1, 1), "z": (2, 2)}
+        axes = {"y": 0, "x": 1, "z": 2}
 
         def __init__(self, order):
             self.order = order
-            self.near, self.far, self.both = [], [], []
+            self.groups = []
             self.left = list(order) + ["w"] + [a for a in reversed(order) if a != "y"]
 
-        def add(self, group, *arrays):
-            for array in arrays:
-                group.append(array.reshape((-1, 2, 2) + array.shape[-2:]))
-
-        def core(self, group, send, token):
-            send = ordered(send, token)
-            self.add(group, swap_heads(send, 1))
-            return send
-
-        def side(self, arrays, axis, index):
-            return [lax.slice_in_dim(t, index, index + 1, axis=axis) for t in arrays]
-
-        def step(self, token):
+        def view(self, array):
+            return View(array.reshape((-1, 2, 2) + array.shape[-2:]))
+
+        def prepare(self, add=add_views):
+            kind = self.left[0]
+            if kind == "y":
+                return [add([view.narrow(0, 1) for view in self.groups[-1]])]
+            if "w" in self.left[1:]:
+                axis = self.axes[kind]
+                return [add([view.narrow(axis, 1) for view in group]) for group in self.groups]
+            return [add(self.groups[0])] if kind == "w" else [self.total]
+
+        def launch(self, sends):
+            self.sends = sends
+            kind = self.left[0]
+            if kind == "y":
+                self.got = [swap_heads(send, 2) for send in sends]
+            else:
+                self.got = [swap_rows(send, 1 << "xzw".index(kind)) for send in sends]
+
+        def deliver(self, got):
             kind = self.left.pop(0)
-            reducing = "w" in self.left
-            if kind == "y":
-                send = ordered(add_low(self.side(self.both, 0, 1) + self.far), token)
-                self.both = self.side(self.both, 0, 0) + self.near + [swap_heads(send, 2)]
-            elif kind == "w":
-                total = add_low(self.both)
-                for level in range(2, levels):
-                    send = ordered(total, token)
-                    total = add_low([send, swap_rows(send, 1 << level)])
-                self.total = total
-            elif reducing:
-                axis, bit = self.axes[kind]
-                send = ordered(add_low(self.side(self.both, axis, 1)), token)
-                self.both = self.side(self.both, axis, 0) + [swap_rows(send, bit)]
+            if kind == "w":
+                self.total = add_low([self.sends[0], got[0]])
+                for level in range(3, levels):
+                    self.total = add_low([self.total, swap_rows(self.total, 1 << level)])
+            elif "w" in self.left:
+                axis = self.axes[kind]
+                if kind == "y":
+                    self.groups = self.groups[:1]
+                self.groups = [
+                    [view.narrow(axis, 0) for view in group] + [View(more)]
+                    for group, more in zip(self.groups, got)
+                ]
+            elif self.left:
+                self.total = jnp.concatenate([self.sends[0], got[0]], self.axes[kind])
             else:
-                axis, bit = self.axes[kind]
-                send = ordered(self.total, token)
-                got = swap_rows(send, bit)
-                if self.left:
-                    self.total = jnp.concatenate([send, got], axis)
-                else:
-                    self.low, self.high = send[0], got[0]
-            return send
+                self.low, self.high = self.sends[0][0], got[0][0]
 
     def program(
         patches, segments, labels, w_in, b_in, pos_table, cls_table, ln1_gain, ln1_bias,
@@ -713,16 +780,16 @@
         def shape(*dims, dtype=F32):
             return jax.ShapeDtypeStruct(dims, dtype)
 
-        def call(kernel, operands, specs, outs, out_specs, scratch=(), work=1.0, **options):
+        def call(kernel, operands, specs, outs, out_specs, scratch=(), room=60, **options):
             return pl.pallas_call(
                 functools.partial(kernel, **options) if options else kernel,
                 in_specs=specs,
                 out_specs=out_specs,
                 out_shape=outs,
                 scratch_shapes=list(scratch),
-                compiler_params=pltpu.CompilerParams(vmem_limit_bytes=60 << 20),
+                compiler_params=pltpu.CompilerParams(vmem_limit_bytes=room << 20),
                 cost_estimate=pl.CostEstimate(
-                    flops=int(work * square), transcendentals=0, bytes_accessed=8 << 20
+                    flops=1, transcendentals=0, bytes_accessed=1
                 ),
             )(*operands)
 
@@ -744,27 +811,28 @@
         far_t = swap_heads(half_t, 2)
         near_t = swap_heads(ordered(pack_t, half_t), 1)
         half_u = lax.dynamic_slice_in_dim(own_u, row_bit * half_rows, half_rows, 0)
+        half_u, half_t = tie(half_u, half_t)
+        far_u = swap_heads(half_u, 2)
         half_d = lax.dynamic_slice_in_dim(own_d, row_bit * half_rows, half_rows, 0)
-        near_u = swap_heads(ordered(own_u, half_t), 1)
-        near_d = swap_heads(ordered(own_d, half_t), 1)
+        half_d, half_u = tie(half_d, half_u)
+        far_d = swap_heads(half_d, 2)
         cls_rows = cls_table[labels.reshape(-1)].astype(F32)
         patches_t = patches.T
         hidden0, normed1 = call(
             embed_kernel,
             (
-                where, segments, ordered(patches_t, half_t), w_in, b_in[None], pos_table, cls_rows,
+                where, segments, ordered(patches_t, half_d), w_in, b_in[None], pos_table, cls_rows,
                 ln1_gain, ln1_bias,
             ),
             [SMEM, SMEM] + [VMEM] * 7,
             (full, low),
             (VMEM, VMEM),
-            work=0.3,
         )
-        far_t = ordered(far_t, normed1)
+        normed1, far_t = tie(normed1, far_t)
         far_other_t = swap_rows(far_t, 1)
-        half_u = ordered(half_u, far_t)
-        far_u = swap_heads(half_u, 2)
         cross_t = swap_heads(far_t, 1)
+        near_u = swap_heads(ordered(own_u, far_t), 1)
+        near_d = swap_heads(ordered(own_d, far_t), 1)
 
         def attend(hidden, normed, parts):
             return call(
@@ -776,138 +844,192 @@
                     shape(row_count * heads // 2, length, length, dtype=BF), half_low, full,
                 ),
                 (VMEM,) * 6,
-                [pltpu.VMEM((4, width // 2, width), BF), dma((8,))],
-                work=5.0,
+                [
+                    pltpu.VMEM((4, width // 2, width), BF),
+                    pltpu.VMEM((row_count, length, length), F32),
+                    dma((8,)),
+                ],
                 length=length,
                 quarter=quarter,
                 count=len(parts),
             )
 
         parts_near = (pack_t, near_t)
-        *saved_near, mixed = attend(hidden0, ordered(normed1, half_u), parts_near)
-        far_other_t = ordered(far_other_t, mixed)
+        *saved_near, mixed = attend(hidden0, normed1, parts_near)
+        mixed, far_other_t, far_u = tie(mixed, far_other_t, far_u)
         cross_other_t = swap_heads(far_other_t, 1)
-        far_u = ordered(far_u, far_other_t)
         far_other_u = swap_rows(far_u, 1)
-        half_d = ordered(half_d, far_u)
-        far_d = swap_heads(half_d, 2)
         cross_u = swap_heads(far_u, 1)
         parts_far = (far_t, far_other_t, cross_t, cross_other_t)
-        *saved_far, hidden1 = attend(mixed, ordered(normed1, half_d), parts_far)
-        far_other_u = ordered(far_other_u, hidden1)
+        *saved_far, hidden1 = attend(mixed, normed1, parts_far)
+        hidden1, far_other_u, far_d = tie(hidden1, far_other_u, far_d)
         cross_other_u = swap_heads(far_other_u, 1)
-        far_d = ordered(far_d, hidden1)
         far_other_d = swap_rows(far_d, 1)
         cross_d = swap_heads(far_d, 1)
         parts_u = (own_u, near_u, far_u, far_other_u, cross_u, cross_other_u)
         four = shape(heads_size, tokens, width, dtype=BF)
         normed2, activated, slope = call(
             up_kernel,
-            (where, ordered(hidden1, far_d), ln2_gain, ln2_bias)
+            (where, hidden1, ln2_gain, ln2_bias)
             + parts_u
             + (pack_t, near_t, far_t, cross_t),
             [SMEM] + [VMEM] * 3 + [HBM] * 10,
             (low, four, four),
-            (VMEM,) * 3,
+            (VMEM, HBM, HBM),
             [
                 pltpu.VMEM((heads_size, width, width), BF),
                 pltpu.VMEM((heads_size, EXTRA, width), BF),
-                dma((6,)),
+                pltpu.VMEM((heads_size, tokens, width), BF),
+                pltpu.VMEM((heads_size, tokens, width), BF),
                 dma((4,)),
+                dma((4,)),
+                dma((2, 4)),
             ],
-            work=6.0,
         )
-        far_other_d = ordered(far_other_d, normed2)
+        normed2, far_other_d = tie(normed2, far_other_d)
         cross_other_d = swap_heads(far_other_d, 1)
         parts_d = (own_d, near_d, far_d, far_other_d, cross_d, cross_other_d)
         pieces = shape(2, PIECES, rows, width, dtype=BF)
+        one = shape(PIECES, rows, width, dtype=BF)
         stage = pltpu.VMEM((2, width, width), BF)
         out_sems = dma((2, PIECES))
-        latents, logdet, stats, direct, grad_hidden2, grad_w_out, gdown, keep_d, send_d = call(
+        latents, logdet, stats, direct, grad_hidden2, grad_w_out, gdown, keep_d, *sends_d = call(
             down_kernel,
             (
                 where, segments, hidden1, activated, b_down, w_out.T, b_out[:, None], patches_t, latent_grad.T,
                 logdet_grad[None],
             )
             + parts_d,
-            [SMEM, SMEM] + [VMEM] * 8 + [HBM] * 6,
+            [SMEM, SMEM, VMEM, HBM] + [VMEM] * 6 + [HBM] * 6,
             (
                 shape(channels, tokens), shape(1, tokens), shape(8, 128), shape(channels, tokens),
-                full, shape(2 * channels, width), shape(8, width), pieces, pieces,
+                full, shape(2 * channels, width), shape(8, width), pieces, one, one,
             ),
-            (VMEM,) * 7 + (HBM, HBM),
-            [pltpu.VMEM((heads_size, width, width), BF), pltpu.VMEM((tokens, width), BF), stage, dma((6,)), out_sems],
-            work=8.0,
+            (VMEM,) * 7 + (HBM,) * 3,
+            [
+                pltpu.VMEM((heads_size, width, width), BF),
+                pltpu.VMEM((heads_size, tokens, width), BF),
+                pltpu.VMEM((tokens, width), F32),
+                pltpu.VMEM((tokens, width), BF),
+                stage,
+                dma((4,)),
+                dma((4,)),
+                out_sems,
+            ],
             length=length,
             quarter=quarter,
         )
         chains = [Chain(order) for order in CHAIN_ORDERS]
         down, up, mix, last = chains
-        down.add(down.both, keep_d)
-        token = down.core(down.both, send_d, grad_hidden2)
-        grad_hidden1, grad_mix, gup, keep_u, send_u = call(
-            up_back_kernel,
-            (where, ordered(grad_hidden2, token), slope, normed2, hidden1, ln2_gain) + parts_d + parts_u,
-            [SMEM] + [VMEM] * 5 + [HBM] * 12,
-            (full, low, shape(8, width), pieces, pieces),
-            (VMEM, VMEM, VMEM, HBM, HBM),
+
+        def add_pieces(views):
+            size = views[0].size
+            block = (views[0].array.shape[3] // 2, views[0].array.shape[4])
+
+            def spec(start):
+                def at(i):
+                    return tuple(a // b for a, b in zip(start, size)) + (i, 0)
+
+                return pl.BlockSpec(size + block, at)
+
+            return pl.pallas_call(
+                add_kernel,
+                grid=(2,),
+                in_specs=[spec(view.start) for view in views],
+                out_specs=spec((0, 0, 0)),
+                out_shape=shape(*size, 2 * block[0], block[1], dtype=BF),
+                cost_estimate=pl.CostEstimate(flops=1, transcendentals=0, bytes_accessed=1),
+            )(*(view.array for view in views))
+
+        def halves(chain, keep, gots):
+            keep = chain.view(keep)
+            return [[keep.narrow(0, index), chain.view(got)] for index, got in enumerate(gots)]
+
+        grad_hidden2, *sends_d = tie(grad_hidden2, *sends_d)
+        got_d = [swap_heads(send, 1) for send in sends_d]
+        pre_grads, gpre = call(
+            grad_pre_kernel,
+            (where, grad_hidden2, slope) + parts_d,
+            [SMEM, VMEM, HBM] + [HBM] * 6,
+            (four, shape(8, width)),
+            (HBM, VMEM),
             [
                 pltpu.VMEM((heads_size, width, width), BF),
+                pltpu.VMEM((heads_size, tokens, width), BF),
+                pltpu.VMEM((tokens, width), BF),
+                pltpu.VMEM((heads_size, tokens, width), BF),
+                dma((4,)),
+                dma((4,)),
+                dma((4,)),
+            ],
+        )
+        pre_grads, *got_d = tie(pre_grads, *got_d)
+        down.groups = halves(down, keep_d, got_d)
+        pre_grads, *sends = tie(pre_grads, *down.prepare(add_pieces))
+        down.launch(sends)
+        grad_hidden1, grad_mix, gup, keep_u, *sends_u = call(
+            up_back_kernel,
+            (where, grad_hidden2, pre_grads, normed2, hidden1, ln2_gain) + parts_u,
+            [SMEM, VMEM, HBM] + [VMEM] * 3 + [HBM] * 6,
+            (full, low, shape(8, width), pieces, one, one),
+            (VMEM, VMEM, VMEM, HBM, HBM, HBM),
+            [
                 pltpu.VMEM((heads_size, width, width), BF),
-                pltpu.VMEM((tokens, width), BF),
+                pltpu.VMEM((heads_size, tokens, width), BF),
                 pltpu.VMEM((tokens, width), F32),
-                pltpu.VMEM((tokens, width), BF),
                 stage,
-                dma((2, 6)),
+                dma((4,)),
+                dma((4,)),
                 out_sems,
             ],
-            work=12.0,
         )
-        up.add(up.both, keep_u)
-        token = up.core(up.both, send_u, grad_mix)
-
-        def advance(order, token):
-            for index in order:
-                token = chains[index].step(token)
-            return token
-
-        def attend_back(saved, parts, before, token):
+        grad_mix, *sends_u = tie(grad_mix, *sends_u)
+        got_u = [swap_heads(send, 1) for send in sends_u]
+
+        def attend_back(saved, parts, before):
             chained = () if before is None else (before,)
             mixed_pieces = shape(PIECES, 3 * unit, width, dtype=BF)
             return call(
                 attend_back_kernel,
-                (where, ordered(grad_mix, token)) + tuple(saved) + (normed1,) + chained + parts,
+                (where, grad_mix) + tuple(saved) + (normed1,) + chained + parts,
                 [SMEM] + [VMEM] * (7 + len(chained)) + [HBM] * len(parts),
                 (full, shape(width // 2, width, dtype=BF), mixed_pieces, mixed_pieces),
                 (VMEM, VMEM, HBM, HBM),
                 [pltpu.VMEM((4, width // 2, width), BF)]
                 + [pltpu.VMEM((tokens, width // 2), BF)] * 4
                 + [pltpu.VMEM((3, width // 2, width), BF), dma((8,)), dma((3, 2 * PIECES))],
-                work=8.0,
                 length=length,
                 quarter=quarter,
                 count=len(parts),
                 chained=before is not None,
             )
 
-        token = advance(BEFORE_FAR, token)
-        total_far, gq_far, keep_far, send_far = attend_back(saved_far, parts_far, None, token)
-        mix.add(mix.far, keep_far)
-        token = mix.core(mix.far, send_far, total_far)
-        token = advance(BEFORE_NEAR, token)
-        total_near, gq_near, keep_near, send_near = attend_back(saved_near, parts_near, total_far, token)
-        mix.add(mix.near, keep_near)
-        token = mix.core(mix.near, send_near, total_near)
-        token = advance(BEFORE_EMBED, token)
+        total_far, gq_far, keep_far, send_far = attend_back(saved_far, parts_far, None)
+        total_far, send_far, *got_d = tie(total_far, send_far, *down.got)
+        total_far, *got_u = tie(total_far, *got_u)
+        got_far = swap_heads(send_far, 1)
+        down.deliver(got_d)
+        up.groups = halves(up, keep_u, got_u)
+        total_far, *sends = tie(total_far, *down.prepare(add_pieces), *up.prepare(add_pieces))
+        down.launch(sends[:1])
+        up.launch(sends[1:])
+        total_near, gq_near, keep_near, send_near = attend_back(saved_near, parts_near, total_far)
+        total_near, send_near, got_far, *got_d = tie(total_near, send_near, got_far, *down.got)
+        got_near = swap_heads(send_near, 1)
+        mix.groups = [[], [mix.view(keep_far), mix.view(got_far)]]
+        down.deliver(got_d)
+        grad_hidden1, *sends = tie(grad_hidden1, *down.prepare(add_pieces), *mix.prepare(add_pieces))
+        down.launch(sends[:1])
+        mix.launch(sends[1:])
         groups = 4 * PIECES
         last_pieces = shape(2, PIECES, unit + GROUP, width, dtype=BF)
         patches_grad, slot_rows, keep_q, send_q = call(
             embed_back_kernel,
             (
-                where, segments, labels, ordered(grad_hidden1, token), total_near, hidden0, ln1_gain, patches_t,
-                direct, w_in, grad_w_out, gdown, gup, gq_near, gq_far,
+                where, segments, labels, grad_hidden1, total_near, hidden0, ln1_gain, patches_t,
+                direct, w_in, grad_w_out, gdown, gup, gpre, gq_near, gq_far,
             ),
-            [SMEM, SMEM, SMEM] + [VMEM] * 12,
+            [SMEM, SMEM, SMEM] + [VMEM] * 13,
             (shape(channels, tokens), shape(row_count * slot_count, width + 128), last_pieces, last_pieces),
             (VMEM, VMEM, HBM, HBM),
             [
@@ -917,25 +1039,59 @@
                 pltpu.VMEM((groups * GROUP, width), BF),
                 dma((2, groups)),
             ],
-            work=3.0,
             length=length,
             quarter=quarter,
         )
-        last.add(last.both, keep_q)
-        token = last.core(last.both, send_q, patches_grad)
+        patches_grad, send_q, *got_u = tie(patches_grad, send_q, *up.got)
+        patches_grad, got_near, *got_d = tie(patches_grad, got_near, *down.got)
+        last.groups = [[last.view(keep_q), last.view(swap_heads(send_q, 1))]]
+        mix.groups[0] = [mix.view(keep_near), mix.view(got_near)]
+        down.got, up.got = got_d, got_u
         gathered = slot_rows.astype(BF)
-        steps = list(TAIL)
-        gathers = [("r", 1 << level) for level in reversed(range(levels))] + [("h", 2), ("h", 1)]
-        while steps or gathers:
-            if steps:
-                token = advance(steps[:1], token)
-                steps = steps[1:]
-            if gathers:
-                kind, bit = gathers.pop(0)
-                gathered = ordered(gathered, token)
-                token = gathered
-                swap = swap_rows if kind == "r" else swap_heads
-                gathered = jnp.concatenate([gathered, swap(gathered, bit)], 0)
+        gathers = [("rows", 1 << level) for level in reversed(range(levels))]
+        gathers += [("heads", 2), ("heads", 1)]
+        share = (len(gathers) - 1) // 4
+        token = got_d[0]
+        pending = {0, 1, 2}
+        heads_left = [2, 1]
+        got = None
+        small = None
+        for index in TAIL:
+            if index == 4:
+                more = gathers[:share] if len(gathers) > 2 + share else gathers[:1]
+                for axis, bit in more:
+                    gathers.pop(0)
+                    if got is not None:
+                        gathered = jnp.concatenate([gathered, ordered(got, token)], 0)
+                    token = gathered = ordered(gathered, token)
+                    got = (swap_rows if axis == "rows" else swap_heads)(gathered, bit)
+                continue
+            if index == 5:
+                if small is None:
+                    last.deliver([ordered(more, token) for more in last.got])
+                    axis = Chain.axes[[a for a in last.order if a != "y"][0]] - 1
+                    small = jnp.concatenate([last.low[:, :, unit:], last.high[:, :, unit:]], axis)
+                    small = small.reshape(1, PIECES, GROUP, width)
+                token = small = ordered(small, token)
+                small_got = swap_heads(small, heads_left.pop(0))
+                small = jnp.concatenate([small, small_got], 0)
+                continue
+            chain = chains[index]
+            if index in pending:
+                chain.deliver([ordered(one, token) for one in chain.got])
+            pending.add(index)
+            sends = []
+            for send in chain.prepare():
+                token = ordered(send, token)
+                sends.append(token)
+            chain.launch(sends)
+        gathered = jnp.concatenate([gathered, got], 0)
+        for axis, bit in gathers:
+            swap = swap_rows if axis == "rows" else swap_heads
+            gathered = jnp.concatenate([gathered, swap(gathered, bit)], 0)
+        for chain in chains[:3]:
+            chain.deliver(chain.got)
+        gathered = gathered.reshape(-1, width + 128)
         digits = gathered[:, width : width + 2].astype(jnp.int32)
         slot_label = digits[:, 0] * 32 + digits[:, 1]
         label_onehot = (
@@ -949,11 +1105,6 @@
             )
 
         sum_down, sum_up = place(down), place(up)
-        axis = Chain.axes[[a for a in last.order if a != "y"][0]][0] - 1
-        small = jnp.concatenate([last.low[:, :, unit:], last.high[:, :, unit:]], axis)
-        small = small.reshape(1, PIECES, GROUP, width)
-        small = jnp.concatenate([small, swap_heads(small, 2)], 0)
-        small = jnp.concatenate([small, swap_heads(small, 1)], 0)
         units = shape(part, width)
         line = shape(1, width)
         sum_k, sum_v, sum_o, sum_q, sum_w_in, sum_w_out, sum_pos, *lines = call(

time: 298 us -> 276 us (0.926)
  waiting for transfers between devices: 93.2 us -> 58.9 us
  Pallas kernels: 121 us -> 135 us
  other arithmetic: 24.6 us -> 17.6 us
  starting transfers between devices: 45.4 us -> 48.9 us
    ppermute x26 -> x28, waiting for transfers between devices: 74 us -> 45.6 us  [swap_rows(): return lax.ppermute(array, 'rows', [(i, i ^ bit) for i in range(rows_size)])]
    pallas_call x0 -> x6, Pallas kernels: none -> 13.2 us  [add_pieces(): pl.pallas_call(add_kernel, grid=(2,), in_specs=[spec(view.start) for view...]
    convert_element_type x20 -> x15, other arithmetic: 16.9 us -> 9 us  [add_low(): return total.astype(BF)]
    ppermute x25 -> x27, waiting for transfers between devices: 19.3 us -> 13.3 us  [swap_heads(): lax.ppermute(array, 'heads', [(i, i ^ bit) for i in range(heads_size)])]
    unnamed x57 -> x65, local copies, waits for them, and re-layouts: 2.86 us -> 6.24 us
    ppermute x26 -> x28, starting transfers between devices: 30.6 us -> 33.6 us  [swap_rows(): return lax.ppermute(array, 'rows', [(i, i ^ bit) for i in range(rows_size)])]
    ppermute x25 -> x27, starting transfers between devices: 14.8 us -> 15.3 us  [swap_heads(): lax.ppermute(array, 'heads', [(i, i ^ bit) for i in range(heads_size)])]
    pallas_call x12 -> x13, Pallas kernels: 121 us -> 121 us  [call(): pl.pallas_call(functools.partial(kernel, **options) if options else kerne...]
  transfers between devices with their start and end apart: 51 -> 55, of which waited for: 23 -> 19; matrix products, arithmetic and copies ran while one was open for 9% -> 8% of each run, Pallas kernels for 32% -> 42%
where the time goes in v3:
time: 276 us; the launch traced here: 275 us
  Pallas kernels  135 us (49%)
  waiting for transfers between devices  58.9 us (21%)
  starting transfers between devices  48.9 us (18%)
  other arithmetic  17.6 us (6%)
  local copies, waits for them, and re-layouts  11.6 us (4%)
    pallas_call x13, Pallas kernels, call(): pl.pallas_call(functools.partial(kernel, **options) if options else kerne...  121 us
    ppermute x28, waiting for transfers between devices, swap_rows(): return lax.ppermute(array, 'rows', [(i, i ^ bit) for i in range(rows_size)])  45.6 us
    ppermute x28, starting transfers between devices, swap_rows(): return lax.ppermute(array, 'rows', [(i, i ^ bit) for i in range(rows_size)])  33.6 us
    ppermute x27, starting transfers between devices, swap_heads(): lax.ppermute(array, 'heads', [(i, i ^ bit) for i in range(heads_size)])  15.3 us
    ppermute x27, waiting for transfers between devices, swap_heads(): lax.ppermute(array, 'heads', [(i, i ^ bit) for i in range(heads_size)])  13.3 us
    pallas_call x6, Pallas kernels, add_pieces(): pl.pallas_call(add_kernel, grid=(2,), in_specs=[spec(view.start) for view...  13.2 us
    convert_element_type x15, other arithmetic, add_low(): return total.astype(BF)  9 us
    unnamed x65, local copies, waits for them, and re-layouts  6.24 us
  transfers between devices with their start and end apart: 55, of which 19 were waited for; matrix products, arithmetic and copies ran while one was open for 8% of the time, Pallas kernels for 42%

profile of v3, /device:TPU:0, one launch (start us, length us, event | category | flops | bytes accessed | tf_op | source)
XLA Modules:
  0.0 275.1 jit_solution(17933054614986268949)
XLA Ops:
  0.7 1.4 fusion.6
  2.3 1.2 fusion.3
  3.9 2.5 collective-permute-start
  8.3 2.1 dynamic-slice_bitcast_fusion
  11.1 3.0 %shard_map.398 = (f32[512,768]{1,0:T(8,128)}, bf16[512,768]{1,0:T(8,128)(2,1)}) custom-call(s32[4]{0:T(128)} %pad_add_fusion.where_ref, s32[2048]{0:T(1024)} %seg_ref.9, f32[48,512]{1,0:T(8,128)} %bitcast.180, bf16[48,768]{1,0:T(8,128)(2,1)} %win_ref.1, f32[1,768]{1,0:T(1,128)} %broadcast_in_dim.29.b_ref, bf16[256,768]{1,0:T(8,128)(2,1)} %pos_ref.1, ...), custom_call_target="tpu_custom_call" | custom-call | flops 1 | bytes 1 | tf_op jit(solution)/shard_map/pallas_call | solution.py:784
  14.1 7.1 %collective-permute-done.rest_0_.far_t = bf16[400,768]{1,0:T(8,128)(2,1)S(1)} collective-permute-done((bf16[400,768]{1,0:T(8,128)(2,1)}, bf16[400,768]{1,0:T(8,128)(2,1)S(1)}, u32[]{:S(2)}, u32[]{:S(2)}) %collective-permute-start) | collective-permute-done | bytes 614432 | tf_op jit(solution)/shard_map/ppermute | solution.py:675
  21.2 1.7 collective-permute-start.2
  22.9 1.5 collective-permute-start.3
  24.4 11.5 %shard_map.399 = (bf16[512,384]{1,0:T(8,128)(2,1)}, bf16[512,384]{1,0:T(8,128)(2,1)}, bf16[512,384]{1,0:T(8,128)(2,1)}, bf16[12,256,256]{2,1,0:T(8,128)(2,1)}, b...) custom-call(s32[4]{0:T(128)} %pad_add_fusion.where_ref, s32[2048]{0:T(1024)} %seg_ref.9, ...), custom_call_target="tpu_custom_call" | custom-call | flops 1 | bytes 1 | tf_op jit(solution)/shard_map/pallas_call | solution.py:784
  35.9 1.7 collective-permute-done.3.far
  37.6 1.6 collective-permute-start.7
  40.5 11.2 %shard_map.400 = (bf16[512,384]{1,0:T(8,128)(2,1)}, bf16[512,384]{1,0:T(8,128)(2,1)}, bf16[512,384]{1,0:T(8,128)(2,1)}, bf16[12,256,256]{2,1,0:T(8,128)(2,1)}, b...) custom-call(s32[4]{0:T(128)} %pad_add_fusion.where_ref, s32[2048]{0:T(1024)} %seg_ref.9, ...), custom_call_target="tpu_custom_call" | custom-call | flops 1 | bytes 1 | tf_op jit(solution)/shard_map/pallas_call | solution.py:784
  51.7 1.9 collective-permute-done.7.far
  53.6 1.2 collective-permute-done.6.far_other
  57.2 14.0 %shard_map.401 = (bf16[512,768]{1,0:T(8,128)(2,1)}, bf16[4,512,768]{2,1,0:T(8,128)(2,1)}, bf16[4,512,768]{2,1,0:T(8,128)(2,1)}) custom-call(s32[4]{0:T(128)} %pad_add_fusion.where_ref, f32[512,768]{1,0:T(8,128)} %get-tuple-element.201.hid_ref, f32[1,768]{1,0:T(1,128)} %gain_ref.6, f32[1,768]{1,0:T(1,128)} %bias_ref.3, bf16[768,768]{1,0:T(8,128)(2,1)} %bitcast.155, ...), custom_call_target="tpu_custom_call" | custom-call | flops 1 | bytes 1 | tf_op jit(solution)/shard_map/pallas_call | solution.py:784
  74.2 13.6 %shard_map.402 = (f32[48,512]{1,0:T(8,128)}, f32[1,512]{1,0:T(1,128)}, f32[8,128]{1,0:T(8,128)}, f32[48,512]{1,0:T(8,128)}, f32[512,768]{1,0:T(8,128)}, /*index=...) custom-call(s32[4]{0:T(128)} %pad_add_fusion.where_ref, ...), custom_call_target="tpu_custom_call" | custom-call | flops 1 | bytes 1 | tf_op jit(solution)/shard_map/pallas_call | solution.py:784
  88.4 8.3 %shard_map.403 = (bf16[4,512,768]{2,1,0:T(8,128)(2,1)}, f32[8,768]{1,0:T(8,128)}) custom-call(s32[4]{0:T(128)} %pad_add_fusion.where_ref, f32[512,768]{1,0:T(8,128)} %get-tuple-element.214.grad_ref, bf16[4,512,768]{2,1,0:T(8,128)(2,1)} %get-tuple-element.215.slope_in, bf16[768,768]{1,0:T(8,128)(2,1)} %bitcast.153, ...), custom_call_target="tpu_custom_call" | custom-call | flops 1 | bytes 1 | tf_op jit(solution)/shard_map/pallas_call | solution.py:784
  97.8 2.6 shard_map.404
  100.9 13.7 %shard_map.405 = (f32[512,768]{1,0:T(8,128)}, bf16[512,768]{1,0:T(8,128)(2,1)}, f32[8,768]{1,0:T(8,128)}, bf16[2,4,192,768]{3,2,1,0:T(8,128)(2,1)}, bf16[4,192,7...) custom-call(s32[4]{0:T(128)} %pad_add_fusion.where_ref, f32[512,768]{1,0:T(8,128)} %get-tuple-element.214.grad_ref, ...), custom_call_target="tpu_custom_call" | custom-call | flops 1 | bytes 1 | tf_op jit(solution)/shard_map/pallas_call | solution.py:784
  115.1 14.1 %shard_map.406 = (f32[512,768]{1,0:T(8,128)}, bf16[384,768]{1,0:T(8,128)(2,1)}, bf16[4,144,768]{2,1,0:T(8,128)(2,1)}, bf16[4,144,768]{2,1,0:T(8,128)(2,1)}) custom-call(s32[4]{0:T(128)} %pad_add_fusion.where_ref, bf16[512,768]{1,0:T(8,128)(2,1)} %get-tuple-element.229.mix_ref, bf16[512,384]{1,0:T(8,128)(2,1)} %get-tuple-element.230.q_ref, ...), custom_call_target="tpu_custom_call" | custom-call | flops 1 | bytes 1 | tf_op jit(solution)/shard_map/pallas_call | solution.py:784
  130.6 2.0 shard_map.408
  132.6 2.0 shard_map.409
  134.6 2.2 shard_map.407
  137.8 1.6 collective-permute-start.22
  139.8 14.4 %shard_map.410 = (f32[512,768]{1,0:T(8,128)}, bf16[384,768]{1,0:T(8,128)(2,1)}, bf16[4,144,768]{2,1,0:T(8,128)(2,1)}, bf16[4,144,768]{2,1,0:T(8,128)(2,1)}) custom-call(s32[4]{0:T(128)} %pad_add_fusion.where_ref, bf16[512,768]{1,0:T(8,128)(2,1)} %get-tuple-element.229.mix_ref, bf16[512,384]{1,0:T(8,128)(2,1)} %get-tuple-element.239.q_ref, ...), custom_call_target="tpu_custom_call" | custom-call | flops 1 | bytes 1 | tf_op jit(solution)/shard_map/pallas_call | solution.py:784
  155.0 2.1 shard_map.411
  157.1 2.3 shard_map.412
  159.4 8.4 %shard_map.413 = (f32[48,512]{1,0:T(8,128)}, f32[8,896]{1,0:T(8,128)}, bf16[2,4,80,768]{3,2,1,0:T(8,128)(2,1)}, bf16[2,4,80,768]{3,2,1,0:T(8,128)(2,1)}) custom-call(s32[4]{0:T(128)} %pad_add_fusion.where_ref, s32[2048]{0:T(1024)} %seg_ref.9, s32[2,4]{1,0:T(2,128)} %label_ref.1, f32[512,768]{1,0:T(8,128)} %get-tuple-element.259.grad_ref, ...), custom_call_target="tpu_custom_call" | custom-call | flops 1 | bytes 1 | tf_op jit(solution)/shard_map/pallas_call | solution.py:784
  167.9 1.6 collective-permute-start.25
  169.6 1.3 slice_bitcast_fusion.16
  171.6 1.5 collective-permute-start.26
  173.1 4.2 %collective-permute-done.25 = bf16[1,1,1,192,768]{4,3,2,1,0:T(8,128)(2,1)S(1)} collective-permute-done((bf16[1,1,1,192,768]{4,3,2,1,0:T(8,128)(2,1)S(1)}, bf16[1,1,1,192,768]{4,3,2,1,0:T(8,128)(2,1)S(1)}, u32[]{:S(2)}, u32[]{:S(2)}) %collective-permute-start.25) | collective-permute-done | bytes 294944 | tf_op jit(solution)/shard_map/ppermute | solution.py:678
  177.3 1.4 add_convert_fusion.7
  178.7 1.2 collective-permute-start.32
  180.9 2.7 collective-permute-start.34
  183.6 1.6 collective-permute-start.28
  185.2 1.3 add_convert_fusion.6
  186.5 2.2 collective-permute-done.32
  188.7 2.6 collective-permute-start.36
  191.3 2.4 collective-permute-done.29
  193.7 1.2 add_convert_fusion.5
  194.9 1.6 collective-permute-start.33
  196.4 4.8 %collective-permute-done.28 = bf16[2,2,1,80,768]{4,3,1,2,0:T(8,128)(2,1)S(1)} collective-permute-done((bf16[2,2,1,80,768]{4,3,1,2,0:T(8,128)(2,1)S(1)}, bf16[2,2,1,80,768]{4,3,1,2,0:T(8,128)(2,1)S(1)}, u32[]{:S(2)}, u32[]{:S(2)}) %collective-permute-start.28) | collective-permute-done | bytes 491552 | tf_op jit(solution)/shard_map/ppermute | solution.py:678
  201.4 1.6 collective-permute-start.31
  202.9 1.2 add_convert_fusion.1
  204.1 1.2 collective-permute-start.30
  206.5 2.2 collective-permute-start.41
  209.9 5.4 %collective-permute-done.30 = bf16[1,1,2,144,768]{4,3,2,1,0:T(8,128)(2,1)S(1)} collective-permute-done((bf16[1,1,2,144,768]{4,3,2,1,0:T(8,128)(2,1)S(1)}, bf16[1,1,2,144,768]{4,3,2,1,0:T(8,128)(2,1)S(1)}, u32[]{:S(2)}, u32[]{:S(2)}) %collective-permute-start.30) | collective-permute-done | bytes 442400 | tf_op jit(solution)/shard_map/ppermute | solution.py:678
  216.8 1.3 collective-permute-start.42
  218.8 12.6 %collective-permute-done.35 = bf16[1,1,1,144,768]{4,3,2,1,0:T(8,128)(2,1)S(1)} collective-permute-done((bf16[1,1,1,144,768]{4,3,2,1,0:T(8,128)(2,1)S(1)}, bf16[1,1,1,144,768]{4,3,2,1,0:T(8,128)(2,1)S(1)}, u32[]{:S(2)}, u32[]{:S(2)}) %collective-permute-start.35) | collective-permute-done | bytes 221216 | tf_op jit(solution)/shard_map/ppermute | solution.py:678
  233.6 1.2 collective-permute-start.45
  235.9 1.7 collective-permute-done.40
  238.1 2.0 collective-permute-done.45
  240.2 1.7 collective-permute-start.48
  244.4 2.0 collective-permute-done.48
  247.3 2.0 collective-permute-start.53
  249.3 2.3 collective-permute-done.46
  253.5 2.2 fusion.1
  256.5 2.8 %shard_map.416 = f32[768,768]{1,0:T(8,128)} custom-call(s32[4]{0:T(128)} %pad_add_fusion.where_ref, bf16[1,2,192,768]{3,2,1,0:T(8,128)(2,1)} %bitcast.166, bf16[1,2,192,768]{3,2,1,0:T(8,128)(2,1)} %bitcast.189), custom_call_target="tpu_custom_call" | custom-call | flops 1 | bytes 1 | tf_op jit(solution)/shard_map/pallas_call | solution.py:784
  259.4 4.5 %collective-permute-done.53 = bf16[1,2,1,192,768]{4,3,1,2,0:T(8,128)(2,1)S(1)} collective-permute-done((bf16[1,2,1,192,768]{4,3,1,2,0:T(8,128)(2,1)S(1)}, bf16[1,2,1,192,768]{4,3,1,2,0:T(8,128)(2,1)S(1)}, u32[]{:S(2)}, u32[]{:S(2)}) %collective-permute-start.53) | collective-permute-done | bytes 589856 | tf_op jit(solution)/shard_map/ppermute | solution.py:678
  264.7 2.8 %shard_map.415 = f32[768,768]{1,0:T(8,128)} custom-call(s32[4]{0:T(128)} %pad_add_fusion.where_ref, bf16[2,1,192,768]{3,2,1,0:T(8,128)(2,1)} %bitcast.167, bf16[2,1,192,768]{3,2,1,0:T(8,128)(2,1)} %bitcast.190), custom_call_target="tpu_custom_call" | custom-call | flops 1 | bytes 1 | tf_op jit(solution)/shard_map/pallas_call | solution.py:784
  267.5 2.1 pad_maximum_fusion.1.all_ref
  270.3 3.5 %shard_map.414 = (f32[192,768]{1,0:T(8,128)}, f32[192,768]{1,0:T(8,128)}, f32[192,768]{1,0:T(8,128)}, f32[192,768]{1,0:T(8,128)}, f32[48,768]{1,0:T(8,128)}, /*i...) custom-call(s32[4]{0:T(128)} %pad_add_fusion.where_ref, ...), custom_call_target="tpu_custom_call" | custom-call | flops 1 | bytes 1 | tf_op jit(solution)/shard_map/pallas_call | solution.py:784
  273.8 1.3 reduce
  (177 shorter events, 33.9 us)
Async XLA Ops:
  3.5 20.9 %collective-permute-start.1 = (bf16[2,400,768]{2,1,0:T(8,128)(2,1)S(1)}, bf16[2,400,768]{2,1,0:T(8,128)(2,1)}, u32[]{:S(2)}, u32[]{:S(2)}) collective-permute-start(bf16[2,400,768]{2,1,0:T(8,128)(2,1)S(1)} %pad_maximum_fusion.rest_0_.own_t.rest_1_), channel_id=1, source_target_pairs={{0,1},{1,0},{2,3},{3,2},{4,5},{5,4},{6,7},{7,6},{8,9},{9,8},{10,11... | collective-permute-start | bytes 3686408 | tf_op jit(solution)/shard_map/ppermute | solution.py:675
  3.9 17.3 %collective-permute-start = (bf16[400,768]{1,0:T(8,128)(2,1)}, bf16[400,768]{1,0:T(8,128)(2,1)S(1)}, u32[]{:S(2)}, u32[]{:S(2)}) collective-permute-start(bf16[400,768]{1,0:T(8,128)(2,1)} %fusion.3), channel_id=1, source_target_pairs={{0,2},{1,3},{2,0},{3,1},{4,6},{5,7},{6,4},{7,5},{8,10},{9,11},{10,... | collective-permute-start | bytes 1843208 | tf_op jit(solution)/shard_map/ppermute | solution.py:675
  21.2 14.7 %copy-start.8 = (bf16[400,768]{1,0:T(8,128)(2,1)}, bf16[400,768]{1,0:T(8,128)(2,1)S(1)}, u32[]{:S(2)}) copy-start(bf16[400,768]{1,0:T(8,128)(2,1)S(1)} %collective-permute-done.rest_0_.far_t) | copy-start | bytes 1843204
  21.2 16.4 %collective-permute-start.2 = (bf16[400,768]{1,0:T(8,128)(2,1)S(1)}, bf16[400,768]{1,0:T(8,128)(2,1)}, u32[]{:S(2)}, u32[]{:S(2)}) collective-permute-start(bf16[400,768]{1,0:T(8,128)(2,1)S(1)} %collective-permute-done.rest_0_.far_t), channel_id=1, source_target_pairs={{0,4},{4,0},{8,12},{12,8},{16,20},{20,16},{24,28},{28,24},{1,5},{5... | collective-permute-start | bytes 1843208 | tf_op jit(solution)/shard_map/ppermute | solution.py:678
  22.9 14.7 %collective-permute-start.3 = (bf16[384,768]{1,0:T(8,128)(2,1)S(1)}, bf16[384,768]{1,0:T(8,128)(2,1)S(1)}, u32[]{:S(2)}, u32[]{:S(2)}) collective-permute-start(bf16[384,768]{1,0:T(8,128)(2,1)S(1)} %get-tuple-element.188), channel_id=1, source_target_pairs={{0,2},{1,3},{2,0},{3,1},{4,6},{5,7},{6,4},{7,5},{8,10},{9,11},{10,... | collective-permute-start | bytes 1769480 | tf_op jit(solution)/shard_map/ppermute | solution.py:675
  24.4 15.6 %collective-permute-start.4 = (bf16[400,768]{1,0:T(8,128)(2,1)S(1)}, bf16[400,768]{1,0:T(8,128)(2,1)}, u32[]{:S(2)}, u32[]{:S(2)}) collective-permute-start(bf16[400,768]{1,0:T(8,128)(2,1)S(1)} %collective-permute-done.rest_0_.far_t), channel_id=1, source_target_pairs={{0,1},{1,0},{2,3},{3,2},{4,5},{5,4},{6,7},{7,6},{8,9},{9,8},{10,11... | collective-permute-start | bytes 1843208 | tf_op jit(solution)/shard_map/ppermute | solution.py:675
  24.4 15.6 %copy-start.5 = (bf16[1,768,768]{2,1,0:T(8,128)(2,1)S(1)}, bf16[1,768,768]{2,1,0:T(8,128)(2,1)}, u32[]{:S(2)}) copy-start(bf16[1,768,768]{2,1,0:T(8,128)(2,1)} %param.38) | copy-start | bytes 3538948
  37.6 3.0 %collective-permute-start.5 = (bf16[400,768]{1,0:T(8,128)(2,1)}, bf16[400,768]{1,0:T(8,128)(2,1)}, u32[]{:S(2)}, u32[]{:S(2)}) collective-permute-start(bf16[400,768]{1,0:T(8,128)(2,1)} %collective-permute-done.2.rest_1_), channel_id=1, source_target_pairs={{0,1},{1,0},{2,3},{3,2},{4,5},{5,4},{6,7},{7,6},{8,9},{9,8},{10,11... | collective-permute-start | bytes 1843208 | tf_op jit(solution)/shard_map/ppermute | solution.py:675
  37.6 16.1 %collective-permute-start.7 = (bf16[384,768]{1,0:T(8,128)(2,1)}, bf16[384,768]{1,0:T(8,128)(2,1)}, u32[]{:S(2)}, u32[]{:S(2)}) collective-permute-start(bf16[384,768]{1,0:T(8,128)(2,1)} %get-tuple-element.189), channel_id=1, source_target_pairs={{0,2},{1,3},{2,0},{3,1},{4,6},{5,7},{6,4},{7,5},{8,10},{9,11},{10,... | collective-permute-start | bytes 1769480 | tf_op jit(solution)/shard_map/ppermute | solution.py:675
  39.2 16.6 %copy-start.4 = (bf16[1,768,768]{2,1,0:T(8,128)(2,1)S(1)}, bf16[1,768,768]{2,1,0:T(8,128)(2,1)}, u32[]{:S(2)}) copy-start(bf16[1,768,768]{2,1,0:T(8,128)(2,1)} %param.40) | copy-start | bytes 3538948
  39.2 15.7 %collective-permute-start.6 = (bf16[384,768]{1,0:T(8,128)(2,1)}, bf16[384,768]{1,0:T(8,128)(2,1)}, u32[]{:S(2)}, u32[]{:S(2)}) collective-permute-start(bf16[384,768]{1,0:T(8,128)(2,1)} %copy-done.16), channel_id=1, source_target_pairs={{0,4},{4,0},{8,12},{12,8},{16,20},{20,16},{24,28},{28,24},{1,5},{5... | collective-permute-start | bytes 1769480 | tf_op jit(solution)/shard_map/ppermute | solution.py:678
  40.0 16.0 %collective-permute-start.8 = (bf16[768,768]{1,0:T(8,128)(2,1)S(1)}, bf16[768,768]{1,0:T(8,128)(2,1)}, u32[]{:S(2)}, u32[]{:S(2)}) collective-permute-start(bf16[768,768]{1,0:T(8,128)(2,1)S(1)} %bitcast.157), channel_id=1, source_target_pairs={{0,1},{1,0},{2,3},{3,2},{4,5},{5,4},{6,7},{7,6},{8,9},{9,8},{10,11... | collective-permute-start | bytes 3538952 | tf_op jit(solution)/shard_map/ppermute | solution.py:675
  40.0 16.3 %collective-permute-start.9 = (bf16[384,768]{1,0:T(8,128)(2,1)}, bf16[384,768]{1,0:T(8,128)(2,1)}, u32[]{:S(2)}, u32[]{:S(2)}) collective-permute-start(bf16[384,768]{1,0:T(8,128)(2,1)} %copy-done.16), channel_id=1, source_target_pairs={{0,1},{1,0},{2,3},{3,2},{4,5},{5,4},{6,7},{7,6},{8,9},{9,8},{10,11... | collective-permute-start | bytes 1769480 | tf_op jit(solution)/shard_map/ppermute | solution.py:675
  54.9 2.3 collective-permute-start.10
  54.9 16.4 %collective-permute-start.12 = (bf16[384,768]{1,0:T(8,128)(2,1)}, bf16[384,768]{1,0:T(8,128)(2,1)S(1)}, u32[]{:S(2)}, u32[]{:S(2)}) collective-permute-start(bf16[384,768]{1,0:T(8,128)(2,1)} %collective-permute-done.7.far), channel_id=1, source_target_pairs={{0,4},{4,0},{8,12},{12,8},{16,20},{20,16},{24,28},{28,24},{1,5},{5... | collective-permute-start | bytes 1769480 | tf_op jit(solution)/shard_map/ppermute | solution.py:678
  55.8 15.7 %copy-start.31 = (f32[96]{0:T(128)S(1)}, f32[96]{0:T(128)}, u32[]{:S(2)}) copy-start(f32[96]{0:T(128)} %param.43) | copy-start | bytes 1156
  55.8 16.4 %collective-permute-start.11 = (bf16[768,768]{1,0:T(8,128)(2,1)S(1)}, bf16[768,768]{1,0:T(8,128)(2,1)}, u32[]{:S(2)}, u32[]{:S(2)}) collective-permute-start(bf16[768,768]{1,0:T(8,128)(2,1)S(1)} %bitcast.154), channel_id=1, source_target_pairs={{0,1},{1,0},{2,3},{3,2},{4,5},{5,4},{6,7},{7,6},{8,9},{9,8},{10,11... | collective-permute-start | bytes 3538952 | tf_op jit(solution)/shard_map/ppermute | solution.py:675
  56.0 16.2 %collective-permute-start.13 = (bf16[384,768]{1,0:T(8,128)(2,1)}, bf16[384,768]{1,0:T(8,128)(2,1)S(1)}, u32[]{:S(2)}, u32[]{:S(2)}) collective-permute-start(bf16[384,768]{1,0:T(8,128)(2,1)} %collective-permute-done.7.far), channel_id=1, source_target_pairs={{0,1},{1,0},{2,3},{3,2},{4,5},{5,4},{6,7},{7,6},{8,9},{9,8},{10,11... | collective-permute-start | bytes 1769480 | tf_op jit(solution)/shard_map/ppermute | solution.py:675
  71.3 2.1 collective-permute-start.14
  87.8 8.9 %collective-permute-start.15 = (bf16[4,192,768]{2,1,0:T(8,128)(2,1)}, bf16[4,192,768]{2,1,0:T(8,128)(2,1)S(1)}, u32[]{:S(2)}, u32[]{:S(2)}) collective-permute-start(bf16[4,192,768]{2,1,0:T(8,128)(2,1)} %get-tuple-element.217), channel_id=1, source_target_pairs={{0,1},{1,0},{2,3},{3,2},{4,5},{5,4},{6,7},{7,6},{8,9},{9,8},{10,11... | collective-permute-start | bytes 3538952 | tf_op jit(solution)/shard_map/ppermute | solution.py:675
  88.0 8.7 %collective-permute-start.16 = (bf16[4,192,768]{2,1,0:T(8,128)(2,1)}, bf16[4,192,768]{2,1,0:T(8,128)(2,1)S(1)}, u32[]{:S(2)}, u32[]{:S(2)}) collective-permute-start(bf16[4,192,768]{2,1,0:T(8,128)(2,1)} %get-tuple-element.218), channel_id=1, source_target_pairs={{0,1},{1,0},{2,3},{3,2},{4,5},{5,4},{6,7},{7,6},{8,9},{9,8},{10,11... | collective-permute-start | bytes 3538952 | tf_op jit(solution)/shard_map/ppermute | solution.py:675
  100.4 28.9 %collective-permute-start.17 = (bf16[1,2,2,192,768]{4,3,2,1,0:T(8,128)(2,1)}, bf16[1,2,2,192,768]{4,3,2,1,0:T(8,128)(2,1)S(1)}, u32[]{:S(2)}, u32[]{:S(2)}) collective-permute-start(bf16[1,2,2,192,768]{4,3,2,1,0:T(8,128)(2,1)} %shard_map.404), channel_id=1, source_target_pairs={{0,2},{1,3},{2,0},{3,1},{4,6},{5,7},{6,4},{7,5},{8,10},{9,11},{10,... | collective-permute-start | bytes 3538952 | tf_op jit(solution)/shard_map/ppermute | solution.py:675
  114.6 14.9 %collective-permute-start.18 = (bf16[4,192,768]{2,1,0:T(8,128)(2,1)}, bf16[4,192,768]{2,1,0:T(8,128)(2,1)S(1)}, u32[]{:S(2)}, u32[]{:S(2)}) collective-permute-start(bf16[4,192,768]{2,1,0:T(8,128)(2,1)} %get-tuple-element.245), channel_id=1, source_target_pairs={{0,1},{1,0},{2,3},{3,2},{4,5},{5,4},{6,7},{7,6},{8,9},{9,8},{10,11... | collective-permute-start | bytes 3538952 | tf_op jit(solution)/shard_map/ppermute | solution.py:675
  114.6 14.8 %collective-permute-start.19 = (bf16[4,192,768]{2,1,0:T(8,128)(2,1)}, bf16[4,192,768]{2,1,0:T(8,128)(2,1)}, u32[]{:S(2)}, u32[]{:S(2)}) collective-permute-start(bf16[4,192,768]{2,1,0:T(8,128)(2,1)} %get-tuple-element.246), channel_id=1, source_target_pairs={{0,1},{1,0},{2,3},{3,2},{4,5},{5,4},{6,7},{7,6},{8,9},{9,8},{10,11... | collective-permute-start | bytes 3538952 | tf_op jit(solution)/shard_map/ppermute | solution.py:675
  129.3 24.9 %collective-permute-start.20 = (bf16[4,144,768]{2,1,0:T(8,128)(2,1)}, bf16[4,144,768]{2,1,0:T(8,128)(2,1)}, u32[]{:S(2)}, u32[]{:S(2)}) collective-permute-start(bf16[4,144,768]{2,1,0:T(8,128)(2,1)} %get-tuple-element.254), channel_id=1, source_target_pairs={{0,1},{1,0},{2,3},{3,2},{4,5},{5,4},{6,7},{7,6},{8,9},{9,8},{10,11... | collective-permute-start | bytes 2654216 | tf_op jit(solution)/shard_map/ppermute | solution.py:675
  136.8 17.4 %collective-permute-start.21 = (bf16[1,1,2,192,768]{4,3,2,1,0:T(8,128)(2,1)}, bf16[1,1,2,192,768]{4,3,2,1,0:T(8,128)(2,1)S(1)}, u32[]{:S(2)}, u32[]{:S(2)}) collective-permute-start(bf16[1,1,2,192,768]{4,3,2,1,0:T(8,128)(2,1)} %shard_map.407), channel_id=1, source_target_pairs={{0,4},{4,0},{8,12},{12,8},{16,20},{20,16},{24,28},{28,24},{1,5},{5... | collective-permute-start | bytes 1769480 | tf_op jit(solution)/shard_map/ppermute | solution.py:678
  137.8 30.1 %collective-permute-start.22 = (bf16[1,2,1,192,768]{4,3,1,2,0:T(8,128)(2,1)}, bf16[1,2,1,192,768]{4,3,1,2,0:T(8,128)(2,1)}, u32[]{:S(2)}, u32[]{:S(2)}) collective-permute-start(bf16[1,2,1,192,768]{4,3,1,2,0:T(8,128)(2,1)} %bitcast.34), channel_id=1, source_target_pairs={{0,8},{4,12},{8,0},{12,4},{16,24},{20,28},{24,16},{28,20},{1,9},{5... | collective-permute-start | bytes 1769480 | tf_op jit(solution)/shard_map/ppermute | solution.py:678
  139.3 28.5 %collective-permute-start.23 = (bf16[1,2,1,192,768]{4,3,1,2,0:T(8,128)(2,1)}, bf16[1,2,1,192,768]{4,3,1,2,0:T(8,128)(2,1)}, u32[]{:S(2)}, u32[]{:S(2)}) collective-permute-start(bf16[1,2,1,192,768]{4,3,1,2,0:T(8,128)(2,1)} %bitcast.35), channel_id=1, source_target_pairs={{0,8},{4,12},{8,0},{12,4},{16,24},{20,28},{24,16},{28,20},{1,9},{5... | collective-permute-start | bytes 1769480 | tf_op jit(solution)/shard_map/ppermute | solution.py:678
  154.2 23.1 %collective-permute-start.24 = (bf16[4,144,768]{2,1,0:T(8,128)(2,1)}, bf16[4,144,768]{2,1,0:T(8,128)(2,1)}, u32[]{:S(2)}, u32[]{:S(2)}) collective-permute-start(bf16[4,144,768]{2,1,0:T(8,128)(2,1)} %get-tuple-element.273), channel_id=1, source_target_pairs={{0,1},{1,0},{2,3},{3,2},{4,5},{5,4},{6,7},{7,6},{8,9},{9,8},{10,11... | collective-permute-start | bytes 2654216 | tf_op jit(solution)/shard_map/ppermute | solution.py:675
  159.4 8.5 %copy-start.28 = (bf16[1,1,1,192,768]{4,3,2,1,0:T(8,128)(2,1)S(1)}, bf16[1,1,1,192,768]{4,3,2,1,0:T(8,128)(2,1)}, u32[]{:S(2)}) copy-start(bf16[1,1,1,192,768]{4,3,2,1,0:T(8,128)(2,1)} %shard_map.411) | copy-start | bytes 884740
  159.4 17.9 %copy-start.3 = (bf16[2,4,192,768]{3,2,1,0:T(8,128)(2,1)S(1)}, bf16[2,4,192,768]{3,2,1,0:T(8,128)(2,1)}, u32[]{:S(2)}) copy-start(bf16[2,4,192,768]{3,2,1,0:T(8,128)(2,1)} %get-tuple-element.248) | copy-start | bytes 7077892
  159.4 17.9 %copy-start.10 = (bf16[4,192,768]{2,1,0:T(8,128)(2,1)S(1)}, bf16[4,192,768]{2,1,0:T(8,128)(2,1)}, u32[]{:S(2)}) copy-start(bf16[4,192,768]{2,1,0:T(8,128)(2,1)} %copy-done.9) | copy-start | bytes 3538948
  167.8 13.0 %copy-start.22 = (bf16[2,4,80,768]{3,2,1,0:T(8,128)(2,1)S(1)}, bf16[2,4,80,768]{3,2,1,0:T(8,128)(2,1)}, u32[]{:S(2)}) copy-start(bf16[2,4,80,768]{3,2,1,0:T(8,128)(2,1)} %get-tuple-element.280) | copy-start | bytes 2949124
  167.8 13.0 %collective-permute-start.27 = (bf16[2,4,80,768]{3,2,1,0:T(8,128)(2,1)}, bf16[2,4,80,768]{3,2,1,0:T(8,128)(2,1)S(1)}, u32[]{:S(2)}, u32[]{:S(2)}) collective-permute-start(bf16[2,4,80,768]{3,2,1,0:T(8,128)(2,1)} %get-tuple-element.281), channel_id=1, source_target_pairs={{0,1},{1,0},{2,3},{3,2},{4,5},{5,4},{6,7},{7,6},{8,9},{9,8},{10,11... | collective-permute-start | bytes 2949128 | tf_op jit(solution)/shard_map/ppermute | solution.py:675
  167.9 9.4 %collective-permute-start.25 = (bf16[1,1,1,192,768]{4,3,2,1,0:T(8,128)(2,1)S(1)}, bf16[1,1,1,192,768]{4,3,2,1,0:T(8,128)(2,1)S(1)}, u32[]{:S(2)}, u32[]{:S(2)}) collective-permute-start(bf16[1,1,1,192,768]{4,3,2,1,0:T(8,128)(2,1)S(1)} %copy-done.28), channel_id=1, source_target_pairs={{0,8},{4,12},{8,0},{12,4},{16,24},{20,28},{24,16},{28,20},{1,9},{5... | collective-permute-start | bytes 884744 | tf_op jit(solution)/shard_map/ppermute | solution.py:678
  171.6 31.3 %collective-permute-start.26 = (bf16[1,2,2,144,768]{4,3,2,1,0:T(8,128)(2,1)}, bf16[1,2,2,144,768]{4,3,2,1,0:T(8,128)(2,1)S(1)}, u32[]{:S(2)}, u32[]{:S(2)}) collective-permute-start(bf16[1,2,2,144,768]{4,3,2,1,0:T(8,128)(2,1)} %shard_map.412), channel_id=1, source_target_pairs={{0,2},{1,3},{2,0},{3,1},{4,6},{5,7},{6,4},{7,5},{8,10},{9,11},{10,... | collective-permute-start | bytes 2654216 | tf_op jit(solution)/shard_map/ppermute | solution.py:675
  178.7 10.0 %collective-permute-start.32 = (bf16[1,1,1,192,768]{4,3,1,2,0:T(8,128)(2,1)S(1)}, bf16[1,1,1,192,768]{4,3,1,2,0:T(8,128)(2,1)S(1)}, u32[]{:S(2)}, u32[]{:S(2)}) collective-permute-start(bf16[1,1,1,192,768]{4,3,1,2,0:T(8,128)(2,1)S(1)} %get-tuple-element.287), channel_id=1, source_target_pairs={{0,4},{4,0},{8,12},{12,8},{16,20},{20,16},{24,28},{28,24},{1,5},{5... | collective-permute-start | bytes 884744 | tf_op jit(solution)/shard_map/ppermute | solution.py:678
  179.9 13.8 %collective-permute-start.29 = (bf16[1,1,1,192,768]{4,3,1,2,0:T(8,128)(2,1)S(1)}, bf16[1,1,1,192,768]{4,3,1,2,0:T(8,128)(2,1)S(1)}, u32[]{:S(2)}, u32[]{:S(2)}) collective-permute-start(bf16[1,1,1,192,768]{4,3,1,2,0:T(8,128)(2,1)S(1)} %get-tuple-element.288), channel_id=1, source_target_pairs={{0,4},{4,0},{8,12},{12,8},{16,20},{20,16},{24,28},{28,24},{1,5},{5... | collective-permute-start | bytes 884744 | tf_op jit(solution)/shard_map/ppermute | solution.py:678
  180.9 24.4 %collective-permute-start.34 = (bf16[8,896]{1,0:T(8,128)(2,1)S(1)}, bf16[8,896]{1,0:T(8,128)(2,1)S(1)}, u32[]{:S(2)}, u32[]{:S(2)}) collective-permute-start(bf16[8,896]{1,0:T(8,128)(2,1)S(1)} %convert_element_type.245), channel_id=1, source_target_pairs={{0,16},{4,20},{8,24},{12,28},{16,0},{20,4},{24,8},{28,12},{1,17},{... | collective-permute-start | bytes 43016 | tf_op jit(solution)/shard_map/ppermute | solution.py:678
  183.6 17.7 %collective-permute-start.28 = (bf16[2,2,1,80,768]{4,3,1,2,0:T(8,128)(2,1)S(1)}, bf16[2,2,1,80,768]{4,3,1,2,0:T(8,128)(2,1)S(1)}, u32[]{:S(2)}, u32[]{:S(2)}) collective-permute-start(bf16[2,2,1,80,768]{4,3,1,2,0:T(8,128)(2,1)S(1)} %add_convert_fusion), channel_id=1, source_target_pairs={{0,8},{4,12},{8,0},{12,4},{16,24},{20,28},{24,16},{28,20},{1,9},{5... | collective-permute-start | bytes 1474568 | tf_op jit(solution)/shard_map/ppermute | solution.py:678
  186.5 16.4 %copy-start.23 = (bf16[4,144,768]{2,1,0:T(8,128)(2,1)S(1)}, bf16[4,144,768]{2,1,0:T(8,128)(2,1)}, u32[]{:S(2)}) copy-start(bf16[4,144,768]{2,1,0:T(8,128)(2,1)} %get-tuple-element.277) | copy-start | bytes 2654212
  188.7 29.4 %collective-permute-start.36 = (bf16[1,1,1,192,768]{4,3,2,1,0:T(8,128)(2,1)S(1)}, bf16[1,1,1,192,768]{4,3,2,1,0:T(8,128)(2,1)S(1)}, u32[]{:S(2)}, u32[]{:S(2)}) collective-permute-start(bf16[1,1,1,192,768]{4,3,2,1,0:T(8,128)(2,1)S(1)} %add_convert_fusion.6), channel_id=1, source_target_pairs={{0,16},{4,20},{8,24},{12,28},{16,0},{20,4},{24,8},{28,12},{1,17},{... | collective-permute-start | bytes 884744 | tf_op jit(solution)/shard_map/ppermute | solution.py:678
  194.9 10.5 %collective-permute-start.33 = (bf16[1,1,1,192,768]{4,3,1,2,0:T(8,128)(2,1)S(1)}, bf16[1,1,1,192,768]{4,3,1,2,0:T(8,128)(2,1)S(1)}, u32[]{:S(2)}, u32[]{:S(2)}) collective-permute-start(bf16[1,1,1,192,768]{4,3,1,2,0:T(8,128)(2,1)S(1)} %add_convert_fusion.5), channel_id=1, source_target_pairs={{0,2},{1,3},{2,0},{3,1},{4,6},{5,7},{6,4},{7,5},{8,10},{9,11},{10,... | collective-permute-start | bytes 884744 | tf_op jit(solution)/shard_map/ppermute | solution.py:675
  201.4 7.3 %collective-permute-start.31 = (bf16[1,2,1,80,768]{4,3,1,2,0:T(8,128)(2,1)S(1)}, bf16[1,2,1,80,768]{4,3,1,2,0:T(8,128)(2,1)S(1)}, u32[]{:S(2)}, u32[]{:S(2)}) collective-permute-start(bf16[1,2,1,80,768]{4,3,1,2,0:T(8,128)(2,1)S(1)} %add_convert_fusion.9), channel_id=1, source_target_pairs={{0,2},{1,3},{2,0},{3,1},{4,6},{5,7},{6,4},{7,5},{8,10},{9,11},{10,... | collective-permute-start | bytes 737288 | tf_op jit(solution)/shard_map/ppermute | solution.py:675
  204.1 11.2 %collective-permute-start.30 = (bf16[1,1,2,144,768]{4,3,2,1,0:T(8,128)(2,1)S(1)}, bf16[1,1,2,144,768]{4,3,2,1,0:T(8,128)(2,1)S(1)}, u32[]{:S(2)}, u32[]{:S(2)}) collective-permute-start(bf16[1,1,2,144,768]{4,3,2,1,0:T(8,128)(2,1)S(1)} %add_convert_fusion.1), channel_id=1, source_target_pairs={{0,4},{4,0},{8,12},{12,8},{16,20},{20,16},{24,28},{28,24},{1,5},{5... | collective-permute-start | bytes 1327112 | tf_op jit(solution)/shard_map/ppermute | solution.py:678
  205.3 27.2 %collective-permute-start.39 = (bf16[16,896]{1,0:T(8,128)(2,1)S(1)}, bf16[16,896]{1,0:T(8,128)(2,1)S(1)}, u32[]{:S(2)}, u32[]{:S(2)}) collective-permute-start(bf16[16,896]{1,0:T(8,128)(2,1)S(1)} %pad_maximum_fusion.11), channel_id=1, source_target_pairs={{0,8},{4,12},{8,0},{12,4},{16,24},{20,28},{24,16},{28,20},{1,9},{5... | collective-permute-start | bytes 86024 | tf_op jit(solution)/shard_map/ppermute | solution.py:678
  206.5 28.3 %collective-permute-start.41 = (bf16[1,1,1,192,768]{4,3,1,2,0:T(8,128)(2,1)S(1)}, bf16[1,1,1,192,768]{4,3,1,2,0:T(8,128)(2,1)S(1)}, u32[]{:S(2)}, u32[]{:S(2)}) collective-permute-start(bf16[1,1,1,192,768]{4,3,1,2,0:T(8,128)(2,1)S(1)} %add_convert_fusion.4), channel_id=1, source_target_pairs={{0,16},{4,20},{8,24},{12,28},{16,0},{20,4},{24,8},{28,12},{1,17},{... | collective-permute-start | bytes 884744 | tf_op jit(solution)/shard_map/ppermute | solution.py:678
  208.8 7.9 %collective-permute-start.37 = (bf16[1,1,1,80,768]{4,3,1,2,0:T(8,128)(2,1)S(1)}, bf16[1,1,1,80,768]{4,3,1,2,0:T(8,128)(2,1)S(1)}, u32[]{:S(2)}, u32[]{:S(2)}) collective-permute-start(bf16[1,1,1,80,768]{4,3,1,2,0:T(8,128)(2,1)S(1)} %add_convert_fusion.15), channel_id=1, source_target_pairs={{0,4},{4,0},{8,12},{12,8},{16,20},{20,16},{24,28},{28,24},{1,5},{5... | collective-permute-start | bytes 368648 | tf_op jit(solution)/shard_map/ppermute | solution.py:678
  216.4 15.0 %collective-permute-start.35 = (bf16[1,1,1,144,768]{4,3,2,1,0:T(8,128)(2,1)S(1)}, bf16[1,1,1,144,768]{4,3,2,1,0:T(8,128)(2,1)S(1)}, u32[]{:S(2)}, u32[]{:S(2)}) collective-permute-start(bf16[1,1,1,144,768]{4,3,2,1,0:T(8,128)(2,1)S(1)} %add_convert_fusion.12), channel_id=1, source_target_pairs={{0,8},{4,12},{8,0},{12,4},{16,24},{20,28},{24,16},{28,20},{1,9},{5... | collective-permute-start | bytes 663560 | tf_op jit(solution)/shard_map/ppermute | solution.py:678
  216.8 16.8 %collective-permute-start.42 = (bf16[1,1,1,80,768]{4,3,1,2,0:T(8,128)(2,1)S(1)}, bf16[1,1,1,80,768]{4,3,1,2,0:T(8,128)(2,1)S(1)}, u32[]{:S(2)}, u32[]{:S(2)}) collective-permute-start(bf16[1,1,1,80,768]{4,3,1,2,0:T(8,128)(2,1)S(1)} %add_convert_fusion.14), channel_id=1, source_target_pairs={{0,16},{4,20},{8,24},{12,28},{16,0},{20,4},{24,8},{28,12},{1,17},{... | collective-permute-start | bytes 368648 | tf_op jit(solution)/shard_map/ppermute | solution.py:678
  218.2 23.7 %collective-permute-start.44 = (bf16[1,1,1,192,768]{4,3,2,1,0:T(8,128)(2,1)S(1)}, bf16[1,1,1,192,768]{4,3,2,1,0:T(8,128)(2,1)S(1)}, u32[]{:S(2)}, u32[]{:S(2)}) collective-permute-start(bf16[1,1,1,192,768]{4,3,2,1,0:T(8,128)(2,1)S(1)} %add_convert_fusion.3), channel_id=1, source_target_pairs={{0,8},{4,12},{8,0},{12,4},{16,24},{20,28},{24,16},{28,20},{1,9},{5... | collective-permute-start | bytes 884744 | tf_op jit(solution)/shard_map/ppermute | solution.py:678
  232.5 10.7 %collective-permute-start.38 = (bf16[1,1,1,144,768]{4,3,2,1,0:T(8,128)(2,1)S(1)}, bf16[1,1,1,144,768]{4,3,2,1,0:T(8,128)(2,1)S(1)}, u32[]{:S(2)}, u32[]{:S(2)}) collective-permute-start(bf16[1,1,1,144,768]{4,3,2,1,0:T(8,128)(2,1)S(1)} %add_convert_fusion.11), channel_id=1, source_target_pairs={{0,16},{4,20},{8,24},{12,28},{16,0},{20,4},{24,8},{28,12},{1,17},{... | collective-permute-start | bytes 663560 | tf_op jit(solution)/shard_map/ppermute | solution.py:678
  232.6 4.9 %collective-permute-start.40 = (bf16[32,896]{1,0:T(8,128)(2,1)S(1)}, bf16[32,896]{1,0:T(8,128)(2,1)S(1)}, u32[]{:S(2)}, u32[]{:S(2)}) collective-permute-start(bf16[32,896]{1,0:T(8,128)(2,1)S(1)} %pad_maximum_fusion.10), channel_id=1, source_target_pairs={{0,4},{4,0},{8,12},{12,8},{16,20},{20,16},{24,28},{28,24},{1,5},{5... | collective-permute-start | bytes 172040 | tf_op jit(solution)/shard_map/ppermute | solution.py:678
  233.6 6.5 %collective-permute-start.45 = (bf16[1,1,1,80,768]{4,3,1,2,0:T(8,128)(2,1)S(1)}, bf16[1,1,1,80,768]{4,3,1,2,0:T(8,128)(2,1)S(1)}, u32[]{:S(2)}, u32[]{:S(2)}) collective-permute-start(bf16[1,1,1,80,768]{4,3,1,2,0:T(8,128)(2,1)S(1)} %add_convert_fusion.13), channel_id=1, source_target_pairs={{0,4},{4,0},{8,12},{12,8},{16,20},{20,16},{24,28},{28,24},{1,5},{5... | collective-permute-start | bytes 368648 | tf_op jit(solution)/shard_map/ppermute | solution.py:678
  234.9 12.3 %collective-permute-start.47 = (bf16[1,1,1,192,768]{4,3,1,2,0:T(8,128)(2,1)S(1)}, bf16[1,1,1,192,768]{4,3,1,2,0:T(8,128)(2,1)S(1)}, u32[]{:S(2)}, u32[]{:S(2)}) collective-permute-start(bf16[1,1,1,192,768]{4,3,1,2,0:T(8,128)(2,1)S(1)} %add_convert_fusion.2), channel_id=1, source_target_pairs={{0,4},{4,0},{8,12},{12,8},{16,20},{20,16},{24,28},{28,24},{1,5},{5... | collective-permute-start | bytes 884744 | tf_op jit(solution)/shard_map/ppermute | solution.py:678
  237.5 5.6 %collective-permute-start.43 = (bf16[64,896]{1,0:T(8,128)(2,1)S(1)}, bf16[64,896]{1,0:T(8,128)(2,1)S(1)}, u32[]{:S(2)}, u32[]{:S(2)}) collective-permute-start(bf16[64,896]{1,0:T(8,128)(2,1)S(1)} %pad_maximum_fusion.9), channel_id=1, source_target_pairs={{0,2},{1,3},{2,0},{3,1},{4,6},{5,7},{6,4},{7,5},{8,10},{9,11},{10,... | collective-permute-start | bytes 344072 | tf_op jit(solution)/shard_map/ppermute | solution.py:675
  240.2 6.3 %collective-permute-start.48 = (bf16[1,2,1,80,768]{4,3,1,2,0:T(8,128)(2,1)S(1)}, bf16[1,2,1,80,768]{4,3,1,2,0:T(8,128)(2,1)S(1)}, u32[]{:S(2)}, u32[]{:S(2)}) collective-permute-start(bf16[1,2,1,80,768]{4,3,1,2,0:T(8,128)(2,1)S(1)} %pad_maximum_fusion.6), channel_id=1, source_target_pairs={{0,8},{4,12},{8,0},{12,4},{16,24},{20,28},{24,16},{28,20},{1,9},{5... | collective-permute-start | bytes 737288 | tf_op jit(solution)/shard_map/ppermute | solution.py:678
  242.0 13.8 %collective-permute-start.54 = (bf16[1,1,2,192,768]{4,3,2,1,0:T(8,128)(2,1)S(1)}, bf16[1,1,2,192,768]{4,3,2,1,0:T(8,128)(2,1)S(1)}, u32[]{:S(2)}, u32[]{:S(2)}) collective-permute-start(bf16[1,1,2,192,768]{4,3,2,1,0:T(8,128)(2,1)S(1)} %pad_maximum_fusion.2), channel_id=1, source_target_pairs={{0,4},{4,0},{8,12},{12,8},{16,20},{20,16},{24,28},{28,24},{1,5},{5... | collective-permute-start | bytes 1769480 | tf_op jit(solution)/shard_map/ppermute | solution.py:678
  243.1 6.2 %collective-permute-start.52 = (bf16[128,896]{1,0:T(8,128)(2,1)S(1)}, bf16[128,896]{1,0:T(8,128)(2,1)S(1)}, u32[]{:S(2)}, u32[]{:S(2)}) collective-permute-start(bf16[128,896]{1,0:T(8,128)(2,1)S(1)} %pad_maximum_fusion.7), channel_id=1, source_target_pairs={{0,1},{1,0},{2,3},{3,2},{4,5},{5,4},{6,7},{7,6},{8,9},{9,8},{10,11... | collective-permute-start | bytes 688136 | tf_op jit(solution)/shard_map/ppermute | solution.py:675
  243.3 8.3 %collective-permute-start.46 = (bf16[1,1,1,144,768]{4,3,2,1,0:T(8,128)(2,1)S(1)}, bf16[1,1,1,144,768]{4,3,2,1,0:T(8,128)(2,1)S(1)}, u32[]{:S(2)}, u32[]{:S(2)}) collective-permute-start(bf16[1,1,1,144,768]{4,3,2,1,0:T(8,128)(2,1)S(1)} %add_convert_fusion.10), channel_id=1, source_target_pairs={{0,8},{4,12},{8,0},{12,4},{16,24},{20,28},{24,16},{28,20},{1,9},{5... | collective-permute-start | bytes 663560 | tf_op jit(solution)/shard_map/ppermute | solution.py:678
  246.5 5.7 %collective-permute-start.50 = (bf16[1,4,32,768]{3,2,1,0:T(8,128)(2,1)S(1)}, bf16[1,4,32,768]{3,2,1,0:T(8,128)(2,1)S(1)}, u32[]{:S(2)}, u32[]{:S(2)}) collective-permute-start(bf16[1,4,32,768]{3,2,1,0:T(8,128)(2,1)S(1)} %bitcast.187), channel_id=1, source_target_pairs={{0,2},{1,3},{2,0},{3,1},{4,6},{5,7},{6,4},{7,5},{8,10},{9,11},{10,... | collective-permute-start | bytes 589832 | tf_op jit(solution)/shard_map/ppermute | solution.py:675
  247.3 16.5 %collective-permute-start.53 = (bf16[1,2,1,192,768]{4,3,1,2,0:T(8,128)(2,1)S(1)}, bf16[1,2,1,192,768]{4,3,1,2,0:T(8,128)(2,1)S(1)}, u32[]{:S(2)}, u32[]{:S(2)}) collective-permute-start(bf16[1,2,1,192,768]{4,3,1,2,0:T(8,128)(2,1)S(1)} %pad_maximum_fusion.3), channel_id=1, source_target_pairs={{0,8},{4,12},{8,0},{12,4},{16,24},{20,28},{24,16},{28,20},{1,9},{5... | collective-permute-start | bytes 1769480 | tf_op jit(solution)/shard_map/ppermute | solution.py:678
  252.3 15.2 %collective-permute-start.51 = (bf16[2,4,32,768]{3,2,1,0:T(8,128)(2,1)S(1)}, bf16[2,4,32,768]{3,2,1,0:T(8,128)(2,1)}, u32[]{:S(2)}, u32[]{:S(2)}) collective-permute-start(bf16[2,4,32,768]{3,2,1,0:T(8,128)(2,1)S(1)} %pad_maximum_fusion.5), channel_id=1, source_target_pairs={{0,1},{1,0},{2,3},{3,2},{4,5},{5,4},{6,7},{7,6},{8,9},{9,8},{10,11... | collective-permute-start | bytes 1179656 | tf_op jit(solution)/shard_map/ppermute | solution.py:675
  252.5 17.0 %collective-permute-start.49 = (bf16[1,1,2,144,768]{4,3,2,1,0:T(8,128)(2,1)S(1)}, bf16[1,1,2,144,768]{4,3,2,1,0:T(8,128)(2,1)S(1)}, u32[]{:S(2)}, u32[]{:S(2)}) collective-permute-start(bf16[1,1,2,144,768]{4,3,2,1,0:T(8,128)(2,1)S(1)} %pad_maximum_fusion.4), channel_id=1, source_target_pairs={{0,4},{4,0},{8,12},{12,8},{16,20},{20,16},{24,28},{28,24},{1,5},{5... | collective-permute-start | bytes 1327112 | tf_op jit(solution)/shard_map/ppermute | solution.py:678
  (23 other events, 78.1 us)

commit v4 on v3

--- a/solution.py
+++ b/solution.py
@@ -285,7 +285,7 @@
 def down_kernel(
     where_ref, seg_ref, hid_ref, act_in, bdown_ref, wout_ref, bout_ref, patch_ref, lgrad_ref, dgrad_ref,
     own, near, far, far_other, cross, cross_other,
-    latent_ref, logdet_ref, stat_ref, direct_ref, grad_ref, gwout_ref, gvec_ref, keep_ref, send_near, send_far,
+    latent_ref, logdet_ref, mean_ref, max_ref, direct_ref, grad_ref, gwout_ref, gvec_ref, keep_ref, send_near, send_far,
     weight_ref, act_ref, total_ref, branch_ref, stage_ref, sems, act_sems, out_sems,
     *, length, quarter,
 ):
@@ -320,15 +320,15 @@
     latents = (patch_ref[...] - shifts) * shrink
     latent_ref[...] = latents
     logdet_ref[...] = -column_sum(logscale)
-    stats = jnp.zeros(stat_ref.shape, F32)
-    lane = lax.broadcasted_iota(jnp.int32, stat_ref.shape, 1)
-    kind = lax.broadcasted_iota(jnp.int32, stat_ref.shape, 0)
+    lane = lax.broadcasted_iota(jnp.int32, mean_ref.shape, 1)
+    means = jnp.zeros(mean_ref.shape, F32)
+    tops = means
     for row in range(row_count):
         part = logscale[:, row * length : (row + 1) * length]
-        mean = jnp.sum(part) * (1.0 / (length * channels))
-        stats = jnp.where((lane == row) & (kind == 0), mean, stats)
-        stats = jnp.where((lane == row) & (kind == 1), jnp.max(part), stats)
-    stat_ref[...] = stats
+        means = jnp.where(lane == row, jnp.sum(part) * (1.0 / (length * channels)), means)
+        tops = jnp.where(lane == row, jnp.max(part), tops)
+    mean_ref[...] = means
+    max_ref[...] = tops
     lgrad = lgrad_ref[...]
     direct = lgrad * shrink
     direct_ref[...] = direct
@@ -612,12 +612,14 @@
         ).wait()
 
 
-def add_kernel(*refs):
-    *sources, out_ref = refs
-    total = sources[0][...].astype(F32)
-    for ref in sources[1:]:
-        total = total + ref[...].astype(F32)
-    out_ref[...] = total.astype(BF)
+def add_kernel(*refs, counts):
+    sources, outs = refs[: sum(counts)], refs[sum(counts) :]
+    for count, out_ref in zip(counts, outs):
+        total = sources[0][...].astype(F32)
+        for ref in sources[1:count]:
+            total = total + ref[...].astype(F32)
+        out_ref[...] = total.astype(BF)
+        sources = sources[count:]
 
 
 def piece_list(low, high):
@@ -629,16 +631,26 @@
     return [(ref, i, j, 2 * x + z) for ref, i, j, x, z in found]
 
 
-def place_kernel(where_ref, low_ref, high_ref, out_ref):
+def place_kernel(where_ref, low_in, high_in, out, low_ref, high_ref, stage_ref, in_sems, out_sems):
     rows = low_ref.shape[2]
-    for ref, i, j, piece in piece_list(low_ref, high_ref):
-        at = pl.multiple_of((piece ^ where_ref[2]) * rows, rows)
-        out_ref[pl.ds(at, rows)] = ref[i, j].astype(F32)
+    start_copies([(low_in, low_ref), (high_in, high_ref)], in_sems)
+    pltpu.make_async_copy(low_in, low_ref, in_sems.at[0]).wait()
+    pieces = piece_list(low_ref, high_ref)
+    copies = []
+    for index, (ref, i, j, piece) in enumerate(pieces):
+        if index == 2:
+            pltpu.make_async_copy(high_in, high_ref, in_sems.at[1]).wait()
+        stage_ref[index] = ref[i, j].astype(F32)
+        at = pl.ds(pl.multiple_of((piece ^ where_ref[2]) * rows, rows), rows)
+        copies.append(pltpu.make_async_copy(stage_ref.at[index], out.at[at], out_sems.at[index]))
+        copies[-1].start()
+    for copy in copies:
+        copy.wait()
 
 
 def place_last_kernel(
-    where_ref, mix_low, mix_high, low_ref, high_ref, all_ref,
-    gk_ref, gv_ref, go_ref, gq_ref, gin_ref, gout_ref, gpos_ref, *rest,
+    where_ref, mix_low, mix_high, low_ref, high_ref, all_ref, cross_ref,
+    gk_ref, gv_ref, go_ref, gq_ref, gin_ref, gout_ref, gpos_ref, gbin_ref, *rest,
 ):
     *vectors, bup_ref, bout_ref, flat_ref = rest
     rows = gq_ref.shape[0] // PIECES
@@ -651,19 +663,22 @@
         at = pl.ds(pl.multiple_of((piece ^ where_ref[2]) * rows, rows), rows)
         gq_ref[at] = ref[i, j, :rows].astype(F32)
     channels = gin_ref.shape[0]
-    for slot in range(4):
-        rel = (0, 2, 1, 3)[slot]
-        for piece in range(PIECES):
-            group = (rel ^ where_ref[3]) * PIECES + (piece ^ where_ref[2])
-            flat_ref[pl.ds(pl.multiple_of(group * GROUP, GROUP), GROUP)] = all_ref[slot, piece].astype(F32)
+    for core, ref in enumerate((all_ref, cross_ref)):
+        for far in range(2):
+            for piece in range(PIECES):
+                head = (2 * far + core) ^ where_ref[3]
+                group = head * PIECES + (piece ^ where_ref[2])
+                flat_ref[pl.ds(pl.multiple_of(group * GROUP, GROUP), GROUP)] = ref[far, piece].astype(F32)
     start = 3 * channels
     gin_ref[...] = flat_ref[:channels]
     gout_ref[...] = flat_ref[channels:start]
     length = gpos_ref.shape[0]
     gpos_ref[...] = flat_ref[start : start + length]
     start += length
+    for index in range(gbin_ref.shape[0]):
+        gbin_ref[index : index + 1] = flat_ref[start : start + 1, index * 128 : (index + 1) * 128]
     for index, ref in enumerate(vectors):
-        ref[...] = flat_ref[start + index : start + index + 1]
+        ref[...] = flat_ref[start + 1 + index : start + 2 + index]
     bout_ref[...] = flat_ref[start + 6 : start + 7, : bout_ref.shape[1]]
     bup_ref[...] = flat_ref[pl.ds(start + 7 + where_ref[3], 1)]
 
@@ -719,14 +734,19 @@
         def view(self, array):
             return View(array.reshape((-1, 2, 2) + array.shape[-2:]))
 
-        def prepare(self, add=add_views):
+        def parts(self):
             kind = self.left[0]
             if kind == "y":
-                return [add([view.narrow(0, 1) for view in self.groups[-1]])]
+                return [[view.narrow(0, 1) for view in self.groups[-1]]]
             if "w" in self.left[1:]:
                 axis = self.axes[kind]
-                return [add([view.narrow(axis, 1) for view in group]) for group in self.groups]
-            return [add(self.groups[0])] if kind == "w" else [self.total]
+                return [[view.narrow(axis, 1) for view in group] for group in self.groups]
+            return [self.groups[0]]
+
+        def prepare(self):
+            if "w" in self.left:
+                return [add_views(part) for part in self.parts()]
+            return [self.total]
 
         def launch(self, sends):
             self.sends = sends
@@ -807,7 +827,14 @@
         )
         own_u, own_d = w_up[0], w_down[0]
         half_rows = width // 2
-        half_t = lax.dynamic_index_in_dim(pack_t, row_bit, 0, keepdims=False)
+        half_t = jnp.concatenate(
+            [
+                jnp.where(row_bit == 0, w_query[0].T, w_value[0].T),
+                jnp.where(row_bit == 0, w_key[0].T, w_attn_out[0]),
+                bias_rows,
+            ],
+            0,
+        )
         far_t = swap_heads(half_t, 2)
         near_t = swap_heads(ordered(pack_t, half_t), 1)
         half_u = lax.dynamic_slice_in_dim(own_u, row_bit * half_rows, half_rows, 0)
@@ -893,7 +920,7 @@
         one = shape(PIECES, rows, width, dtype=BF)
         stage = pltpu.VMEM((2, width, width), BF)
         out_sems = dma((2, PIECES))
-        latents, logdet, stats, direct, grad_hidden2, grad_w_out, gdown, keep_d, *sends_d = call(
+        latents, logdet, means, tops, direct, grad_hidden2, grad_w_out, gdown, keep_d, *sends_d = call(
             down_kernel,
             (
                 where, segments, hidden1, activated, b_down, w_out.T, b_out[:, None], patches_t, latent_grad.T,
@@ -902,10 +929,11 @@
             + parts_d,
             [SMEM, SMEM, VMEM, HBM] + [VMEM] * 6 + [HBM] * 6,
             (
-                shape(channels, tokens), shape(1, tokens), shape(8, 128), shape(channels, tokens),
+                shape(channels, tokens), shape(1, tokens), shape(1, row_count), shape(1, row_count),
+                shape(channels, tokens),
                 full, shape(2 * channels, width), shape(8, width), pieces, one, one,
             ),
-            (VMEM,) * 7 + (HBM,) * 3,
+            (VMEM,) * 8 + (HBM,) * 3,
             [
                 pltpu.VMEM((heads_size, width, width), BF),
                 pltpu.VMEM((heads_size, tokens, width), BF),
@@ -922,22 +950,24 @@
         chains = [Chain(order) for order in CHAIN_ORDERS]
         down, up, mix, last = chains
 
-        def add_pieces(views):
-            size = views[0].size
-            block = (views[0].array.shape[3] // 2, views[0].array.shape[4])
-
-            def spec(start):
+        def add_groups(*groups):
+            def spec(view, start):
+                size = view.size
+                block = (view.array.shape[3] // 2, view.array.shape[4])
+
                 def at(i):
                     return tuple(a // b for a, b in zip(start, size)) + (i, 0)
 
                 return pl.BlockSpec(size + block, at)
 
+            views = [view for group in groups for view in group]
             return pl.pallas_call(
-                add_kernel,
+                functools.partial(add_kernel, counts=tuple(len(group) for group in groups)),
                 grid=(2,),
-                in_specs=[spec(view.start) for view in views],
-                out_specs=spec((0, 0, 0)),
-                out_shape=shape(*size, 2 * block[0], block[1], dtype=BF),
+                in_specs=[spec(view, view.start) for view in views],
+                out_specs=[spec(group[0], (0, 0, 0)) for group in groups],
+                out_shape=[shape(*group[0].size, *group[0].array.shape[3:], dtype=BF) for group in groups],
+                compiler_params=pltpu.CompilerParams(vmem_limit_bytes=60 << 20),
                 cost_estimate=pl.CostEstimate(flops=1, transcendentals=0, bytes_accessed=1),
             )(*(view.array for view in views))
 
@@ -965,7 +995,7 @@
         )
         pre_grads, *got_d = tie(pre_grads, *got_d)
         down.groups = halves(down, keep_d, got_d)
-        pre_grads, *sends = tie(pre_grads, *down.prepare(add_pieces))
+        pre_grads, *sends = tie(pre_grads, *add_groups(*down.parts()))
         down.launch(sends)
         grad_hidden1, grad_mix, gup, keep_u, *sends_u = call(
             up_back_kernel,
@@ -1010,7 +1040,7 @@
         got_far = swap_heads(send_far, 1)
         down.deliver(got_d)
         up.groups = halves(up, keep_u, got_u)
-        total_far, *sends = tie(total_far, *down.prepare(add_pieces), *up.prepare(add_pieces))
+        total_far, *sends = tie(total_far, *add_groups(*down.parts(), *up.parts()))
         down.launch(sends[:1])
         up.launch(sends[1:])
         total_near, gq_near, keep_near, send_near = attend_back(saved_near, parts_near, total_far)
@@ -1018,7 +1048,7 @@
         got_near = swap_heads(send_near, 1)
         mix.groups = [[], [mix.view(keep_far), mix.view(got_far)]]
         down.deliver(got_d)
-        grad_hidden1, *sends = tie(grad_hidden1, *down.prepare(add_pieces), *mix.prepare(add_pieces))
+        grad_hidden1, *sends = tie(grad_hidden1, *add_groups(*down.parts(), *mix.parts()))
         down.launch(sends[:1])
         mix.launch(sends[1:])
         groups = 4 * PIECES
@@ -1042,8 +1072,9 @@
             length=length,
             quarter=quarter,
         )
-        patches_grad, send_q, *got_u = tie(patches_grad, send_q, *up.got)
-        patches_grad, got_near, *got_d = tie(patches_grad, got_near, *down.got)
+        patches_grad, *got_u = tie(patches_grad, *up.got)
+        patches_grad, *got_d = tie(patches_grad, *down.got)
+        patches_grad, send_q = tie(patches_grad, send_q)
         last.groups = [[last.view(keep_q), last.view(swap_heads(send_q, 1))]]
         mix.groups[0] = [mix.view(keep_near), mix.view(got_near)]
         down.got, up.got = got_d, got_u
@@ -1074,7 +1105,8 @@
                     small = small.reshape(1, PIECES, GROUP, width)
                 token = small = ordered(small, token)
                 small_got = swap_heads(small, heads_left.pop(0))
-                small = jnp.concatenate([small, small_got], 0)
+                if heads_left:
+                    small = jnp.concatenate([small, small_got], 0)
                 continue
             chain = chains[index]
             if index in pending:
@@ -1101,7 +1133,18 @@
 
         def place(chain):
             return call(
-                place_kernel, (where, chain.low, chain.high), [SMEM, VMEM, VMEM], shape(width, width), VMEM
+                place_kernel,
+                (where, chain.low, chain.high),
+                [SMEM, HBM, HBM],
+                shape(width, width),
+                HBM,
+                [
+                    pltpu.VMEM(chain.low.shape, BF),
+                    pltpu.VMEM(chain.high.shape, BF),
+                    pltpu.VMEM((PIECES, rows, width), F32),
+                    dma((2,)),
+                    dma((PIECES,)),
+                ],
             )
 
         sum_down, sum_up = place(down), place(up)
@@ -1109,11 +1152,12 @@
         line = shape(1, width)
         sum_k, sum_v, sum_o, sum_q, sum_w_in, sum_w_out, sum_pos, *lines = call(
             place_last_kernel,
-            (where, mix.low, mix.high, last.low, last.high, small),
-            [SMEM] + [VMEM] * 5,
+            (where, mix.low, mix.high, last.low, last.high, small, small_got),
+            [SMEM] + [VMEM] * 6,
             (units,) * 4
             + (shape(channels, width), shape(2 * channels, width), shape(length, width))
-            + (line,) * 7
+            + (shape(width // 128, 128),)
+            + (line,) * 6
             + (shape(1, 2 * channels),),
             (VMEM,) * 15,
             [pltpu.VMEM((groups * GROUP, width), F32)],
@@ -1123,8 +1167,8 @@
             latents.T,
             logdet.reshape(tokens),
             patches_grad.T,
-            stats[0, :row_count],
-            stats[1, :row_count],
+            means.reshape(row_count),
+            tops.reshape(row_count),
             sum_w_in,
             sum_b_in.reshape(width),
             sum_pos,

time: 276 us -> 266 us (0.964)
  other arithmetic: 17.6 us -> 11.1 us
  starting transfers between devices: 48.9 us -> 54 us
  waiting for transfers between devices: 58.9 us -> 54.6 us
  Pallas kernels: 135 us -> 131 us
    ppermute x28, waiting for transfers between devices: 45.6 us -> 35 us  [swap_rows(): return lax.ppermute(array, 'rows', [(i, i ^ bit) for i in range(rows_size)])]
    ppermute x27, waiting for transfers between devices: 13.3 us -> 19.6 us  [swap_heads(): lax.ppermute(array, 'heads', [(i, i ^ bit) for i in range(heads_size)])]
    ppermute x28, starting transfers between devices: 33.6 us -> 39.6 us  [swap_rows(): return lax.ppermute(array, 'rows', [(i, i ^ bit) for i in range(rows_size)])]
    pallas_call x6 -> x3, Pallas kernels: 13.2 us -> 8.72 us  [add_groups(): pl.pallas_call(functools.partial(add_kernel, counts=tuple((len(group) for...]
    convert_element_type x15, other arithmetic: 9 us -> 6.17 us  [add_low(): return total.astype(BF)]
    unnamed x65 -> x77, local copies, waits for them, and re-layouts: 6.24 us -> 6.19 us
  transfers between devices with their start and end apart: 55 -> 55, of which waited for: 19 -> 19; matrix products, arithmetic and copies ran while one was open for 8% -> 6% of each run, Pallas kernels for 42% -> 42%
where the time goes in v4:
time: 266 us; the launch traced here: 265 us
  Pallas kernels  131 us (49%)
  waiting for transfers between devices  54.6 us (21%)
  starting transfers between devices  54 us (20%)
  other arithmetic  11.1 us (4%)
  local copies, waits for them, and re-layouts  10.3 us (4%)
    pallas_call x13, Pallas kernels, call(): pl.pallas_call(functools.partial(kernel, **options) if options else kerne...  122 us
    ppermute x28, starting transfers between devices, swap_rows(): return lax.ppermute(array, 'rows', [(i, i ^ bit) for i in range(rows_size)])  39.6 us
    ppermute x28, waiting for transfers between devices, swap_rows(): return lax.ppermute(array, 'rows', [(i, i ^ bit) for i in range(rows_size)])  35 us
    ppermute x27, waiting for transfers between devices, swap_heads(): lax.ppermute(array, 'heads', [(i, i ^ bit) for i in range(heads_size)])  19.6 us
    ppermute x27, starting transfers between devices, swap_heads(): lax.ppermute(array, 'heads', [(i, i ^ bit) for i in range(heads_size)])  14.4 us
    pallas_call x3, Pallas kernels, add_groups(): pl.pallas_call(functools.partial(add_kernel, counts=tuple((len(group) for...  8.72 us
    unnamed x77, local copies, waits for them, and re-layouts  6.19 us
    convert_element_type x15, other arithmetic, add_low(): return total.astype(BF)  6.17 us
  transfers between devices with their start and end apart: 55, of which 19 were waited for; matrix products, arithmetic and copies ran while one was open for 6% of the time, Pallas kernels for 42%

profile of v4, /device:TPU:0, one launch (start us, length us, event | category | flops | bytes accessed | tf_op | source)
XLA Modules:
  0.0 264.8 jit_solution(2668590042024722877)
XLA Ops:
  0.7 1.4 broadcast_select_fusion
  4.0 2.6 collective-permute-start
  8.4 2.1 dynamic-slice_bitcast_fusion
  11.2 3.0 %shard_map.398 = (f32[512,768]{1,0:T(8,128)}, bf16[512,768]{1,0:T(8,128)(2,1)}) custom-call(s32[4]{0:T(128)} %pad_add_fusion.where_ref, s32[2048]{0:T(1024)} %seg_ref.9, f32[48,512]{1,0:T(8,128)} %bitcast.188, bf16[48,768]{1,0:T(8,128)(2,1)} %win_ref.1, f32[1,768]{1,0:T(1,128)} %broadcast_in_dim.29.b_ref, bf16[256,768]{1,0:T(8,128)(2,1)} %pos_ref.1, ...), custom_call_target="tpu_custom_call" | custom-call | flops 1 | bytes 1 | tf_op jit(solution)/shard_map/pallas_call | solution.py:804
  14.2 7.0 %collective-permute-done.rest_0_.far_t = bf16[400,768]{1,0:T(8,128)(2,1)S(1)} collective-permute-done((bf16[400,768]{1,0:T(8,128)(2,1)}, bf16[400,768]{1,0:T(8,128)(2,1)S(1)}, u32[]{:S(2)}, u32[]{:S(2)}) %collective-permute-start) | collective-permute-done | bytes 614432 | tf_op jit(solution)/shard_map/ppermute | solution.py:690
  21.2 1.7 collective-permute-start.2
  23.0 1.5 collective-permute-start.3
  24.5 11.4 %shard_map.399 = (bf16[512,384]{1,0:T(8,128)(2,1)}, bf16[512,384]{1,0:T(8,128)(2,1)}, bf16[512,384]{1,0:T(8,128)(2,1)}, bf16[12,256,256]{2,1,0:T(8,128)(2,1)}, b...) custom-call(s32[4]{0:T(128)} %pad_add_fusion.where_ref, s32[2048]{0:T(1024)} %seg_ref.9, ...), custom_call_target="tpu_custom_call" | custom-call | flops 1 | bytes 1 | tf_op jit(solution)/shard_map/pallas_call | solution.py:804
  36.0 1.6 collective-permute-done.3.far
  37.6 1.6 collective-permute-start.7
  40.5 11.2 %shard_map.400 = (bf16[512,384]{1,0:T(8,128)(2,1)}, bf16[512,384]{1,0:T(8,128)(2,1)}, bf16[512,384]{1,0:T(8,128)(2,1)}, bf16[12,256,256]{2,1,0:T(8,128)(2,1)}, b...) custom-call(s32[4]{0:T(128)} %pad_add_fusion.where_ref, s32[2048]{0:T(1024)} %seg_ref.9, ...), custom_call_target="tpu_custom_call" | custom-call | flops 1 | bytes 1 | tf_op jit(solution)/shard_map/pallas_call | solution.py:804
  51.7 1.9 collective-permute-done.7.far
  53.6 1.2 collective-permute-done.6.far_other
  57.2 14.1 %shard_map.401 = (bf16[512,768]{1,0:T(8,128)(2,1)}, bf16[4,512,768]{2,1,0:T(8,128)(2,1)}, bf16[4,512,768]{2,1,0:T(8,128)(2,1)}) custom-call(s32[4]{0:T(128)} %pad_add_fusion.where_ref, f32[512,768]{1,0:T(8,128)} %get-tuple-element.207.hid_ref, f32[1,768]{1,0:T(1,128)} %gain_ref.6, f32[1,768]{1,0:T(1,128)} %bias_ref.3, bf16[768,768]{1,0:T(8,128)(2,1)} %bitcast.156, ...), custom_call_target="tpu_custom_call" | custom-call | flops 1 | bytes 1 | tf_op jit(solution)/shard_map/pallas_call | solution.py:804
  72.3 1.1 collective-permute-done.14.cross_other
  74.2 13.5 %shard_map.402 = (f32[48,512]{1,0:T(8,128)}, f32[1,512]{1,0:T(1,128)}, f32[1,2]{1,0:T(1,128)}, f32[1,2]{1,0:T(1,128)}, f32[48,512]{1,0:T(8,128)}, /*index=5*/f32...) custom-call(s32[4]{0:T(128)} %pad_add_fusion.where_ref, ...), custom_call_target="tpu_custom_call" | custom-call | flops 1 | bytes 1 | tf_op jit(solution)/shard_map/pallas_call | solution.py:804
  88.3 8.3 %shard_map.403 = (bf16[4,512,768]{2,1,0:T(8,128)(2,1)}, f32[8,768]{1,0:T(8,128)}) custom-call(s32[4]{0:T(128)} %pad_add_fusion.where_ref, f32[512,768]{1,0:T(8,128)} %get-tuple-element.220.grad_ref, bf16[4,512,768]{2,1,0:T(8,128)(2,1)} %get-tuple-element.221.slope_in, bf16[768,768]{1,0:T(8,128)(2,1)} %bitcast.154, ...), custom_call_target="tpu_custom_call" | custom-call | flops 1 | bytes 1 | tf_op jit(solution)/shard_map/pallas_call | solution.py:804
  96.7 1.0 copy-done.23
  97.7 2.6 shard_map.404
  100.8 13.7 %shard_map.405 = (f32[512,768]{1,0:T(8,128)}, bf16[512,768]{1,0:T(8,128)(2,1)}, f32[8,768]{1,0:T(8,128)}, bf16[2,4,192,768]{3,2,1,0:T(8,128)(2,1)}, bf16[4,192,7...) custom-call(s32[4]{0:T(128)} %pad_add_fusion.where_ref, f32[512,768]{1,0:T(8,128)} %get-tuple-element.220.grad_ref, ...), custom_call_target="tpu_custom_call" | custom-call | flops 1 | bytes 1 | tf_op jit(solution)/shard_map/pallas_call | solution.py:804
  115.1 14.1 %shard_map.406 = (f32[512,768]{1,0:T(8,128)}, bf16[384,768]{1,0:T(8,128)(2,1)}, bf16[4,144,768]{2,1,0:T(8,128)(2,1)}, bf16[4,144,768]{2,1,0:T(8,128)(2,1)}) custom-call(s32[4]{0:T(128)} %pad_add_fusion.where_ref, bf16[512,768]{1,0:T(8,128)(2,1)} %get-tuple-element.235.mix_ref, bf16[512,384]{1,0:T(8,128)(2,1)} %get-tuple-element.236.q_ref, ...), custom_call_target="tpu_custom_call" | custom-call | flops 1 | bytes 1 | tf_op jit(solution)/shard_map/pallas_call | solution.py:804
  131.0 3.3 %shard_map.407 = (bf16[1,1,2,192,768]{4,3,2,1,0:T(8,128)(2,1)}, bf16[1,2,1,192,768]{4,3,2,1,0:T(8,128)(2,1)}, bf16[1,2,1,192,768]{4,3,2,1,0:T(8,128)(2,1)}) custom-call(bf16[2,2,2,192,768]{4,3,2,1,0:T(8,128)(2,1)} %bitcast.145, bf16[1,2,2,192,768]{4,3,2,1,0:T(8,128)(2,1)} %bitcast.159, bf16[1,2,2,192,768]{4,3,2,1,0:T(8,128)(2,1)} %copy-done.7, ...), custom_call_target="tpu_custom_call" | custom-call | flops 1 | bytes 1 | tf_op jit(solution)/shard_map/pallas_call | solution.py:964
  134.3 1.0 collective-permute-start.21
  135.3 1.6 collective-permute-start.22
  137.3 14.4 %shard_map.408 = (f32[512,768]{1,0:T(8,128)}, bf16[384,768]{1,0:T(8,128)(2,1)}, bf16[4,144,768]{2,1,0:T(8,128)(2,1)}, bf16[4,144,768]{2,1,0:T(8,128)(2,1)}) custom-call(s32[4]{0:T(128)} %pad_add_fusion.where_ref, bf16[512,768]{1,0:T(8,128)(2,1)} %get-tuple-element.235.mix_ref, bf16[512,384]{1,0:T(8,128)(2,1)} %get-tuple-element.245.q_ref, ...), custom_call_target="tpu_custom_call" | custom-call | flops 1 | bytes 1 | tf_op jit(solution)/shard_map/pallas_call | solution.py:804
  152.6 2.9 %shard_map.409 = (bf16[1,1,1,192,768]{4,3,2,1,0:T(8,128)(2,1)}, bf16[1,2,2,144,768]{4,3,2,1,0:T(8,128)(2,1)}) custom-call(bf16[2,2,2,192,768]{4,3,2,1,0:T(8,128)(2,1)} %bitcast.146, bf16[1,2,2,192,768]{4,3,2,1,0:T(8,128)(2,1)} %bitcast.160, bf16[1,2,2,192,768]{4,3,2,1,0:T(8,128)(2,1)} %copy-done.7, bf16[1,1,2,192,768]{4,3,2,1,0:T(8,128)(2,1)} %copy-done.21, ...), custom_call_target="tpu_custom_call" | custom-call | flops 1 | bytes 1 | tf_op jit(solution)/shard_map/pallas_call | solution.py:964
  155.4 1.6 collective-permute-start.24
  157.0 8.4 %shard_map.410 = (f32[48,512]{1,0:T(8,128)}, f32[8,896]{1,0:T(8,128)}, bf16[2,4,80,768]{3,2,1,0:T(8,128)(2,1)}, bf16[2,4,80,768]{3,2,1,0:T(8,128)(2,1)}) custom-call(s32[4]{0:T(128)} %pad_add_fusion.where_ref, s32[2048]{0:T(1024)} %seg_ref.9, s32[2,4]{1,0:T(2,128)} %label_ref.1, f32[512,768]{1,0:T(8,128)} %get-tuple-element.270.grad_ref, ...), custom_call_target="tpu_custom_call" | custom-call | flops 1 | bytes 1 | tf_op jit(solution)/shard_map/pallas_call | solution.py:804
  165.4 4.2 %collective-permute-done.24 = bf16[1,1,1,192,768]{4,3,2,1,0:T(8,128)(2,1)S(1)} collective-permute-done((bf16[1,1,1,192,768]{4,3,2,1,0:T(8,128)(2,1)}, bf16[1,1,1,192,768]{4,3,2,1,0:T(8,128)(2,1)S(1)}, u32[]{:S(2)}, u32[]{:S(2)}) %collective-permute-start.24) | collective-permute-done | bytes 294944 | tf_op jit(solution)/shard_map/ppermute | solution.py:693
  170.4 1.5 collective-permute-start.26
  172.1 1.4 add_convert_fusion.7
  173.5 1.1 collective-permute-start.32
  175.7 1.6 collective-permute-start.28
  177.4 1.4 add_convert_fusion.6
  178.8 4.6 %collective-permute-done.32 = bf16[1,1,1,192,768]{4,3,1,2,0:T(8,128)(2,1)S(1)} collective-permute-done((bf16[1,1,1,192,768]{4,3,1,2,0:T(8,128)(2,1)S(1)}, bf16[1,1,1,192,768]{4,3,1,2,0:T(8,128)(2,1)S(1)}, u32[]{:S(2)}, u32[]{:S(2)}) %collective-permute-start.32) | collective-permute-done | bytes 294944 | tf_op jit(solution)/shard_map/ppermute | solution.py:693
  183.4 2.6 collective-permute-start.34
  186.0 3.1 %collective-permute-done.29 = bf16[1,1,1,192,768]{4,3,1,2,0:T(8,128)(2,1)S(1)} collective-permute-done((bf16[1,1,1,192,768]{4,3,1,2,0:T(8,128)(2,1)S(1)}, bf16[1,1,1,192,768]{4,3,1,2,0:T(8,128)(2,1)S(1)}, u32[]{:S(2)}, u32[]{:S(2)}) %collective-permute-start.29) | collective-permute-done | bytes 294944 | tf_op jit(solution)/shard_map/ppermute | solution.py:693
  189.1 2.6 collective-permute-start.36
  191.7 1.2 add_convert_fusion.5
  193.6 1.6 collective-permute-start.31
  195.3 1.1 collective-permute-start.30
  196.5 1.6 collective-permute-start.39
  198.1 4.8 %collective-permute-done.33 = bf16[1,1,1,192,768]{4,3,1,2,0:T(8,128)(2,1)S(1)} collective-permute-done((bf16[1,1,1,192,768]{4,3,1,2,0:T(8,128)(2,1)S(1)}, bf16[1,1,1,192,768]{4,3,1,2,0:T(8,128)(2,1)S(1)}, u32[]{:S(2)}, u32[]{:S(2)}) %collective-permute-start.33) | collective-permute-done | bytes 294944 | tf_op jit(solution)/shard_map/ppermute | solution.py:690
  202.9 1.2 add_convert_fusion.4
  204.5 1.9 collective-permute-done.31
  206.4 1.1 collective-permute-start.37
  207.6 1.7 collective-permute-start.35
  209.3 2.0 collective-permute-done.37
  212.3 1.6 collective-permute-start.44
  213.9 8.5 %collective-permute-done.35 = bf16[1,1,1,144,768]{4,3,2,1,0:T(8,128)(2,1)S(1)} collective-permute-done((bf16[1,1,1,144,768]{4,3,2,1,0:T(8,128)(2,1)S(1)}, bf16[1,1,1,144,768]{4,3,2,1,0:T(8,128)(2,1)S(1)}, u32[]{:S(2)}, u32[]{:S(2)}) %collective-permute-start.35) | collective-permute-done | bytes 221216 | tf_op jit(solution)/shard_map/ppermute | solution.py:693
  222.6 1.8 collective-permute-start.38
  224.3 1.7 collective-permute-start.40
  226.6 1.7 collective-permute-start.47
  229.1 1.0 collective-permute-start.43
  231.1 4.4 %collective-permute-start.48 = (bf16[1,2,1,80,768]{4,3,1,2,0:T(8,128)(2,1)S(1)}, bf16[1,2,1,80,768]{4,3,1,2,0:T(8,128)(2,1)S(1)}, u32[]{:S(2)}, u32[]{:S(2)}) collective-permute-start(bf16[1,2,1,80,768]{4,3,1,2,0:T(8,128)(2,1)S(1)} %pad_maximum_fusion.5), channel_id=1, source_target_pairs={{0,8},{4,12},{8,0},{12,4},{16,24},{20,28},{24,16},{28,20},{1,9},{5... | collective-permute-start | bytes 737288 | tf_op jit(solution)/shard_map/ppermute | solution.py:693
  235.8 1.1 collective-permute-start.46
  236.9 3.9 %collective-permute-done.48 = bf16[1,2,1,80,768]{4,3,1,2,0:T(8,128)(2,1)S(1)} collective-permute-done((bf16[1,2,1,80,768]{4,3,1,2,0:T(8,128)(2,1)S(1)}, bf16[1,2,1,80,768]{4,3,1,2,0:T(8,128)(2,1)S(1)}, u32[]{:S(2)}, u32[]{:S(2)}) %collective-permute-start.48) | collective-permute-done | bytes 245792 | tf_op jit(solution)/shard_map/ppermute | solution.py:693
  241.0 2.5 collective-permute-start.53
  243.6 1.9 collective-permute-done.46
  246.9 2.2 fusion.1
  250.0 3.2 %shard_map.413 = f32[768,768]{1,0:T(8,128)} custom-call(s32[4]{0:T(128)} %pad_add_fusion.where_ref, bf16[1,2,192,768]{3,2,1,0:T(8,128)(2,1)} %bitcast.170, bf16[1,2,192,768]{3,2,1,0:T(8,128)(2,1)} %bitcast.200), custom_call_target="tpu_custom_call" | custom-call | flops 1 | bytes 1 | tf_op jit(solution)/shard_map/pallas_call | solution.py:804
  253.2 3.8 %collective-permute-done.53 = bf16[1,2,1,192,768]{4,3,1,2,0:T(8,128)(2,1)S(1)} collective-permute-done((bf16[1,2,1,192,768]{4,3,1,2,0:T(8,128)(2,1)S(1)}, bf16[1,2,1,192,768]{4,3,1,2,0:T(8,128)(2,1)S(1)}, u32[]{:S(2)}, u32[]{:S(2)}) %collective-permute-start.53) | collective-permute-done | bytes 589856 | tf_op jit(solution)/shard_map/ppermute | solution.py:693
  257.8 3.3 %shard_map.412 = f32[768,768]{1,0:T(8,128)} custom-call(s32[4]{0:T(128)} %pad_add_fusion.where_ref, bf16[2,1,192,768]{3,2,1,0:T(8,128)(2,1)} %bitcast.171, bf16[2,1,192,768]{3,2,1,0:T(8,128)(2,1)} %bitcast.201), custom_call_target="tpu_custom_call" | custom-call | flops 1 | bytes 1 | tf_op jit(solution)/shard_map/pallas_call | solution.py:804
  261.2 3.5 %shard_map.411 = (f32[192,768]{1,0:T(8,128)}, f32[192,768]{1,0:T(8,128)}, f32[192,768]{1,0:T(8,128)}, f32[192,768]{1,0:T(8,128)}, f32[48,768]{1,0:T(8,128)}, /*i...) custom-call(s32[4]{0:T(128)} %pad_add_fusion.where_ref, ...), custom_call_target="tpu_custom_call" | custom-call | flops 1 | bytes 1 | tf_op jit(solution)/shard_map/pallas_call | solution.py:804
  (183 shorter events, 24.8 us)
Async XLA Ops:
  3.4 7.1 %copy-start.2 = (bf16[2,400,768]{2,1,0:T(8,128)(2,1)}, bf16[2,400,768]{2,1,0:T(8,128)(2,1)S(1)}, u32[]{:S(2)}) copy-start(bf16[2,400,768]{2,1,0:T(8,128)(2,1)S(1)} %pad_maximum_fusion.rest_0_.own_t.rest_1_) | copy-start | bytes 3686404
  3.5 21.0 %collective-permute-start.1 = (bf16[2,400,768]{2,1,0:T(8,128)(2,1)S(1)}, bf16[2,400,768]{2,1,0:T(8,128)(2,1)}, u32[]{:S(2)}, u32[]{:S(2)}) collective-permute-start(bf16[2,400,768]{2,1,0:T(8,128)(2,1)S(1)} %pad_maximum_fusion.rest_0_.own_t.rest_1_), channel_id=1, source_target_pairs={{0,1},{1,0},{2,3},{3,2},{4,5},{5,4},{6,7},{7,6},{8,9},{9,8},{10,11... | collective-permute-start | bytes 3686408 | tf_op jit(solution)/shard_map/ppermute | solution.py:690
  4.0 17.3 %collective-permute-start = (bf16[400,768]{1,0:T(8,128)(2,1)}, bf16[400,768]{1,0:T(8,128)(2,1)S(1)}, u32[]{:S(2)}, u32[]{:S(2)}) collective-permute-start(bf16[400,768]{1,0:T(8,128)(2,1)} %get-tuple-element.368), channel_id=1, source_target_pairs={{0,2},{1,3},{2,0},{3,1},{4,6},{5,7},{6,4},{7,5},{8,10},{9,11},{10,... | collective-permute-start | bytes 1843208 | tf_op jit(solution)/shard_map/ppermute | solution.py:690
  21.2 14.7 %copy-start.8 = (bf16[400,768]{1,0:T(8,128)(2,1)}, bf16[400,768]{1,0:T(8,128)(2,1)S(1)}, u32[]{:S(2)}) copy-start(bf16[400,768]{1,0:T(8,128)(2,1)S(1)} %collective-permute-done.rest_0_.far_t) | copy-start | bytes 1843204
  21.2 16.3 %collective-permute-start.2 = (bf16[400,768]{1,0:T(8,128)(2,1)S(1)}, bf16[400,768]{1,0:T(8,128)(2,1)}, u32[]{:S(2)}, u32[]{:S(2)}) collective-permute-start(bf16[400,768]{1,0:T(8,128)(2,1)S(1)} %collective-permute-done.rest_0_.far_t), channel_id=1, source_target_pairs={{0,4},{4,0},{8,12},{12,8},{16,20},{20,16},{24,28},{28,24},{1,5},{5... | collective-permute-start | bytes 1843208 | tf_op jit(solution)/shard_map/ppermute | solution.py:693
  23.0 14.6 %collective-permute-start.3 = (bf16[384,768]{1,0:T(8,128)(2,1)S(1)}, bf16[384,768]{1,0:T(8,128)(2,1)S(1)}, u32[]{:S(2)}, u32[]{:S(2)}) collective-permute-start(bf16[384,768]{1,0:T(8,128)(2,1)S(1)} %get-tuple-element.194), channel_id=1, source_target_pairs={{0,2},{1,3},{2,0},{3,1},{4,6},{5,7},{6,4},{7,5},{8,10},{9,11},{10,... | collective-permute-start | bytes 1769480 | tf_op jit(solution)/shard_map/ppermute | solution.py:690
  24.5 15.5 %collective-permute-start.4 = (bf16[400,768]{1,0:T(8,128)(2,1)S(1)}, bf16[400,768]{1,0:T(8,128)(2,1)}, u32[]{:S(2)}, u32[]{:S(2)}) collective-permute-start(bf16[400,768]{1,0:T(8,128)(2,1)S(1)} %collective-permute-done.rest_0_.far_t), channel_id=1, source_target_pairs={{0,1},{1,0},{2,3},{3,2},{4,5},{5,4},{6,7},{7,6},{8,9},{9,8},{10,11... | collective-permute-start | bytes 1843208 | tf_op jit(solution)/shard_map/ppermute | solution.py:690
  24.5 15.5 %copy-start.5 = (bf16[1,768,768]{2,1,0:T(8,128)(2,1)S(1)}, bf16[1,768,768]{2,1,0:T(8,128)(2,1)}, u32[]{:S(2)}) copy-start(bf16[1,768,768]{2,1,0:T(8,128)(2,1)} %param.38) | copy-start | bytes 3538948
  37.6 3.0 %collective-permute-start.5 = (bf16[400,768]{1,0:T(8,128)(2,1)}, bf16[400,768]{1,0:T(8,128)(2,1)}, u32[]{:S(2)}, u32[]{:S(2)}) collective-permute-start(bf16[400,768]{1,0:T(8,128)(2,1)} %collective-permute-done.2.rest_1_), channel_id=1, source_target_pairs={{0,1},{1,0},{2,3},{3,2},{4,5},{5,4},{6,7},{7,6},{8,9},{9,8},{10,11... | collective-permute-start | bytes 1843208 | tf_op jit(solution)/shard_map/ppermute | solution.py:690
  37.6 16.1 %collective-permute-start.7 = (bf16[384,768]{1,0:T(8,128)(2,1)}, bf16[384,768]{1,0:T(8,128)(2,1)}, u32[]{:S(2)}, u32[]{:S(2)}) collective-permute-start(bf16[384,768]{1,0:T(8,128)(2,1)} %get-tuple-element.195), channel_id=1, source_target_pairs={{0,2},{1,3},{2,0},{3,1},{4,6},{5,7},{6,4},{7,5},{8,10},{9,11},{10,... | collective-permute-start | bytes 1769480 | tf_op jit(solution)/shard_map/ppermute | solution.py:690
  39.2 16.6 %copy-start.4 = (bf16[1,768,768]{2,1,0:T(8,128)(2,1)S(1)}, bf16[1,768,768]{2,1,0:T(8,128)(2,1)}, u32[]{:S(2)}) copy-start(bf16[1,768,768]{2,1,0:T(8,128)(2,1)} %param.40) | copy-start | bytes 3538948
  39.2 15.7 %collective-permute-start.6 = (bf16[384,768]{1,0:T(8,128)(2,1)}, bf16[384,768]{1,0:T(8,128)(2,1)}, u32[]{:S(2)}, u32[]{:S(2)}) collective-permute-start(bf16[384,768]{1,0:T(8,128)(2,1)} %copy-done.17), channel_id=1, source_target_pairs={{0,4},{4,0},{8,12},{12,8},{16,20},{20,16},{24,28},{28,24},{1,5},{5... | collective-permute-start | bytes 1769480 | tf_op jit(solution)/shard_map/ppermute | solution.py:693
  40.0 16.0 %collective-permute-start.8 = (bf16[768,768]{1,0:T(8,128)(2,1)S(1)}, bf16[768,768]{1,0:T(8,128)(2,1)}, u32[]{:S(2)}, u32[]{:S(2)}) collective-permute-start(bf16[768,768]{1,0:T(8,128)(2,1)S(1)} %bitcast.158), channel_id=1, source_target_pairs={{0,1},{1,0},{2,3},{3,2},{4,5},{5,4},{6,7},{7,6},{8,9},{9,8},{10,11... | collective-permute-start | bytes 3538952 | tf_op jit(solution)/shard_map/ppermute | solution.py:690
  40.0 16.3 %collective-permute-start.9 = (bf16[384,768]{1,0:T(8,128)(2,1)}, bf16[384,768]{1,0:T(8,128)(2,1)}, u32[]{:S(2)}, u32[]{:S(2)}) collective-permute-start(bf16[384,768]{1,0:T(8,128)(2,1)} %copy-done.17), channel_id=1, source_target_pairs={{0,1},{1,0},{2,3},{3,2},{4,5},{5,4},{6,7},{7,6},{8,9},{9,8},{10,11... | collective-permute-start | bytes 1769480 | tf_op jit(solution)/shard_map/ppermute | solution.py:690
  54.9 2.3 collective-permute-start.10
  54.9 16.4 %collective-permute-start.12 = (bf16[384,768]{1,0:T(8,128)(2,1)}, bf16[384,768]{1,0:T(8,128)(2,1)S(1)}, u32[]{:S(2)}, u32[]{:S(2)}) collective-permute-start(bf16[384,768]{1,0:T(8,128)(2,1)} %collective-permute-done.7.far), channel_id=1, source_target_pairs={{0,4},{4,0},{8,12},{12,8},{16,20},{20,16},{24,28},{28,24},{1,5},{5... | collective-permute-start | bytes 1769480 | tf_op jit(solution)/shard_map/ppermute | solution.py:693
  55.8 15.7 %copy-start.37 = (f32[96]{0:T(128)S(1)}, f32[96]{0:T(128)}, u32[]{:S(2)}) copy-start(f32[96]{0:T(128)} %param.43) | copy-start | bytes 1156
  55.8 16.5 %collective-permute-start.11 = (bf16[768,768]{1,0:T(8,128)(2,1)S(1)}, bf16[768,768]{1,0:T(8,128)(2,1)}, u32[]{:S(2)}, u32[]{:S(2)}) collective-permute-start(bf16[768,768]{1,0:T(8,128)(2,1)S(1)} %bitcast.155), channel_id=1, source_target_pairs={{0,1},{1,0},{2,3},{3,2},{4,5},{5,4},{6,7},{7,6},{8,9},{9,8},{10,11... | collective-permute-start | bytes 3538952 | tf_op jit(solution)/shard_map/ppermute | solution.py:690
  56.0 16.2 %collective-permute-start.13 = (bf16[384,768]{1,0:T(8,128)(2,1)}, bf16[384,768]{1,0:T(8,128)(2,1)S(1)}, u32[]{:S(2)}, u32[]{:S(2)}) collective-permute-start(bf16[384,768]{1,0:T(8,128)(2,1)} %collective-permute-done.7.far), channel_id=1, source_target_pairs={{0,1},{1,0},{2,3},{3,2},{4,5},{5,4},{6,7},{7,6},{8,9},{9,8},{10,11... | collective-permute-start | bytes 1769480 | tf_op jit(solution)/shard_map/ppermute | solution.py:690
  71.3 2.1 collective-permute-start.14
  87.7 8.9 %collective-permute-start.15 = (bf16[4,192,768]{2,1,0:T(8,128)(2,1)}, bf16[4,192,768]{2,1,0:T(8,128)(2,1)S(1)}, u32[]{:S(2)}, u32[]{:S(2)}) collective-permute-start(bf16[4,192,768]{2,1,0:T(8,128)(2,1)} %get-tuple-element.223), channel_id=1, source_target_pairs={{0,1},{1,0},{2,3},{3,2},{4,5},{5,4},{6,7},{7,6},{8,9},{9,8},{10,11... | collective-permute-start | bytes 3538952 | tf_op jit(solution)/shard_map/ppermute | solution.py:690
  87.9 8.7 %collective-permute-start.16 = (bf16[4,192,768]{2,1,0:T(8,128)(2,1)}, bf16[4,192,768]{2,1,0:T(8,128)(2,1)S(1)}, u32[]{:S(2)}, u32[]{:S(2)}) collective-permute-start(bf16[4,192,768]{2,1,0:T(8,128)(2,1)} %get-tuple-element.224), channel_id=1, source_target_pairs={{0,1},{1,0},{2,3},{3,2},{4,5},{5,4},{6,7},{7,6},{8,9},{9,8},{10,11... | collective-permute-start | bytes 3538952 | tf_op jit(solution)/shard_map/ppermute | solution.py:690
  100.3 29.0 %collective-permute-start.17 = (bf16[1,2,2,192,768]{4,3,2,1,0:T(8,128)(2,1)}, bf16[1,2,2,192,768]{4,3,2,1,0:T(8,128)(2,1)S(1)}, u32[]{:S(2)}, u32[]{:S(2)}) collective-permute-start(bf16[1,2,2,192,768]{4,3,2,1,0:T(8,128)(2,1)} %shard_map.404), channel_id=1, source_target_pairs={{0,2},{1,3},{2,0},{3,1},{4,6},{5,7},{6,4},{7,5},{8,10},{9,11},{10,... | collective-permute-start | bytes 3538952 | tf_op jit(solution)/shard_map/ppermute | solution.py:690
  114.5 14.9 %collective-permute-start.18 = (bf16[4,192,768]{2,1,0:T(8,128)(2,1)}, bf16[4,192,768]{2,1,0:T(8,128)(2,1)S(1)}, u32[]{:S(2)}, u32[]{:S(2)}) collective-permute-start(bf16[4,192,768]{2,1,0:T(8,128)(2,1)} %get-tuple-element.251), channel_id=1, source_target_pairs={{0,1},{1,0},{2,3},{3,2},{4,5},{5,4},{6,7},{7,6},{8,9},{9,8},{10,11... | collective-permute-start | bytes 3538952 | tf_op jit(solution)/shard_map/ppermute | solution.py:690
  114.6 14.8 %collective-permute-start.19 = (bf16[4,192,768]{2,1,0:T(8,128)(2,1)}, bf16[4,192,768]{2,1,0:T(8,128)(2,1)S(1)}, u32[]{:S(2)}, u32[]{:S(2)}) collective-permute-start(bf16[4,192,768]{2,1,0:T(8,128)(2,1)} %get-tuple-element.252), channel_id=1, source_target_pairs={{0,1},{1,0},{2,3},{3,2},{4,5},{5,4},{6,7},{7,6},{8,9},{9,8},{10,11... | collective-permute-start | bytes 3538952 | tf_op jit(solution)/shard_map/ppermute | solution.py:690
  129.3 22.5 %collective-permute-start.20 = (bf16[4,144,768]{2,1,0:T(8,128)(2,1)}, bf16[4,144,768]{2,1,0:T(8,128)(2,1)}, u32[]{:S(2)}, u32[]{:S(2)}) collective-permute-start(bf16[4,144,768]{2,1,0:T(8,128)(2,1)} %get-tuple-element.263), channel_id=1, source_target_pairs={{0,1},{1,0},{2,3},{3,2},{4,5},{5,4},{6,7},{7,6},{8,9},{9,8},{10,11... | collective-permute-start | bytes 2654216 | tf_op jit(solution)/shard_map/ppermute | solution.py:690
  134.3 17.4 %collective-permute-start.21 = (bf16[1,1,2,192,768]{4,3,2,1,0:T(8,128)(2,1)}, bf16[1,1,2,192,768]{4,3,2,1,0:T(8,128)(2,1)S(1)}, u32[]{:S(2)}, u32[]{:S(2)}) collective-permute-start(bf16[1,1,2,192,768]{4,3,2,1,0:T(8,128)(2,1)} %get-tuple-element.264), channel_id=1, source_target_pairs={{0,4},{4,0},{8,12},{12,8},{16,20},{20,16},{24,28},{28,24},{1,5},{5... | collective-permute-start | bytes 1769480 | tf_op jit(solution)/shard_map/ppermute | solution.py:693
  135.3 30.1 %collective-permute-start.22 = (bf16[1,2,1,192,768]{4,3,1,2,0:T(8,128)(2,1)}, bf16[1,2,1,192,768]{4,3,1,2,0:T(8,128)(2,1)}, u32[]{:S(2)}, u32[]{:S(2)}) collective-permute-start(bf16[1,2,1,192,768]{4,3,1,2,0:T(8,128)(2,1)} %bitcast.209), channel_id=1, source_target_pairs={{0,8},{4,12},{8,0},{12,4},{16,24},{20,28},{24,16},{28,20},{1,9},{5... | collective-permute-start | bytes 1769480 | tf_op jit(solution)/shard_map/ppermute | solution.py:693
  136.8 28.6 %collective-permute-start.23 = (bf16[1,2,1,192,768]{4,3,1,2,0:T(8,128)(2,1)}, bf16[1,2,1,192,768]{4,3,1,2,0:T(8,128)(2,1)}, u32[]{:S(2)}, u32[]{:S(2)}) collective-permute-start(bf16[1,2,1,192,768]{4,3,1,2,0:T(8,128)(2,1)} %bitcast.208), channel_id=1, source_target_pairs={{0,8},{4,12},{8,0},{12,4},{16,24},{20,28},{24,16},{28,20},{1,9},{5... | collective-permute-start | bytes 1769480 | tf_op jit(solution)/shard_map/ppermute | solution.py:693
  155.4 14.2 %collective-permute-start.24 = (bf16[1,1,1,192,768]{4,3,2,1,0:T(8,128)(2,1)}, bf16[1,1,1,192,768]{4,3,2,1,0:T(8,128)(2,1)S(1)}, u32[]{:S(2)}, u32[]{:S(2)}) collective-permute-start(bf16[1,1,1,192,768]{4,3,2,1,0:T(8,128)(2,1)} %get-tuple-element.283), channel_id=1, source_target_pairs={{0,8},{4,12},{8,0},{12,4},{16,24},{20,28},{24,16},{28,20},{1,9},{5... | collective-permute-start | bytes 884744 | tf_op jit(solution)/shard_map/ppermute | solution.py:693
  157.0 15.2 %copy-start.3 = (bf16[2,4,192,768]{3,2,1,0:T(8,128)(2,1)S(1)}, bf16[2,4,192,768]{3,2,1,0:T(8,128)(2,1)}, u32[]{:S(2)}) copy-start(bf16[2,4,192,768]{3,2,1,0:T(8,128)(2,1)} %get-tuple-element.254) | copy-start | bytes 7077892
  157.0 15.2 %copy-start.10 = (bf16[4,192,768]{2,1,0:T(8,128)(2,1)S(1)}, bf16[4,192,768]{2,1,0:T(8,128)(2,1)}, u32[]{:S(2)}) copy-start(bf16[4,192,768]{2,1,0:T(8,128)(2,1)} %copy-done.9) | copy-start | bytes 3538948
  165.4 10.2 %copy-start.28 = (bf16[2,4,80,768]{3,2,1,0:T(8,128)(2,1)S(1)}, bf16[2,4,80,768]{3,2,1,0:T(8,128)(2,1)}, u32[]{:S(2)}) copy-start(bf16[2,4,80,768]{3,2,1,0:T(8,128)(2,1)} %get-tuple-element.292) | copy-start | bytes 2949124
  169.6 6.0 %collective-permute-start.27 = (bf16[2,4,80,768]{3,2,1,0:T(8,128)(2,1)}, bf16[2,4,80,768]{3,2,1,0:T(8,128)(2,1)S(1)}, u32[]{:S(2)}, u32[]{:S(2)}) collective-permute-start(bf16[2,4,80,768]{3,2,1,0:T(8,128)(2,1)} %get-tuple-element.293), channel_id=1, source_target_pairs={{0,1},{1,0},{2,3},{3,2},{4,5},{5,4},{6,7},{7,6},{8,9},{9,8},{10,11... | collective-permute-start | bytes 2949128 | tf_op jit(solution)/shard_map/ppermute | solution.py:690
  170.4 23.2 %collective-permute-start.26 = (bf16[1,2,2,144,768]{4,3,2,1,0:T(8,128)(2,1)}, bf16[1,2,2,144,768]{4,3,2,1,0:T(8,128)(2,1)S(1)}, u32[]{:S(2)}, u32[]{:S(2)}) collective-permute-start(bf16[1,2,2,144,768]{4,3,2,1,0:T(8,128)(2,1)} %get-tuple-element.291), channel_id=1, source_target_pairs={{0,2},{1,3},{2,0},{3,1},{4,6},{5,7},{6,4},{7,5},{8,10},{9,11},{10,... | collective-permute-start | bytes 2654216 | tf_op jit(solution)/shard_map/ppermute | solution.py:690
  171.9 23.2 %collective-permute-start.25 = (bf16[4,144,768]{2,1,0:T(8,128)(2,1)}, bf16[4,144,768]{2,1,0:T(8,128)(2,1)S(1)}, u32[]{:S(2)}, u32[]{:S(2)}) collective-permute-start(bf16[4,144,768]{2,1,0:T(8,128)(2,1)} %get-tuple-element.290), channel_id=1, source_target_pairs={{0,1},{1,0},{2,3},{3,2},{4,5},{5,4},{6,7},{7,6},{8,9},{9,8},{10,11... | collective-permute-start | bytes 2654216 | tf_op jit(solution)/shard_map/ppermute | solution.py:690
  173.5 9.9 %collective-permute-start.32 = (bf16[1,1,1,192,768]{4,3,1,2,0:T(8,128)(2,1)S(1)}, bf16[1,1,1,192,768]{4,3,1,2,0:T(8,128)(2,1)S(1)}, u32[]{:S(2)}, u32[]{:S(2)}) collective-permute-start(bf16[1,1,1,192,768]{4,3,1,2,0:T(8,128)(2,1)S(1)} %get-tuple-element.299), channel_id=1, source_target_pairs={{0,4},{4,0},{8,12},{12,8},{16,20},{20,16},{24,28},{28,24},{1,5},{5... | collective-permute-start | bytes 884744 | tf_op jit(solution)/shard_map/ppermute | solution.py:693
  174.6 14.5 %collective-permute-start.29 = (bf16[1,1,1,192,768]{4,3,1,2,0:T(8,128)(2,1)S(1)}, bf16[1,1,1,192,768]{4,3,1,2,0:T(8,128)(2,1)S(1)}, u32[]{:S(2)}, u32[]{:S(2)}) collective-permute-start(bf16[1,1,1,192,768]{4,3,1,2,0:T(8,128)(2,1)S(1)} %get-tuple-element.300), channel_id=1, source_target_pairs={{0,4},{4,0},{8,12},{12,8},{16,20},{20,16},{24,28},{28,24},{1,5},{5... | collective-permute-start | bytes 884744 | tf_op jit(solution)/shard_map/ppermute | solution.py:693
  175.7 17.1 %collective-permute-start.28 = (bf16[2,2,1,80,768]{4,3,1,2,0:T(8,128)(2,1)S(1)}, bf16[2,2,1,80,768]{4,3,1,2,0:T(8,128)(2,1)S(1)}, u32[]{:S(2)}, u32[]{:S(2)}) collective-permute-start(bf16[2,2,1,80,768]{4,3,1,2,0:T(8,128)(2,1)S(1)} %add_convert_fusion), channel_id=1, source_target_pairs={{0,8},{4,12},{8,0},{12,4},{16,24},{20,28},{24,16},{28,20},{1,9},{5... | collective-permute-start | bytes 1474568 | tf_op jit(solution)/shard_map/ppermute | solution.py:693
  178.8 16.4 %copy-start.29 = (bf16[4,144,768]{2,1,0:T(8,128)(2,1)S(1)}, bf16[4,144,768]{2,1,0:T(8,128)(2,1)}, u32[]{:S(2)}) copy-start(bf16[4,144,768]{2,1,0:T(8,128)(2,1)} %get-tuple-element.289) | copy-start | bytes 2654212
  183.4 13.0 %collective-permute-start.34 = (bf16[8,896]{1,0:T(8,128)(2,1)S(1)}, bf16[8,896]{1,0:T(8,128)(2,1)S(1)}, u32[]{:S(2)}, u32[]{:S(2)}) collective-permute-start(bf16[8,896]{1,0:T(8,128)(2,1)S(1)} %convert_element_type.245), channel_id=1, source_target_pairs={{0,16},{4,20},{8,24},{12,28},{16,0},{20,4},{24,8},{28,12},{1,17},{... | collective-permute-start | bytes 43016 | tf_op jit(solution)/shard_map/ppermute | solution.py:693
  189.1 23.1 %collective-permute-start.36 = (bf16[1,1,1,192,768]{4,3,2,1,0:T(8,128)(2,1)S(1)}, bf16[1,1,1,192,768]{4,3,2,1,0:T(8,128)(2,1)S(1)}, u32[]{:S(2)}, u32[]{:S(2)}) collective-permute-start(bf16[1,1,1,192,768]{4,3,2,1,0:T(8,128)(2,1)S(1)} %add_convert_fusion.6), channel_id=1, source_target_pairs={{0,16},{4,20},{8,24},{12,28},{16,0},{20,4},{24,8},{28,12},{1,17},{... | collective-permute-start | bytes 884744 | tf_op jit(solution)/shard_map/ppermute | solution.py:693
  192.9 10.0 %collective-permute-start.33 = (bf16[1,1,1,192,768]{4,3,1,2,0:T(8,128)(2,1)S(1)}, bf16[1,1,1,192,768]{4,3,1,2,0:T(8,128)(2,1)S(1)}, u32[]{:S(2)}, u32[]{:S(2)}) collective-permute-start(bf16[1,1,1,192,768]{4,3,1,2,0:T(8,128)(2,1)S(1)} %add_convert_fusion.5), channel_id=1, source_target_pairs={{0,2},{1,3},{2,0},{3,1},{4,6},{5,7},{6,4},{7,5},{8,10},{9,11},{10,... | collective-permute-start | bytes 884744 | tf_op jit(solution)/shard_map/ppermute | solution.py:690
  193.6 12.8 %collective-permute-start.31 = (bf16[1,2,1,80,768]{4,3,1,2,0:T(8,128)(2,1)S(1)}, bf16[1,2,1,80,768]{4,3,1,2,0:T(8,128)(2,1)S(1)}, u32[]{:S(2)}, u32[]{:S(2)}) collective-permute-start(bf16[1,2,1,80,768]{4,3,1,2,0:T(8,128)(2,1)S(1)} %add_convert_fusion.9), channel_id=1, source_target_pairs={{0,2},{1,3},{2,0},{3,1},{4,6},{5,7},{6,4},{7,5},{8,10},{9,11},{10,... | collective-permute-start | bytes 737288 | tf_op jit(solution)/shard_map/ppermute | solution.py:690
  195.3 12.2 %collective-permute-start.30 = (bf16[1,1,2,144,768]{4,3,2,1,0:T(8,128)(2,1)S(1)}, bf16[1,1,2,144,768]{4,3,2,1,0:T(8,128)(2,1)S(1)}, u32[]{:S(2)}, u32[]{:S(2)}) collective-permute-start(bf16[1,1,2,144,768]{4,3,2,1,0:T(8,128)(2,1)S(1)} %add_convert_fusion.1), channel_id=1, source_target_pairs={{0,4},{4,0},{8,12},{12,8},{16,20},{20,16},{24,28},{28,24},{1,5},{5... | collective-permute-start | bytes 1327112 | tf_op jit(solution)/shard_map/ppermute | solution.py:693
  196.5 27.9 %collective-permute-start.39 = (bf16[16,896]{1,0:T(8,128)(2,1)S(1)}, bf16[16,896]{1,0:T(8,128)(2,1)S(1)}, u32[]{:S(2)}, u32[]{:S(2)}) collective-permute-start(bf16[16,896]{1,0:T(8,128)(2,1)S(1)} %pad_maximum_fusion.10), channel_id=1, source_target_pairs={{0,8},{4,12},{8,0},{12,4},{16,24},{20,28},{24,16},{28,20},{1,9},{5... | collective-permute-start | bytes 86024 | tf_op jit(solution)/shard_map/ppermute | solution.py:693
  204.1 22.5 %collective-permute-start.41 = (bf16[1,1,1,192,768]{4,3,1,2,0:T(8,128)(2,1)S(1)}, bf16[1,1,1,192,768]{4,3,1,2,0:T(8,128)(2,1)S(1)}, u32[]{:S(2)}, u32[]{:S(2)}) collective-permute-start(bf16[1,1,1,192,768]{4,3,1,2,0:T(8,128)(2,1)S(1)} %add_convert_fusion.4), channel_id=1, source_target_pairs={{0,16},{4,20},{8,24},{12,28},{16,0},{20,4},{24,8},{28,12},{1,17},{... | collective-permute-start | bytes 884744 | tf_op jit(solution)/shard_map/ppermute | solution.py:693
  206.4 4.9 %collective-permute-start.37 = (bf16[1,1,1,80,768]{4,3,1,2,0:T(8,128)(2,1)S(1)}, bf16[1,1,1,80,768]{4,3,1,2,0:T(8,128)(2,1)S(1)}, u32[]{:S(2)}, u32[]{:S(2)}) collective-permute-start(bf16[1,1,1,80,768]{4,3,1,2,0:T(8,128)(2,1)S(1)} %add_convert_fusion.15), channel_id=1, source_target_pairs={{0,4},{4,0},{8,12},{12,8},{16,20},{20,16},{24,28},{28,24},{1,5},{5... | collective-permute-start | bytes 368648 | tf_op jit(solution)/shard_map/ppermute | solution.py:693
  207.6 14.8 %collective-permute-start.35 = (bf16[1,1,1,144,768]{4,3,2,1,0:T(8,128)(2,1)S(1)}, bf16[1,1,1,144,768]{4,3,2,1,0:T(8,128)(2,1)S(1)}, u32[]{:S(2)}, u32[]{:S(2)}) collective-permute-start(bf16[1,1,1,144,768]{4,3,2,1,0:T(8,128)(2,1)S(1)} %add_convert_fusion.12), channel_id=1, source_target_pairs={{0,8},{4,12},{8,0},{12,4},{16,24},{20,28},{24,16},{28,20},{1,9},{5... | collective-permute-start | bytes 663560 | tf_op jit(solution)/shard_map/ppermute | solution.py:693
  211.4 14.6 %collective-permute-start.42 = (bf16[1,1,1,80,768]{4,3,1,2,0:T(8,128)(2,1)S(1)}, bf16[1,1,1,80,768]{4,3,1,2,0:T(8,128)(2,1)S(1)}, u32[]{:S(2)}, u32[]{:S(2)}) collective-permute-start(bf16[1,1,1,80,768]{4,3,1,2,0:T(8,128)(2,1)S(1)} %add_convert_fusion.14), channel_id=1, source_target_pairs={{0,16},{4,20},{8,24},{12,28},{16,0},{20,4},{24,8},{28,12},{1,17},{... | collective-permute-start | bytes 368648 | tf_op jit(solution)/shard_map/ppermute | solution.py:693
  212.3 23.1 %collective-permute-start.44 = (bf16[1,1,1,192,768]{4,3,2,1,0:T(8,128)(2,1)S(1)}, bf16[1,1,1,192,768]{4,3,2,1,0:T(8,128)(2,1)S(1)}, u32[]{:S(2)}, u32[]{:S(2)}) collective-permute-start(bf16[1,1,1,192,768]{4,3,2,1,0:T(8,128)(2,1)S(1)} %add_convert_fusion.3), channel_id=1, source_target_pairs={{0,8},{4,12},{8,0},{12,4},{16,24},{20,28},{24,16},{28,20},{1,9},{5... | collective-permute-start | bytes 884744 | tf_op jit(solution)/shard_map/ppermute | solution.py:693
  222.6 13.2 %collective-permute-start.38 = (bf16[1,1,1,144,768]{4,3,2,1,0:T(8,128)(2,1)S(1)}, bf16[1,1,1,144,768]{4,3,2,1,0:T(8,128)(2,1)S(1)}, u32[]{:S(2)}, u32[]{:S(2)}) collective-permute-start(bf16[1,1,1,144,768]{4,3,2,1,0:T(8,128)(2,1)S(1)} %add_convert_fusion.11), channel_id=1, source_target_pairs={{0,16},{4,20},{8,24},{12,28},{16,0},{20,4},{24,8},{28,12},{1,17},{... | collective-permute-start | bytes 663560 | tf_op jit(solution)/shard_map/ppermute | solution.py:693
  224.3 4.8 %collective-permute-start.40 = (bf16[32,896]{1,0:T(8,128)(2,1)S(1)}, bf16[32,896]{1,0:T(8,128)(2,1)S(1)}, u32[]{:S(2)}, u32[]{:S(2)}) collective-permute-start(bf16[32,896]{1,0:T(8,128)(2,1)S(1)} %pad_maximum_fusion.9), channel_id=1, source_target_pairs={{0,4},{4,0},{8,12},{12,8},{16,20},{20,16},{24,28},{28,24},{1,5},{5... | collective-permute-start | bytes 172040 | tf_op jit(solution)/shard_map/ppermute | solution.py:693
  226.1 4.9 %collective-permute-start.45 = (bf16[1,1,1,80,768]{4,3,1,2,0:T(8,128)(2,1)S(1)}, bf16[1,1,1,80,768]{4,3,1,2,0:T(8,128)(2,1)S(1)}, u32[]{:S(2)}, u32[]{:S(2)}) collective-permute-start(bf16[1,1,1,80,768]{4,3,1,2,0:T(8,128)(2,1)S(1)} %add_convert_fusion.13), channel_id=1, source_target_pairs={{0,4},{4,0},{8,12},{12,8},{16,20},{20,16},{24,28},{28,24},{1,5},{5... | collective-permute-start | bytes 368648 | tf_op jit(solution)/shard_map/ppermute | solution.py:693
  226.6 14.3 %collective-permute-start.47 = (bf16[1,1,1,192,768]{4,3,1,2,0:T(8,128)(2,1)S(1)}, bf16[1,1,1,192,768]{4,3,1,2,0:T(8,128)(2,1)S(1)}, u32[]{:S(2)}, u32[]{:S(2)}) collective-permute-start(bf16[1,1,1,192,768]{4,3,1,2,0:T(8,128)(2,1)S(1)} %add_convert_fusion.2), channel_id=1, source_target_pairs={{0,4},{4,0},{8,12},{12,8},{16,20},{20,16},{24,28},{28,24},{1,5},{5... | collective-permute-start | bytes 884744 | tf_op jit(solution)/shard_map/ppermute | solution.py:693
  229.1 6.5 %collective-permute-start.43 = (bf16[64,896]{1,0:T(8,128)(2,1)S(1)}, bf16[64,896]{1,0:T(8,128)(2,1)S(1)}, u32[]{:S(2)}, u32[]{:S(2)}) collective-permute-start(bf16[64,896]{1,0:T(8,128)(2,1)S(1)} %pad_maximum_fusion.8), channel_id=1, source_target_pairs={{0,2},{1,3},{2,0},{3,1},{4,6},{5,7},{6,4},{7,5},{8,10},{9,11},{10,... | collective-permute-start | bytes 344072 | tf_op jit(solution)/shard_map/ppermute | solution.py:690
  231.1 9.7 %collective-permute-start.48 = (bf16[1,2,1,80,768]{4,3,1,2,0:T(8,128)(2,1)S(1)}, bf16[1,2,1,80,768]{4,3,1,2,0:T(8,128)(2,1)S(1)}, u32[]{:S(2)}, u32[]{:S(2)}) collective-permute-start(bf16[1,2,1,80,768]{4,3,1,2,0:T(8,128)(2,1)S(1)} %pad_maximum_fusion.5), channel_id=1, source_target_pairs={{0,8},{4,12},{8,0},{12,4},{16,24},{20,28},{24,16},{28,20},{1,9},{5... | collective-permute-start | bytes 737288 | tf_op jit(solution)/shard_map/ppermute | solution.py:693
  235.5 13.6 %collective-permute-start.54 = (bf16[1,1,2,192,768]{4,3,2,1,0:T(8,128)(2,1)S(1)}, bf16[1,1,2,192,768]{4,3,2,1,0:T(8,128)(2,1)S(1)}, u32[]{:S(2)}, u32[]{:S(2)}) collective-permute-start(bf16[1,1,2,192,768]{4,3,2,1,0:T(8,128)(2,1)S(1)} %pad_maximum_fusion.1), channel_id=1, source_target_pairs={{0,4},{4,0},{8,12},{12,8},{16,20},{20,16},{24,28},{28,24},{1,5},{5... | collective-permute-start | bytes 1769480 | tf_op jit(solution)/shard_map/ppermute | solution.py:693
  235.6 7.9 %collective-permute-start.52 = (bf16[128,896]{1,0:T(8,128)(2,1)S(1)}, bf16[128,896]{1,0:T(8,128)(2,1)S(1)}, u32[]{:S(2)}, u32[]{:S(2)}) collective-permute-start(bf16[128,896]{1,0:T(8,128)(2,1)S(1)} %pad_maximum_fusion.6), channel_id=1, source_target_pairs={{0,1},{1,0},{2,3},{3,2},{4,5},{5,4},{6,7},{7,6},{8,9},{9,8},{10,11... | collective-permute-start | bytes 688136 | tf_op jit(solution)/shard_map/ppermute | solution.py:690
  235.8 9.7 %collective-permute-start.46 = (bf16[1,1,1,144,768]{4,3,2,1,0:T(8,128)(2,1)S(1)}, bf16[1,1,1,144,768]{4,3,2,1,0:T(8,128)(2,1)S(1)}, u32[]{:S(2)}, u32[]{:S(2)}) collective-permute-start(bf16[1,1,1,144,768]{4,3,2,1,0:T(8,128)(2,1)S(1)} %add_convert_fusion.10), channel_id=1, source_target_pairs={{0,8},{4,12},{8,0},{12,4},{16,24},{20,28},{24,16},{28,20},{1,9},{5... | collective-permute-start | bytes 663560 | tf_op jit(solution)/shard_map/ppermute | solution.py:693
  240.8 5.7 %collective-permute-start.50 = (bf16[1,4,32,768]{3,2,1,0:T(8,128)(2,1)S(1)}, bf16[1,4,32,768]{3,2,1,0:T(8,128)(2,1)S(1)}, u32[]{:S(2)}, u32[]{:S(2)}) collective-permute-start(bf16[1,4,32,768]{3,2,1,0:T(8,128)(2,1)S(1)} %bitcast.198), channel_id=1, source_target_pairs={{0,2},{1,3},{2,0},{3,1},{4,6},{5,7},{6,4},{7,5},{8,10},{9,11},{10,... | collective-permute-start | bytes 589832 | tf_op jit(solution)/shard_map/ppermute | solution.py:690
  241.0 16.0 %collective-permute-start.53 = (bf16[1,2,1,192,768]{4,3,1,2,0:T(8,128)(2,1)S(1)}, bf16[1,2,1,192,768]{4,3,1,2,0:T(8,128)(2,1)S(1)}, u32[]{:S(2)}, u32[]{:S(2)}) collective-permute-start(bf16[1,2,1,192,768]{4,3,1,2,0:T(8,128)(2,1)S(1)} %pad_maximum_fusion.2), channel_id=1, source_target_pairs={{0,8},{4,12},{8,0},{12,4},{16,24},{20,28},{24,16},{28,20},{1,9},{5... | collective-permute-start | bytes 1769480 | tf_op jit(solution)/shard_map/ppermute | solution.py:693
  245.6 15.5 %collective-permute-start.49 = (bf16[1,1,2,144,768]{4,3,2,1,0:T(8,128)(2,1)S(1)}, bf16[1,1,2,144,768]{4,3,2,1,0:T(8,128)(2,1)}, u32[]{:S(2)}, u32[]{:S(2)}) collective-permute-start(bf16[1,1,2,144,768]{4,3,2,1,0:T(8,128)(2,1)S(1)} %pad_maximum_fusion.3), channel_id=1, source_target_pairs={{0,4},{4,0},{8,12},{12,8},{16,20},{20,16},{24,28},{28,24},{1,5},{5... | collective-permute-start | bytes 1327112 | tf_op jit(solution)/shard_map/ppermute | solution.py:693
  246.6 14.5 %collective-permute-start.51 = (bf16[2,4,32,768]{3,2,1,0:T(8,128)(2,1)S(1)}, bf16[2,4,32,768]{3,2,1,0:T(8,128)(2,1)}, u32[]{:S(2)}, u32[]{:S(2)}) collective-permute-start(bf16[2,4,32,768]{3,2,1,0:T(8,128)(2,1)S(1)} %pad_maximum_fusion.4.all_ref), channel_id=1, source_target_pairs={{0,1},{1,0},{2,3},{3,2},{4,5},{5,4},{6,7},{7,6},{8,9},{9,8},{10,11... | collective-permute-start | bytes 1179656 | tf_op jit(solution)/shard_map/ppermute | solution.py:690
  (29 other events, 81.5 us)

commit v5 on v4

--- a/solution.py
+++ b/solution.py
@@ -18,7 +18,7 @@
 CHUNK = 64
 GATHER_ROWS = 32
 CHAIN_ORDERS = ("yxz", "zxy", "yxz", "zyx")
-TAIL = (1, 3, 4, 0, 1, 3, 2, 4, 1, 3, 2, 3, 0, 2, 4, 3, 1, 4, 3, 0, 4, 2, 5, 1, 2, 5)
+TAIL = (0, 1, 3, 1, 3, 4, 2, 1, 3, 2, 4, 3, 0, 2, 3, 4, 1, 3, 4, 0, 2, 4, 5, 1, 2, 5)
 
 VMEM = pl.BlockSpec(memory_space=pltpu.VMEM)
 SMEM = pl.BlockSpec(memory_space=pltpu.SMEM)
@@ -56,12 +56,12 @@
     return jnp.sum(values, 0, keepdims=True)
 
 
-def over_rows(tokens, body):
+def over_rows(tokens, body, first=0):
     def step(index, carry):
         body(pl.ds(pl.multiple_of(index * CHUNK, CHUNK), CHUNK))
         return carry
 
-    lax.fori_loop(0, tokens // CHUNK, step, 0)
+    lax.fori_loop(first // CHUNK, tokens // CHUNK, step, 0)
 
 
 def gelu_pair(values):
@@ -106,33 +106,26 @@
             norm_ref[at] = (xhat * gain_ref[...] + bias_ref[...]).astype(BF)
 
 
-def fetch_near(parts, weight_ref, sems):
+def fetch_kind(where_ref, parts, weight_ref, sems, kind):
     unit = weight_ref.shape[1] // 2
-    copies = []
-    for slot, ref in enumerate(parts):
-        for half in range(2):
-            for u in range(2):
-                source = ref.at[half, pl.ds(unit * u, unit)]
-                copies.append((source, weight_ref.at[2 * half + u, pl.ds(unit * slot, unit)]))
-    return start_copies(copies, sems)
-
-
-def fetch_far(where_ref, parts, weight_ref, sems):
-    far, far_other, cross, cross_other = parts
+    half, rows = kind // 2, pl.ds(unit * (kind % 2), unit)
+    for slot in range(2):
+        target, sem = weight_ref.at[kind, pl.ds(unit * slot, unit)], sems.at[2 * kind + slot]
+        if len(parts) == 2:
+            pltpu.make_async_copy(parts[slot].at[half, rows], target, sem).start()
+            continue
+        for other in range(2):
+
+            @pl.when((where_ref[1] == half) == (other == 0))
+            def _():
+                pltpu.make_async_copy(parts[2 * slot + other].at[rows], target, sem).start()
+
+
+def wait_kind(weight_ref, sems, kind):
     unit = weight_ref.shape[1] // 2
-    x = where_ref[1]
-    copies = []
-    for slot, ref, half in ((0, far, x), (0, far_other, 1 - x), (1, cross, x), (1, cross_other, 1 - x)):
-        for u in range(2):
-            source = ref.at[pl.ds(unit * u, unit)]
-            copies.append((source, weight_ref.at[2 * half + u, pl.ds(unit * slot, unit)]))
-    return start_copies(copies, sems)
-
-
-def fetch_half(where_ref, parts, weight_ref, sems):
-    if len(parts) == 2:
-        return fetch_near(parts, weight_ref, sems)
-    return fetch_far(where_ref, parts, weight_ref, sems)
+    for slot in range(2):
+        target = weight_ref.at[kind, pl.ds(unit * slot, unit)]
+        pltpu.make_async_copy(target, target, sems.at[2 * kind + slot]).wait()
 
 
 def start_copies(copies, sems):
@@ -163,33 +156,55 @@
     pltpu.make_async_copy(source, into_ref.at[slot], sems.at[slot]).wait()
 
 
-def mask_bias(packed, quarter, length):
-    q = lax.broadcasted_iota(jnp.int32, (length, length), 1)
+def mask_bias(packed, quarter, length, part):
+    block = length // 2
+    q = (lax.broadcasted_iota(jnp.int32, (length, length), 1) & (block - 1)) + part * block
     k = lax.broadcasted_iota(jnp.int32, (length, length), 0)
     shift = quarter.bit_length() - 1
     same = (q >> shift) == (k >> shift)
     return jnp.where((k <= q) & (same | jnp.logical_not(packed)), 0.0, -1e30)
 
 
+def by_head(values, lanes):
+    return jnp.concatenate([values * lanes[0], values * lanes[1]], 0)
+
+
+def own_lanes(values):
+    block = values.shape[0] // 2
+    lane = lax.broadcasted_iota(jnp.int32, (1, 128), 1)
+    return jnp.where(lane < HEAD_DIM, values[:block], values[block:])
+
+
 def head_lanes(value):
     lane = lax.broadcasted_iota(jnp.int32, (1, 128), 1)
     return [jnp.where(side, value, 0.0).astype(BF) for side in (lane < HEAD_DIM, lane >= HEAD_DIM)]
 
 
-def attend_kernel(where_ref, seg_ref, hid_ref, norm_ref, *rest, length, quarter, count):
+def attend_kernel(where_ref, seg_ref, hid_in, norm_ref, *rest, length, quarter, count):
     parts = rest[:count]
-    q_ref, k_ref, v_ref, prob_ref, att_ref, out_ref, weight_ref, bias_ref, sems = rest[count:]
+    (
+        q_out, k_out, v_out, prob_out, att_out, out_ref,
+        weight_ref, bias_ref, hid_ref, q_ref, k_ref, v_ref, prob_ref, att_ref, sems, io_sems, prob_sems,
+    ) = rest[count:]
     tokens = hid_ref.shape[0]
-    copies = fetch_half(where_ref, parts, weight_ref, sems)
+    for kind in range(4):
+        fetch_kind(where_ref, parts, weight_ref, sems, kind)
+    moves = [
+        pltpu.make_async_copy(source, target, io_sems.at[index])
+        for index, (source, target) in enumerate(
+            ((hid_in, hid_ref), (q_ref, q_out), (k_ref, k_out), (v_ref, v_out), (att_ref, att_out))
+        )
+    ]
+    moves[0].start()
     for row in range(tokens // length):
-        bias_ref[row] = mask_bias(packed_flag(where_ref, seg_ref, row, length), quarter, length)
-    for copy in copies:
-        copy.wait()
-    q_ref[...] = nt(norm_ref[...], weight_ref[0]).astype(BF)
-    k_ref[...] = nt(norm_ref[...], weight_ref[1]).astype(BF)
-    v_ref[...] = nt(norm_ref[...], weight_ref[2]).astype(BF)
+        for part in range(2):
+            packed = packed_flag(where_ref, seg_ref, row, length)
+            bias_ref[row, part] = mask_bias(packed, quarter, length, part)
+    for kind, ref in enumerate((q_ref, k_ref, v_ref)):
+        wait_kind(weight_ref, sems, kind)
+        ref[...] = nt(norm_ref[...], weight_ref[kind]).astype(BF)
+        moves[1 + kind].start()
     pairs = q_ref.shape[1] // 128
-    lefts = head_lanes(1.0)
     scaled = head_lanes(SCALE)
     block = length // 2
 
@@ -201,24 +216,30 @@
             keys = (part + 1) * block
             here = pl.ds(pl.multiple_of(row * length + part * block, block), block)
             upto = pl.ds(pl.multiple_of(row * length, length), keys)
-            bias = bias_ref[row, :keys, part * block : (part + 1) * block]
             queries = q_ref[here, lanes]
             key_rows = k_ref[upto, lanes]
             values = v_ref[upto, lanes]
-            result = None
-            for head in range(2):
-                scores = nt(key_rows, queries * scaled[head]) + bias
-                top = jnp.max(scores, 0, keepdims=True)
-                grown = jnp.exp(scores - top)
-                probs = (grown * (1.0 / jnp.sum(grown, 0, keepdims=True))).astype(BF)
-                prob_ref[2 * index + head, :keys, part * block : (part + 1) * block] = probs
-                term = tn(probs, values * lefts[head])
-                result = term if result is None else result + term
+            scores = nt(key_rows, by_head(queries, scaled)) + bias_ref[row, part, :keys]
+            top = jnp.max(scores, 0, keepdims=True)
+            grown = jnp.exp(scores - top)
+            probs = (grown * (1.0 / jnp.sum(grown, 0, keepdims=True))).astype(BF)
+            prob_ref[2 * index + part, :keys] = probs
+            result = own_lanes(tn(probs, values))
             att_ref[here, lanes] = result.astype(BF)
+        both = pl.ds(2 * index, 2)
+        pltpu.make_async_copy(prob_ref.at[both], prob_out.at[both], prob_sems.at[index]).start()
         return carry
 
     lax.fori_loop(0, tokens // length * pairs, step, 0)
+    moves[4].start()
+    moves[0].wait()
+    wait_kind(weight_ref, sems, 3)
     out_ref[...] = hid_ref[...] + nn(att_ref[...], weight_ref[3])
+    for move in moves[1:]:
+        move.wait()
+    for index in range(tokens // length * pairs):
+        both = slice(2 * index, 2 * index + 2)
+        pltpu.make_async_copy(prob_ref.at[both], prob_out.at[both], prob_sems.at[index]).wait()
 
 
 def up_kernel(
@@ -283,18 +304,20 @@
 
 
 def down_kernel(
-    where_ref, seg_ref, hid_ref, act_in, bdown_ref, wout_ref, bout_ref, patch_ref, lgrad_ref, dgrad_ref,
+    where_ref, seg_ref, hid_in, act_in, bdown_ref, wout_ref, bout_ref, patch_ref, lgrad_ref, dgrad_ref,
     own, near, far, far_other, cross, cross_other,
     latent_ref, logdet_ref, mean_ref, max_ref, direct_ref, grad_ref, gwout_ref, gvec_ref, keep_ref, send_near, send_far,
-    weight_ref, act_ref, total_ref, branch_ref, stage_ref, sems, act_sems, out_sems,
+    weight_ref, act_ref, total_ref, branch_ref, stage_ref, hid_ref, sems, act_sems, out_sems, hid_sem,
     *, length, quarter,
 ):
-    tokens, width = hid_ref.shape
+    tokens, width = total_ref.shape
     channels = patch_ref.shape[0]
     send_refs = (send_near, send_far)
     start_copies([(act_in.at[slot], act_ref.at[slot]) for slot in range(4)], act_sems)
     fetch_full(where_ref, (own, near, far, far_other, cross, cross_other), weight_ref, sems)
-    total_ref[...] = hid_ref[...] + bdown_ref[...]
+    hidden = pltpu.make_async_copy(hid_in, hid_ref, hid_sem)
+    hidden.start()
+    total_ref[...] = jnp.zeros(total_ref.shape, F32)
 
     def gather(slot, carry):
         wait_slot(act_in.at[slot], act_ref, act_sems, slot)
@@ -303,7 +326,8 @@
         return carry
 
     lax.fori_loop(0, 4, gather, 0)
-    top_low = total_ref[...].astype(BF)
+    hidden.wait()
+    top_low = (total_ref[...] + hid_ref[...] + bdown_ref[...]).astype(BF)
     head_out = nt(wout_ref[...], top_low) + bout_ref[...]
     token = lax.broadcasted_iota(jnp.int32, (1, tokens), 1)
     row_count = tokens // length
@@ -383,13 +407,14 @@
 
 
 def up_back_kernel(
-    where_ref, grad_ref, pre_in, norm_ref, hid_ref, gain_ref, own, near, far, far_other, cross, cross_other,
+    where_ref, grad_in, pre_in, norm_ref, hid_in, gain_ref, own, near, far, far_other, cross, cross_other,
     gout_ref, mix_ref, gvec_ref, keep_ref, send_near, send_far,
-    weight_ref, pre_ref, total_ref, stage_ref, sems, pre_sems, out_sems,
+    weight_ref, pre_ref, total_ref, stage_ref, grad_ref, hid_ref, sems, pre_sems, out_sems, late_sems,
 ):
     tokens, width = grad_ref.shape
     send_refs = (send_near, send_far)
     start_copies([(pre_in.at[slot], pre_ref.at[slot]) for slot in range(4)], pre_sems)
+    late = start_copies([(grad_in, grad_ref), (hid_in, hid_ref)], late_sems)
     total_ref[...] = jnp.zeros(total_ref.shape, F32)
     fetch_full(where_ref, (own, near, far, far_other, cross, cross_other), weight_ref, sems)
     gvec_ref[...] = jnp.zeros(gvec_ref.shape, F32)
@@ -418,24 +443,35 @@
         gvec_ref[0:1, :] += column_sum(grad * xhat)
         gvec_ref[1:2, :] += column_sum(grad)
 
+    for copy in late:
+        copy.wait()
     over_rows(tokens, finish)
     for slot in range(2):
         wait_pieces(stage_ref.at[slot], keep_ref, out_sems.at[slot], rows)
 
 
 def attend_back_kernel(
-    where_ref, mix_ref, q_ref, k_ref, v_ref, prob_ref, att_ref, norm_ref, *rest, length, quarter, count, chained
+    where_ref, mix_in, q_in, k_in, v_in, prob_in, att_in, norm_in, *rest, length, quarter, count, chained
 ):
-    before_ref = rest[0] if chained else None
+    before_in = rest[0] if chained else None
     rest = rest[1:] if chained else rest
     parts = rest[:count]
     (
         total_ref, gq_ref, keep_ref, send_ref,
         weight_ref, gatt_ref, dq_ref, dk_ref, dv_ref, stage_ref, sems, out_sems,
+        mix_ref, q_ref, k_ref, v_ref, prob_ref, att_ref, norm_ref, before_ref, in_sems,
     ) = rest[count:]
     tokens = mix_ref.shape[0]
-    for copy in fetch_half(where_ref, parts, weight_ref, sems):
-        copy.wait()
+    fetch_kind(where_ref, parts, weight_ref, sems, 3)
+    moves = [
+        (mix_in, mix_ref), (att_in, att_ref), (q_in, q_ref), (k_in, k_ref), (v_in, v_ref), (prob_in, prob_ref),
+        (norm_in, norm_ref),
+    ]
+    moves = start_copies(moves + ([(before_in, before_ref)] if chained else []), in_sems)
+    for kind in range(3):
+        fetch_kind(where_ref, parts, weight_ref, sems, kind)
+    moves[0].wait()
+    wait_kind(weight_ref, sems, 3)
     gatt_ref[...] = nt(mix_ref[...], weight_ref[3]).astype(BF)
     pairs = q_ref.shape[1] // 128
     lefts = head_lanes(1.0)
@@ -455,7 +491,10 @@
                     out_sems.at[kind, slot * PIECES + piece],
                 ).start()
 
+    moves[1].wait()
     publish(2, att_ref[...], mix_ref[...])
+    for move in moves[2:6]:
+        move.wait()
 
     def step(index, carry):
         row = index // pairs
@@ -471,20 +510,15 @@
             key_rows = k_ref[upto, lanes]
             values = v_ref[upto, lanes]
             grad_out = gatt_ref[here, lanes]
-            result = None
-            for head in range(2):
-                probs = prob_ref[2 * index + head, :keys, part * block : (part + 1) * block]
-                wide = probs.astype(F32)
-                grad_mine = grad_out * lefts[head]
-                grad_probs = nt(values, grad_mine)
-                inner = jnp.sum(wide * grad_probs, 0, keepdims=True)
-                grad_scores = (wide * (grad_probs - inner)).astype(BF)
-                term = tn(grad_scores, key_rows * scaled[head])
-                result = term if result is None else result + term
-                term_k = nn(grad_scores, queries * scaled[head])
-                term_v = nn(probs, grad_mine)
-                grads_k[part] = term_k if grads_k[part] is None else grads_k[part] + term_k
-                grads_v[part] = term_v if grads_v[part] is None else grads_v[part] + term_v
+            probs = prob_ref[2 * index + part, :keys]
+            wide = probs.astype(F32)
+            grad_both = by_head(grad_out, lefts)
+            grad_probs = nt(values, grad_both)
+            inner = jnp.sum(wide * grad_probs, 0, keepdims=True)
+            grad_scores = (wide * (grad_probs - inner)).astype(BF)
+            result = own_lanes(tn(grad_scores, key_rows)) * SCALE
+            grads_k[part] = nn(grad_scores, by_head(queries, scaled))
+            grads_v[part] = nn(probs, grad_both)
             dq_ref[here, lanes] = result.astype(BF)
         low = pl.ds(pl.multiple_of(row * length, length), block)
         high = pl.ds(pl.multiple_of(row * length + block, block), block)
@@ -495,11 +529,15 @@
         return carry
 
     lax.fori_loop(0, tokens // length * pairs, step, 0)
+    moves[6].wait()
     publish(0, dk_ref[...], norm_ref[...])
     publish(1, dv_ref[...], norm_ref[...])
     gq_ref[...] = tn(dq_ref[...], norm_ref[...]).astype(BF)
+    for kind in range(3):
+        wait_kind(weight_ref, sems, kind)
     total = nn(dq_ref[...], weight_ref[0]) + nn(dk_ref[...], weight_ref[1]) + nn(dv_ref[...], weight_ref[2])
     if chained:
+        moves[7].wait()
         total = total + before_ref[...]
     total_ref[...] = total
     for kind in range(3):
@@ -510,13 +548,20 @@
 
 
 def embed_back_kernel(
-    where_ref, seg_ref, label_ref, grad_ref, total_ref, hid_ref, gain_ref, patch_ref, direct_ref, win_ref,
+    where_ref, seg_ref, label_ref, grad_in, total_in, hid_in, gain_ref, patch_ref, direct_ref, win_ref,
     gwout_ref, gdown_ref, gup_ref, gpre_ref, gq_near, gq_far,
     pgrad_ref, slot_ref, keep_ref, send_ref,
-    value_ref, embed_ref, acc_ref, small_ref, sems,
+    value_ref, embed_ref, acc_ref, small_ref, grad_ref, total_ref, hid_ref, sems, in_sems,
     *, length, quarter,
 ):
     tokens, width = hid_ref.shape
+    half = tokens // 2
+    moves = [
+        (source.at[first : first + half], target.at[first : first + half])
+        for first in (0, half)
+        for source, target in ((grad_in, grad_ref), (total_in, total_ref), (hid_in, hid_ref))
+    ]
+    moves = start_copies(moves, in_sems)
     channels = patch_ref.shape[0]
     unit = width // 4
     rows = unit // PIECES
@@ -541,7 +586,10 @@
         embed_ref[at] = embed
         acc_ref[0:1, :] += column_sum(embed.astype(F32))
 
-    over_rows(tokens, finish)
+    for side in range(2):
+        for move in moves[3 * side : 3 * side + 3]:
+            move.wait()
+        over_rows((side + 1) * half, finish, side * half)
     acc_ref[3:5, :] = gup_ref[0:2, :]
     acc_ref[5:7, :] = gdown_ref[0:2, :]
     for slot in range(4):
@@ -865,16 +913,24 @@
             return call(
                 attend_kernel,
                 (where, segments, hidden, normed) + parts,
-                [SMEM, SMEM, VMEM, VMEM] + [HBM] * len(parts),
+                [SMEM, SMEM, HBM, VMEM] + [HBM] * len(parts),
                 (
                     half_low, half_low, half_low,
                     shape(row_count * heads // 2, length, length, dtype=BF), half_low, full,
                 ),
-                (VMEM,) * 6,
+                (HBM,) * 5 + (VMEM,),
                 [
                     pltpu.VMEM((4, width // 2, width), BF),
-                    pltpu.VMEM((row_count, length, length), F32),
+                    pltpu.VMEM((row_count, 2, length, length), F32),
+                    pltpu.VMEM((tokens, width), F32),
+                ]
+                + [pltpu.VMEM((tokens, width // 2), BF)] * 3
+                + [
+                    pltpu.VMEM((row_count * heads // 2, length, length), BF),
+                    pltpu.VMEM((tokens, width // 2), BF),
                     dma((8,)),
+                    dma((5,)),
+                    dma((row_count * heads // 4,)),
                 ],
                 length=length,
                 quarter=quarter,
@@ -927,7 +983,7 @@
                 logdet_grad[None],
             )
             + parts_d,
-            [SMEM, SMEM, VMEM, HBM] + [VMEM] * 6 + [HBM] * 6,
+            [SMEM, SMEM, HBM, HBM] + [VMEM] * 6 + [HBM] * 6,
             (
                 shape(channels, tokens), shape(1, tokens), shape(1, row_count), shape(1, row_count),
                 shape(channels, tokens),
@@ -940,9 +996,11 @@
                 pltpu.VMEM((tokens, width), F32),
                 pltpu.VMEM((tokens, width), BF),
                 stage,
+                pltpu.VMEM((tokens, width), F32),
                 dma((4,)),
                 dma((4,)),
                 out_sems,
+                dma(()),
             ],
             length=length,
             quarter=quarter,
@@ -1000,7 +1058,7 @@
         grad_hidden1, grad_mix, gup, keep_u, *sends_u = call(
             up_back_kernel,
             (where, grad_hidden2, pre_grads, normed2, hidden1, ln2_gain) + parts_u,
-            [SMEM, VMEM, HBM] + [VMEM] * 3 + [HBM] * 6,
+            [SMEM, HBM, HBM, VMEM, HBM, VMEM] + [HBM] * 6,
             (full, low, shape(8, width), pieces, one, one),
             (VMEM, VMEM, VMEM, HBM, HBM, HBM),
             [
@@ -1008,9 +1066,12 @@
                 pltpu.VMEM((heads_size, tokens, width), BF),
                 pltpu.VMEM((tokens, width), F32),
                 stage,
+                pltpu.VMEM((tokens, width), F32),
+                pltpu.VMEM((tokens, width), F32),
                 dma((4,)),
                 dma((4,)),
                 out_sems,
+                dma((2,)),
             ],
         )
         grad_mix, *sends_u = tie(grad_mix, *sends_u)
@@ -1022,12 +1083,21 @@
             return call(
                 attend_back_kernel,
                 (where, grad_mix) + tuple(saved) + (normed1,) + chained + parts,
-                [SMEM] + [VMEM] * (7 + len(chained)) + [HBM] * len(parts),
+                [SMEM] + [HBM] * (7 + len(chained) + len(parts)),
                 (full, shape(width // 2, width, dtype=BF), mixed_pieces, mixed_pieces),
                 (VMEM, VMEM, HBM, HBM),
                 [pltpu.VMEM((4, width // 2, width), BF)]
                 + [pltpu.VMEM((tokens, width // 2), BF)] * 4
-                + [pltpu.VMEM((3, width // 2, width), BF), dma((8,)), dma((3, 2 * PIECES))],
+                + [pltpu.VMEM((3, width // 2, width), BF), dma((8,)), dma((3, 2 * PIECES))]
+                + [pltpu.VMEM((tokens, width), BF)]
+                + [pltpu.VMEM((tokens, width // 2), BF)] * 3
+                + [
+                    pltpu.VMEM((row_count * heads // 2, length, length), BF),
+                    pltpu.VMEM((tokens, width // 2), BF),
+                    pltpu.VMEM((tokens, width), BF),
+                    pltpu.VMEM((tokens, width), F32),
+                    dma((8,)),
+                ],
                 length=length,
                 quarter=quarter,
                 count=len(parts),
@@ -1059,7 +1129,7 @@
                 where, segments, labels, grad_hidden1, total_near, hidden0, ln1_gain, patches_t,
                 direct, w_in, grad_w_out, gdown, gup, gpre, gq_near, gq_far,
             ),
-            [SMEM, SMEM, SMEM] + [VMEM] * 13,
+            [SMEM] * 3 + [HBM] * 3 + [VMEM] * 10,
             (shape(channels, tokens), shape(row_count * slot_count, width + 128), last_pieces, last_pieces),
             (VMEM, VMEM, HBM, HBM),
             [
@@ -1067,7 +1137,11 @@
                 pltpu.VMEM((tokens, width), BF),
                 pltpu.VMEM((EXTRA, width), F32),
                 pltpu.VMEM((groups * GROUP, width), BF),
+                pltpu.VMEM((tokens, width), F32),
+                pltpu.VMEM((tokens, width), F32),
+                pltpu.VMEM((tokens, width), F32),
                 dma((2, groups)),
+                dma((6,)),
             ],
             length=length,
             quarter=quarter,

time: 266 us -> 262 us (0.985)
  Pallas kernels: 131 us -> 128 us
  waiting for transfers between devices: 54.6 us -> 57.4 us
    ppermute x27, waiting for transfers between devices: 19.6 us -> 23.3 us  [swap_heads(): lax.ppermute(array, 'heads', [(i, i ^ bit) for i in range(heads_size)])]
    pallas_call x13, Pallas kernels: 122 us -> 119 us  [call(): pl.pallas_call(functools.partial(kernel, **options) if options else kerne...]
  transfers between devices with their start and end apart: 55 -> 55, of which waited for: 19 -> 22; matrix products, arithmetic and copies ran while one was open for 6% -> 6% of each run, Pallas kernels for 42% -> 41%
where the time goes in v5:
time: 262 us
  Pallas kernels  128 us (49%)
  waiting for transfers between devices  57.4 us (22%)
  starting transfers between devices  51.6 us (20%)
  local copies, waits for them, and re-layouts  10.6 us (4%)
  other arithmetic  10.5 us (4%)
    pallas_call x13, Pallas kernels, call(): pl.pallas_call(functools.partial(kernel, **options) if options else kerne...  119 us
    ppermute x28, starting transfers between devices, swap_rows(): return lax.ppermute(array, 'rows', [(i, i ^ bit) for i in range(rows_size)])  37.3 us
    ppermute x28, waiting for transfers between devices, swap_rows(): return lax.ppermute(array, 'rows', [(i, i ^ bit) for i in range(rows_size)])  34.2 us
    ppermute x27, waiting for transfers between devices, swap_heads(): lax.ppermute(array, 'heads', [(i, i ^ bit) for i in range(heads_size)])  23.3 us
    ppermute x27, starting transfers between devices, swap_heads(): lax.ppermute(array, 'heads', [(i, i ^ bit) for i in range(heads_size)])  14.3 us
    pallas_call x3, Pallas kernels, add_groups(): pl.pallas_call(functools.partial(add_kernel, counts=tuple((len(group) for...  8.76 us
    unnamed x77, local copies, waits for them, and re-layouts  6.49 us
    convert_element_type x15, other arithmetic, add_low(): return total.astype(BF)  6.33 us
  transfers between devices with their start and end apart: 55, of which 22 were waited for; matrix products, arithmetic and copies ran while one was open for 6% of the time, Pallas kernels for 41%

profile of v5, /device:TPU:0, one launch (start us, length us, event | category | flops | bytes accessed | tf_op | source)
XLA Modules:
  0.0 261.5 jit_solution(15775564501534478730)
XLA Ops:
  0.7 1.4 broadcast_select_fusion
  4.0 2.6 collective-permute-start
  8.4 2.1 dynamic-slice_bitcast_fusion
  11.2 3.0 %shard_map.398 = (f32[512,768]{1,0:T(8,128)}, bf16[512,768]{1,0:T(8,128)(2,1)}) custom-call(s32[4]{0:T(128)} %pad_add_fusion.where_ref, s32[2048]{0:T(1024)} %seg_ref.9, f32[48,512]{1,0:T(8,128)} %bitcast.188, bf16[48,768]{1,0:T(8,128)(2,1)} %win_ref.1, f32[1,768]{1,0:T(1,128)} %broadcast_in_dim.29.b_ref, bf16[256,768]{1,0:T(8,128)(2,1)} %pos_ref.1, ...), custom_call_target="tpu_custom_call" | custom-call | flops 1 | bytes 1 | tf_op jit(solution)/shard_map/pallas_call | solution.py:852
  14.2 7.0 %collective-permute-done.rest_0_.far_t = bf16[400,768]{1,0:T(8,128)(2,1)S(1)} collective-permute-done((bf16[400,768]{1,0:T(8,128)(2,1)}, bf16[400,768]{1,0:T(8,128)(2,1)S(1)}, u32[]{:S(2)}, u32[]{:S(2)}) %collective-permute-start) | collective-permute-done | bytes 614432 | tf_op jit(solution)/shard_map/ppermute | solution.py:738
  21.2 1.7 collective-permute-start.2
  23.0 1.5 collective-permute-start.3
  24.5 11.2 %shard_map.399 = (bf16[512,384]{1,0:T(8,128)(2,1)}, bf16[512,384]{1,0:T(8,128)(2,1)}, bf16[512,384]{1,0:T(8,128)(2,1)}, bf16[12,256,256]{2,1,0:T(8,128)(2,1)}, b...) custom-call(s32[4]{0:T(128)} %pad_add_fusion.where_ref, s32[2048]{0:T(1024)} %seg_ref.9, ...), custom_call_target="tpu_custom_call" | custom-call | flops 1 | bytes 1 | tf_op jit(solution)/shard_map/pallas_call | solution.py:852
  35.7 1.9 collective-permute-done.3.far
  37.6 1.6 collective-permute-start.7
  40.5 10.9 %shard_map.400 = (bf16[512,384]{1,0:T(8,128)(2,1)}, bf16[512,384]{1,0:T(8,128)(2,1)}, bf16[512,384]{1,0:T(8,128)(2,1)}, bf16[12,256,256]{2,1,0:T(8,128)(2,1)}, b...) custom-call(s32[4]{0:T(128)} %pad_add_fusion.where_ref, s32[2048]{0:T(1024)} %seg_ref.9, ...), custom_call_target="tpu_custom_call" | custom-call | flops 1 | bytes 1 | tf_op jit(solution)/shard_map/pallas_call | solution.py:852
  51.5 2.2 collective-permute-done.7.far
  53.6 1.2 collective-permute-done.6.far_other
  57.2 14.1 %shard_map.401 = (bf16[512,768]{1,0:T(8,128)(2,1)}, bf16[4,512,768]{2,1,0:T(8,128)(2,1)}, bf16[4,512,768]{2,1,0:T(8,128)(2,1)}) custom-call(s32[4]{0:T(128)} %pad_add_fusion.where_ref, f32[512,768]{1,0:T(8,128)} %get-tuple-element.207.hid_ref.hid_in, f32[1,768]{1,0:T(1,128)} %gain_ref.6, f32[1,768]{1,0:T(1,128)} %bias_ref.3, bf16[768,768]{1,0:T(8,128)(2,1)} %bitcast.156, ...), custom_call_target="tpu_custom_call" | custom-call | flops 1 | bytes 1 | tf_op jit(solution)/shard_map/pallas_call | solution.py:852
  72.3 1.1 collective-permute-done.14.cross_other
  74.2 13.1 %shard_map.402 = (f32[48,512]{1,0:T(8,128)}, f32[1,512]{1,0:T(1,128)}, f32[1,2]{1,0:T(1,128)}, f32[1,2]{1,0:T(1,128)}, f32[48,512]{1,0:T(8,128)}, /*index=5*/f32...) custom-call(s32[4]{0:T(128)} %pad_add_fusion.where_ref, ...), custom_call_target="tpu_custom_call" | custom-call | flops 1 | bytes 1 | tf_op jit(solution)/shard_map/pallas_call | solution.py:852
  87.9 8.3 %shard_map.403 = (bf16[4,512,768]{2,1,0:T(8,128)(2,1)}, f32[8,768]{1,0:T(8,128)}) custom-call(s32[4]{0:T(128)} %pad_add_fusion.where_ref, f32[512,768]{1,0:T(8,128)} %get-tuple-element.220.grad_ref.grad_in, bf16[4,512,768]{2,1,0:T(8,128)(2,1)} %get-tuple-element.221.slope_in, bf16[768,768]{1,0:T(8,128)(2,1)} %bitcast.154, ...), custom_call_target="tpu_custom_call" | custom-call | flops 1 | bytes 1 | tf_op jit(solution)/shard_map/pallas_call | solution.py:852
  96.3 1.0 copy-done.22
  97.3 2.6 shard_map.404
  100.4 13.0 %shard_map.405 = (f32[512,768]{1,0:T(8,128)}, bf16[512,768]{1,0:T(8,128)(2,1)}, f32[8,768]{1,0:T(8,128)}, bf16[2,4,192,768]{3,2,1,0:T(8,128)(2,1)}, bf16[4,192,7...) custom-call(s32[4]{0:T(128)} %pad_add_fusion.where_ref, f32[512,768]{1,0:T(8,128)} %get-tuple-element.220.grad_ref.grad_in, ...), custom_call_target="tpu_custom_call" | custom-call | flops 1 | bytes 1 | tf_op jit(solution)/shard_map/pallas_call | solution.py:852
  113.9 13.1 %shard_map.406 = (f32[512,768]{1,0:T(8,128)}, bf16[384,768]{1,0:T(8,128)(2,1)}, bf16[4,144,768]{2,1,0:T(8,128)(2,1)}, bf16[4,144,768]{2,1,0:T(8,128)(2,1)}) custom-call(s32[4]{0:T(128)} %pad_add_fusion.where_ref, bf16[512,768]{1,0:T(8,128)(2,1)} %get-tuple-element.235.mix_in, bf16[512,384]{1,0:T(8,128)(2,1)} %get-tuple-element.236.q_in, ...), custom_call_target="tpu_custom_call" | custom-call | flops 1 | bytes 1 | tf_op jit(solution)/shard_map/pallas_call | solution.py:852
  127.0 1.0 collective-permute-done.17.refs_2_
  128.1 1.0 copy-done.7
  129.8 3.3 %shard_map.407 = (bf16[1,1,2,192,768]{4,3,2,1,0:T(8,128)(2,1)}, bf16[1,2,1,192,768]{4,3,2,1,0:T(8,128)(2,1)}, bf16[1,2,1,192,768]{4,3,2,1,0:T(8,128)(2,1)}) custom-call(bf16[2,2,2,192,768]{4,3,2,1,0:T(8,128)(2,1)} %bitcast.145, bf16[1,2,2,192,768]{4,3,2,1,0:T(8,128)(2,1)} %bitcast.159, bf16[1,2,2,192,768]{4,3,2,1,0:T(8,128)(2,1)} %copy-done.7, ...), custom_call_target="tpu_custom_call" | custom-call | flops 1 | bytes 1 | tf_op jit(solution)/shard_map/pallas_call | solution.py:1022
  134.1 1.6 collective-permute-start.22
  136.1 13.0 %shard_map.408 = (f32[512,768]{1,0:T(8,128)}, bf16[384,768]{1,0:T(8,128)(2,1)}, bf16[4,144,768]{2,1,0:T(8,128)(2,1)}, bf16[4,144,768]{2,1,0:T(8,128)(2,1)}) custom-call(s32[4]{0:T(128)} %pad_add_fusion.where_ref, bf16[512,768]{1,0:T(8,128)(2,1)} %get-tuple-element.235.mix_in, bf16[512,384]{1,0:T(8,128)(2,1)} %get-tuple-element.245.q_in, ...), custom_call_target="tpu_custom_call" | custom-call | flops 1 | bytes 1 | tf_op jit(solution)/shard_map/pallas_call | solution.py:852
  149.9 2.9 %shard_map.409 = (bf16[1,1,1,192,768]{4,3,2,1,0:T(8,128)(2,1)}, bf16[1,2,2,144,768]{4,3,2,1,0:T(8,128)(2,1)}) custom-call(bf16[2,2,2,192,768]{4,3,2,1,0:T(8,128)(2,1)} %bitcast.146, bf16[1,2,2,192,768]{4,3,2,1,0:T(8,128)(2,1)} %bitcast.160, bf16[1,2,2,192,768]{4,3,2,1,0:T(8,128)(2,1)} %copy-done.7, bf16[1,1,2,192,768]{4,3,2,1,0:T(8,128)(2,1)} %copy-done.21, ...), custom_call_target="tpu_custom_call" | custom-call | flops 1 | bytes 1 | tf_op jit(solution)/shard_map/pallas_call | solution.py:1022
  152.8 1.6 collective-permute-start.24
  154.4 9.1 %shard_map.410 = (f32[48,512]{1,0:T(8,128)}, f32[8,896]{1,0:T(8,128)}, bf16[2,4,80,768]{3,2,1,0:T(8,128)(2,1)}, bf16[2,4,80,768]{3,2,1,0:T(8,128)(2,1)}) custom-call(s32[4]{0:T(128)} %pad_add_fusion.where_ref, s32[2048]{0:T(1024)} %seg_ref.9, s32[2,4]{1,0:T(2,128)} %label_ref.1, f32[512,768]{1,0:T(8,128)} %get-tuple-element.270.grad_in, ...), custom_call_target="tpu_custom_call" | custom-call | flops 1 | bytes 1 | tf_op jit(solution)/shard_map/pallas_call | solution.py:852
  163.5 4.9 %collective-permute-done.24 = bf16[1,1,1,192,768]{4,3,2,1,0:T(8,128)(2,1)S(1)} collective-permute-done((bf16[1,1,1,192,768]{4,3,2,1,0:T(8,128)(2,1)}, bf16[1,1,1,192,768]{4,3,2,1,0:T(8,128)(2,1)S(1)}, u32[]{:S(2)}, u32[]{:S(2)}) %collective-permute-start.24) | collective-permute-done | bytes 294944 | tf_op jit(solution)/shard_map/ppermute | solution.py:741
  169.1 1.5 add_convert_fusion.8
  170.7 1.4 add_convert_fusion.6
  172.1 1.2 collective-permute-start.32
  174.3 1.6 collective-permute-start.28
  176.0 6.0 %collective-permute-done.32 = bf16[1,1,1,192,768]{4,3,1,2,0:T(8,128)(2,1)S(1)} collective-permute-done((bf16[1,1,1,192,768]{4,3,1,2,0:T(8,128)(2,1)S(1)}, bf16[1,1,1,192,768]{4,3,1,2,0:T(8,128)(2,1)S(1)}, u32[]{:S(2)}, u32[]{:S(2)}) %collective-permute-start.32) | collective-permute-done | bytes 294944 | tf_op jit(solution)/shard_map/ppermute | solution.py:741
  182.0 2.6 collective-permute-start.35
  184.6 3.3 %collective-permute-done.29 = bf16[1,1,1,192,768]{4,3,1,2,0:T(8,128)(2,1)S(1)} collective-permute-done((bf16[1,1,1,192,768]{4,3,1,2,0:T(8,128)(2,1)S(1)}, bf16[1,1,1,192,768]{4,3,1,2,0:T(8,128)(2,1)S(1)}, u32[]{:S(2)}, u32[]{:S(2)}) %collective-permute-start.29) | collective-permute-done | bytes 294944 | tf_op jit(solution)/shard_map/ppermute | solution.py:741
  187.9 1.2 add_convert_fusion.5
  189.1 1.4 collective-permute-start.33
  190.5 1.7 collective-permute-done.28
  192.3 1.6 collective-permute-start.31
  194.1 1.2 collective-permute-start.30
  195.3 3.8 %collective-permute-done.33 = bf16[1,1,1,192,768]{4,3,1,2,0:T(8,128)(2,1)S(1)} collective-permute-done((bf16[1,1,1,192,768]{4,3,1,2,0:T(8,128)(2,1)S(1)}, bf16[1,1,1,192,768]{4,3,1,2,0:T(8,128)(2,1)S(1)}, u32[]{:S(2)}, u32[]{:S(2)}) %collective-permute-start.33) | collective-permute-done | bytes 294944 | tf_op jit(solution)/shard_map/ppermute | solution.py:738
  199.1 1.2 add_convert_fusion.4
  200.2 2.6 %collective-permute-start.44 = (bf16[1,1,1,192,768]{4,3,1,2,0:T(8,128)(2,1)S(1)}, bf16[1,1,1,192,768]{4,3,1,2,0:T(8,128)(2,1)S(1)}, u32[]{:S(2)}, u32[]{:S(2)}) collective-permute-start(bf16[1,1,1,192,768]{4,3,1,2,0:T(8,128)(2,1)S(1)} %add_convert_fusion.4), channel_id=1, source_target_pairs={{0,16},{4,20},{8,24},{12,28},{16,0},{20,4},{24,8},{28,12},{1,17},{... | collective-permute-start | bytes 884744 | tf_op jit(solution)/shard_map/ppermute | solution.py:741
  203.1 1.1 collective-permute-start.36
  204.2 1.4 collective-permute-done.30
  205.7 1.6 collective-permute-start.34
  208.1 2.7 %collective-permute-start.41 = (bf16[1,1,1,80,768]{4,3,1,2,0:T(8,128)(2,1)S(1)}, bf16[1,1,1,80,768]{4,3,1,2,0:T(8,128)(2,1)S(1)}, u32[]{:S(2)}, u32[]{:S(2)}) collective-permute-start(bf16[1,1,1,80,768]{4,3,1,2,0:T(8,128)(2,1)S(1)} %add_convert_fusion.14), channel_id=1, source_target_pairs={{0,16},{4,20},{8,24},{12,28},{16,0},{20,4},{24,8},{28,12},{1,17},{... | collective-permute-start | bytes 368648 | tf_op jit(solution)/shard_map/ppermute | solution.py:741
  210.9 1.6 collective-permute-start.39
  212.5 10.2 %collective-permute-done.34 = bf16[1,1,1,144,768]{4,3,2,1,0:T(8,128)(2,1)S(1)} collective-permute-done((bf16[1,1,1,144,768]{4,3,2,1,0:T(8,128)(2,1)S(1)}, bf16[1,1,1,144,768]{4,3,2,1,0:T(8,128)(2,1)S(1)}, u32[]{:S(2)}, u32[]{:S(2)}) %collective-permute-start.34) | collective-permute-done | bytes 221216 | tf_op jit(solution)/shard_map/ppermute | solution.py:741
  223.9 1.2 collective-permute-start.42
  226.1 1.8 collective-permute-done.43
  227.9 4.4 %collective-permute-start.47 = (bf16[1,2,1,80,768]{4,3,1,2,0:T(8,128)(2,1)S(1)}, bf16[1,2,1,80,768]{4,3,1,2,0:T(8,128)(2,1)S(1)}, u32[]{:S(2)}, u32[]{:S(2)}) collective-permute-start(bf16[1,2,1,80,768]{4,3,1,2,0:T(8,128)(2,1)S(1)} %pad_maximum_fusion.5), channel_id=1, source_target_pairs={{0,8},{4,12},{8,0},{12,4},{16,24},{20,28},{24,16},{28,20},{1,9},{5... | collective-permute-start | bytes 737288 | tf_op jit(solution)/shard_map/ppermute | solution.py:741
  233.1 1.1 collective-permute-start.54
  234.2 1.2 collective-permute-start.45
  235.4 1.8 collective-permute-done.48
  240.3 1.0 collective-permute-start.49
  241.4 3.4 %collective-permute-done.50 = bf16[1,4,32,768]{3,2,1,0:T(8,128)(2,1)S(1)} collective-permute-done((bf16[1,4,32,768]{3,2,1,0:T(8,128)(2,1)S(1)}, bf16[1,4,32,768]{3,2,1,0:T(8,128)(2,1)S(1)}, u32[]{:S(2)}, u32[]{:S(2)}) %collective-permute-start.50) | collective-permute-done | bytes 196640 | tf_op jit(solution)/shard_map/ppermute | solution.py:738
  245.1 2.2 fusion.1
  248.1 3.2 %shard_map.413 = f32[768,768]{1,0:T(8,128)} custom-call(s32[4]{0:T(128)} %pad_add_fusion.where_ref, bf16[1,2,192,768]{3,2,1,0:T(8,128)(2,1)} %bitcast.170, bf16[1,2,192,768]{3,2,1,0:T(8,128)(2,1)} %bitcast.200), custom_call_target="tpu_custom_call" | custom-call | flops 1 | bytes 1 | tf_op jit(solution)/shard_map/pallas_call | solution.py:852
  251.4 2.3 collective-permute-done.53
  254.5 3.3 %shard_map.412 = f32[768,768]{1,0:T(8,128)} custom-call(s32[4]{0:T(128)} %pad_add_fusion.where_ref, bf16[2,1,192,768]{3,2,1,0:T(8,128)(2,1)} %bitcast.171, bf16[2,1,192,768]{3,2,1,0:T(8,128)(2,1)} %bitcast.201), custom_call_target="tpu_custom_call" | custom-call | flops 1 | bytes 1 | tf_op jit(solution)/shard_map/pallas_call | solution.py:852
  257.8 3.5 %shard_map.411 = (f32[192,768]{1,0:T(8,128)}, f32[192,768]{1,0:T(8,128)}, f32[192,768]{1,0:T(8,128)}, f32[192,768]{1,0:T(8,128)}, f32[48,768]{1,0:T(8,128)}, /*i...) custom-call(s32[4]{0:T(128)} %pad_add_fusion.where_ref, ...), custom_call_target="tpu_custom_call" | custom-call | flops 1 | bytes 1 | tf_op jit(solution)/shard_map/pallas_call | solution.py:852
  (183 shorter events, 25.7 us)
Async XLA Ops:
  3.4 7.1 %copy-start.2 = (bf16[2,400,768]{2,1,0:T(8,128)(2,1)}, bf16[2,400,768]{2,1,0:T(8,128)(2,1)S(1)}, u32[]{:S(2)}) copy-start(bf16[2,400,768]{2,1,0:T(8,128)(2,1)S(1)} %pad_maximum_fusion.rest_0_.own_t.rest_1_) | copy-start | bytes 3686404
  3.5 21.0 %collective-permute-start.1 = (bf16[2,400,768]{2,1,0:T(8,128)(2,1)S(1)}, bf16[2,400,768]{2,1,0:T(8,128)(2,1)}, u32[]{:S(2)}, u32[]{:S(2)}) collective-permute-start(bf16[2,400,768]{2,1,0:T(8,128)(2,1)S(1)} %pad_maximum_fusion.rest_0_.own_t.rest_1_), channel_id=1, source_target_pairs={{0,1},{1,0},{2,3},{3,2},{4,5},{5,4},{6,7},{7,6},{8,9},{9,8},{10,11... | collective-permute-start | bytes 3686408 | tf_op jit(solution)/shard_map/ppermute | solution.py:738
  4.0 17.3 %collective-permute-start = (bf16[400,768]{1,0:T(8,128)(2,1)}, bf16[400,768]{1,0:T(8,128)(2,1)S(1)}, u32[]{:S(2)}, u32[]{:S(2)}) collective-permute-start(bf16[400,768]{1,0:T(8,128)(2,1)} %get-tuple-element.368), channel_id=1, source_target_pairs={{0,2},{1,3},{2,0},{3,1},{4,6},{5,7},{6,4},{7,5},{8,10},{9,11},{10,... | collective-permute-start | bytes 1843208 | tf_op jit(solution)/shard_map/ppermute | solution.py:738
  21.2 14.5 %copy-start.8 = (bf16[400,768]{1,0:T(8,128)(2,1)}, bf16[400,768]{1,0:T(8,128)(2,1)S(1)}, u32[]{:S(2)}) copy-start(bf16[400,768]{1,0:T(8,128)(2,1)S(1)} %collective-permute-done.rest_0_.far_t) | copy-start | bytes 1843204
  21.2 16.3 %collective-permute-start.2 = (bf16[400,768]{1,0:T(8,128)(2,1)S(1)}, bf16[400,768]{1,0:T(8,128)(2,1)}, u32[]{:S(2)}, u32[]{:S(2)}) collective-permute-start(bf16[400,768]{1,0:T(8,128)(2,1)S(1)} %collective-permute-done.rest_0_.far_t), channel_id=1, source_target_pairs={{0,4},{4,0},{8,12},{12,8},{16,20},{20,16},{24,28},{28,24},{1,5},{5... | collective-permute-start | bytes 1843208 | tf_op jit(solution)/shard_map/ppermute | solution.py:741
  23.0 14.6 %collective-permute-start.3 = (bf16[384,768]{1,0:T(8,128)(2,1)S(1)}, bf16[384,768]{1,0:T(8,128)(2,1)S(1)}, u32[]{:S(2)}, u32[]{:S(2)}) collective-permute-start(bf16[384,768]{1,0:T(8,128)(2,1)S(1)} %get-tuple-element.194), channel_id=1, source_target_pairs={{0,2},{1,3},{2,0},{3,1},{4,6},{5,7},{6,4},{7,5},{8,10},{9,11},{10,... | collective-permute-start | bytes 1769480 | tf_op jit(solution)/shard_map/ppermute | solution.py:738
  24.5 15.5 %collective-permute-start.4 = (bf16[400,768]{1,0:T(8,128)(2,1)S(1)}, bf16[400,768]{1,0:T(8,128)(2,1)}, u32[]{:S(2)}, u32[]{:S(2)}) collective-permute-start(bf16[400,768]{1,0:T(8,128)(2,1)S(1)} %collective-permute-done.rest_0_.far_t), channel_id=1, source_target_pairs={{0,1},{1,0},{2,3},{3,2},{4,5},{5,4},{6,7},{7,6},{8,9},{9,8},{10,11... | collective-permute-start | bytes 1843208 | tf_op jit(solution)/shard_map/ppermute | solution.py:738
  24.5 15.5 %copy-start.5 = (bf16[1,768,768]{2,1,0:T(8,128)(2,1)S(1)}, bf16[1,768,768]{2,1,0:T(8,128)(2,1)}, u32[]{:S(2)}) copy-start(bf16[1,768,768]{2,1,0:T(8,128)(2,1)} %param.38) | copy-start | bytes 3538948
  37.6 3.0 %collective-permute-start.5 = (bf16[400,768]{1,0:T(8,128)(2,1)}, bf16[400,768]{1,0:T(8,128)(2,1)}, u32[]{:S(2)}, u32[]{:S(2)}) collective-permute-start(bf16[400,768]{1,0:T(8,128)(2,1)} %collective-permute-done.2.rest_1_), channel_id=1, source_target_pairs={{0,1},{1,0},{2,3},{3,2},{4,5},{5,4},{6,7},{7,6},{8,9},{9,8},{10,11... | collective-permute-start | bytes 1843208 | tf_op jit(solution)/shard_map/ppermute | solution.py:738
  37.6 16.1 %collective-permute-start.7 = (bf16[384,768]{1,0:T(8,128)(2,1)}, bf16[384,768]{1,0:T(8,128)(2,1)}, u32[]{:S(2)}, u32[]{:S(2)}) collective-permute-start(bf16[384,768]{1,0:T(8,128)(2,1)} %get-tuple-element.195), channel_id=1, source_target_pairs={{0,2},{1,3},{2,0},{3,1},{4,6},{5,7},{6,4},{7,5},{8,10},{9,11},{10,... | collective-permute-start | bytes 1769480 | tf_op jit(solution)/shard_map/ppermute | solution.py:738
  39.2 16.6 %copy-start.4 = (bf16[1,768,768]{2,1,0:T(8,128)(2,1)S(1)}, bf16[1,768,768]{2,1,0:T(8,128)(2,1)}, u32[]{:S(2)}) copy-start(bf16[1,768,768]{2,1,0:T(8,128)(2,1)} %param.40) | copy-start | bytes 3538948
  39.2 15.7 %collective-permute-start.6 = (bf16[384,768]{1,0:T(8,128)(2,1)}, bf16[384,768]{1,0:T(8,128)(2,1)}, u32[]{:S(2)}, u32[]{:S(2)}) collective-permute-start(bf16[384,768]{1,0:T(8,128)(2,1)} %copy-done.17), channel_id=1, source_target_pairs={{0,4},{4,0},{8,12},{12,8},{16,20},{20,16},{24,28},{28,24},{1,5},{5... | collective-permute-start | bytes 1769480 | tf_op jit(solution)/shard_map/ppermute | solution.py:741
  40.0 16.0 %collective-permute-start.8 = (bf16[768,768]{1,0:T(8,128)(2,1)S(1)}, bf16[768,768]{1,0:T(8,128)(2,1)}, u32[]{:S(2)}, u32[]{:S(2)}) collective-permute-start(bf16[768,768]{1,0:T(8,128)(2,1)S(1)} %bitcast.158), channel_id=1, source_target_pairs={{0,1},{1,0},{2,3},{3,2},{4,5},{5,4},{6,7},{7,6},{8,9},{9,8},{10,11... | collective-permute-start | bytes 3538952 | tf_op jit(solution)/shard_map/ppermute | solution.py:738
  40.0 16.3 %collective-permute-start.9 = (bf16[384,768]{1,0:T(8,128)(2,1)}, bf16[384,768]{1,0:T(8,128)(2,1)}, u32[]{:S(2)}, u32[]{:S(2)}) collective-permute-start(bf16[384,768]{1,0:T(8,128)(2,1)} %copy-done.17), channel_id=1, source_target_pairs={{0,1},{1,0},{2,3},{3,2},{4,5},{5,4},{6,7},{7,6},{8,9},{9,8},{10,11... | collective-permute-start | bytes 1769480 | tf_op jit(solution)/shard_map/ppermute | solution.py:738
  54.9 2.3 collective-permute-start.10
  54.9 16.4 %collective-permute-start.12 = (bf16[384,768]{1,0:T(8,128)(2,1)}, bf16[384,768]{1,0:T(8,128)(2,1)S(1)}, u32[]{:S(2)}, u32[]{:S(2)}) collective-permute-start(bf16[384,768]{1,0:T(8,128)(2,1)} %collective-permute-done.7.far), channel_id=1, source_target_pairs={{0,4},{4,0},{8,12},{12,8},{16,20},{20,16},{24,28},{28,24},{1,5},{5... | collective-permute-start | bytes 1769480 | tf_op jit(solution)/shard_map/ppermute | solution.py:741
  55.8 15.7 %copy-start.37 = (f32[96]{0:T(128)S(1)}, f32[96]{0:T(128)}, u32[]{:S(2)}) copy-start(f32[96]{0:T(128)} %param.43) | copy-start | bytes 1156
  55.8 16.5 %collective-permute-start.11 = (bf16[768,768]{1,0:T(8,128)(2,1)S(1)}, bf16[768,768]{1,0:T(8,128)(2,1)}, u32[]{:S(2)}, u32[]{:S(2)}) collective-permute-start(bf16[768,768]{1,0:T(8,128)(2,1)S(1)} %bitcast.155), channel_id=1, source_target_pairs={{0,1},{1,0},{2,3},{3,2},{4,5},{5,4},{6,7},{7,6},{8,9},{9,8},{10,11... | collective-permute-start | bytes 3538952 | tf_op jit(solution)/shard_map/ppermute | solution.py:738
  56.0 16.2 %collective-permute-start.13 = (bf16[384,768]{1,0:T(8,128)(2,1)}, bf16[384,768]{1,0:T(8,128)(2,1)S(1)}, u32[]{:S(2)}, u32[]{:S(2)}) collective-permute-start(bf16[384,768]{1,0:T(8,128)(2,1)} %collective-permute-done.7.far), channel_id=1, source_target_pairs={{0,1},{1,0},{2,3},{3,2},{4,5},{5,4},{6,7},{7,6},{8,9},{9,8},{10,11... | collective-permute-start | bytes 1769480 | tf_op jit(solution)/shard_map/ppermute | solution.py:738
  71.3 2.1 collective-permute-start.14
  87.3 8.9 %collective-permute-start.15 = (bf16[4,192,768]{2,1,0:T(8,128)(2,1)}, bf16[4,192,768]{2,1,0:T(8,128)(2,1)S(1)}, u32[]{:S(2)}, u32[]{:S(2)}) collective-permute-start(bf16[4,192,768]{2,1,0:T(8,128)(2,1)} %get-tuple-element.223), channel_id=1, source_target_pairs={{0,1},{1,0},{2,3},{3,2},{4,5},{5,4},{6,7},{7,6},{8,9},{9,8},{10,11... | collective-permute-start | bytes 3538952 | tf_op jit(solution)/shard_map/ppermute | solution.py:738
  87.5 8.7 %collective-permute-start.16 = (bf16[4,192,768]{2,1,0:T(8,128)(2,1)}, bf16[4,192,768]{2,1,0:T(8,128)(2,1)S(1)}, u32[]{:S(2)}, u32[]{:S(2)}) collective-permute-start(bf16[4,192,768]{2,1,0:T(8,128)(2,1)} %get-tuple-element.224), channel_id=1, source_target_pairs={{0,1},{1,0},{2,3},{3,2},{4,5},{5,4},{6,7},{7,6},{8,9},{9,8},{10,11... | collective-permute-start | bytes 3538952 | tf_op jit(solution)/shard_map/ppermute | solution.py:738
  99.9 28.2 %collective-permute-start.17 = (bf16[1,2,2,192,768]{4,3,2,1,0:T(8,128)(2,1)}, bf16[1,2,2,192,768]{4,3,2,1,0:T(8,128)(2,1)S(1)}, u32[]{:S(2)}, u32[]{:S(2)}) collective-permute-start(bf16[1,2,2,192,768]{4,3,2,1,0:T(8,128)(2,1)} %shard_map.404), channel_id=1, source_target_pairs={{0,2},{1,3},{2,0},{3,1},{4,6},{5,7},{6,4},{7,5},{8,10},{9,11},{10,... | collective-permute-start | bytes 3538952 | tf_op jit(solution)/shard_map/ppermute | solution.py:738
  113.3 14.8 %collective-permute-start.18 = (bf16[4,192,768]{2,1,0:T(8,128)(2,1)}, bf16[4,192,768]{2,1,0:T(8,128)(2,1)S(1)}, u32[]{:S(2)}, u32[]{:S(2)}) collective-permute-start(bf16[4,192,768]{2,1,0:T(8,128)(2,1)} %get-tuple-element.251), channel_id=1, source_target_pairs={{0,1},{1,0},{2,3},{3,2},{4,5},{5,4},{6,7},{7,6},{8,9},{9,8},{10,11... | collective-permute-start | bytes 3538952 | tf_op jit(solution)/shard_map/ppermute | solution.py:738
  113.4 14.7 %collective-permute-start.19 = (bf16[4,192,768]{2,1,0:T(8,128)(2,1)}, bf16[4,192,768]{2,1,0:T(8,128)(2,1)S(1)}, u32[]{:S(2)}, u32[]{:S(2)}) collective-permute-start(bf16[4,192,768]{2,1,0:T(8,128)(2,1)} %get-tuple-element.252), channel_id=1, source_target_pairs={{0,1},{1,0},{2,3},{3,2},{4,5},{5,4},{6,7},{7,6},{8,9},{9,8},{10,11... | collective-permute-start | bytes 3538952 | tf_op jit(solution)/shard_map/ppermute | solution.py:738
  128.1 21.0 %collective-permute-start.20 = (bf16[4,144,768]{2,1,0:T(8,128)(2,1)}, bf16[4,144,768]{2,1,0:T(8,128)(2,1)}, u32[]{:S(2)}, u32[]{:S(2)}) collective-permute-start(bf16[4,144,768]{2,1,0:T(8,128)(2,1)} %get-tuple-element.263), channel_id=1, source_target_pairs={{0,1},{1,0},{2,3},{3,2},{4,5},{5,4},{6,7},{7,6},{8,9},{9,8},{10,11... | collective-permute-start | bytes 2654216 | tf_op jit(solution)/shard_map/ppermute | solution.py:738
  133.1 16.0 %collective-permute-start.21 = (bf16[1,1,2,192,768]{4,3,2,1,0:T(8,128)(2,1)}, bf16[1,1,2,192,768]{4,3,2,1,0:T(8,128)(2,1)S(1)}, u32[]{:S(2)}, u32[]{:S(2)}) collective-permute-start(bf16[1,1,2,192,768]{4,3,2,1,0:T(8,128)(2,1)} %get-tuple-element.264), channel_id=1, source_target_pairs={{0,4},{4,0},{8,12},{12,8},{16,20},{20,16},{24,28},{28,24},{1,5},{5... | collective-permute-start | bytes 1769480 | tf_op jit(solution)/shard_map/ppermute | solution.py:741
  134.1 29.4 %collective-permute-start.22 = (bf16[1,2,1,192,768]{4,3,1,2,0:T(8,128)(2,1)}, bf16[1,2,1,192,768]{4,3,1,2,0:T(8,128)(2,1)}, u32[]{:S(2)}, u32[]{:S(2)}) collective-permute-start(bf16[1,2,1,192,768]{4,3,1,2,0:T(8,128)(2,1)} %bitcast.209), channel_id=1, source_target_pairs={{0,8},{4,12},{8,0},{12,4},{16,24},{20,28},{24,16},{28,20},{1,9},{5... | collective-permute-start | bytes 1769480 | tf_op jit(solution)/shard_map/ppermute | solution.py:741
  135.7 27.9 %collective-permute-start.23 = (bf16[1,2,1,192,768]{4,3,1,2,0:T(8,128)(2,1)}, bf16[1,2,1,192,768]{4,3,1,2,0:T(8,128)(2,1)}, u32[]{:S(2)}, u32[]{:S(2)}) collective-permute-start(bf16[1,2,1,192,768]{4,3,1,2,0:T(8,128)(2,1)} %bitcast.208), channel_id=1, source_target_pairs={{0,8},{4,12},{8,0},{12,4},{16,24},{20,28},{24,16},{28,20},{1,9},{5... | collective-permute-start | bytes 1769480 | tf_op jit(solution)/shard_map/ppermute | solution.py:741
  152.8 15.6 %collective-permute-start.24 = (bf16[1,1,1,192,768]{4,3,2,1,0:T(8,128)(2,1)}, bf16[1,1,1,192,768]{4,3,2,1,0:T(8,128)(2,1)S(1)}, u32[]{:S(2)}, u32[]{:S(2)}) collective-permute-start(bf16[1,1,1,192,768]{4,3,2,1,0:T(8,128)(2,1)} %get-tuple-element.283), channel_id=1, source_target_pairs={{0,8},{4,12},{8,0},{12,4},{16,24},{20,28},{24,16},{28,20},{1,9},{5... | collective-permute-start | bytes 884744 | tf_op jit(solution)/shard_map/ppermute | solution.py:741
  154.4 16.3 %copy-start.3 = (bf16[2,4,192,768]{3,2,1,0:T(8,128)(2,1)S(1)}, bf16[2,4,192,768]{3,2,1,0:T(8,128)(2,1)}, u32[]{:S(2)}) copy-start(bf16[2,4,192,768]{3,2,1,0:T(8,128)(2,1)} %get-tuple-element.254) | copy-start | bytes 7077892
  163.5 7.2 %copy-start.10 = (bf16[4,192,768]{2,1,0:T(8,128)(2,1)S(1)}, bf16[4,192,768]{2,1,0:T(8,128)(2,1)}, u32[]{:S(2)}) copy-start(bf16[4,192,768]{2,1,0:T(8,128)(2,1)} %copy-done.9) | copy-start | bytes 3538948
  168.4 5.8 %collective-permute-start.27 = (bf16[2,4,80,768]{3,2,1,0:T(8,128)(2,1)}, bf16[2,4,80,768]{3,2,1,0:T(8,128)(2,1)S(1)}, u32[]{:S(2)}, u32[]{:S(2)}) collective-permute-start(bf16[2,4,80,768]{3,2,1,0:T(8,128)(2,1)} %get-tuple-element.294), channel_id=1, source_target_pairs={{0,1},{1,0},{2,3},{3,2},{4,5},{5,4},{6,7},{7,6},{8,9},{9,8},{10,11... | collective-permute-start | bytes 2949128 | tf_op jit(solution)/shard_map/ppermute | solution.py:738
  168.4 25.5 %collective-permute-start.26 = (bf16[1,2,2,144,768]{4,3,2,1,0:T(8,128)(2,1)}, bf16[1,2,2,144,768]{4,3,2,1,0:T(8,128)(2,1)S(1)}, u32[]{:S(2)}, u32[]{:S(2)}) collective-permute-start(bf16[1,2,2,144,768]{4,3,2,1,0:T(8,128)(2,1)} %get-tuple-element.291), channel_id=1, source_target_pairs={{0,2},{1,3},{2,0},{3,1},{4,6},{5,7},{6,4},{7,5},{8,10},{9,11},{10,... | collective-permute-start | bytes 2654216 | tf_op jit(solution)/shard_map/ppermute | solution.py:738
  169.1 24.8 %collective-permute-start.25 = (bf16[4,144,768]{2,1,0:T(8,128)(2,1)}, bf16[4,144,768]{2,1,0:T(8,128)(2,1)S(1)}, u32[]{:S(2)}, u32[]{:S(2)}) collective-permute-start(bf16[4,144,768]{2,1,0:T(8,128)(2,1)} %get-tuple-element.290), channel_id=1, source_target_pairs={{0,1},{1,0},{2,3},{3,2},{4,5},{5,4},{6,7},{7,6},{8,9},{9,8},{10,11... | collective-permute-start | bytes 2654216 | tf_op jit(solution)/shard_map/ppermute | solution.py:738
  172.1 9.9 %collective-permute-start.32 = (bf16[1,1,1,192,768]{4,3,1,2,0:T(8,128)(2,1)S(1)}, bf16[1,1,1,192,768]{4,3,1,2,0:T(8,128)(2,1)S(1)}, u32[]{:S(2)}, u32[]{:S(2)}) collective-permute-start(bf16[1,1,1,192,768]{4,3,1,2,0:T(8,128)(2,1)S(1)} %get-tuple-element.302), channel_id=1, source_target_pairs={{0,4},{4,0},{8,12},{12,8},{16,20},{20,16},{24,28},{28,24},{1,5},{5... | collective-permute-start | bytes 884744 | tf_op jit(solution)/shard_map/ppermute | solution.py:741
  173.3 14.6 %collective-permute-start.29 = (bf16[1,1,1,192,768]{4,3,1,2,0:T(8,128)(2,1)S(1)}, bf16[1,1,1,192,768]{4,3,1,2,0:T(8,128)(2,1)S(1)}, u32[]{:S(2)}, u32[]{:S(2)}) collective-permute-start(bf16[1,1,1,192,768]{4,3,1,2,0:T(8,128)(2,1)S(1)} %get-tuple-element.303), channel_id=1, source_target_pairs={{0,4},{4,0},{8,12},{12,8},{16,20},{20,16},{24,28},{28,24},{1,5},{5... | collective-permute-start | bytes 884744 | tf_op jit(solution)/shard_map/ppermute | solution.py:741
  174.3 17.9 %collective-permute-start.28 = (bf16[2,2,1,80,768]{4,3,1,2,0:T(8,128)(2,1)S(1)}, bf16[2,2,1,80,768]{4,3,1,2,0:T(8,128)(2,1)S(1)}, u32[]{:S(2)}, u32[]{:S(2)}) collective-permute-start(bf16[2,2,1,80,768]{4,3,1,2,0:T(8,128)(2,1)S(1)} %add_convert_fusion), channel_id=1, source_target_pairs={{0,8},{4,12},{8,0},{12,4},{16,24},{20,28},{24,16},{28,20},{1,9},{5... | collective-permute-start | bytes 1474568 | tf_op jit(solution)/shard_map/ppermute | solution.py:741
  176.0 18.0 %copy-start.28 = (bf16[4,144,768]{2,1,0:T(8,128)(2,1)S(1)}, bf16[4,144,768]{2,1,0:T(8,128)(2,1)}, u32[]{:S(2)}) copy-start(bf16[4,144,768]{2,1,0:T(8,128)(2,1)} %get-tuple-element.289) | copy-start | bytes 2654212
  182.0 28.8 %collective-permute-start.35 = (bf16[1,1,1,192,768]{4,3,2,1,0:T(8,128)(2,1)S(1)}, bf16[1,1,1,192,768]{4,3,2,1,0:T(8,128)(2,1)S(1)}, u32[]{:S(2)}, u32[]{:S(2)}) collective-permute-start(bf16[1,1,1,192,768]{4,3,2,1,0:T(8,128)(2,1)S(1)} %add_convert_fusion.8), channel_id=1, source_target_pairs={{0,16},{4,20},{8,24},{12,28},{16,0},{20,4},{24,8},{28,12},{1,17},{... | collective-permute-start | bytes 884744 | tf_op jit(solution)/shard_map/ppermute | solution.py:741
  189.1 10.0 %collective-permute-start.33 = (bf16[1,1,1,192,768]{4,3,1,2,0:T(8,128)(2,1)S(1)}, bf16[1,1,1,192,768]{4,3,1,2,0:T(8,128)(2,1)S(1)}, u32[]{:S(2)}, u32[]{:S(2)}) collective-permute-start(bf16[1,1,1,192,768]{4,3,1,2,0:T(8,128)(2,1)S(1)} %add_convert_fusion.5), channel_id=1, source_target_pairs={{0,2},{1,3},{2,0},{3,1},{4,6},{5,7},{6,4},{7,5},{8,10},{9,11},{10,... | collective-permute-start | bytes 884744 | tf_op jit(solution)/shard_map/ppermute | solution.py:738
  192.3 10.7 %collective-permute-start.31 = (bf16[1,2,1,80,768]{4,3,1,2,0:T(8,128)(2,1)S(1)}, bf16[1,2,1,80,768]{4,3,1,2,0:T(8,128)(2,1)S(1)}, u32[]{:S(2)}, u32[]{:S(2)}) collective-permute-start(bf16[1,2,1,80,768]{4,3,1,2,0:T(8,128)(2,1)S(1)} %add_convert_fusion.9), channel_id=1, source_target_pairs={{0,2},{1,3},{2,0},{3,1},{4,6},{5,7},{6,4},{7,5},{8,10},{9,11},{10,... | collective-permute-start | bytes 737288 | tf_op jit(solution)/shard_map/ppermute | solution.py:738
  193.9 13.4 %collective-permute-start.37 = (bf16[8,896]{1,0:T(8,128)(2,1)S(1)}, bf16[8,896]{1,0:T(8,128)(2,1)S(1)}, u32[]{:S(2)}, u32[]{:S(2)}) collective-permute-start(bf16[8,896]{1,0:T(8,128)(2,1)S(1)} %convert_element_type.225), channel_id=1, source_target_pairs={{0,16},{4,20},{8,24},{12,28},{16,0},{20,4},{24,8},{28,12},{1,17},{... | collective-permute-start | bytes 43016 | tf_op jit(solution)/shard_map/ppermute | solution.py:741
  194.1 11.5 %collective-permute-start.30 = (bf16[1,1,2,144,768]{4,3,2,1,0:T(8,128)(2,1)S(1)}, bf16[1,1,2,144,768]{4,3,2,1,0:T(8,128)(2,1)S(1)}, u32[]{:S(2)}, u32[]{:S(2)}) collective-permute-start(bf16[1,1,2,144,768]{4,3,2,1,0:T(8,128)(2,1)S(1)} %add_convert_fusion.1), channel_id=1, source_target_pairs={{0,4},{4,0},{8,12},{12,8},{16,20},{20,16},{24,28},{28,24},{1,5},{5... | collective-permute-start | bytes 1327112 | tf_op jit(solution)/shard_map/ppermute | solution.py:741
  200.2 24.9 %collective-permute-start.44 = (bf16[1,1,1,192,768]{4,3,1,2,0:T(8,128)(2,1)S(1)}, bf16[1,1,1,192,768]{4,3,1,2,0:T(8,128)(2,1)S(1)}, u32[]{:S(2)}, u32[]{:S(2)}) collective-permute-start(bf16[1,1,1,192,768]{4,3,1,2,0:T(8,128)(2,1)S(1)} %add_convert_fusion.4), channel_id=1, source_target_pairs={{0,16},{4,20},{8,24},{12,28},{16,0},{20,4},{24,8},{28,12},{1,17},{... | collective-permute-start | bytes 884744 | tf_op jit(solution)/shard_map/ppermute | solution.py:741
  203.1 4.9 %collective-permute-start.36 = (bf16[1,1,1,80,768]{4,3,1,2,0:T(8,128)(2,1)S(1)}, bf16[1,1,1,80,768]{4,3,1,2,0:T(8,128)(2,1)S(1)}, u32[]{:S(2)}, u32[]{:S(2)}) collective-permute-start(bf16[1,1,1,80,768]{4,3,1,2,0:T(8,128)(2,1)S(1)} %add_convert_fusion.15), channel_id=1, source_target_pairs={{0,4},{4,0},{8,12},{12,8},{16,20},{20,16},{24,28},{28,24},{1,5},{5... | collective-permute-start | bytes 368648 | tf_op jit(solution)/shard_map/ppermute | solution.py:741
  205.7 16.9 %collective-permute-start.34 = (bf16[1,1,1,144,768]{4,3,2,1,0:T(8,128)(2,1)S(1)}, bf16[1,1,1,144,768]{4,3,2,1,0:T(8,128)(2,1)S(1)}, u32[]{:S(2)}, u32[]{:S(2)}) collective-permute-start(bf16[1,1,1,144,768]{4,3,2,1,0:T(8,128)(2,1)S(1)} %add_convert_fusion.12), channel_id=1, source_target_pairs={{0,8},{4,12},{8,0},{12,4},{16,24},{20,28},{24,16},{28,20},{1,9},{5... | collective-permute-start | bytes 663560 | tf_op jit(solution)/shard_map/ppermute | solution.py:741
  207.3 16.6 %collective-permute-start.40 = (bf16[16,896]{1,0:T(8,128)(2,1)S(1)}, bf16[16,896]{1,0:T(8,128)(2,1)S(1)}, u32[]{:S(2)}, u32[]{:S(2)}) collective-permute-start(bf16[16,896]{1,0:T(8,128)(2,1)S(1)} %pad_maximum_fusion.10), channel_id=1, source_target_pairs={{0,8},{4,12},{8,0},{12,4},{16,24},{20,28},{24,16},{28,20},{1,9},{5... | collective-permute-start | bytes 86024 | tf_op jit(solution)/shard_map/ppermute | solution.py:741
  208.1 14.8 %collective-permute-start.41 = (bf16[1,1,1,80,768]{4,3,1,2,0:T(8,128)(2,1)S(1)}, bf16[1,1,1,80,768]{4,3,1,2,0:T(8,128)(2,1)S(1)}, u32[]{:S(2)}, u32[]{:S(2)}) collective-permute-start(bf16[1,1,1,80,768]{4,3,1,2,0:T(8,128)(2,1)S(1)} %add_convert_fusion.14), channel_id=1, source_target_pairs={{0,16},{4,20},{8,24},{12,28},{16,0},{20,4},{24,8},{28,12},{1,17},{... | collective-permute-start | bytes 368648 | tf_op jit(solution)/shard_map/ppermute | solution.py:741
  210.9 22.1 %collective-permute-start.39 = (bf16[1,1,1,192,768]{4,3,2,1,0:T(8,128)(2,1)S(1)}, bf16[1,1,1,192,768]{4,3,2,1,0:T(8,128)(2,1)S(1)}, u32[]{:S(2)}, u32[]{:S(2)}) collective-permute-start(bf16[1,1,1,192,768]{4,3,2,1,0:T(8,128)(2,1)S(1)} %add_convert_fusion.3), channel_id=1, source_target_pairs={{0,8},{4,12},{8,0},{12,4},{16,24},{20,28},{24,16},{28,20},{1,9},{5... | collective-permute-start | bytes 884744 | tf_op jit(solution)/shard_map/ppermute | solution.py:741
  222.8 11.4 %collective-permute-start.38 = (bf16[1,1,1,144,768]{4,3,2,1,0:T(8,128)(2,1)S(1)}, bf16[1,1,1,144,768]{4,3,2,1,0:T(8,128)(2,1)S(1)}, u32[]{:S(2)}, u32[]{:S(2)}) collective-permute-start(bf16[1,1,1,144,768]{4,3,2,1,0:T(8,128)(2,1)S(1)} %add_convert_fusion.11), channel_id=1, source_target_pairs={{0,16},{4,20},{8,24},{12,28},{16,0},{20,4},{24,8},{28,12},{1,17},{... | collective-permute-start | bytes 663560 | tf_op jit(solution)/shard_map/ppermute | solution.py:741
  223.0 4.9 %collective-permute-start.43 = (bf16[1,1,1,80,768]{4,3,1,2,0:T(8,128)(2,1)S(1)}, bf16[1,1,1,80,768]{4,3,1,2,0:T(8,128)(2,1)S(1)}, u32[]{:S(2)}, u32[]{:S(2)}) collective-permute-start(bf16[1,1,1,80,768]{4,3,1,2,0:T(8,128)(2,1)S(1)} %add_convert_fusion.13), channel_id=1, source_target_pairs={{0,4},{4,0},{8,12},{12,8},{16,20},{20,16},{24,28},{28,24},{1,5},{5... | collective-permute-start | bytes 368648 | tf_op jit(solution)/shard_map/ppermute | solution.py:741
  223.9 8.4 %collective-permute-start.42 = (bf16[32,896]{1,0:T(8,128)(2,1)S(1)}, bf16[32,896]{1,0:T(8,128)(2,1)S(1)}, u32[]{:S(2)}, u32[]{:S(2)}) collective-permute-start(bf16[32,896]{1,0:T(8,128)(2,1)S(1)} %pad_maximum_fusion.9), channel_id=1, source_target_pairs={{0,4},{4,0},{8,12},{12,8},{16,20},{20,16},{24,28},{28,24},{1,5},{5... | collective-permute-start | bytes 172040 | tf_op jit(solution)/shard_map/ppermute | solution.py:741
  225.2 13.2 %collective-permute-start.46 = (bf16[1,1,1,192,768]{4,3,1,2,0:T(8,128)(2,1)S(1)}, bf16[1,1,1,192,768]{4,3,1,2,0:T(8,128)(2,1)S(1)}, u32[]{:S(2)}, u32[]{:S(2)}) collective-permute-start(bf16[1,1,1,192,768]{4,3,1,2,0:T(8,128)(2,1)S(1)} %add_convert_fusion.2), channel_id=1, source_target_pairs={{0,4},{4,0},{8,12},{12,8},{16,20},{20,16},{24,28},{28,24},{1,5},{5... | collective-permute-start | bytes 884744 | tf_op jit(solution)/shard_map/ppermute | solution.py:741
  227.9 9.3 %copy-start.20 = (bf16[1,2,1,80,768]{4,3,1,2,0:T(8,128)(2,1)}, bf16[1,2,1,80,768]{4,3,1,2,0:T(8,128)(2,1)S(1)}, u32[]{:S(2)}) copy-start(bf16[1,2,1,80,768]{4,3,1,2,0:T(8,128)(2,1)S(1)} %pad_maximum_fusion.5) | copy-start | bytes 737284
  227.9 9.6 %collective-permute-start.47 = (bf16[1,2,1,80,768]{4,3,1,2,0:T(8,128)(2,1)S(1)}, bf16[1,2,1,80,768]{4,3,1,2,0:T(8,128)(2,1)S(1)}, u32[]{:S(2)}, u32[]{:S(2)}) collective-permute-start(bf16[1,2,1,80,768]{4,3,1,2,0:T(8,128)(2,1)S(1)} %pad_maximum_fusion.5), channel_id=1, source_target_pairs={{0,8},{4,12},{8,0},{12,4},{16,24},{20,28},{24,16},{28,20},{1,9},{5... | collective-permute-start | bytes 737288 | tf_op jit(solution)/shard_map/ppermute | solution.py:741
  232.3 4.9 %collective-permute-start.48 = (bf16[64,896]{1,0:T(8,128)(2,1)S(1)}, bf16[64,896]{1,0:T(8,128)(2,1)S(1)}, u32[]{:S(2)}, u32[]{:S(2)}) collective-permute-start(bf16[64,896]{1,0:T(8,128)(2,1)S(1)} %pad_maximum_fusion.8), channel_id=1, source_target_pairs={{0,2},{1,3},{2,0},{3,1},{4,6},{5,7},{6,4},{7,5},{8,10},{9,11},{10,... | collective-permute-start | bytes 344072 | tf_op jit(solution)/shard_map/ppermute | solution.py:738
  233.1 14.2 %collective-permute-start.54 = (bf16[1,1,2,192,768]{4,3,2,1,0:T(8,128)(2,1)S(1)}, bf16[1,1,2,192,768]{4,3,2,1,0:T(8,128)(2,1)S(1)}, u32[]{:S(2)}, u32[]{:S(2)}) collective-permute-start(bf16[1,1,2,192,768]{4,3,2,1,0:T(8,128)(2,1)S(1)} %pad_maximum_fusion.1), channel_id=1, source_target_pairs={{0,4},{4,0},{8,12},{12,8},{16,20},{20,16},{24,28},{28,24},{1,5},{5... | collective-permute-start | bytes 1769480 | tf_op jit(solution)/shard_map/ppermute | solution.py:741
  234.2 6.0 %collective-permute-start.45 = (bf16[1,1,1,144,768]{4,3,2,1,0:T(8,128)(2,1)S(1)}, bf16[1,1,1,144,768]{4,3,2,1,0:T(8,128)(2,1)S(1)}, u32[]{:S(2)}, u32[]{:S(2)}) collective-permute-start(bf16[1,1,1,144,768]{4,3,2,1,0:T(8,128)(2,1)S(1)} %add_convert_fusion.10), channel_id=1, source_target_pairs={{0,8},{4,12},{8,0},{12,4},{16,24},{20,28},{24,16},{28,20},{1,9},{5... | collective-permute-start | bytes 663560 | tf_op jit(solution)/shard_map/ppermute | solution.py:741
  237.2 4.1 %collective-permute-start.52 = (bf16[128,896]{1,0:T(8,128)(2,1)S(1)}, bf16[128,896]{1,0:T(8,128)(2,1)S(1)}, u32[]{:S(2)}, u32[]{:S(2)}) collective-permute-start(bf16[128,896]{1,0:T(8,128)(2,1)S(1)} %pad_maximum_fusion.6), channel_id=1, source_target_pairs={{0,1},{1,0},{2,3},{3,2},{4,5},{5,4},{6,7},{7,6},{8,9},{9,8},{10,11... | collective-permute-start | bytes 688136 | tf_op jit(solution)/shard_map/ppermute | solution.py:738
  237.6 7.2 %collective-permute-start.50 = (bf16[1,4,32,768]{3,2,1,0:T(8,128)(2,1)S(1)}, bf16[1,4,32,768]{3,2,1,0:T(8,128)(2,1)S(1)}, u32[]{:S(2)}, u32[]{:S(2)}) collective-permute-start(bf16[1,4,32,768]{3,2,1,0:T(8,128)(2,1)S(1)} %bitcast.198), channel_id=1, source_target_pairs={{0,2},{1,3},{2,0},{3,1},{4,6},{5,7},{6,4},{7,5},{8,10},{9,11},{10,... | collective-permute-start | bytes 589832 | tf_op jit(solution)/shard_map/ppermute | solution.py:738
  238.5 15.2 %collective-permute-start.53 = (bf16[1,2,1,192,768]{4,3,1,2,0:T(8,128)(2,1)S(1)}, bf16[1,2,1,192,768]{4,3,1,2,0:T(8,128)(2,1)S(1)}, u32[]{:S(2)}, u32[]{:S(2)}) collective-permute-start(bf16[1,2,1,192,768]{4,3,1,2,0:T(8,128)(2,1)S(1)} %pad_maximum_fusion.2), channel_id=1, source_target_pairs={{0,8},{4,12},{8,0},{12,4},{16,24},{20,28},{24,16},{28,20},{1,9},{5... | collective-permute-start | bytes 1769480 | tf_op jit(solution)/shard_map/ppermute | solution.py:741
  240.3 17.5 %collective-permute-start.49 = (bf16[1,1,2,144,768]{4,3,2,1,0:T(8,128)(2,1)S(1)}, bf16[1,1,2,144,768]{4,3,2,1,0:T(8,128)(2,1)}, u32[]{:S(2)}, u32[]{:S(2)}) collective-permute-start(bf16[1,1,2,144,768]{4,3,2,1,0:T(8,128)(2,1)S(1)} %pad_maximum_fusion.3), channel_id=1, source_target_pairs={{0,4},{4,0},{8,12},{12,8},{16,20},{20,16},{24,28},{28,24},{1,5},{5... | collective-permute-start | bytes 1327112 | tf_op jit(solution)/shard_map/ppermute | solution.py:741
  244.8 13.0 %collective-permute-start.51 = (bf16[2,4,32,768]{3,2,1,0:T(8,128)(2,1)S(1)}, bf16[2,4,32,768]{3,2,1,0:T(8,128)(2,1)}, u32[]{:S(2)}, u32[]{:S(2)}) collective-permute-start(bf16[2,4,32,768]{3,2,1,0:T(8,128)(2,1)S(1)} %pad_maximum_fusion.4.all_ref), channel_id=1, source_target_pairs={{0,1},{1,0},{2,3},{3,2},{4,5},{5,4},{6,7},{7,6},{8,9},{9,8},{10,11... | collective-permute-start | bytes 1179656 | tf_op jit(solution)/shard_map/ppermute | solution.py:738
  (29 other events, 77.2 us)

commit v6 on v5

--- a/solution.py
+++ b/solution.py
@@ -18,7 +18,7 @@
 CHUNK = 64
 GATHER_ROWS = 32
 CHAIN_ORDERS = ("yxz", "zxy", "yxz", "zyx")
-TAIL = (0, 1, 3, 1, 3, 4, 2, 1, 3, 2, 4, 3, 0, 2, 3, 4, 1, 3, 4, 0, 2, 4, 5, 1, 2, 5)
+TAIL = (0, 1, 3, 1, 3, 2, 4, 1, 3, 2, 3, 4, 2, 0, 3, 4, 1, 3, 4, 2, 0, 4, 5, 1, 2, 5)
 
 VMEM = pl.BlockSpec(memory_space=pltpu.VMEM)
 SMEM = pl.BlockSpec(memory_space=pltpu.SMEM)
@@ -551,7 +551,7 @@
     where_ref, seg_ref, label_ref, grad_in, total_in, hid_in, gain_ref, patch_ref, direct_ref, win_ref,
     gwout_ref, gdown_ref, gup_ref, gpre_ref, gq_near, gq_far,
     pgrad_ref, slot_ref, keep_ref, send_ref,
-    value_ref, embed_ref, acc_ref, small_ref, grad_ref, total_ref, hid_ref, sems, in_sems,
+    value_ref, embed_ref, acc_ref, small_ref, rows_ref, grad_ref, total_ref, hid_ref, sems, in_sems,
     *, length, quarter,
 ):
     tokens, width = hid_ref.shape
@@ -647,10 +647,11 @@
         for slot in range(slots):
             other = every if slot == 0 else jnp.zeros_like(every)
             index = row * slots + slot
-            slot_ref[index : index + 1, :width] = jnp.where(packed[row], sums[slot], other)
+            rows_ref[index : index + 1, :width] = jnp.where(packed[row], sums[slot], other)
             label = label_ref[row, slot]
             digits = jnp.where(lane == 0, label >> 5, jnp.where(lane == 1, label & 31, 0))
-            slot_ref[index : index + 1, width:] = digits.astype(F32)
+            rows_ref[index : index + 1, width:] = digits.astype(F32)
+    slot_ref[...] = rows_ref[...].astype(BF)
     pgrad_ref[...] = direct_ref[...] + nt(win_ref[...], embed_ref[...])
     for copy in copies:
         copy.wait()
@@ -1130,13 +1131,14 @@
                 direct, w_in, grad_w_out, gdown, gup, gpre, gq_near, gq_far,
             ),
             [SMEM] * 3 + [HBM] * 3 + [VMEM] * 10,
-            (shape(channels, tokens), shape(row_count * slot_count, width + 128), last_pieces, last_pieces),
+            (shape(channels, tokens), shape(row_count * slot_count, width + 128, dtype=BF), last_pieces, last_pieces),
             (VMEM, VMEM, HBM, HBM),
             [
                 pltpu.VMEM((tokens, width), F32),
                 pltpu.VMEM((tokens, width), BF),
                 pltpu.VMEM((EXTRA, width), F32),
                 pltpu.VMEM((groups * GROUP, width), BF),
+                pltpu.VMEM((row_count * slot_count, width + 128), F32),
                 pltpu.VMEM((tokens, width), F32),
                 pltpu.VMEM((tokens, width), F32),
                 pltpu.VMEM((tokens, width), F32),
@@ -1152,7 +1154,7 @@
         last.groups = [[last.view(keep_q), last.view(swap_heads(send_q, 1))]]
         mix.groups[0] = [mix.view(keep_near), mix.view(got_near)]
         down.got, up.got = got_d, got_u
-        gathered = slot_rows.astype(BF)
+        gathered = slot_rows
         gathers = [("rows", 1 << level) for level in reversed(range(levels))]
         gathers += [("heads", 2), ("heads", 1)]
         share = (len(gathers) - 1) // 4

time: 262 us -> 262 us (level)
    ppermute x28, waiting for transfers between devices: 34.2 us -> 37.1 us  [swap_rows(): return lax.ppermute(array, 'rows', [(i, i ^ bit) for i in range(rows_size)])]
  transfers between devices with their start and end apart: 55 -> 55, of which waited for: 22 -> 23; matrix products, arithmetic and copies ran while one was open for 6% -> 6% of each run, Pallas kernels for 41% -> 41%
where the time goes in v6:
time: 262 us; the launch traced here: 261 us
  Pallas kernels  128 us (49%)
  waiting for transfers between devices  59.6 us (23%)
  starting transfers between devices  49.3 us (19%)
  local copies, waits for them, and re-layouts  10.6 us (4%)
  other arithmetic  10.6 us (4%)
    pallas_call x13, Pallas kernels, call(): pl.pallas_call(functools.partial(kernel, **options) if options else kerne...  119 us
    ppermute x28, waiting for transfers between devices, swap_rows(): return lax.ppermute(array, 'rows', [(i, i ^ bit) for i in range(rows_size)])  37.1 us
    ppermute x28, starting transfers between devices, swap_rows(): return lax.ppermute(array, 'rows', [(i, i ^ bit) for i in range(rows_size)])  36 us
    ppermute x27, waiting for transfers between devices, swap_heads(): lax.ppermute(array, 'heads', [(i, i ^ bit) for i in range(heads_size)])  22.5 us
    ppermute x27, starting transfers between devices, swap_heads(): lax.ppermute(array, 'heads', [(i, i ^ bit) for i in range(heads_size)])  13.4 us
    pallas_call x3, Pallas kernels, add_groups(): pl.pallas_call(functools.partial(add_kernel, counts=tuple((len(group) for...  8.76 us
    unnamed x77, local copies, waits for them, and re-layouts  6.49 us
    convert_element_type x15, other arithmetic, add_low(): return total.astype(BF)  6.35 us
  transfers between devices with their start and end apart: 55, of which 23 were waited for; matrix products, arithmetic and copies ran while one was open for 6% of the time, Pallas kernels for 41%

profile of v6, /device:TPU:0, one launch (start us, length us, event | category | flops | bytes accessed | tf_op | source)
XLA Modules:
  0.0 261.5 jit_solution(13659009851737341370)
XLA Ops:
  0.7 1.4 broadcast_select_fusion
  4.0 2.6 collective-permute-start
  8.4 2.1 dynamic-slice_bitcast_fusion
  11.2 3.0 %shard_map.398 = (f32[512,768]{1,0:T(8,128)}, bf16[512,768]{1,0:T(8,128)(2,1)}) custom-call(s32[4]{0:T(128)} %pad_add_fusion.where_ref, s32[2048]{0:T(1024)} %seg_ref.9, f32[48,512]{1,0:T(8,128)} %bitcast.188, bf16[48,768]{1,0:T(8,128)(2,1)} %win_ref.1, f32[1,768]{1,0:T(1,128)} %broadcast_in_dim.29.b_ref, bf16[256,768]{1,0:T(8,128)(2,1)} %pos_ref.1, ...), custom_call_target="tpu_custom_call" | custom-call | flops 1 | bytes 1 | tf_op jit(solution)/shard_map/pallas_call | solution.py:853
  14.2 7.0 %collective-permute-done.rest_0_.far_t = bf16[400,768]{1,0:T(8,128)(2,1)S(1)} collective-permute-done((bf16[400,768]{1,0:T(8,128)(2,1)}, bf16[400,768]{1,0:T(8,128)(2,1)S(1)}, u32[]{:S(2)}, u32[]{:S(2)}) %collective-permute-start) | collective-permute-done | bytes 614432 | tf_op jit(solution)/shard_map/ppermute | solution.py:739
  21.2 1.7 collective-permute-start.2
  23.0 1.5 collective-permute-start.3
  24.5 11.2 %shard_map.399 = (bf16[512,384]{1,0:T(8,128)(2,1)}, bf16[512,384]{1,0:T(8,128)(2,1)}, bf16[512,384]{1,0:T(8,128)(2,1)}, bf16[12,256,256]{2,1,0:T(8,128)(2,1)}, b...) custom-call(s32[4]{0:T(128)} %pad_add_fusion.where_ref, s32[2048]{0:T(1024)} %seg_ref.9, ...), custom_call_target="tpu_custom_call" | custom-call | flops 1 | bytes 1 | tf_op jit(solution)/shard_map/pallas_call | solution.py:853
  35.7 1.9 collective-permute-done.3.far
  37.6 1.6 collective-permute-start.7
  40.5 10.9 %shard_map.400 = (bf16[512,384]{1,0:T(8,128)(2,1)}, bf16[512,384]{1,0:T(8,128)(2,1)}, bf16[512,384]{1,0:T(8,128)(2,1)}, bf16[12,256,256]{2,1,0:T(8,128)(2,1)}, b...) custom-call(s32[4]{0:T(128)} %pad_add_fusion.where_ref, s32[2048]{0:T(1024)} %seg_ref.9, ...), custom_call_target="tpu_custom_call" | custom-call | flops 1 | bytes 1 | tf_op jit(solution)/shard_map/pallas_call | solution.py:853
  51.5 2.2 collective-permute-done.7.far
  53.6 1.2 collective-permute-done.6.far_other
  57.2 14.1 %shard_map.401 = (bf16[512,768]{1,0:T(8,128)(2,1)}, bf16[4,512,768]{2,1,0:T(8,128)(2,1)}, bf16[4,512,768]{2,1,0:T(8,128)(2,1)}) custom-call(s32[4]{0:T(128)} %pad_add_fusion.where_ref, f32[512,768]{1,0:T(8,128)} %get-tuple-element.207.hid_ref.hid_in, f32[1,768]{1,0:T(1,128)} %gain_ref.6, f32[1,768]{1,0:T(1,128)} %bias_ref.3, bf16[768,768]{1,0:T(8,128)(2,1)} %bitcast.156, ...), custom_call_target="tpu_custom_call" | custom-call | flops 1 | bytes 1 | tf_op jit(solution)/shard_map/pallas_call | solution.py:853
  72.3 1.1 collective-permute-done.14.cross_other
  74.2 13.1 %shard_map.402 = (f32[48,512]{1,0:T(8,128)}, f32[1,512]{1,0:T(1,128)}, f32[1,2]{1,0:T(1,128)}, f32[1,2]{1,0:T(1,128)}, f32[48,512]{1,0:T(8,128)}, /*index=5*/f32...) custom-call(s32[4]{0:T(128)} %pad_add_fusion.where_ref, ...), custom_call_target="tpu_custom_call" | custom-call | flops 1 | bytes 1 | tf_op jit(solution)/shard_map/pallas_call | solution.py:853
  87.9 8.3 %shard_map.403 = (bf16[4,512,768]{2,1,0:T(8,128)(2,1)}, f32[8,768]{1,0:T(8,128)}) custom-call(s32[4]{0:T(128)} %pad_add_fusion.where_ref, f32[512,768]{1,0:T(8,128)} %get-tuple-element.220.grad_ref.grad_in, bf16[4,512,768]{2,1,0:T(8,128)(2,1)} %get-tuple-element.221.slope_in, bf16[768,768]{1,0:T(8,128)(2,1)} %bitcast.154, ...), custom_call_target="tpu_custom_call" | custom-call | flops 1 | bytes 1 | tf_op jit(solution)/shard_map/pallas_call | solution.py:853
  97.3 2.6 shard_map.404
  100.4 13.0 %shard_map.405 = (f32[512,768]{1,0:T(8,128)}, bf16[512,768]{1,0:T(8,128)(2,1)}, f32[8,768]{1,0:T(8,128)}, bf16[2,4,192,768]{3,2,1,0:T(8,128)(2,1)}, bf16[4,192,7...) custom-call(s32[4]{0:T(128)} %pad_add_fusion.where_ref, f32[512,768]{1,0:T(8,128)} %get-tuple-element.220.grad_ref.grad_in, ...), custom_call_target="tpu_custom_call" | custom-call | flops 1 | bytes 1 | tf_op jit(solution)/shard_map/pallas_call | solution.py:853
  113.9 13.1 %shard_map.406 = (f32[512,768]{1,0:T(8,128)}, bf16[384,768]{1,0:T(8,128)(2,1)}, bf16[4,144,768]{2,1,0:T(8,128)(2,1)}, bf16[4,144,768]{2,1,0:T(8,128)(2,1)}) custom-call(s32[4]{0:T(128)} %pad_add_fusion.where_ref, bf16[512,768]{1,0:T(8,128)(2,1)} %get-tuple-element.235.mix_in, bf16[512,384]{1,0:T(8,128)(2,1)} %get-tuple-element.236.q_in, ...), custom_call_target="tpu_custom_call" | custom-call | flops 1 | bytes 1 | tf_op jit(solution)/shard_map/pallas_call | solution.py:853
  129.8 3.3 %shard_map.407 = (bf16[1,1,2,192,768]{4,3,2,1,0:T(8,128)(2,1)}, bf16[1,2,1,192,768]{4,3,2,1,0:T(8,128)(2,1)}, bf16[1,2,1,192,768]{4,3,2,1,0:T(8,128)(2,1)}) custom-call(bf16[2,2,2,192,768]{4,3,2,1,0:T(8,128)(2,1)} %bitcast.145, bf16[1,2,2,192,768]{4,3,2,1,0:T(8,128)(2,1)} %bitcast.159, bf16[1,2,2,192,768]{4,3,2,1,0:T(8,128)(2,1)} %copy-done.7, ...), custom_call_target="tpu_custom_call" | custom-call | flops 1 | bytes 1 | tf_op jit(solution)/shard_map/pallas_call | solution.py:1023
  134.1 1.6 collective-permute-start.22
  136.1 13.0 %shard_map.408 = (f32[512,768]{1,0:T(8,128)}, bf16[384,768]{1,0:T(8,128)(2,1)}, bf16[4,144,768]{2,1,0:T(8,128)(2,1)}, bf16[4,144,768]{2,1,0:T(8,128)(2,1)}) custom-call(s32[4]{0:T(128)} %pad_add_fusion.where_ref, bf16[512,768]{1,0:T(8,128)(2,1)} %get-tuple-element.235.mix_in, bf16[512,384]{1,0:T(8,128)(2,1)} %get-tuple-element.245.q_in, ...), custom_call_target="tpu_custom_call" | custom-call | flops 1 | bytes 1 | tf_op jit(solution)/shard_map/pallas_call | solution.py:853
  149.9 2.9 %shard_map.409 = (bf16[1,1,1,192,768]{4,3,2,1,0:T(8,128)(2,1)}, bf16[1,2,2,144,768]{4,3,2,1,0:T(8,128)(2,1)}) custom-call(bf16[2,2,2,192,768]{4,3,2,1,0:T(8,128)(2,1)} %bitcast.146, bf16[1,2,2,192,768]{4,3,2,1,0:T(8,128)(2,1)} %bitcast.160, bf16[1,2,2,192,768]{4,3,2,1,0:T(8,128)(2,1)} %copy-done.7, bf16[1,1,2,192,768]{4,3,2,1,0:T(8,128)(2,1)} %copy-done.21, ...), custom_call_target="tpu_custom_call" | custom-call | flops 1 | bytes 1 | tf_op jit(solution)/shard_map/pallas_call | solution.py:1023
  152.8 1.6 collective-permute-start.24
  154.4 9.1 %shard_map.410 = (f32[48,512]{1,0:T(8,128)}, bf16[8,896]{1,0:T(8,128)(2,1)}, bf16[2,4,80,768]{3,2,1,0:T(8,128)(2,1)}, bf16[2,4,80,768]{3,2,1,0:T(8,128)(2,1)}) custom-call(s32[4]{0:T(128)} %pad_add_fusion.where_ref, s32[2048]{0:T(1024)} %seg_ref.9, s32[2,4]{1,0:T(2,128)} %label_ref.1, f32[512,768]{1,0:T(8,128)} %get-tuple-element.270.grad_in, ...), custom_call_target="tpu_custom_call" | custom-call | flops 1 | bytes 1 | tf_op jit(solution)/shard_map/pallas_call | solution.py:853
  163.5 4.9 %collective-permute-done.24 = bf16[1,1,1,192,768]{4,3,2,1,0:T(8,128)(2,1)S(1)} collective-permute-done((bf16[1,1,1,192,768]{4,3,2,1,0:T(8,128)(2,1)}, bf16[1,1,1,192,768]{4,3,2,1,0:T(8,128)(2,1)S(1)}, u32[]{:S(2)}, u32[]{:S(2)}) %collective-permute-start.24) | collective-permute-done | bytes 294944 | tf_op jit(solution)/shard_map/ppermute | solution.py:742
  169.1 1.5 add_convert_fusion.8
  170.7 1.4 add_convert_fusion.6
  172.1 1.2 collective-permute-start.32
  174.3 1.6 collective-permute-start.28
  176.0 6.0 %collective-permute-done.32 = bf16[1,1,1,192,768]{4,3,1,2,0:T(8,128)(2,1)S(1)} collective-permute-done((bf16[1,1,1,192,768]{4,3,1,2,0:T(8,128)(2,1)S(1)}, bf16[1,1,1,192,768]{4,3,1,2,0:T(8,128)(2,1)S(1)}, u32[]{:S(2)}, u32[]{:S(2)}) %collective-permute-start.32) | collective-permute-done | bytes 294944 | tf_op jit(solution)/shard_map/ppermute | solution.py:742
  182.0 2.6 collective-permute-start.40
  184.6 3.3 %collective-permute-done.29 = bf16[1,1,1,192,768]{4,3,1,2,0:T(8,128)(2,1)S(1)} collective-permute-done((bf16[1,1,1,192,768]{4,3,1,2,0:T(8,128)(2,1)S(1)}, bf16[1,1,1,192,768]{4,3,1,2,0:T(8,128)(2,1)S(1)}, u32[]{:S(2)}, u32[]{:S(2)}) %collective-permute-start.29) | collective-permute-done | bytes 294944 | tf_op jit(solution)/shard_map/ppermute | solution.py:742
  187.9 1.2 add_convert_fusion.5
  189.1 1.4 collective-permute-start.33
  190.5 1.7 collective-permute-done.28
  192.3 1.6 collective-permute-start.31
  194.1 1.1 collective-permute-start.30
  195.3 3.8 %collective-permute-done.33 = bf16[1,1,1,192,768]{4,3,1,2,0:T(8,128)(2,1)S(1)} collective-permute-done((bf16[1,1,1,192,768]{4,3,1,2,0:T(8,128)(2,1)S(1)}, bf16[1,1,1,192,768]{4,3,1,2,0:T(8,128)(2,1)S(1)}, u32[]{:S(2)}, u32[]{:S(2)}) %collective-permute-start.33) | collective-permute-done | bytes 294944 | tf_op jit(solution)/shard_map/ppermute | solution.py:739
  199.1 1.2 add_convert_fusion.4
  200.2 2.6 %collective-permute-start.43 = (bf16[1,1,1,192,768]{4,3,1,2,0:T(8,128)(2,1)S(1)}, bf16[1,1,1,192,768]{4,3,1,2,0:T(8,128)(2,1)S(1)}, u32[]{:S(2)}, u32[]{:S(2)}) collective-permute-start(bf16[1,1,1,192,768]{4,3,1,2,0:T(8,128)(2,1)S(1)} %add_convert_fusion.4), channel_id=1, source_target_pairs={{0,16},{4,20},{8,24},{12,28},{16,0},{20,4},{24,8},{28,12},{1,17},{... | collective-permute-start | bytes 884744 | tf_op jit(solution)/shard_map/ppermute | solution.py:742
  203.1 1.1 collective-permute-start.36
  206.0 2.0 collective-permute-done.36
  208.1 2.7 %collective-permute-start.39 = (bf16[1,1,1,80,768]{4,3,1,2,0:T(8,128)(2,1)S(1)}, bf16[1,1,1,80,768]{4,3,1,2,0:T(8,128)(2,1)S(1)}, u32[]{:S(2)}, u32[]{:S(2)}) collective-permute-start(bf16[1,1,1,80,768]{4,3,1,2,0:T(8,128)(2,1)S(1)} %add_convert_fusion.14), channel_id=1, source_target_pairs={{0,16},{4,20},{8,24},{12,28},{16,0},{20,4},{24,8},{28,12},{1,17},{... | collective-permute-start | bytes 368648 | tf_op jit(solution)/shard_map/ppermute | solution.py:742
  210.8 1.5 collective-permute-start.38
  212.4 3.6 %collective-permute-done.34 = bf16[1,1,1,144,768]{4,3,2,1,0:T(8,128)(2,1)S(1)} collective-permute-done((bf16[1,1,1,144,768]{4,3,2,1,0:T(8,128)(2,1)S(1)}, bf16[1,1,1,144,768]{4,3,2,1,0:T(8,128)(2,1)S(1)}, u32[]{:S(2)}, u32[]{:S(2)}) %collective-permute-start.34) | collective-permute-done | bytes 221216 | tf_op jit(solution)/shard_map/ppermute | solution.py:742
  216.1 1.8 collective-permute-start.37
  217.9 2.5 collective-permute-start.48
  220.5 4.8 %collective-permute-done.39 = bf16[1,1,1,80,768]{4,3,1,2,0:T(8,128)(2,1)S(1)} collective-permute-done((bf16[1,1,1,80,768]{4,3,1,2,0:T(8,128)(2,1)S(1)}, bf16[1,1,1,80,768]{4,3,1,2,0:T(8,128)(2,1)S(1)}, u32[]{:S(2)}, u32[]{:S(2)}) %collective-permute-start.39) | collective-permute-done | bytes 122912 | tf_op jit(solution)/shard_map/ppermute | solution.py:742
  225.3 1.1 collective-permute-start.42
  227.6 1.1 collective-permute-start.45
  228.7 1.6 collective-permute-done.42
  231.7 1.2 collective-permute-start.44
  232.9 1.1 collective-permute-start.54
  234.0 2.2 collective-permute-done.47
  236.3 1.8 collective-permute-done.46
  238.9 2.2 collective-permute-done.44
  241.7 2.2 collective-permute-done.50
  244.2 2.2 fusion.1
  246.4 3.1 %collective-permute-done.54 = bf16[1,1,2,192,768]{4,3,2,1,0:T(8,128)(2,1)S(1)} collective-permute-done((bf16[1,1,2,192,768]{4,3,2,1,0:T(8,128)(2,1)S(1)}, bf16[1,1,2,192,768]{4,3,2,1,0:T(8,128)(2,1)S(1)}, u32[]{:S(2)}, u32[]{:S(2)}) %collective-permute-start.54) | collective-permute-done | bytes 589856 | tf_op jit(solution)/shard_map/ppermute | solution.py:742
  250.4 3.2 %shard_map.413 = f32[768,768]{1,0:T(8,128)} custom-call(s32[4]{0:T(128)} %pad_add_fusion.where_ref, bf16[1,2,192,768]{3,2,1,0:T(8,128)(2,1)} %bitcast.170, bf16[1,2,192,768]{3,2,1,0:T(8,128)(2,1)} %bitcast.200), custom_call_target="tpu_custom_call" | custom-call | flops 1 | bytes 1 | tf_op jit(solution)/shard_map/pallas_call | solution.py:853
  254.4 3.3 %shard_map.412 = f32[768,768]{1,0:T(8,128)} custom-call(s32[4]{0:T(128)} %pad_add_fusion.where_ref, bf16[2,1,192,768]{3,2,1,0:T(8,128)(2,1)} %bitcast.171, bf16[2,1,192,768]{3,2,1,0:T(8,128)(2,1)} %bitcast.201), custom_call_target="tpu_custom_call" | custom-call | flops 1 | bytes 1 | tf_op jit(solution)/shard_map/pallas_call | solution.py:853
  257.8 3.5 %shard_map.411 = (f32[192,768]{1,0:T(8,128)}, f32[192,768]{1,0:T(8,128)}, f32[192,768]{1,0:T(8,128)}, f32[192,768]{1,0:T(8,128)}, f32[48,768]{1,0:T(8,128)}, /*i...) custom-call(s32[4]{0:T(128)} %pad_add_fusion.where_ref, ...), custom_call_target="tpu_custom_call" | custom-call | flops 1 | bytes 1 | tf_op jit(solution)/shard_map/pallas_call | solution.py:853
  (182 shorter events, 27.8 us)
Async XLA Ops:
  3.4 7.1 %copy-start.2 = (bf16[2,400,768]{2,1,0:T(8,128)(2,1)}, bf16[2,400,768]{2,1,0:T(8,128)(2,1)S(1)}, u32[]{:S(2)}) copy-start(bf16[2,400,768]{2,1,0:T(8,128)(2,1)S(1)} %pad_maximum_fusion.rest_0_.own_t.rest_1_) | copy-start | bytes 3686404
  3.5 21.0 %collective-permute-start.1 = (bf16[2,400,768]{2,1,0:T(8,128)(2,1)S(1)}, bf16[2,400,768]{2,1,0:T(8,128)(2,1)}, u32[]{:S(2)}, u32[]{:S(2)}) collective-permute-start(bf16[2,400,768]{2,1,0:T(8,128)(2,1)S(1)} %pad_maximum_fusion.rest_0_.own_t.rest_1_), channel_id=1, source_target_pairs={{0,1},{1,0},{2,3},{3,2},{4,5},{5,4},{6,7},{7,6},{8,9},{9,8},{10,11... | collective-permute-start | bytes 3686408 | tf_op jit(solution)/shard_map/ppermute | solution.py:739
  4.0 17.3 %collective-permute-start = (bf16[400,768]{1,0:T(8,128)(2,1)}, bf16[400,768]{1,0:T(8,128)(2,1)S(1)}, u32[]{:S(2)}, u32[]{:S(2)}) collective-permute-start(bf16[400,768]{1,0:T(8,128)(2,1)} %get-tuple-element.368), channel_id=1, source_target_pairs={{0,2},{1,3},{2,0},{3,1},{4,6},{5,7},{6,4},{7,5},{8,10},{9,11},{10,... | collective-permute-start | bytes 1843208 | tf_op jit(solution)/shard_map/ppermute | solution.py:739
  21.2 14.5 %copy-start.8 = (bf16[400,768]{1,0:T(8,128)(2,1)}, bf16[400,768]{1,0:T(8,128)(2,1)S(1)}, u32[]{:S(2)}) copy-start(bf16[400,768]{1,0:T(8,128)(2,1)S(1)} %collective-permute-done.rest_0_.far_t) | copy-start | bytes 1843204
  21.2 16.3 %collective-permute-start.2 = (bf16[400,768]{1,0:T(8,128)(2,1)S(1)}, bf16[400,768]{1,0:T(8,128)(2,1)}, u32[]{:S(2)}, u32[]{:S(2)}) collective-permute-start(bf16[400,768]{1,0:T(8,128)(2,1)S(1)} %collective-permute-done.rest_0_.far_t), channel_id=1, source_target_pairs={{0,4},{4,0},{8,12},{12,8},{16,20},{20,16},{24,28},{28,24},{1,5},{5... | collective-permute-start | bytes 1843208 | tf_op jit(solution)/shard_map/ppermute | solution.py:742
  23.0 14.6 %collective-permute-start.3 = (bf16[384,768]{1,0:T(8,128)(2,1)S(1)}, bf16[384,768]{1,0:T(8,128)(2,1)S(1)}, u32[]{:S(2)}, u32[]{:S(2)}) collective-permute-start(bf16[384,768]{1,0:T(8,128)(2,1)S(1)} %get-tuple-element.194), channel_id=1, source_target_pairs={{0,2},{1,3},{2,0},{3,1},{4,6},{5,7},{6,4},{7,5},{8,10},{9,11},{10,... | collective-permute-start | bytes 1769480 | tf_op jit(solution)/shard_map/ppermute | solution.py:739
  24.5 15.5 %collective-permute-start.4 = (bf16[400,768]{1,0:T(8,128)(2,1)S(1)}, bf16[400,768]{1,0:T(8,128)(2,1)}, u32[]{:S(2)}, u32[]{:S(2)}) collective-permute-start(bf16[400,768]{1,0:T(8,128)(2,1)S(1)} %collective-permute-done.rest_0_.far_t), channel_id=1, source_target_pairs={{0,1},{1,0},{2,3},{3,2},{4,5},{5,4},{6,7},{7,6},{8,9},{9,8},{10,11... | collective-permute-start | bytes 1843208 | tf_op jit(solution)/shard_map/ppermute | solution.py:739
  24.5 15.5 %copy-start.5 = (bf16[1,768,768]{2,1,0:T(8,128)(2,1)S(1)}, bf16[1,768,768]{2,1,0:T(8,128)(2,1)}, u32[]{:S(2)}) copy-start(bf16[1,768,768]{2,1,0:T(8,128)(2,1)} %param.38) | copy-start | bytes 3538948
  37.6 3.0 %collective-permute-start.5 = (bf16[400,768]{1,0:T(8,128)(2,1)}, bf16[400,768]{1,0:T(8,128)(2,1)}, u32[]{:S(2)}, u32[]{:S(2)}) collective-permute-start(bf16[400,768]{1,0:T(8,128)(2,1)} %collective-permute-done.2.rest_1_), channel_id=1, source_target_pairs={{0,1},{1,0},{2,3},{3,2},{4,5},{5,4},{6,7},{7,6},{8,9},{9,8},{10,11... | collective-permute-start | bytes 1843208 | tf_op jit(solution)/shard_map/ppermute | solution.py:739
  37.6 16.1 %collective-permute-start.7 = (bf16[384,768]{1,0:T(8,128)(2,1)}, bf16[384,768]{1,0:T(8,128)(2,1)}, u32[]{:S(2)}, u32[]{:S(2)}) collective-permute-start(bf16[384,768]{1,0:T(8,128)(2,1)} %get-tuple-element.195), channel_id=1, source_target_pairs={{0,2},{1,3},{2,0},{3,1},{4,6},{5,7},{6,4},{7,5},{8,10},{9,11},{10,... | collective-permute-start | bytes 1769480 | tf_op jit(solution)/shard_map/ppermute | solution.py:739
  39.2 16.6 %copy-start.4 = (bf16[1,768,768]{2,1,0:T(8,128)(2,1)S(1)}, bf16[1,768,768]{2,1,0:T(8,128)(2,1)}, u32[]{:S(2)}) copy-start(bf16[1,768,768]{2,1,0:T(8,128)(2,1)} %param.40) | copy-start | bytes 3538948
  39.2 15.7 %collective-permute-start.6 = (bf16[384,768]{1,0:T(8,128)(2,1)}, bf16[384,768]{1,0:T(8,128)(2,1)}, u32[]{:S(2)}, u32[]{:S(2)}) collective-permute-start(bf16[384,768]{1,0:T(8,128)(2,1)} %copy-done.17), channel_id=1, source_target_pairs={{0,4},{4,0},{8,12},{12,8},{16,20},{20,16},{24,28},{28,24},{1,5},{5... | collective-permute-start | bytes 1769480 | tf_op jit(solution)/shard_map/ppermute | solution.py:742
  40.0 16.0 %collective-permute-start.8 = (bf16[768,768]{1,0:T(8,128)(2,1)S(1)}, bf16[768,768]{1,0:T(8,128)(2,1)}, u32[]{:S(2)}, u32[]{:S(2)}) collective-permute-start(bf16[768,768]{1,0:T(8,128)(2,1)S(1)} %bitcast.158), channel_id=1, source_target_pairs={{0,1},{1,0},{2,3},{3,2},{4,5},{5,4},{6,7},{7,6},{8,9},{9,8},{10,11... | collective-permute-start | bytes 3538952 | tf_op jit(solution)/shard_map/ppermute | solution.py:739
  40.0 16.3 %collective-permute-start.9 = (bf16[384,768]{1,0:T(8,128)(2,1)}, bf16[384,768]{1,0:T(8,128)(2,1)}, u32[]{:S(2)}, u32[]{:S(2)}) collective-permute-start(bf16[384,768]{1,0:T(8,128)(2,1)} %copy-done.17), channel_id=1, source_target_pairs={{0,1},{1,0},{2,3},{3,2},{4,5},{5,4},{6,7},{7,6},{8,9},{9,8},{10,11... | collective-permute-start | bytes 1769480 | tf_op jit(solution)/shard_map/ppermute | solution.py:739
  54.9 2.3 collective-permute-start.10
  54.9 16.4 %collective-permute-start.12 = (bf16[384,768]{1,0:T(8,128)(2,1)}, bf16[384,768]{1,0:T(8,128)(2,1)S(1)}, u32[]{:S(2)}, u32[]{:S(2)}) collective-permute-start(bf16[384,768]{1,0:T(8,128)(2,1)} %collective-permute-done.7.far), channel_id=1, source_target_pairs={{0,4},{4,0},{8,12},{12,8},{16,20},{20,16},{24,28},{28,24},{1,5},{5... | collective-permute-start | bytes 1769480 | tf_op jit(solution)/shard_map/ppermute | solution.py:742
  55.8 15.7 %copy-start.37 = (f32[96]{0:T(128)S(1)}, f32[96]{0:T(128)}, u32[]{:S(2)}) copy-start(f32[96]{0:T(128)} %param.43) | copy-start | bytes 1156
  55.8 16.5 %collective-permute-start.11 = (bf16[768,768]{1,0:T(8,128)(2,1)S(1)}, bf16[768,768]{1,0:T(8,128)(2,1)}, u32[]{:S(2)}, u32[]{:S(2)}) collective-permute-start(bf16[768,768]{1,0:T(8,128)(2,1)S(1)} %bitcast.155), channel_id=1, source_target_pairs={{0,1},{1,0},{2,3},{3,2},{4,5},{5,4},{6,7},{7,6},{8,9},{9,8},{10,11... | collective-permute-start | bytes 3538952 | tf_op jit(solution)/shard_map/ppermute | solution.py:739
  56.0 16.2 %collective-permute-start.13 = (bf16[384,768]{1,0:T(8,128)(2,1)}, bf16[384,768]{1,0:T(8,128)(2,1)S(1)}, u32[]{:S(2)}, u32[]{:S(2)}) collective-permute-start(bf16[384,768]{1,0:T(8,128)(2,1)} %collective-permute-done.7.far), channel_id=1, source_target_pairs={{0,1},{1,0},{2,3},{3,2},{4,5},{5,4},{6,7},{7,6},{8,9},{9,8},{10,11... | collective-permute-start | bytes 1769480 | tf_op jit(solution)/shard_map/ppermute | solution.py:739
  71.3 2.1 collective-permute-start.14
  87.3 8.9 %collective-permute-start.15 = (bf16[4,192,768]{2,1,0:T(8,128)(2,1)}, bf16[4,192,768]{2,1,0:T(8,128)(2,1)S(1)}, u32[]{:S(2)}, u32[]{:S(2)}) collective-permute-start(bf16[4,192,768]{2,1,0:T(8,128)(2,1)} %get-tuple-element.223), channel_id=1, source_target_pairs={{0,1},{1,0},{2,3},{3,2},{4,5},{5,4},{6,7},{7,6},{8,9},{9,8},{10,11... | collective-permute-start | bytes 3538952 | tf_op jit(solution)/shard_map/ppermute | solution.py:739
  87.5 8.7 %collective-permute-start.16 = (bf16[4,192,768]{2,1,0:T(8,128)(2,1)}, bf16[4,192,768]{2,1,0:T(8,128)(2,1)S(1)}, u32[]{:S(2)}, u32[]{:S(2)}) collective-permute-start(bf16[4,192,768]{2,1,0:T(8,128)(2,1)} %get-tuple-element.224), channel_id=1, source_target_pairs={{0,1},{1,0},{2,3},{3,2},{4,5},{5,4},{6,7},{7,6},{8,9},{9,8},{10,11... | collective-permute-start | bytes 3538952 | tf_op jit(solution)/shard_map/ppermute | solution.py:739
  99.9 28.2 %collective-permute-start.17 = (bf16[1,2,2,192,768]{4,3,2,1,0:T(8,128)(2,1)}, bf16[1,2,2,192,768]{4,3,2,1,0:T(8,128)(2,1)S(1)}, u32[]{:S(2)}, u32[]{:S(2)}) collective-permute-start(bf16[1,2,2,192,768]{4,3,2,1,0:T(8,128)(2,1)} %shard_map.404), channel_id=1, source_target_pairs={{0,2},{1,3},{2,0},{3,1},{4,6},{5,7},{6,4},{7,5},{8,10},{9,11},{10,... | collective-permute-start | bytes 3538952 | tf_op jit(solution)/shard_map/ppermute | solution.py:739
  113.3 14.8 %collective-permute-start.18 = (bf16[4,192,768]{2,1,0:T(8,128)(2,1)}, bf16[4,192,768]{2,1,0:T(8,128)(2,1)S(1)}, u32[]{:S(2)}, u32[]{:S(2)}) collective-permute-start(bf16[4,192,768]{2,1,0:T(8,128)(2,1)} %get-tuple-element.251), channel_id=1, source_target_pairs={{0,1},{1,0},{2,3},{3,2},{4,5},{5,4},{6,7},{7,6},{8,9},{9,8},{10,11... | collective-permute-start | bytes 3538952 | tf_op jit(solution)/shard_map/ppermute | solution.py:739
  113.4 14.7 %collective-permute-start.19 = (bf16[4,192,768]{2,1,0:T(8,128)(2,1)}, bf16[4,192,768]{2,1,0:T(8,128)(2,1)S(1)}, u32[]{:S(2)}, u32[]{:S(2)}) collective-permute-start(bf16[4,192,768]{2,1,0:T(8,128)(2,1)} %get-tuple-element.252), channel_id=1, source_target_pairs={{0,1},{1,0},{2,3},{3,2},{4,5},{5,4},{6,7},{7,6},{8,9},{9,8},{10,11... | collective-permute-start | bytes 3538952 | tf_op jit(solution)/shard_map/ppermute | solution.py:739
  128.1 21.0 %collective-permute-start.20 = (bf16[4,144,768]{2,1,0:T(8,128)(2,1)}, bf16[4,144,768]{2,1,0:T(8,128)(2,1)}, u32[]{:S(2)}, u32[]{:S(2)}) collective-permute-start(bf16[4,144,768]{2,1,0:T(8,128)(2,1)} %get-tuple-element.263), channel_id=1, source_target_pairs={{0,1},{1,0},{2,3},{3,2},{4,5},{5,4},{6,7},{7,6},{8,9},{9,8},{10,11... | collective-permute-start | bytes 2654216 | tf_op jit(solution)/shard_map/ppermute | solution.py:739
  133.1 16.0 %collective-permute-start.21 = (bf16[1,1,2,192,768]{4,3,2,1,0:T(8,128)(2,1)}, bf16[1,1,2,192,768]{4,3,2,1,0:T(8,128)(2,1)S(1)}, u32[]{:S(2)}, u32[]{:S(2)}) collective-permute-start(bf16[1,1,2,192,768]{4,3,2,1,0:T(8,128)(2,1)} %get-tuple-element.264), channel_id=1, source_target_pairs={{0,4},{4,0},{8,12},{12,8},{16,20},{20,16},{24,28},{28,24},{1,5},{5... | collective-permute-start | bytes 1769480 | tf_op jit(solution)/shard_map/ppermute | solution.py:742
  134.1 29.4 %collective-permute-start.22 = (bf16[1,2,1,192,768]{4,3,1,2,0:T(8,128)(2,1)}, bf16[1,2,1,192,768]{4,3,1,2,0:T(8,128)(2,1)}, u32[]{:S(2)}, u32[]{:S(2)}) collective-permute-start(bf16[1,2,1,192,768]{4,3,1,2,0:T(8,128)(2,1)} %bitcast.209), channel_id=1, source_target_pairs={{0,8},{4,12},{8,0},{12,4},{16,24},{20,28},{24,16},{28,20},{1,9},{5... | collective-permute-start | bytes 1769480 | tf_op jit(solution)/shard_map/ppermute | solution.py:742
  135.7 27.9 %collective-permute-start.23 = (bf16[1,2,1,192,768]{4,3,1,2,0:T(8,128)(2,1)}, bf16[1,2,1,192,768]{4,3,1,2,0:T(8,128)(2,1)}, u32[]{:S(2)}, u32[]{:S(2)}) collective-permute-start(bf16[1,2,1,192,768]{4,3,1,2,0:T(8,128)(2,1)} %bitcast.208), channel_id=1, source_target_pairs={{0,8},{4,12},{8,0},{12,4},{16,24},{20,28},{24,16},{28,20},{1,9},{5... | collective-permute-start | bytes 1769480 | tf_op jit(solution)/shard_map/ppermute | solution.py:742
  152.8 15.6 %collective-permute-start.24 = (bf16[1,1,1,192,768]{4,3,2,1,0:T(8,128)(2,1)}, bf16[1,1,1,192,768]{4,3,2,1,0:T(8,128)(2,1)S(1)}, u32[]{:S(2)}, u32[]{:S(2)}) collective-permute-start(bf16[1,1,1,192,768]{4,3,2,1,0:T(8,128)(2,1)} %get-tuple-element.283), channel_id=1, source_target_pairs={{0,8},{4,12},{8,0},{12,4},{16,24},{20,28},{24,16},{28,20},{1,9},{5... | collective-permute-start | bytes 884744 | tf_op jit(solution)/shard_map/ppermute | solution.py:742
  154.4 16.3 %copy-start.3 = (bf16[2,4,192,768]{3,2,1,0:T(8,128)(2,1)S(1)}, bf16[2,4,192,768]{3,2,1,0:T(8,128)(2,1)}, u32[]{:S(2)}) copy-start(bf16[2,4,192,768]{3,2,1,0:T(8,128)(2,1)} %get-tuple-element.254) | copy-start | bytes 7077892
  163.5 7.1 %copy-start.10 = (bf16[4,192,768]{2,1,0:T(8,128)(2,1)S(1)}, bf16[4,192,768]{2,1,0:T(8,128)(2,1)}, u32[]{:S(2)}) copy-start(bf16[4,192,768]{2,1,0:T(8,128)(2,1)} %copy-done.9) | copy-start | bytes 3538948
  168.4 5.8 %collective-permute-start.27 = (bf16[2,4,80,768]{3,2,1,0:T(8,128)(2,1)}, bf16[2,4,80,768]{3,2,1,0:T(8,128)(2,1)S(1)}, u32[]{:S(2)}, u32[]{:S(2)}) collective-permute-start(bf16[2,4,80,768]{3,2,1,0:T(8,128)(2,1)} %get-tuple-element.293), channel_id=1, source_target_pairs={{0,1},{1,0},{2,3},{3,2},{4,5},{5,4},{6,7},{7,6},{8,9},{9,8},{10,11... | collective-permute-start | bytes 2949128 | tf_op jit(solution)/shard_map/ppermute | solution.py:739
  168.4 25.5 %collective-permute-start.26 = (bf16[1,2,2,144,768]{4,3,2,1,0:T(8,128)(2,1)}, bf16[1,2,2,144,768]{4,3,2,1,0:T(8,128)(2,1)S(1)}, u32[]{:S(2)}, u32[]{:S(2)}) collective-permute-start(bf16[1,2,2,144,768]{4,3,2,1,0:T(8,128)(2,1)} %get-tuple-element.291), channel_id=1, source_target_pairs={{0,2},{1,3},{2,0},{3,1},{4,6},{5,7},{6,4},{7,5},{8,10},{9,11},{10,... | collective-permute-start | bytes 2654216 | tf_op jit(solution)/shard_map/ppermute | solution.py:739
  169.1 24.8 %collective-permute-start.25 = (bf16[4,144,768]{2,1,0:T(8,128)(2,1)}, bf16[4,144,768]{2,1,0:T(8,128)(2,1)S(1)}, u32[]{:S(2)}, u32[]{:S(2)}) collective-permute-start(bf16[4,144,768]{2,1,0:T(8,128)(2,1)} %get-tuple-element.290), channel_id=1, source_target_pairs={{0,1},{1,0},{2,3},{3,2},{4,5},{5,4},{6,7},{7,6},{8,9},{9,8},{10,11... | collective-permute-start | bytes 2654216 | tf_op jit(solution)/shard_map/ppermute | solution.py:739
  172.1 9.9 %collective-permute-start.32 = (bf16[1,1,1,192,768]{4,3,1,2,0:T(8,128)(2,1)S(1)}, bf16[1,1,1,192,768]{4,3,1,2,0:T(8,128)(2,1)S(1)}, u32[]{:S(2)}, u32[]{:S(2)}) collective-permute-start(bf16[1,1,1,192,768]{4,3,1,2,0:T(8,128)(2,1)S(1)} %get-tuple-element.301), channel_id=1, source_target_pairs={{0,4},{4,0},{8,12},{12,8},{16,20},{20,16},{24,28},{28,24},{1,5},{5... | collective-permute-start | bytes 884744 | tf_op jit(solution)/shard_map/ppermute | solution.py:742
  173.3 14.6 %collective-permute-start.29 = (bf16[1,1,1,192,768]{4,3,1,2,0:T(8,128)(2,1)S(1)}, bf16[1,1,1,192,768]{4,3,1,2,0:T(8,128)(2,1)S(1)}, u32[]{:S(2)}, u32[]{:S(2)}) collective-permute-start(bf16[1,1,1,192,768]{4,3,1,2,0:T(8,128)(2,1)S(1)} %get-tuple-element.302), channel_id=1, source_target_pairs={{0,4},{4,0},{8,12},{12,8},{16,20},{20,16},{24,28},{28,24},{1,5},{5... | collective-permute-start | bytes 884744 | tf_op jit(solution)/shard_map/ppermute | solution.py:742
  174.3 19.6 %copy-start.28 = (bf16[4,144,768]{2,1,0:T(8,128)(2,1)S(1)}, bf16[4,144,768]{2,1,0:T(8,128)(2,1)}, u32[]{:S(2)}) copy-start(bf16[4,144,768]{2,1,0:T(8,128)(2,1)} %get-tuple-element.289) | copy-start | bytes 2654212
  174.3 17.9 %collective-permute-start.28 = (bf16[2,2,1,80,768]{4,3,1,2,0:T(8,128)(2,1)S(1)}, bf16[2,2,1,80,768]{4,3,1,2,0:T(8,128)(2,1)S(1)}, u32[]{:S(2)}, u32[]{:S(2)}) collective-permute-start(bf16[2,2,1,80,768]{4,3,1,2,0:T(8,128)(2,1)S(1)} %add_convert_fusion), channel_id=1, source_target_pairs={{0,8},{4,12},{8,0},{12,4},{16,24},{20,28},{24,16},{28,20},{1,9},{5... | collective-permute-start | bytes 1474568 | tf_op jit(solution)/shard_map/ppermute | solution.py:742
  182.0 35.9 %collective-permute-start.40 = (bf16[1,1,1,192,768]{4,3,2,1,0:T(8,128)(2,1)S(1)}, bf16[1,1,1,192,768]{4,3,2,1,0:T(8,128)(2,1)S(1)}, u32[]{:S(2)}, u32[]{:S(2)}) collective-permute-start(bf16[1,1,1,192,768]{4,3,2,1,0:T(8,128)(2,1)S(1)} %add_convert_fusion.8), channel_id=1, source_target_pairs={{0,16},{4,20},{8,24},{12,28},{16,0},{20,4},{24,8},{28,12},{1,17},{... | collective-permute-start | bytes 884744 | tf_op jit(solution)/shard_map/ppermute | solution.py:742
  189.1 10.0 %collective-permute-start.33 = (bf16[1,1,1,192,768]{4,3,1,2,0:T(8,128)(2,1)S(1)}, bf16[1,1,1,192,768]{4,3,1,2,0:T(8,128)(2,1)S(1)}, u32[]{:S(2)}, u32[]{:S(2)}) collective-permute-start(bf16[1,1,1,192,768]{4,3,1,2,0:T(8,128)(2,1)S(1)} %add_convert_fusion.5), channel_id=1, source_target_pairs={{0,2},{1,3},{2,0},{3,1},{4,6},{5,7},{6,4},{7,5},{8,10},{9,11},{10,... | collective-permute-start | bytes 884744 | tf_op jit(solution)/shard_map/ppermute | solution.py:739
  192.3 10.7 %collective-permute-start.31 = (bf16[1,2,1,80,768]{4,3,1,2,0:T(8,128)(2,1)S(1)}, bf16[1,2,1,80,768]{4,3,1,2,0:T(8,128)(2,1)S(1)}, u32[]{:S(2)}, u32[]{:S(2)}) collective-permute-start(bf16[1,2,1,80,768]{4,3,1,2,0:T(8,128)(2,1)S(1)} %add_convert_fusion.9), channel_id=1, source_target_pairs={{0,2},{1,3},{2,0},{3,1},{4,6},{5,7},{6,4},{7,5},{8,10},{9,11},{10,... | collective-permute-start | bytes 737288 | tf_op jit(solution)/shard_map/ppermute | solution.py:739
  194.1 10.9 %collective-permute-start.30 = (bf16[1,1,2,144,768]{4,3,2,1,0:T(8,128)(2,1)S(1)}, bf16[1,1,2,144,768]{4,3,2,1,0:T(8,128)(2,1)S(1)}, u32[]{:S(2)}, u32[]{:S(2)}) collective-permute-start(bf16[1,1,2,144,768]{4,3,2,1,0:T(8,128)(2,1)S(1)} %add_convert_fusion.1), channel_id=1, source_target_pairs={{0,4},{4,0},{8,12},{12,8},{16,20},{20,16},{24,28},{28,24},{1,5},{5... | collective-permute-start | bytes 1327112 | tf_op jit(solution)/shard_map/ppermute | solution.py:742
  195.3 15.5 %collective-permute-start.35 = (bf16[8,896]{1,0:T(8,128)(2,1)S(1)}, bf16[8,896]{1,0:T(8,128)(2,1)S(1)}, u32[]{:S(2)}, u32[]{:S(2)}) collective-permute-start(bf16[8,896]{1,0:T(8,128)(2,1)S(1)} %copy-done.33), channel_id=1, source_target_pairs={{0,16},{4,20},{8,24},{12,28},{16,0},{20,4},{24,8},{28,12},{1,17},{... | collective-permute-start | bytes 43016 | tf_op jit(solution)/shard_map/ppermute | solution.py:742
  200.2 27.3 %collective-permute-start.43 = (bf16[1,1,1,192,768]{4,3,1,2,0:T(8,128)(2,1)S(1)}, bf16[1,1,1,192,768]{4,3,1,2,0:T(8,128)(2,1)S(1)}, u32[]{:S(2)}, u32[]{:S(2)}) collective-permute-start(bf16[1,1,1,192,768]{4,3,1,2,0:T(8,128)(2,1)S(1)} %add_convert_fusion.4), channel_id=1, source_target_pairs={{0,16},{4,20},{8,24},{12,28},{16,0},{20,4},{24,8},{28,12},{1,17},{... | collective-permute-start | bytes 884744 | tf_op jit(solution)/shard_map/ppermute | solution.py:742
  203.1 4.9 %collective-permute-start.36 = (bf16[1,1,1,80,768]{4,3,1,2,0:T(8,128)(2,1)S(1)}, bf16[1,1,1,80,768]{4,3,1,2,0:T(8,128)(2,1)S(1)}, u32[]{:S(2)}, u32[]{:S(2)}) collective-permute-start(bf16[1,1,1,80,768]{4,3,1,2,0:T(8,128)(2,1)S(1)} %add_convert_fusion.15), channel_id=1, source_target_pairs={{0,4},{4,0},{8,12},{12,8},{16,20},{20,16},{24,28},{28,24},{1,5},{5... | collective-permute-start | bytes 368648 | tf_op jit(solution)/shard_map/ppermute | solution.py:742
  205.1 10.8 %collective-permute-start.34 = (bf16[1,1,1,144,768]{4,3,2,1,0:T(8,128)(2,1)S(1)}, bf16[1,1,1,144,768]{4,3,2,1,0:T(8,128)(2,1)S(1)}, u32[]{:S(2)}, u32[]{:S(2)}) collective-permute-start(bf16[1,1,1,144,768]{4,3,2,1,0:T(8,128)(2,1)S(1)} %add_convert_fusion.12), channel_id=1, source_target_pairs={{0,8},{4,12},{8,0},{12,4},{16,24},{20,28},{24,16},{28,20},{1,9},{5... | collective-permute-start | bytes 663560 | tf_op jit(solution)/shard_map/ppermute | solution.py:742
  208.1 17.2 %collective-permute-start.39 = (bf16[1,1,1,80,768]{4,3,1,2,0:T(8,128)(2,1)S(1)}, bf16[1,1,1,80,768]{4,3,1,2,0:T(8,128)(2,1)S(1)}, u32[]{:S(2)}, u32[]{:S(2)}) collective-permute-start(bf16[1,1,1,80,768]{4,3,1,2,0:T(8,128)(2,1)S(1)} %add_convert_fusion.14), channel_id=1, source_target_pairs={{0,16},{4,20},{8,24},{12,28},{16,0},{20,4},{24,8},{28,12},{1,17},{... | collective-permute-start | bytes 368648 | tf_op jit(solution)/shard_map/ppermute | solution.py:742
  210.8 15.6 %collective-permute-start.38 = (bf16[16,896]{1,0:T(8,128)(2,1)S(1)}, bf16[16,896]{1,0:T(8,128)(2,1)S(1)}, u32[]{:S(2)}, u32[]{:S(2)}) collective-permute-start(bf16[16,896]{1,0:T(8,128)(2,1)S(1)} %pad_maximum_fusion.10), channel_id=1, source_target_pairs={{0,8},{4,12},{8,0},{12,4},{16,24},{20,28},{24,16},{28,20},{1,9},{5... | collective-permute-start | bytes 86024 | tf_op jit(solution)/shard_map/ppermute | solution.py:742
  216.1 15.6 %collective-permute-start.37 = (bf16[1,1,1,144,768]{4,3,2,1,0:T(8,128)(2,1)S(1)}, bf16[1,1,1,144,768]{4,3,2,1,0:T(8,128)(2,1)S(1)}, u32[]{:S(2)}, u32[]{:S(2)}) collective-permute-start(bf16[1,1,1,144,768]{4,3,2,1,0:T(8,128)(2,1)S(1)} %add_convert_fusion.11), channel_id=1, source_target_pairs={{0,16},{4,20},{8,24},{12,28},{16,0},{20,4},{24,8},{28,12},{1,17},{... | collective-permute-start | bytes 663560 | tf_op jit(solution)/shard_map/ppermute | solution.py:742
  217.9 14.9 %collective-permute-start.48 = (bf16[1,1,1,192,768]{4,3,2,1,0:T(8,128)(2,1)S(1)}, bf16[1,1,1,192,768]{4,3,2,1,0:T(8,128)(2,1)S(1)}, u32[]{:S(2)}, u32[]{:S(2)}) collective-permute-start(bf16[1,1,1,192,768]{4,3,2,1,0:T(8,128)(2,1)S(1)} %add_convert_fusion.3), channel_id=1, source_target_pairs={{0,8},{4,12},{8,0},{12,4},{16,24},{20,28},{24,16},{28,20},{1,9},{5... | collective-permute-start | bytes 884744 | tf_op jit(solution)/shard_map/ppermute | solution.py:742
  225.3 4.9 %collective-permute-start.42 = (bf16[1,1,1,80,768]{4,3,1,2,0:T(8,128)(2,1)S(1)}, bf16[1,1,1,80,768]{4,3,1,2,0:T(8,128)(2,1)S(1)}, u32[]{:S(2)}, u32[]{:S(2)}) collective-permute-start(bf16[1,1,1,80,768]{4,3,1,2,0:T(8,128)(2,1)S(1)} %add_convert_fusion.13), channel_id=1, source_target_pairs={{0,4},{4,0},{8,12},{12,8},{16,20},{20,16},{24,28},{28,24},{1,5},{5... | collective-permute-start | bytes 368648 | tf_op jit(solution)/shard_map/ppermute | solution.py:742
  226.4 4.9 %collective-permute-start.41 = (bf16[32,896]{1,0:T(8,128)(2,1)S(1)}, bf16[32,896]{1,0:T(8,128)(2,1)S(1)}, u32[]{:S(2)}, u32[]{:S(2)}) collective-permute-start(bf16[32,896]{1,0:T(8,128)(2,1)S(1)} %pad_maximum_fusion.9), channel_id=1, source_target_pairs={{0,4},{4,0},{8,12},{12,8},{16,20},{20,16},{24,28},{28,24},{1,5},{5... | collective-permute-start | bytes 172040 | tf_op jit(solution)/shard_map/ppermute | solution.py:742
  227.6 10.9 %collective-permute-start.45 = (bf16[1,1,1,192,768]{4,3,1,2,0:T(8,128)(2,1)S(1)}, bf16[1,1,1,192,768]{4,3,1,2,0:T(8,128)(2,1)S(1)}, u32[]{:S(2)}, u32[]{:S(2)}) collective-permute-start(bf16[1,1,1,192,768]{4,3,1,2,0:T(8,128)(2,1)S(1)} %add_convert_fusion.2), channel_id=1, source_target_pairs={{0,4},{4,0},{8,12},{12,8},{16,20},{20,16},{24,28},{28,24},{1,5},{5... | collective-permute-start | bytes 884744 | tf_op jit(solution)/shard_map/ppermute | solution.py:742
  230.3 7.8 %collective-permute-start.46 = (bf16[1,2,1,80,768]{4,3,1,2,0:T(8,128)(2,1)S(1)}, bf16[1,2,1,80,768]{4,3,1,2,0:T(8,128)(2,1)S(1)}, u32[]{:S(2)}, u32[]{:S(2)}) collective-permute-start(bf16[1,2,1,80,768]{4,3,1,2,0:T(8,128)(2,1)S(1)} %pad_maximum_fusion.5), channel_id=1, source_target_pairs={{0,8},{4,12},{8,0},{12,4},{16,24},{20,28},{24,16},{28,20},{1,9},{5... | collective-permute-start | bytes 737288 | tf_op jit(solution)/shard_map/ppermute | solution.py:742
  231.4 4.9 %collective-permute-start.47 = (bf16[64,896]{1,0:T(8,128)(2,1)S(1)}, bf16[64,896]{1,0:T(8,128)(2,1)S(1)}, u32[]{:S(2)}, u32[]{:S(2)}) collective-permute-start(bf16[64,896]{1,0:T(8,128)(2,1)S(1)} %pad_maximum_fusion.8), channel_id=1, source_target_pairs={{0,2},{1,3},{2,0},{3,1},{4,6},{5,7},{6,4},{7,5},{8,10},{9,11},{10,... | collective-permute-start | bytes 344072 | tf_op jit(solution)/shard_map/ppermute | solution.py:739
  231.7 9.4 %collective-permute-start.44 = (bf16[1,1,1,144,768]{4,3,2,1,0:T(8,128)(2,1)S(1)}, bf16[1,1,1,144,768]{4,3,2,1,0:T(8,128)(2,1)S(1)}, u32[]{:S(2)}, u32[]{:S(2)}) collective-permute-start(bf16[1,1,1,144,768]{4,3,2,1,0:T(8,128)(2,1)S(1)} %add_convert_fusion.10), channel_id=1, source_target_pairs={{0,8},{4,12},{8,0},{12,4},{16,24},{20,28},{24,16},{28,20},{1,9},{5... | collective-permute-start | bytes 663560 | tf_op jit(solution)/shard_map/ppermute | solution.py:742
  232.9 16.6 %collective-permute-start.54 = (bf16[1,1,2,192,768]{4,3,2,1,0:T(8,128)(2,1)S(1)}, bf16[1,1,2,192,768]{4,3,2,1,0:T(8,128)(2,1)S(1)}, u32[]{:S(2)}, u32[]{:S(2)}) collective-permute-start(bf16[1,1,2,192,768]{4,3,2,1,0:T(8,128)(2,1)S(1)} %pad_maximum_fusion.1), channel_id=1, source_target_pairs={{0,4},{4,0},{8,12},{12,8},{16,20},{20,16},{24,28},{28,24},{1,5},{5... | collective-permute-start | bytes 1769480 | tf_op jit(solution)/shard_map/ppermute | solution.py:742
  236.2 5.4 %collective-permute-start.52 = (bf16[128,896]{1,0:T(8,128)(2,1)S(1)}, bf16[128,896]{1,0:T(8,128)(2,1)S(1)}, u32[]{:S(2)}, u32[]{:S(2)}) collective-permute-start(bf16[128,896]{1,0:T(8,128)(2,1)S(1)} %pad_maximum_fusion.6), channel_id=1, source_target_pairs={{0,1},{1,0},{2,3},{3,2},{4,5},{5,4},{6,7},{7,6},{8,9},{9,8},{10,11... | collective-permute-start | bytes 688136 | tf_op jit(solution)/shard_map/ppermute | solution.py:739
  238.2 5.7 %collective-permute-start.50 = (bf16[1,4,32,768]{3,2,1,0:T(8,128)(2,1)S(1)}, bf16[1,4,32,768]{3,2,1,0:T(8,128)(2,1)S(1)}, u32[]{:S(2)}, u32[]{:S(2)}) collective-permute-start(bf16[1,4,32,768]{3,2,1,0:T(8,128)(2,1)S(1)} %bitcast.198), channel_id=1, source_target_pairs={{0,2},{1,3},{2,0},{3,1},{4,6},{5,7},{6,4},{7,5},{8,10},{9,11},{10,... | collective-permute-start | bytes 589832 | tf_op jit(solution)/shard_map/ppermute | solution.py:739
  238.5 15.0 %collective-permute-start.53 = (bf16[1,2,1,192,768]{4,3,1,2,0:T(8,128)(2,1)S(1)}, bf16[1,2,1,192,768]{4,3,1,2,0:T(8,128)(2,1)S(1)}, u32[]{:S(2)}, u32[]{:S(2)}) collective-permute-start(bf16[1,2,1,192,768]{4,3,1,2,0:T(8,128)(2,1)S(1)} %pad_maximum_fusion.2), channel_id=1, source_target_pairs={{0,8},{4,12},{8,0},{12,4},{16,24},{20,28},{24,16},{28,20},{1,9},{5... | collective-permute-start | bytes 1769480 | tf_op jit(solution)/shard_map/ppermute | solution.py:742
  241.2 16.5 %collective-permute-start.49 = (bf16[1,1,2,144,768]{4,3,2,1,0:T(8,128)(2,1)S(1)}, bf16[1,1,2,144,768]{4,3,2,1,0:T(8,128)(2,1)}, u32[]{:S(2)}, u32[]{:S(2)}) collective-permute-start(bf16[1,1,2,144,768]{4,3,2,1,0:T(8,128)(2,1)S(1)} %pad_maximum_fusion.3), channel_id=1, source_target_pairs={{0,4},{4,0},{8,12},{12,8},{16,20},{20,16},{24,28},{28,24},{1,5},{5... | collective-permute-start | bytes 1327112 | tf_op jit(solution)/shard_map/ppermute | solution.py:742
  243.9 13.8 %collective-permute-start.51 = (bf16[2,4,32,768]{3,2,1,0:T(8,128)(2,1)S(1)}, bf16[2,4,32,768]{3,2,1,0:T(8,128)(2,1)}, u32[]{:S(2)}, u32[]{:S(2)}) collective-permute-start(bf16[2,4,32,768]{3,2,1,0:T(8,128)(2,1)S(1)} %pad_maximum_fusion.4.all_ref), channel_id=1, source_target_pairs={{0,1},{1,0},{2,3},{3,2},{4,5},{5,4},{6,7},{7,6},{8,9},{9,8},{10,11... | collective-permute-start | bytes 1179656 | tf_op jit(solution)/shard_map/ppermute | solution.py:739
  254.4 6.8 %copy-start.1 = (bf16[1000,768]{1,0:T(8,128)(2,1)S(1)}, bf16[1000,768]{1,0:T(8,128)(2,1)}, u32[]{:S(2)}) copy-start(bf16[1000,768]{1,0:T(8,128)(2,1)} %param.29) | copy-start | bytes 4608004
  (29 other events, 76.4 us)
